TPU v7x, 256 devices: a whole 4x4x8 slice. The times are simulated.
256 devices in a mesh: blk: 32 (over x_lo, z, core), tp: 8 (over x_hi, y).
Axes of the slice: x: 4 (x_hi: 2, x_lo: 2; x = x_hi * 2 + x_lo), y: 4, z: 8, core: 2. Of those that a mesh axis runs over, the one named last changes fastest.
Arguments:
- tokens: bfloat16 [8192, 8192], P('blk', 'tp'), may hold values from -6 to 6
- weight: bfloat16 [8192, 2048], P('tp'), may hold values from -0.0625 to 0.0625
- bank_a: bfloat16 [32, 8192, 32], P('blk', 'tp'), may hold values from -0.0625 to 0.0625
- bank_b: bfloat16 [32, 32, 1024], P('blk'), may hold values from -1.5 to 1.5
- tile_map: int32 [64, 1], P('blk'), may hold values from 0 to 31
- grad_out: bfloat16 [8192, 2048], P(('blk', 'tp')), may hold values from -6 to 6
Outputs:
- key_value_output: bfloat16 [8192, 2048], P(('blk', 'tp'))
- token_gradient: bfloat16 [8192, 8192], P('blk', 'tp')
- grad_a: float32 [32, 8192, 32], P('blk', 'tp')
- grad_b: float32 [32, 32, 1024], P('blk', None, 'tp')
Inputs may be any that keep to these rules, and one draw needn't show every extreme that they name: `tile_map`: every one of the 32 adapters is the adapter of at least one tile.
All inputs are finite; a program needn't handle non-finite values.
Results may differ from a plain program's by a relative error of at most 0.003.
Values may be sent and summed in bfloat16 or wider, within the bound.
A program may use at most 64 MiB of HBM per device.

v0:
```python
import jax
import jax.numpy as jnp
from jax import lax
from jax.sharding import PartitionSpec as P

adapter_scale = 0.5


def on_device(tokens, weight, bank_a, bank_b, tile_map, grad_out):
    tile_index_list = tile_map[:, 0]
    grouped_row_count = tokens.shape[0]
    feature_shard = tokens.shape[1]
    tile_count = tile_index_list.shape[0]
    tile_rows = grouped_row_count // tile_count
    rank_two = bank_a.shape[2]
    rank_one = rank_two // 2
    kv_width = bank_b.shape[2]
    tp_count = lax.axis_size("tp")
    local_row_block = grouped_row_count // tp_count
    kv_dev = kv_width // tp_count
    adapt_local = bank_a.shape[0]
    empty = (
        jnp.zeros((tile_count, feature_shard, rank_two), jnp.bfloat16),
        jnp.zeros((tile_count, rank_two, kv_width), jnp.bfloat16),
    )
    whole_a, whole_b = (
        lax.all_gather(bank_a, "blk", axis=0, tiled=True),
        lax.all_gather(bank_b, "blk", axis=0, tiled=True),
    )
    pieces = (whole_a, whole_b)
    piece_rows = pieces[0].shape[0]
    one_hot = (tile_index_list[:, None] == jnp.arange(piece_rows, dtype=jnp.int32)[None, :]).astype(
        jnp.bfloat16
    )
    picked_a = jnp.dot(
        one_hot, pieces[0].reshape(piece_rows, -1), preferred_element_type=jnp.float32
    )
    picked_b = jnp.dot(
        one_hot, pieces[1].reshape(piece_rows, -1), preferred_element_type=jnp.float32
    )
    factor_down = picked_a.reshape(empty[0].shape).astype(jnp.bfloat16)
    fac_b = picked_b.reshape(empty[1].shape).astype(jnp.bfloat16)
    token_tile_index = tokens.reshape(tile_count, tile_rows, feature_shard)
    rank_part = jnp.einsum(
        "tre,tek->trk", token_tile_index, factor_down, preferred_element_type=jnp.float32
    )
    rank_act = lax.psum(rank_part, "tp").astype(jnp.bfloat16)
    base_local_rows = lax.psum_scatter(
        jnp.dot(tokens, weight, preferred_element_type=jnp.float32),
        "tp",
        scatter_dimension=0,
        tiled=True,
    )
    adapter_complete = jnp.concatenate(
        [
            jnp.einsum(
                "trk,tkc->trc",
                rank_act[:, :, :rank_one],
                fac_b[:, :rank_one],
                preferred_element_type=jnp.float32,
            ),
            jnp.einsum(
                "trk,tkc->trc",
                rank_act[:, :, rank_one:],
                fac_b[:, rank_one:],
                preferred_element_type=jnp.float32,
            ),
        ],
        axis=2,
    ).reshape(grouped_row_count, 2 * kv_width)
    first_row_index = lax.axis_index("tp") * local_row_block
    adapter_local_rows = lax.dynamic_slice_in_dim(
        adapter_complete, first_row_index, local_row_block, 0
    )
    key_value_output = (base_local_rows + adapter_scale * adapter_local_rows).astype(jnp.bfloat16)
    grad_rows = lax.all_gather(grad_out, "tp", axis=0, tiled=True)
    gradient_per_tile = grad_rows.reshape(tile_count, tile_rows, 2 * kv_width)
    low_rank_gradient = jnp.concatenate(
        [
            jnp.einsum(
                "trc,tkc->trk",
                gradient_per_tile[:, :, :kv_width],
                fac_b[:, :rank_one],
                preferred_element_type=jnp.float32,
            ),
            jnp.einsum(
                "trc,tkc->trk",
                gradient_per_tile[:, :, kv_width:],
                fac_b[:, rank_one:],
                preferred_element_type=jnp.float32,
            ),
        ],
        axis=2,
    ).astype(jnp.bfloat16)
    backward_pass = jnp.einsum("rc,ec->re", grad_rows, weight, preferred_element_type=jnp.float32)
    backward_adapter_term = jnp.einsum(
        "qdu,qyu->qdy", low_rank_gradient, factor_down, preferred_element_type=jnp.float32
    )
    token_gradient = (
        backward_pass
        + adapter_scale * backward_adapter_term.reshape(grouped_row_count, feature_shard)
    ).astype(jnp.bfloat16)
    tile_down_gradient = adapter_scale * jnp.einsum(
        "tre,trk->tek", token_tile_index, low_rank_gradient, preferred_element_type=jnp.float32
    )
    col_start = lax.axis_index("tp") * kv_dev
    key_cols = lax.dynamic_slice_in_dim(gradient_per_tile[:, :, :kv_width], col_start, kv_dev, 2)
    value_cols = lax.dynamic_slice_in_dim(gradient_per_tile[:, :, kv_width:], col_start, kv_dev, 2)
    tile_up_gradient = adapter_scale * jnp.concatenate(
        [
            jnp.einsum(
                "trk,trc->tkc",
                rank_act[:, :, :rank_one],
                key_cols,
                preferred_element_type=jnp.float32,
            ),
            jnp.einsum(
                "trk,trc->tkc",
                rank_act[:, :, rank_one:],
                value_cols,
                preferred_element_type=jnp.float32,
            ),
        ],
        axis=1,
    )
    size_a = feature_shard * rank_two
    flat_grads = jnp.concatenate(
        [tile_down_gradient.reshape(tile_count, -1), tile_up_gradient.reshape(tile_count, -1)],
        axis=1,
    )
    one_hot = (
        tile_index_list[:, None]
        == jnp.arange(adapt_local * lax.axis_size("blk"), dtype=jnp.int32)[None, :]
    ).astype(jnp.float32)
    summed = lax.psum_scatter(
        jnp.dot(
            one_hot.T,
            flat_grads,
            precision=lax.Precision.HIGHEST,
            preferred_element_type=jnp.float32,
        ),
        "blk",
        scatter_dimension=0,
        tiled=True,
    )
    grad_a = summed[:, :size_a].reshape(adapt_local, feature_shard, rank_two)
    grad_b = summed[:, size_a:].reshape(adapt_local, rank_two, kv_dev)
    return (key_value_output, token_gradient, grad_a, grad_b)


def solution(mesh):
    in_specs = (
        P("blk", "tp"),
        P("tp", None),
        P("blk", "tp", None),
        P("blk", None, None),
        P("blk", None),
        P(("blk", "tp"), None),
    )
    out_specs = (P(("blk", "tp"), None), P("blk", "tp"), P("blk", "tp", None), P("blk", None, "tp"))
    return jax.shard_map(
        on_device, mesh=mesh, in_specs=in_specs, out_specs=out_specs, check_vma=False
    )
```

profile of v0, /device:TPU:2, one launch (start us, length us, event | category | flops | bytes accessed | tf_op | source)
XLA Modules:
  0.0 529.2 jit_solution(16734941255564982452)
XLA Ops:
  7.2 0.7 all-gather.8.cloned.1.call-update
  8.0 0.7 all-gather.4.cloned.1.call-update
  8.7 0.7 all-gather.6.cloned.1.call-update
  9.5 4.8 fusion.45
  14.3 49.8 %all-gather.8.cloned.1.call-done = bf16[256,2048]{1,0:T(8,128)(2,1)} async-done(((bf16[32,2048]{1,0:T(8,128)(2,1)}), bf16[256,2048]{1,0:T(8,128)(2,1)}) %all-gather.8.cloned.1.call-update) | async-done | bytes 1048592 | tf_op jit(solution)/shard_map/all_gather | solution.py:76
  64.1 2.1 fusion.43
  66.2 63.8 %all-gather.4.cloned.1.call-done = bf16[32,1024,32]{1,2,0:T(8,128)(2,1)} async-done(((bf16[1,1024,32]{1,2,0:T(8,128)(2,1)}), bf16[32,1024,32]{1,2,0:T(8,128)(2,1)}) %all-gather.4.cloned.1.call-update) | async-done | bytes 2097168 | tf_op jit(solution)/shard_map/all_gather | solution.py:27
  130.0 7.8 %copy.28 = bf16[32,1024,32]{2,1,0:T(8,128)(2,1)} copy(bf16[32,1024,32]{1,2,0:T(8,128)(2,1)} %all-gather.4.cloned.1.call-done) | data formatting | bytes 4194304 | tf_op jit(solution)/shard_map/all_gather | solution.py:27
  137.7 10.5 %reshape.43 = bf16[32,32768]{1,0:T(8,128)(2,1)S(1)} reshape(bf16[32,1024,32]{2,1,0:T(8,128)(2,1)} %copy.28) | data formatting | bytes 4194304 | tf_op jit(solution)/shard_map/reshape | solution.py:36
  148.3 8.0 %dot_general.58 = bf16[1024,32,32]{1,0,2:T(8,128)(2,1)} reshape(bf16[32768,32]{0,1:T(8,128)(2,1)S(1)} %bitcast.50) | data formatting | bytes 4194304 | tf_op jit(solution)/shard_map/dot_general | solution.py:35
  156.3 7.5 %copy.29 = bf16[1024,32,32]{0,2,1:T(8,128)(2,1)S(1)} copy(bf16[1024,32,32]{1,0,2:T(8,128)(2,1)} %dot_general.58) | data formatting | bytes 4194304 | tf_op jit(solution)/shard_map/dot_general | solution.py:35
  163.9 0.5 convolution_convert_fusion
  164.6 40.9 %psum.7 = bf16[2,128,32]{1,2,0:T(8,128)(2,1)S(1)} all-reduce(f32[2,128,32]{1,2,0:T(8,128)S(1)} %convolution_bitcast_fusion), channel_id=1, replica_groups=mesh['blk'=32,'tp'=8] {'tp'}, use_global_device_ids=true, to_apply=%region_1.0 | all-reduce | flops 8192 | bytes 49152 | tf_op jit(solution)/shard_map/psum | solution.py:47
  205.6 1.0 fusion.16
  206.7 3.9 fusion.5
  211.5 0.3 copy.37
  211.8 0.6 reshape.48
  212.4 3.9 fusion.10
  216.3 0.6 copy-done.5
  217.0 0.6 dynamic-slice
  217.5 0.3 fusion.21
  217.9 0.3 fusion.24
  218.2 0.3 convolution_multiply_fusion
  218.7 1.7 copy-done.4
  220.4 0.4 copy-done.2
  220.8 2.1 fusion.3
  222.9 56.6 %reduce-scatter.2.cloned.1.call-done = f32[32,2048]{1,0:T(8,128)} async-done(((f32[256,2048]{1,0:T(8,128)}), f32[32,2048]{1,0:T(8,128)}) %reduce-scatter.2.cloned.1.call-update) | async-done | bytes 262160 | tf_op jit(solution)/shard_map/reduce_scatter | solution.py:48
  279.5 1.6 add_convert_fusion
  281.1 236.2 %all-reduce.3.cloned.1.call-done = f32[32,36864]{1,0:T(8,128)} async-done(((f32[32,36864]{1,0:T(8,128)}), f32[32,36864]{1,0:T(8,128)}) %all-reduce.3.cloned.1.call-update) | async-done | bytes 4718608
  517.4 2.1 dynamic-slice_reduce_fusion
  519.7 0.8 copy.38
  520.5 2.2 dynamic-slice.3
  (27 shorter events, 1.8 us)
Async XLA Ops:
  7.2 2.3 copy-start
  7.2 56.9 %all-gather.8.cloned.1.call-start = ((), (), s32[]{:S(2)}) async-start(), calls=%async_computation.4 | async-start | bytes 1179648 | tf_op jit(solution)/shard_map/all_gather | solution.py:76
  7.9 122.1 %all-gather.4.cloned.1.call-start = ((), (), s32[]{:S(2)}) async-start(), calls=%async_computation.2 | async-start | bytes 2162688 | tf_op jit(solution)/shard_map/all_gather | solution.py:27
  8.7 198.1 %all-gather.6.cloned.1.call-start = ((), (), s32[]{:S(2)}) async-start(), calls=%async_computation.3 | async-start | bytes 2162688 | tf_op jit(solution)/shard_map/all_gather | solution.py:28
  9.4 270.1 %reduce-scatter.2.cloned.1.call-start = ((), (), s32[]{:S(2)}) async-start(), calls=%async_computation.1 | async-start | bytes 2359296 | tf_op jit(solution)/shard_map/reduce_scatter | solution.py:48
  14.2 503.1 %all-reduce.3.cloned.1.call-start = ((), (), s32[]{:S(2)}) async-start(), calls=%async_computation.5 | async-start | bytes 9437184
  156.3 7.5 %copy-start.3 = (s32[2,1]{0,1:T(1,128)S(1)}, s32[2,1]{0,1:T(1,128)}, u32[]{:S(2)}) copy-start(s32[2,1]{0,1:T(1,128)} %param.10) | copy-start | bytes 28
  164.3 46.4 %copy-start.1 = (bf16[256,2048]{1,0:T(8,128)(2,1)S(1)}, bf16[256,2048]{1,0:T(8,128)(2,1)}, u32[]{:S(2)}) copy-start(bf16[256,2048]{1,0:T(8,128)(2,1)} %all-gather.8.cloned.1.call-done) | copy-start | bytes 3145732
  216.3 0.7 copy-start.5
  218.2 2.2 copy-start.4
  218.6 2.2 copy-start.2
Sparse Core Ops, SparseCore 0:
  10.7 53.4 all-gather.7
  66.0 63.9 all-gather.3
  131.9 64.3 all-gather.5
  200.1 79.3 reduce-scatter.1
  282.0 235.2 all-reduce.2
where the time goes:
time: 532 us; the launch traced here: 529 us
  waiting for transfers between devices  409 us (77%)
  local copies, waits for them, and re-layouts  45.6 us (9%)
  blocking collectives  40.9 us (8%)
  matrix products  18.2 us (3%)
  between operations  13.9 us (3%)
    unnamed x6, waiting for transfers between devices  238 us
    all_gather x1, waiting for transfers between devices, on_device(): lax.all_gather(bank_a, 'blk', axis=0, tiled=True)  63.8 us
    reduce_scatter x1, waiting for transfers between devices, on_device(): lax.psum_scatter(jnp.dot(tokens, weight, preferred_element_type=jnp.float...  56.6 us
    all_gather x1, waiting for transfers between devices, on_device(): grad_rows = lax.all_gather(grad_out, 'tp', axis=0, tiled=True)  49.8 us
    psum x1, blocking collectives, on_device(): rank_act = lax.psum(rank_part, 'tp').astype(jnp.bfloat16)  40.9 us
    dot_general x2, local copies, waits for them, and re-layouts, on_device(): jnp.dot(one_hot, pieces[0].reshape(piece_rows, -1), preferred_element_typ...  15.6 us
  transfers between devices with their start and end apart: 5, of which 4 were waited for; matrix products, arithmetic and copies ran while one was open for 11% of the time, Pallas kernels for 0%

commit v1 on v0

v1 whole, which is shorter than its diff:
```python
import jax
import jax.numpy as jnp
from jax import lax
from jax.sharding import PartitionSpec as P

adapter_scale = 0.5


def on_device(tokens, weight, bank_a, bank_b, tile_map, grad_out):
    f32, bf16 = jnp.float32, jnp.bfloat16
    tile_ids = tile_map[:, 0]
    rows, feats = tokens.shape
    tiles = tile_ids.shape[0]
    tile_rows = rows // tiles
    rank_two = bank_a.shape[2]
    rank_one = rank_two // 2
    kv_width = bank_b.shape[2]
    tp_count = lax.axis_size("tp")
    tp_id = lax.axis_index("tp")
    kv_dev = kv_width // tp_count
    col0 = tp_id * kv_dev

    b_cols = lax.dynamic_slice_in_dim(bank_b, col0, kv_dev, 2)
    all_b = lax.all_gather(b_cols, "blk", axis=0, tiled=True)
    all_a = lax.all_gather(bank_a, "blk", axis=0, tiled=True)
    grad_rows = lax.all_gather(grad_out, "tp", axis=0, tiled=True)

    fac_a = jnp.stack([all_a[tile_ids[t]] for t in range(tiles)])
    fac_b = jnp.stack([all_b[tile_ids[t]] for t in range(tiles)])

    tok_t = tokens.reshape(tiles, tile_rows, feats)
    g_t = grad_rows.reshape(tiles, tile_rows, 2 * kv_width)
    g_key = lax.dynamic_slice_in_dim(g_t, col0, kv_dev, 2)
    g_val = lax.dynamic_slice_in_dim(g_t, kv_width + col0, kv_dev, 2)

    act_part = jnp.einsum("tre,tek->trk", tok_t, fac_a, preferred_element_type=f32)
    grad_part = jnp.concatenate(
        [
            jnp.einsum("trc,tkc->trk", g_key, fac_b[:, :rank_one], preferred_element_type=f32),
            jnp.einsum("trc,tkc->trk", g_val, fac_b[:, rank_one:], preferred_element_type=f32),
        ],
        axis=2,
    )
    both = lax.psum(jnp.stack([act_part, grad_part]), "tp")
    rank_act = both[0].astype(bf16)
    rank_grad = both[1].astype(bf16)

    lora_key = jnp.einsum(
        "trk,tkc->trc", rank_act[:, :, :rank_one], fac_b[:, :rank_one], preferred_element_type=f32
    ).reshape(rows, kv_dev)
    lora_val = jnp.einsum(
        "trk,tkc->trc", rank_act[:, :, rank_one:], fac_b[:, rank_one:], preferred_element_type=f32
    ).reshape(rows, kv_dev)
    base = jnp.dot(tokens, weight, preferred_element_type=f32)
    base = lax.dynamic_update_slice_in_dim(
        base, lax.dynamic_slice_in_dim(base, col0, kv_dev, 1) + adapter_scale * lora_key, col0, 1
    )
    base = lax.dynamic_update_slice_in_dim(
        base,
        lax.dynamic_slice_in_dim(base, kv_width + col0, kv_dev, 1) + adapter_scale * lora_val,
        kv_width + col0,
        1,
    )
    key_value_output = lax.psum_scatter(base, "tp", scatter_dimension=0, tiled=True).astype(bf16)

    backward = jnp.dot(grad_rows, weight.T, preferred_element_type=f32)
    adapter_back = jnp.einsum("tru,tyu->try", rank_grad, fac_a, preferred_element_type=f32)
    token_gradient = (backward + adapter_scale * adapter_back.reshape(rows, feats)).astype(bf16)

    down_grad = adapter_scale * jnp.einsum("tre,trk->tek", tok_t, rank_grad, preferred_element_type=f32)
    up_grad = adapter_scale * jnp.concatenate(
        [
            jnp.einsum("trk,trc->tkc", rank_act[:, :, :rank_one], g_key, preferred_element_type=f32),
            jnp.einsum("trk,trc->tkc", rank_act[:, :, rank_one:], g_val, preferred_element_type=f32),
        ],
        axis=1,
    )
    size_a = feats * rank_two
    flat = jnp.concatenate([down_grad.reshape(tiles, -1), up_grad.reshape(tiles, -1)], axis=1)
    adapters = bank_a.shape[0] * lax.axis_size("blk")
    one_hot = (tile_ids[:, None] == jnp.arange(adapters, dtype=jnp.int32)[None, :]).astype(f32)
    dense = jnp.dot(one_hot.T, flat, precision=lax.Precision.HIGHEST, preferred_element_type=f32)
    summed = lax.psum_scatter(dense.reshape(adapters, -1, 128), "blk", scatter_dimension=0, tiled=True).reshape(bank_a.shape[0], -1)
    grad_a = summed[:, :size_a].reshape(bank_a.shape[0], feats, rank_two)
    grad_b = summed[:, size_a:].reshape(bank_a.shape[0], rank_two, kv_dev)
    return (key_value_output, token_gradient, grad_a, grad_b)


def solution(mesh):
    in_specs = (
        P("blk", "tp"),
        P("tp", None),
        P("blk", "tp", None),
        P("blk", None, None),
        P("blk", None),
        P(("blk", "tp"), None),
    )
    out_specs = (P(("blk", "tp"), None), P("blk", "tp"), P("blk", "tp", None), P("blk", None, "tp"))
    return jax.shard_map(
        on_device, mesh=mesh, in_specs=in_specs, out_specs=out_specs, check_vma=False
    )
```

time: 532 us -> 387 us (0.73)
  waiting for transfers between devices: 409 us -> 260 us
  blocking collectives: 40.9 us -> 78.1 us
  local copies, waits for them, and re-layouts: 45.6 us -> 12.7 us
    unnamed x6 -> x4, waiting for transfers between devices: 238 us -> 1.41 us
    reduce_scatter x1 -> x2, waiting for transfers between devices: 56.6 us -> 185 us  [the longest x1 123 us: on_device(): lax.psum_scatter(dense.reshape(adapters, -1, 128), 'blk', scatter_dimensi...]
    all_gather x1, waiting for transfers between devices: 49.8 us -> 9.24 us  [on_device(): grad_rows = lax.all_gather(grad_out, 'tp', axis=0, tiled=True)]
    all_gather x0 -> x1, blocking collectives: none -> 37 us  [on_device(): all_b = lax.all_gather(b_cols, 'blk', axis=0, tiled=True)]
    dot_general x2 -> x0, local copies, waits for them, and re-layouts: 15.6 us -> none  [on_device(): jnp.dot(one_hot, pieces[0].reshape(piece_rows, -1), preferred_element_typ...]
    reshape x3 -> x2, local copies, waits for them, and re-layouts: 11.3 us -> 0.74 us  [the longest x1 0.57 us: on_device(): down_grad.reshape(tiles, -1)]
    all_gather x1 -> x0, local copies, waits for them, and re-layouts: 7.76 us -> none  [on_device(): lax.all_gather(bank_a, 'blk', axis=0, tiled=True)]
    dot_general x12 -> x10, matrix products: 17.5 us -> 14.6 us  [the longest x1 4.27 us: on_device(): backward = jnp.dot(grad_rows, weight.T, preferred_element_type=f32)]
  transfers between devices with their start and end apart: 5 -> 4, of which waited for: 4 -> 4; matrix products, arithmetic and copies ran while one was open for 11% -> 6% of each run, Pallas kernels for 0% -> 0%
where the time goes in v1:
time: 387 us; the launch traced here: 385 us
  waiting for transfers between devices  260 us (67%)
  blocking collectives  78.1 us (20%)
  between operations  17.8 us (5%)
  matrix products  15 us (4%)
  local copies, waits for them, and re-layouts  12.7 us (3%)
    reduce_scatter x1, waiting for transfers between devices, on_device(): lax.psum_scatter(dense.reshape(adapters, -1, 128), 'blk', scatter_dimensi...  123 us
    all_gather x1, waiting for transfers between devices, on_device(): all_a = lax.all_gather(bank_a, 'blk', axis=0, tiled=True)  63.8 us
    reduce_scatter x1, waiting for transfers between devices, on_device(): lax.psum_scatter(base, 'tp', scatter_dimension=0, tiled=True).astype(bf16)  62.7 us
    psum x1, blocking collectives, on_device(): both = lax.psum(jnp.stack([act_part, grad_part]), 'tp')  41.2 us
    all_gather x1, blocking collectives, on_device(): all_b = lax.all_gather(b_cols, 'blk', axis=0, tiled=True)  37 us
    all_gather x1, waiting for transfers between devices, on_device(): grad_rows = lax.all_gather(grad_out, 'tp', axis=0, tiled=True)  9.24 us
  transfers between devices with their start and end apart: 4, of which 4 were waited for; matrix products, arithmetic and copies ran while one was open for 6% of the time, Pallas kernels for 0%

profile of v1, /device:TPU:2, one launch (start us, length us, event | category | flops | bytes accessed | tf_op | source)
XLA Modules:
  0.0 385.4 jit_solution(8638338468976449265)
XLA Ops:
  7.2 0.7 all-gather.5.cloned.1.call-update
  8.0 0.7 all-gather.3.cloned.1.call-update
  8.7 1.3 fusion.33
  13.9 0.7 constant_dynamic-slice_fusion.2
  14.6 37.0 %all_gather.11 = bf16[32,32,128]{2,1,0:T(8,128)(2,1)S(1)} all-gather(bf16[1,32,128]{2,1,0:T(8,128)(2,1)S(1)} %constant_dynamic-slice_fusion.2), channel_id=1, replica_groups=mesh['blk'=32,'tp'=8] {'blk'}, dimensions={0}, use_global_device_ids=true | all-gather | bytes 270336 | tf_op jit(solution)/shard_map/all_gather | solution.py:24
  51.6 3.4 fusion.34
  55.0 9.2 %all-gather.5.cloned.1.call-done = bf16[256,2048]{1,0:T(8,128)(2,1)} async-done(((bf16[32,2048]{1,0:T(8,128)(2,1)}), bf16[256,2048]{1,0:T(8,128)(2,1)}) %all-gather.5.cloned.1.call-update) | async-done | bytes 1048592 | tf_op jit(solution)/shard_map/all_gather | solution.py:26
  64.3 1.0 fusion.7
  65.2 1.0 fusion.11
  66.2 63.8 %all-gather.3.cloned.1.call-done = bf16[32,1024,32]{1,2,0:T(8,128)(2,1)} async-done(((bf16[1,1024,32]{1,2,0:T(8,128)(2,1)}), bf16[32,1024,32]{1,2,0:T(8,128)(2,1)}) %all-gather.3.cloned.1.call-update) | async-done | bytes 2097168 | tf_op jit(solution)/shard_map/all_gather | solution.py:25
  130.0 0.9 constant_dynamic-slice_fusion.4
  130.9 0.3 convolution_bitcast_fusion.1
  131.2 41.2 %psum.7 = bf16[2,2,128,32]{2,3,1,0:T(8,128)(2,1)S(1)} all-reduce(f32[2,2,128,32]{2,3,1,0:T(8,128)S(1)} %pad_maximum_fusion.3), channel_id=1, replica_groups=mesh['blk'=32,'tp'=8] {'tp'}, use_global_device_ids=true, to_apply=%region_0.0 | all-reduce | flops 16384 | bytes 98304 | tf_op jit(solution)/shard_map/psum | solution.py:44
  172.4 0.2 convolution_multiply_fusion.2
  172.6 0.2 convolution_multiply_fusion.3
  172.9 1.4 copy-done.1
  174.4 1.0 fusion.9
  175.4 1.0 fusion.5
  176.4 0.2 fusion.1
  176.6 0.3 copy.12
  176.9 0.6 reshape.50
  177.5 2.1 convolution_bitcast_fusion
  179.7 3.0 copy.15
  182.7 0.3 convolution_multiply_fusion
  183.0 0.9 copy-done.2
  184.0 4.3 %fusion = bf16[256,1024]{1,0:T(8,128)(2,1)} fusion(f32[256,1024]{1,0:T(8,128)S(1)} %bitcast.43, bf16[256,2048]{1,0:T(8,128)(2,1)S(1)} %copy-done.2, bf16[1024,2048]{1,0:T(8,128)(2,1)} %param.7), kind=kOutput, calls=%fused_computation.3 | convolution fusion | flops 1074266112 | bytes 6815744 | tf_op jit(solution)/shard_map/dot_general | solution.py:66
  188.2 62.7 %reduce-scatter.3.cloned.1.call-done = f32[32,2048]{1,0:T(8,128)} async-done(((f32[256,2048]{1,0:T(8,128)}), f32[32,2048]{1,0:T(8,128)}) %reduce-scatter.3.cloned.1.call-update) | async-done | bytes 262160 | tf_op jit(solution)/shard_map/reduce_scatter | solution.py:64
  250.9 1.6 convert_element_type.16
  252.6 122.8 %reduce-scatter.5.cloned.1.call-done = f32[1,288,128]{2,1,0:T(8,128)} async-done(((f32[32,288,128]{2,1,0:T(8,128)}), f32[1,288,128]{2,1,0:T(8,128)}) %reduce-scatter.5.cloned.1.call-update) | async-done | bytes 147472 | tf_op jit(solution)/shard_map/reduce_scatter | solution.py:83
  375.3 1.3 slice.57
  376.6 1.2 slice_reduce_fusion
  378.1 0.8 copy.13
  (21 shorter events, 0.5 us)
Async XLA Ops:
  7.2 44.4 %copy-start = (bf16[256,1024]{1,0:T(8,128)(2,1)S(1)}, bf16[256,1024]{1,0:T(8,128)(2,1)}, u32[]{:S(2)}) copy-start(bf16[256,1024]{1,0:T(8,128)(2,1)} %param.6) | copy-start | bytes 1572868
  7.2 57.1 %all-gather.5.cloned.1.call-start = ((), (), s32[]{:S(2)}) async-start(), calls=%async_computation.3 | async-start | bytes 1179648 | tf_op jit(solution)/shard_map/all_gather | solution.py:26
  7.9 122.1 %all-gather.3.cloned.1.call-start = ((), (), s32[]{:S(2)}) async-start(), calls=%async_computation.2 | async-start | bytes 2162688 | tf_op jit(solution)/shard_map/all_gather | solution.py:25
  8.7 242.3 %reduce-scatter.3.cloned.1.call-start = ((), (), s32[]{:S(2)}) async-start(), calls=%async_computation.4 | async-start | bytes 2359296 | tf_op jit(solution)/shard_map/reduce_scatter | solution.py:64
  64.3 113.2 %copy-start.3 = (s32[2,1]{0,1:T(1,128)S(1)}, s32[2,1]{0,1:T(1,128)}, u32[]{:S(2)}) copy-start(s32[2,1]{0,1:T(1,128)} %param.10) | copy-start | bytes 28
  172.9 1.4 copy-start.1
  174.3 201.0 %reduce-scatter.5.cloned.1.call-start = ((), (), s32[]{:S(2)}) async-start(), calls=%async_computation.5 | async-start | bytes 4866048 | tf_op jit(solution)/shard_map/reduce_scatter | solution.py:83
  182.7 1.3 copy-start.2
Sparse Core Ops, SparseCore 0:
  10.7 53.5 all-gather.4
  66.1 63.8 all-gather.2
  174.5 76.4 reduce-scatter.2
  253.3 121.9 reduce-scatter.4

commit v2 on v1

--- a/solution.py
+++ b/solution.py
@@ -1,9 +1,72 @@
+import functools
+
 import jax
 import jax.numpy as jnp
 from jax import lax
+from jax.experimental import pallas as pl
+from jax.experimental.pallas import tpu as pltpu
 from jax.sharding import PartitionSpec as P
 
 adapter_scale = 0.5
+MESH = pl.DeviceIdType.MESH
+
+
+def _peer(axis, me, other, k, n):
+    peer = lax.rem(me + k, n)
+    return (other, peer) if axis == "tp" else (peer, other)
+
+
+def _gather_kernel(axis, n, x_ref, o_ref, slots, send_sem, recv_sem):
+    me = lax.axis_index(axis)
+    other = lax.axis_index("blk" if axis == "tp" else "tp")
+    barrier = pltpu.get_barrier_semaphore()
+    for k in range(1, n):
+        pl.semaphore_signal(
+            barrier, inc=1, device_id=_peer(axis, me, other, k, n), device_id_type=MESH
+        )
+    pl.semaphore_wait(barrier, n - 1)
+    sends = []
+    for k in range(1, n):
+        copy = pltpu.make_async_remote_copy(
+            src_ref=x_ref,
+            dst_ref=slots.at[me],
+            send_sem=send_sem.at[k],
+            recv_sem=recv_sem.at[me],
+            device_id=_peer(axis, me, other, k, n),
+            device_id_type=MESH,
+        )
+        copy.start()
+        sends.append(copy)
+    slots[me] = x_ref[...]
+    for k in range(1, n):
+        src = lax.rem(me + n - k, n)
+        pltpu.make_async_remote_copy(
+            src_ref=x_ref,
+            dst_ref=slots.at[src],
+            send_sem=send_sem.at[k],
+            recv_sem=recv_sem.at[src],
+            device_id=_peer(axis, me, other, n - k, n),
+            device_id_type=MESH,
+        ).wait_recv()
+    for copy in sends:
+        copy.wait_send()
+    o_ref[...] = slots[...]
+
+
+def gather_axis(x, axis, cid):
+    n = lax.axis_size(axis)
+    return pl.pallas_call(
+        functools.partial(_gather_kernel, axis, n),
+        out_shape=jax.ShapeDtypeStruct((n,) + x.shape, x.dtype),
+        in_specs=[pl.BlockSpec(memory_space=pltpu.VMEM)],
+        out_specs=pl.BlockSpec(memory_space=pltpu.VMEM),
+        scratch_shapes=[
+            pltpu.VMEM((n,) + x.shape, x.dtype),
+            pltpu.SemaphoreType.DMA((n,)),
+            pltpu.SemaphoreType.DMA((n,)),
+        ],
+        compiler_params=pltpu.CompilerParams(collective_id=cid, has_side_effects=True),
+    )(x)
 
 
 def on_device(tokens, weight, bank_a, bank_b, tile_map, grad_out):
@@ -21,9 +84,9 @@
     col0 = tp_id * kv_dev
 
     b_cols = lax.dynamic_slice_in_dim(bank_b, col0, kv_dev, 2)
-    all_b = lax.all_gather(b_cols, "blk", axis=0, tiled=True)
+    all_b = gather_axis(b_cols.reshape(-1, kv_dev), "blk", 0).reshape(-1, rank_two, kv_dev)
     all_a = lax.all_gather(bank_a, "blk", axis=0, tiled=True)
-    grad_rows = lax.all_gather(grad_out, "tp", axis=0, tiled=True)
+    grad_rows = gather_axis(grad_out, "tp", 1).reshape(rows, 2 * kv_width)
 
     fac_a = jnp.stack([all_a[tile_ids[t]] for t in range(tiles)])
     fac_b = jnp.stack([all_b[tile_ids[t]] for t in range(tiles)])
@@ -41,7 +104,8 @@
         ],
         axis=2,
     )
-    both = lax.psum(jnp.stack([act_part, grad_part]), "tp")
+    parts = jnp.stack([act_part, grad_part])
+    both = gather_axis(parts.reshape(-1, 128), "tp", 2).sum(0).reshape(parts.shape)
     rank_act = both[0].astype(bf16)
     rank_grad = both[1].astype(bf16)
 

time: 387 us -> 312 us (0.81)
  blocking collectives: 78.1 us -> 0 us
  waiting for transfers between devices: 260 us -> 206 us
  Pallas kernels: 0 us -> 53.7 us
    pallas_call x0 -> x3, Pallas kernels: none -> 53.7 us  [gather_axis(): pl.pallas_call(functools.partial(_gather_kernel, axis, n), out_shape=jax....]
    all_gather x1, waiting for transfers between devices: 63.8 us -> 16.6 us  [on_device(): all_a = lax.all_gather(bank_a, 'blk', axis=0, tiled=True)]
    psum x1 -> x0, blocking collectives: 41.2 us -> none  [on_device(): both = lax.psum(jnp.stack([act_part, grad_part]), 'tp')]
    all_gather x1 -> x0, blocking collectives: 37 us -> none  [on_device(): all_b = lax.all_gather(b_cols, 'blk', axis=0, tiled=True)]
    all_gather x1 -> x0, waiting for transfers between devices: 9.24 us -> none  [on_device(): grad_rows = lax.all_gather(grad_out, 'tp', axis=0, tiled=True)]
  transfers between devices with their start and end apart: 4 -> 3, of which waited for: 4 -> 3; matrix products, arithmetic and copies ran while one was open for 6% -> 8% of each run, Pallas kernels for 0% -> 13%
where the time goes in v2:
time: 312 us; the launch traced here: 311 us
  waiting for transfers between devices  206 us (66%)
  Pallas kernels  53.7 us (17%)
  between operations  17.8 us (6%)
  local copies, waits for them, and re-layouts  15.1 us (5%)
  matrix products  15.1 us (5%)
    reduce_scatter x1, waiting for transfers between devices, on_device(): lax.psum_scatter(dense.reshape(adapters, -1, 128), 'blk', scatter_dimensi...  123 us
    reduce_scatter x1, waiting for transfers between devices, on_device(): lax.psum_scatter(base, 'tp', scatter_dimension=0, tiled=True).astype(bf16)  66 us
    pallas_call x3, Pallas kernels, gather_axis(): pl.pallas_call(functools.partial(_gather_kernel, axis, n), out_shape=jax....  53.7 us
    all_gather x1, waiting for transfers between devices, on_device(): all_a = lax.all_gather(bank_a, 'blk', axis=0, tiled=True)  16.6 us
  transfers between devices with their start and end apart: 3, of which 3 were waited for; matrix products, arithmetic and copies ran while one was open for 8% of the time, Pallas kernels for 13%

profile of v2, /device:TPU:2, one launch (start us, length us, event | category | flops | bytes accessed | tf_op | source)
XLA Modules:
  0.0 310.7 jit_solution(3328533342231551098)
XLA Ops:
  7.2 0.7 all-gather.2.cloned.1.call-update
  8.0 1.3 fusion.34
  11.9 1.3 dynamic-slice_bitcast_fusion.x_ref
  13.2 17.5 %shard_map.94 = bf16[32,32,128]{2,1,0:T(8,128)(2,1)} custom-call(bf16[32,128]{1,0:T(8,128)(2,1)} %dynamic-slice_bitcast_fusion.x_ref), custom_call_target="tpu_custom_call" | custom-call | tf_op jit(solution)/shard_map/pallas_call | solution.py:58
  30.7 22.3 %shard_map.93 = bf16[8,32,2048]{2,1,0:T(8,128)(2,1)} custom-call(bf16[32,2048]{1,0:T(8,128)(2,1)} %x_ref.1), custom_call_target="tpu_custom_call" | custom-call | tf_op jit(solution)/shard_map/pallas_call | solution.py:58
  54.2 0.7 constant_dynamic-slice_fusion.1
  55.0 1.0 fusion.12
  55.9 1.0 fusion.15
  56.9 3.5 %fusion.35 = f32[256,2048]{1,0:T(8,128)S(1)} fusion(bf16[256,1024]{1,0:T(8,128)(2,1)S(1)} %copy-done, bf16[1024,2048]{1,0:T(8,128)(2,1)} %param.7), kind=kOutput, calls=%fused_computation.58 | convolution fusion | flops 1073741824 | bytes 6815744 | tf_op jit(solution)/shard_map/dot_general | solution.py:118
  60.4 16.6 %all-gather.2.cloned.1.call-done = bf16[32,1024,32]{1,2,0:T(8,128)(2,1)} async-done(((bf16[1,1024,32]{1,2,0:T(8,128)(2,1)}), bf16[32,1024,32]{1,2,0:T(8,128)(2,1)}) %all-gather.2.cloned.1.call-update) | async-done | bytes 2097168 | tf_op jit(solution)/shard_map/all_gather | solution.py:88
  76.9 0.9 constant_dynamic-slice_fusion.3
  77.8 0.3 convolution_bitcast_fusion.1
  78.3 0.7 reshape.61.x_ref
  79.0 14.0 %shard_map.95 = f32[8,128,128]{2,1,0:T(8,128)} custom-call(f32[128,128]{1,0:T(8,128)} %reshape.61.x_ref), custom_call_target="tpu_custom_call" | custom-call | tf_op jit(solution)/shard_map/pallas_call | solution.py:58
  93.0 1.1 reduce_sum.9
  94.7 1.4 copy-done.1
  96.2 1.0 fusion.9
  97.2 1.1 fusion.6
  98.4 0.2 fusion.1
  98.6 0.3 copy.23
  99.0 0.6 reshape.63
  99.5 2.1 convolution_bitcast_fusion
  101.7 3.0 copy.30
  104.7 0.3 convolution_multiply_fusion
  105.0 0.9 copy-done.2
  105.9 4.3 %fusion = bf16[256,1024]{1,0:T(8,128)(2,1)} fusion(f32[256,1024]{1,0:T(8,128)S(1)} %bitcast.49, bf16[256,2048]{1,0:T(8,128)(2,1)S(1)} %bitcast.48, bf16[1024,2048]{1,0:T(8,128)(2,1)} %param.7), kind=kOutput, calls=%fused_computation.3 | convolution fusion | flops 1074266112 | bytes 6815744 | tf_op jit(solution)/shard_map/dot_general | solution.py:130
  110.2 66.0 %reduce-scatter.3.cloned.1.call-done = f32[32,2048]{1,0:T(8,128)} async-done(((f32[256,2048]{1,0:T(8,128)}), f32[32,2048]{1,0:T(8,128)}) %reduce-scatter.3.cloned.1.call-update) | async-done | bytes 262160 | tf_op jit(solution)/shard_map/reduce_scatter | solution.py:128
  176.2 1.6 convert_element_type.16
  177.8 122.8 %reduce-scatter.5.cloned.1.call-done = f32[1,288,128]{2,1,0:T(8,128)} async-done(((f32[32,288,128]{2,1,0:T(8,128)}), f32[1,288,128]{2,1,0:T(8,128)}) %reduce-scatter.5.cloned.1.call-update) | async-done | bytes 147472 | tf_op jit(solution)/shard_map/reduce_scatter | solution.py:147
  300.6 1.3 slice.59
  301.9 1.2 slice_reduce_fusion
  303.4 0.8 copy.24
  (24 shorter events, 1.2 us)
Async XLA Ops:
  7.2 49.8 %copy-start = (bf16[256,1024]{1,0:T(8,128)(2,1)S(1)}, bf16[256,1024]{1,0:T(8,128)(2,1)}, u32[]{:S(2)}) copy-start(bf16[256,1024]{1,0:T(8,128)(2,1)} %param.6) | copy-start | bytes 1572868
  7.2 69.8 %all-gather.2.cloned.1.call-start = ((), (), s32[]{:S(2)}) async-start(), calls=%async_computation.2 | async-start | bytes 2162688 | tf_op jit(solution)/shard_map/all_gather | solution.py:88
  7.9 168.3 %reduce-scatter.3.cloned.1.call-start = ((), (), s32[]{:S(2)}) async-start(), calls=%async_computation.3 | async-start | bytes 2359296 | tf_op jit(solution)/shard_map/reduce_scatter | solution.py:128
  79.0 20.5 %copy-start.3 = (s32[2,1]{0,1:T(1,128)S(1)}, s32[2,1]{0,1:T(1,128)}, u32[]{:S(2)}) copy-start(s32[2,1]{0,1:T(1,128)} %param.10) | copy-start | bytes 28
  94.6 1.4 copy-start.1
  96.1 204.6 %reduce-scatter.5.cloned.1.call-start = ((), (), s32[]{:S(2)}) async-start(), calls=%async_computation.4 | async-start | bytes 4866048 | tf_op jit(solution)/shard_map/reduce_scatter | solution.py:147
  104.7 1.2 copy-start.2
Sparse Core Ops, SparseCore 0:
  9.9 67.0 all-gather.1
  96.2 79.9 reduce-scatter.2
  178.7 121.8 reduce-scatter.4

commit v3 on v2

--- a/solution.py
+++ b/solution.py
@@ -67,6 +67,37 @@
         ],
         compiler_params=pltpu.CompilerParams(collective_id=cid, has_side_effects=True),
     )(x)
+
+
+def _swap(x, bit, count):
+    return lax.ppermute(x, "blk", [(i, i ^ bit) for i in range(count)])
+
+
+def reduce_to_owner(rows, ids, per):
+    count = lax.axis_size("blk")
+    me = lax.axis_index("blk")
+    nbits = count.bit_length() - 1
+    order = [count // 2] + [1 << k for k in range(nbits - 1)]
+    sparse = min(2, nbits)
+    for bit in order[:sparse]:
+        rows = jnp.concatenate([rows, _swap(rows, bit, count)])
+        ids = jnp.concatenate([ids, _swap(ids, bit, count)])
+        owner = ids // per
+        ids = jnp.where((ids >= 0) & ((owner & bit) == (me & bit)), ids, -1)
+    rest = order[sparse:]
+    owner = ids // per
+    slot = ids % per
+    for k, bit in enumerate(rest):
+        slot = slot + ((owner & bit) != 0).astype(jnp.int32) * (per << (len(rest) - 1 - k))
+    hit = (slot[:, None] == jnp.arange(per << len(rest))[None, :]) & (ids >= 0)[:, None]
+    dense = jnp.sum(jnp.where(hit[:, :, None, None], rows[:, None], 0.0), axis=0)
+    for bit in rest:
+        half = dense.shape[0] // 2
+        upper = (me & bit) != 0
+        keep = jnp.where(upper, dense[half:], dense[:half])
+        send = jnp.where(upper, dense[:half], dense[half:])
+        dense = keep + _swap(send, bit, count)
+    return dense
 
 
 def on_device(tokens, weight, bank_a, bank_b, tile_map, grad_out):
@@ -141,10 +172,7 @@
     )
     size_a = feats * rank_two
     flat = jnp.concatenate([down_grad.reshape(tiles, -1), up_grad.reshape(tiles, -1)], axis=1)
-    adapters = bank_a.shape[0] * lax.axis_size("blk")
-    one_hot = (tile_ids[:, None] == jnp.arange(adapters, dtype=jnp.int32)[None, :]).astype(f32)
-    dense = jnp.dot(one_hot.T, flat, precision=lax.Precision.HIGHEST, preferred_element_type=f32)
-    summed = lax.psum_scatter(dense.reshape(adapters, -1, 128), "blk", scatter_dimension=0, tiled=True).reshape(bank_a.shape[0], -1)
+    summed = reduce_to_owner(flat.reshape(tiles, -1, 128), tile_ids, bank_a.shape[0]).reshape(bank_a.shape[0], -1)
     grad_a = summed[:, :size_a].reshape(bank_a.shape[0], feats, rank_two)
     grad_b = summed[:, size_a:].reshape(bank_a.shape[0], rank_two, kv_dev)
     return (key_value_output, token_gradient, grad_a, grad_b)

time: 312 us -> 192 us (0.62)
  waiting for transfers between devices: 206 us -> 76.4 us
  starting transfers between devices: 0.12 us -> 12.1 us
  local copies, waits for them, and re-layouts: 15.1 us -> 8.19 us
  other arithmetic: 2.79 us -> 8.92 us
    reduce_scatter x1 -> x0, waiting for transfers between devices: 123 us -> none  [on_device(): lax.psum_scatter(dense.reshape(adapters, -1, 128), 'blk', scatter_dimensi...]
    reduce_scatter x1, waiting for transfers between devices: 66 us -> 24.9 us  [on_device(): lax.psum_scatter(base, 'tp', scatter_dimension=0, tiled=True).astype(bf16)]
    ppermute x0 -> x7, waiting for transfers between devices: none -> 37 us  [_swap(): return lax.ppermute(x, 'blk', [(i, i ^ bit) for i in range(count)])]
    ppermute x0 -> x7, starting transfers between devices: none -> 12 us  [_swap(): return lax.ppermute(x, 'blk', [(i, i ^ bit) for i in range(count)])]
    unnamed x11 -> x9, local copies, waits for them, and re-layouts: 6.16 us -> 0.9 us
  transfers between devices with their start and end apart: 3 -> 9, of which waited for: 3 -> 7; matrix products, arithmetic and copies ran while one was open for 8% -> 15% of each run, Pallas kernels for 13% -> 28%
where the time goes in v3:
time: 192 us; the launch traced here: 190 us
  waiting for transfers between devices  76.4 us (40%)
  Pallas kernels  53.3 us (28%)
  between operations  18.2 us (9%)
  matrix products  13.3 us (7%)
  starting transfers between devices  12.1 us (6%)
  other arithmetic  8.92 us (5%)
  local copies, waits for them, and re-layouts  8.19 us (4%)
    pallas_call x3, Pallas kernels, gather_axis(): pl.pallas_call(functools.partial(_gather_kernel, axis, n), out_shape=jax....  53.3 us
    ppermute x7, waiting for transfers between devices, _swap(): return lax.ppermute(x, 'blk', [(i, i ^ bit) for i in range(count)])  37 us
    reduce_scatter x1, waiting for transfers between devices, on_device(): lax.psum_scatter(base, 'tp', scatter_dimension=0, tiled=True).astype(bf16)  24.9 us
    all_gather x1, waiting for transfers between devices, on_device(): all_a = lax.all_gather(bank_a, 'blk', axis=0, tiled=True)  13.8 us
    ppermute x7, starting transfers between devices, _swap(): return lax.ppermute(x, 'blk', [(i, i ^ bit) for i in range(count)])  12 us
    dot_general x1, matrix products, on_device(): base = jnp.dot(tokens, weight, preferred_element_type=f32)  4.82 us
    dot_general x1, matrix products, on_device(): backward = jnp.dot(grad_rows, weight.T, preferred_element_type=f32)  4.31 us
  transfers between devices with their start and end apart: 9, of which 7 were waited for; matrix products, arithmetic and copies ran while one was open for 15% of the time, Pallas kernels for 28%

profile of v3, /device:TPU:2, one launch (start us, length us, event | category | flops | bytes accessed | tf_op | source)
XLA Modules:
  0.0 190.5 jit_solution(2595180038556795827)
XLA Ops:
  8.0 2.4 %collective-permute-start = (s32[2]{0:T(128)}, s32[2]{0:T(128)S(1)}, u32[]{:S(2)}, u32[]{:S(2)}) collective-permute-start(s32[2]{0:T(128)} %bitcast.58), channel_id=1, source_target_pairs={{0,128},{8,136},{16,144},{24,152},{32,160},{40,168},{48,176},{56,1... | collective-permute-start | bytes 32 | tf_op jit(solution)/shard_map/ppermute | solution.py:73
  10.3 1.3 fusion.30
  14.2 1.3 dynamic-slice_bitcast_fusion.x_ref
  15.5 16.6 %shard_map.94 = bf16[32,32,128]{2,1,0:T(8,128)(2,1)} custom-call(bf16[32,128]{1,0:T(8,128)(2,1)} %dynamic-slice_bitcast_fusion.x_ref), custom_call_target="tpu_custom_call" | custom-call | tf_op jit(solution)/shard_map/pallas_call | solution.py:58
  32.1 22.5 %shard_map.93 = bf16[8,32,2048]{2,1,0:T(8,128)(2,1)} custom-call(bf16[32,2048]{1,0:T(8,128)(2,1)} %x_ref.1), custom_call_target="tpu_custom_call" | custom-call | tf_op jit(solution)/shard_map/pallas_call | solution.py:58
  55.9 0.7 constant_dynamic-slice_fusion.1
  56.6 1.0 fusion.9
  57.6 1.0 fusion.12
  58.6 4.8 %fusion.31 = f32[256,2048]{1,0:T(8,128)} fusion(bf16[256,1024]{1,0:T(8,128)(2,1)S(1)} %copy-done, bf16[1024,2048]{1,0:T(8,128)(2,1)} %param.7), kind=kOutput, calls=%fused_computation.73 | convolution fusion | flops 1073741824 | bytes 6815744 | tf_op jit(solution)/shard_map/dot_general | solution.py:149
  63.4 13.8 %all-gather.2.cloned.1.call-done = bf16[32,1024,32]{1,2,0:T(8,128)(2,1)} async-done(((bf16[1,1024,32]{1,2,0:T(8,128)(2,1)}), bf16[32,1024,32]{1,2,0:T(8,128)(2,1)}) %all-gather.2.cloned.1.call-update) | async-done | bytes 2097168 | tf_op jit(solution)/shard_map/all_gather | solution.py:119
  77.2 0.9 constant_dynamic-slice_fusion.3
  78.5 0.7 reshape.179.x_ref
  79.3 14.2 %shard_map.95 = f32[8,128,128]{2,1,0:T(8,128)} custom-call(f32[128,128]{1,0:T(8,128)} %reshape.179.x_ref), custom_call_target="tpu_custom_call" | custom-call | tf_op jit(solution)/shard_map/pallas_call | solution.py:58
  93.5 1.1 reduce_sum.18
  95.1 0.8 convolution_multiply_fusion.3
  97.4 1.7 collective-permute-start.2
  99.1 1.7 constant_dynamic-update-slice_fusion.1
  101.0 1.6 constant_dynamic-update-slice_fusion
  102.6 3.7 %collective-permute-done.2 = f32[2,288,128]{2,1,0:T(8,128)S(1)} collective-permute-done((f32[2,288,128]{2,1,0:T(8,128)S(1)}, f32[2,288,128]{2,1,0:T(8,128)S(1)}, u32[]{:S(2)}, u32[]{:S(2)}) %collective-permute-start.2) | collective-permute-done | bytes 294944 | tf_op jit(solution)/shard_map/ppermute | solution.py:73
  107.0 1.4 collective-permute-done.1
  108.6 1.1 select_reduce_fusion
  109.8 0.8 collective-permute-start.4
  110.6 14.7 %collective-permute-done.4 = f32[4,288,128]{2,1,0:T(8,128)} collective-permute-done((f32[4,288,128]{2,1,0:T(8,128)S(1)}, f32[4,288,128]{2,1,0:T(8,128)}, u32[]{:S(2)}, u32[]{:S(2)}) %collective-permute-start.4) | collective-permute-done | bytes 589856 | tf_op jit(solution)/shard_map/ppermute | solution.py:73
  125.4 1.2 select_add_fusion
  126.6 2.2 %collective-permute-start.5 = (f32[2,288,128]{2,1,0:T(8,128)S(1)}, f32[2,288,128]{2,1,0:T(8,128)S(1)}, u32[]{:S(2)}, u32[]{:S(2)}) collective-permute-start(f32[2,288,128]{2,1,0:T(8,128)S(1)} %slice_select_fusion.1), channel_id=1, source_target_pairs={{0,32},{8,40},{16,48},{24,56},{32,0},{40,8},{48,16},{56,24},{64,96... | collective-permute-start | bytes 884744 | tf_op jit(solution)/shard_map/ppermute | solution.py:73
  129.0 13.1 %collective-permute-done.5 = f32[2,288,128]{2,1,0:T(8,128)S(1)} collective-permute-done((f32[2,288,128]{2,1,0:T(8,128)S(1)}, f32[2,288,128]{2,1,0:T(8,128)S(1)}, u32[]{:S(2)}, u32[]{:S(2)}) %collective-permute-start.5) | collective-permute-done | bytes 294944 | tf_op jit(solution)/shard_map/ppermute | solution.py:73
  142.2 4.4 %collective-permute-start.6 = (f32[1,288,128]{2,1,0:T(8,128)S(1)}, f32[1,288,128]{2,1,0:T(8,128)S(1)}, u32[]{:S(2)}, u32[]{:S(2)}) collective-permute-start(f32[1,288,128]{2,1,0:T(8,128)S(1)} %slice_select_fusion.2), channel_id=1, source_target_pairs={{0,64},{8,72},{16,80},{24,88},{32,96},{40,104},{48,112},{56,120},{... | collective-permute-start | bytes 442376 | tf_op jit(solution)/shard_map/ppermute | solution.py:73
  146.6 4.3 %fusion = bf16[256,1024]{1,0:T(8,128)(2,1)} fusion(f32[256,1024]{1,0:T(8,128)S(1)} %bitcast.53, bf16[256,2048]{1,0:T(8,128)(2,1)S(1)} %bitcast.52, bf16[1024,2048]{1,0:T(8,128)(2,1)} %param.7), kind=kOutput, calls=%fused_computation.3 | convolution fusion | flops 1074266112 | bytes 6815744 | tf_op jit(solution)/shard_map/dot_general | solution.py:161
  150.9 4.1 %collective-permute-done.6 = f32[1,288,128]{2,1,0:T(8,128)S(1)} collective-permute-done((f32[1,288,128]{2,1,0:T(8,128)S(1)}, f32[1,288,128]{2,1,0:T(8,128)S(1)}, u32[]{:S(2)}, u32[]{:S(2)}) %collective-permute-start.6) | collective-permute-done | bytes 147488 | tf_op jit(solution)/shard_map/ppermute | solution.py:73
  156.2 0.8 copy.31
  157.1 24.9 %reduce-scatter.2.cloned.1.call-done = f32[32,2048]{1,0:T(8,128)} async-done(((f32[256,2048]{1,0:T(8,128)}), f32[32,2048]{1,0:T(8,128)}) %reduce-scatter.2.cloned.1.call-update) | async-done | bytes 262160 | tf_op jit(solution)/shard_map/reduce_scatter | solution.py:159
  182.0 1.6 convert_element_type.24
  (46 shorter events, 5.9 us)
Async XLA Ops:
  7.2 51.4 %copy-start = (bf16[256,1024]{1,0:T(8,128)(2,1)S(1)}, bf16[256,1024]{1,0:T(8,128)(2,1)}, u32[]{:S(2)}) copy-start(bf16[256,1024]{1,0:T(8,128)(2,1)} %param.6) | copy-start | bytes 1572868
  7.2 70.0 %all-gather.2.cloned.1.call-start = ((), (), s32[]{:S(2)}) async-start(), calls=%async_computation.1 | async-start | bytes 2162688 | tf_op jit(solution)/shard_map/all_gather | solution.py:119
  7.9 174.1 %reduce-scatter.2.cloned.1.call-start = ((), (), s32[]{:S(2)}) async-start(), calls=%async_computation.2 | async-start | bytes 2359296 | tf_op jit(solution)/shard_map/reduce_scatter | solution.py:159
  8.0 98.4 %collective-permute-start = (s32[2]{0:T(128)}, s32[2]{0:T(128)S(1)}, u32[]{:S(2)}, u32[]{:S(2)}) collective-permute-start(s32[2]{0:T(128)} %bitcast.58), channel_id=1, source_target_pairs={{0,128},{8,136},{16,144},{24,152},{32,160},{40,168},{48,176},{56,1... | collective-permute-start | bytes 32 | tf_op jit(solution)/shard_map/ppermute | solution.py:73
  63.4 31.3 %copy-start.1 = (bf16[8,32,2048]{2,1,0:T(8,128)(2,1)S(1)}, bf16[8,32,2048]{2,1,0:T(8,128)(2,1)}, u32[]{:S(2)}) copy-start(bf16[8,32,2048]{2,1,0:T(8,128)(2,1)} %shard_map.93) | copy-start | bytes 3145732
  97.4 9.0 %copy-start.2 = (s32[2,1]{0,1:T(1,128)S(1)}, s32[2,1]{0,1:T(1,128)}, u32[]{:S(2)}) copy-start(s32[2,1]{0,1:T(1,128)} %param.10) | copy-start | bytes 28
  97.4 8.8 %collective-permute-start.2 = (f32[2,288,128]{2,1,0:T(8,128)S(1)}, f32[2,288,128]{2,1,0:T(8,128)S(1)}, u32[]{:S(2)}, u32[]{:S(2)}) collective-permute-start(f32[2,288,128]{2,1,0:T(8,128)S(1)} %bitcast.45), channel_id=1, source_target_pairs={{0,128},{8,136},{16,144},{24,152},{32,160},{40,168},{48,176},{56,1... | collective-permute-start | bytes 884744 | tf_op jit(solution)/shard_map/ppermute | solution.py:73
  106.3 2.3 %collective-permute-start.3 = (f32[4,288,128]{2,1,0:T(8,128)S(1)}, f32[4,288,128]{2,1,0:T(8,128)S(1)}, u32[]{:S(2)}, u32[]{:S(2)}) collective-permute-start(f32[4,288,128]{2,1,0:T(8,128)S(1)} %pad_maximum_fusion.1), channel_id=1, source_target_pairs={{0,8},{8,0},{16,24},{24,16},{32,40},{40,32},{48,56},{56,48},{64,72... | collective-permute-start | bytes 1769480 | tf_op jit(solution)/shard_map/ppermute | solution.py:73
  106.5 1.9 collective-permute-start.1
  109.8 15.6 %collective-permute-start.4 = (f32[4,288,128]{2,1,0:T(8,128)S(1)}, f32[4,288,128]{2,1,0:T(8,128)}, u32[]{:S(2)}, u32[]{:S(2)}) collective-permute-start(f32[4,288,128]{2,1,0:T(8,128)S(1)} %slice_select_fusion), channel_id=1, source_target_pairs={{0,16},{8,24},{16,0},{24,8},{32,48},{40,56},{48,32},{56,40},{64,80... | collective-permute-start | bytes 1769480 | tf_op jit(solution)/shard_map/ppermute | solution.py:73
  126.6 15.5 %collective-permute-start.5 = (f32[2,288,128]{2,1,0:T(8,128)S(1)}, f32[2,288,128]{2,1,0:T(8,128)S(1)}, u32[]{:S(2)}, u32[]{:S(2)}) collective-permute-start(f32[2,288,128]{2,1,0:T(8,128)S(1)} %slice_select_fusion.1), channel_id=1, source_target_pairs={{0,32},{8,40},{16,48},{24,56},{32,0},{40,8},{48,16},{56,24},{64,96... | collective-permute-start | bytes 884744 | tf_op jit(solution)/shard_map/ppermute | solution.py:73
  142.2 12.9 %collective-permute-start.6 = (f32[1,288,128]{2,1,0:T(8,128)S(1)}, f32[1,288,128]{2,1,0:T(8,128)S(1)}, u32[]{:S(2)}, u32[]{:S(2)}) collective-permute-start(f32[1,288,128]{2,1,0:T(8,128)S(1)} %slice_select_fusion.2), channel_id=1, source_target_pairs={{0,64},{8,72},{16,80},{24,88},{32,96},{40,104},{48,112},{56,120},{... | collective-permute-start | bytes 442376 | tf_op jit(solution)/shard_map/ppermute | solution.py:73
Sparse Core Ops, SparseCore 0:
  9.9 67.2 all-gather.1
  102.7 79.2 reduce-scatter.1

commit v4 on v3

--- a/solution.py
+++ b/solution.py
@@ -115,19 +115,23 @@
     col0 = tp_id * kv_dev
 
     b_cols = lax.dynamic_slice_in_dim(bank_b, col0, kv_dev, 2)
-    all_b = gather_axis(b_cols.reshape(-1, kv_dev), "blk", 0).reshape(-1, rank_two, kv_dev)
-    all_a = lax.all_gather(bank_a, "blk", axis=0, tiled=True)
-    grad_rows = gather_axis(grad_out, "tp", 1).reshape(rows, 2 * kv_width)
+    local = bank_a.shape[0]
+    a_len = feats * rank_two // 128
+    packed = jnp.concatenate([bank_a.reshape(local, -1, 128), b_cols.reshape(local, -1, 128)], axis=1)
+    all_ab = gather_axis(packed.reshape(-1, 128), "blk", 0).reshape(-1, packed.shape[1], 128)
+    grad_rows = lax.all_gather(grad_out, "tp", axis=0, tiled=True)
 
-    fac_a = jnp.stack([all_a[tile_ids[t]] for t in range(tiles)])
-    fac_b = jnp.stack([all_b[tile_ids[t]] for t in range(tiles)])
+    picked = jnp.stack([all_ab[tile_ids[t]] for t in range(tiles)])
+    fac_a = picked[:, :a_len].reshape(tiles, feats, rank_two)
+    fac_b = picked[:, a_len:].reshape(tiles, rank_two, kv_dev)
 
     tok_t = tokens.reshape(tiles, tile_rows, feats)
+    act_part = jnp.einsum("tre,tek->trk", tok_t, fac_a, preferred_element_type=f32)
+    rank_act = gather_axis(act_part.reshape(-1, 128), "tp", 2).sum(0).reshape(act_part.shape).astype(bf16)
+
     g_t = grad_rows.reshape(tiles, tile_rows, 2 * kv_width)
     g_key = lax.dynamic_slice_in_dim(g_t, col0, kv_dev, 2)
     g_val = lax.dynamic_slice_in_dim(g_t, kv_width + col0, kv_dev, 2)
-
-    act_part = jnp.einsum("tre,tek->trk", tok_t, fac_a, preferred_element_type=f32)
     grad_part = jnp.concatenate(
         [
             jnp.einsum("trc,tkc->trk", g_key, fac_b[:, :rank_one], preferred_element_type=f32),
@@ -135,10 +139,7 @@
         ],
         axis=2,
     )
-    parts = jnp.stack([act_part, grad_part])
-    both = gather_axis(parts.reshape(-1, 128), "tp", 2).sum(0).reshape(parts.shape)
-    rank_act = both[0].astype(bf16)
-    rank_grad = both[1].astype(bf16)
+    rank_grad = gather_axis(grad_part.reshape(-1, 128), "tp", 3).sum(0).reshape(grad_part.shape).astype(bf16)
 
     lora_key = jnp.einsum(
         "trk,tkc->trc", rank_act[:, :, :rank_one], fac_b[:, :rank_one], preferred_element_type=f32

time: 192 us -> 214 us (1.11)
  Pallas kernels: 53.3 us -> 86.2 us
  waiting for transfers between devices: 76.4 us -> 64.2 us
    pallas_call x3, Pallas kernels: 53.3 us -> 86.2 us  [gather_axis(): pl.pallas_call(functools.partial(_gather_kernel, axis, n), out_shape=jax....]
    all_gather x1, waiting for transfers between devices: 13.8 us -> 0.01 us  [on_device(): grad_rows = lax.all_gather(grad_out, 'tp', axis=0, tiled=True)]
  transfers between devices with their start and end apart: 9 -> 9, of which waited for: 7 -> 6; matrix products, arithmetic and copies ran while one was open for 15% -> 11% of each run, Pallas kernels for 28% -> 35%
where the time goes in v4:
time: 214 us; the launch traced here: 212 us
  Pallas kernels  86.2 us (40%)
  waiting for transfers between devices  64.2 us (30%)
  between operations  18.2 us (9%)
  matrix products  14.4 us (7%)
  starting transfers between devices  11 us (5%)
  other arithmetic  9.27 us (4%)
  local copies, waits for them, and re-layouts  9.11 us (4%)
    pallas_call x3, Pallas kernels, gather_axis(): pl.pallas_call(functools.partial(_gather_kernel, axis, n), out_shape=jax....  86.2 us
    ppermute x7, waiting for transfers between devices, _swap(): return lax.ppermute(x, 'blk', [(i, i ^ bit) for i in range(count)])  36.8 us
    reduce_scatter x1, waiting for transfers between devices, on_device(): lax.psum_scatter(base, 'tp', scatter_dimension=0, tiled=True).astype(bf16)  26.7 us
    ppermute x7, starting transfers between devices, _swap(): return lax.ppermute(x, 'blk', [(i, i ^ bit) for i in range(count)])  10.9 us
    dot_general x1, matrix products, on_device(): base = jnp.dot(tokens, weight, preferred_element_type=f32)  4.77 us
    dot_general x1, matrix products, on_device(): backward = jnp.dot(grad_rows, weight.T, preferred_element_type=f32)  4.31 us
  transfers between devices with their start and end apart: 9, of which 6 were waited for; matrix products, arithmetic and copies ran while one was open for 11% of the time, Pallas kernels for 35%

profile of v4, /device:TPU:2, one launch (start us, length us, event | category | flops | bytes accessed | tf_op | source)
XLA Modules:
  0.0 212.3 jit_solution(3570285580610549484)
XLA Ops:
  7.2 0.7 all-gather.2.cloned.1.call-update
  8.0 1.3 fusion.26
  11.9 1.0 copy.26
  13.1 0.7 constant_dynamic-slice_fusion.2
  14.4 63.2 %shard_map.93 = bf16[32,288,128]{2,1,0:T(8,128)(2,1)} custom-call(bf16[288,128]{1,0:T(8,128)(2,1)} %maximum_bitcast_fusion.1.x_ref), custom_call_target="tpu_custom_call" | custom-call | tf_op jit(solution)/shard_map/pallas_call | solution.py:58
  78.9 0.9 constant_dynamic-slice_fusion
  80.5 0.7 reshape.187.x_ref
  81.2 11.9 %shard_map.94 = f32[8,64,128]{2,1,0:T(8,128)} custom-call(f32[64,128]{1,0:T(8,128)} %reshape.187.x_ref), custom_call_target="tpu_custom_call" | custom-call | tf_op jit(solution)/shard_map/pallas_call | solution.py:58
  93.1 1.0 reduce_sum.27
  94.4 4.8 %fusion.27 = f32[256,2048]{1,0:T(8,128)} fusion(bf16[256,1024]{1,0:T(8,128)(2,1)S(1)} %copy-done, bf16[1024,2048]{1,0:T(8,128)(2,1)} %param.7), kind=kOutput, calls=%fused_computation.68 | convolution fusion | flops 1073741824 | bytes 6815744 | tf_op jit(solution)/shard_map/dot_general | solution.py:150
  99.1 1.6 constant_dynamic-update-slice_fusion.1
  100.7 1.0 fusion.13
  101.7 1.0 fusion.7
  102.7 1.1 fusion.4
  103.8 1.0 fusion.10
  104.9 0.7 reshape.189.x_ref
  105.6 11.2 %shard_map.95 = f32[8,64,128]{2,1,0:T(8,128)} custom-call(f32[64,128]{1,0:T(8,128)} %reshape.189.x_ref), custom_call_target="tpu_custom_call" | custom-call | tf_op jit(solution)/shard_map/pallas_call | solution.py:58
  116.8 1.0 reduce_sum.28
  119.3 2.1 collective-permute-start.2
  121.6 1.6 constant_dynamic-update-slice_fusion
  123.3 4.0 %collective-permute-done.2 = f32[2,288,128]{2,1,0:T(8,128)S(1)} collective-permute-done((f32[2,288,128]{2,1,0:T(8,128)S(1)}, f32[2,288,128]{2,1,0:T(8,128)S(1)}, u32[]{:S(2)}, u32[]{:S(2)}) %collective-permute-start.2) | collective-permute-done | bytes 294944 | tf_op jit(solution)/shard_map/ppermute | solution.py:73
  128.1 1.4 collective-permute-done.1
  129.7 1.1 select_reduce_fusion
  131.0 15.4 %collective-permute-done.4 = f32[4,288,128]{2,1,0:T(8,128)S(1)} collective-permute-done((f32[4,288,128]{2,1,0:T(8,128)S(1)}, f32[4,288,128]{2,1,0:T(8,128)S(1)}, u32[]{:S(2)}, u32[]{:S(2)}) %collective-permute-start.4) | collective-permute-done | bytes 589856 | tf_op jit(solution)/shard_map/ppermute | solution.py:73
  146.5 1.8 collective-permute-start.5
  148.6 13.5 %collective-permute-done.5 = f32[2,288,128]{2,1,0:T(8,128)S(1)} collective-permute-done((f32[2,288,128]{2,1,0:T(8,128)S(1)}, f32[2,288,128]{2,1,0:T(8,128)S(1)}, u32[]{:S(2)}, u32[]{:S(2)}) %collective-permute-start.5) | collective-permute-done | bytes 294944 | tf_op jit(solution)/shard_map/ppermute | solution.py:73
  162.2 6.2 %collective-permute-start.6 = (f32[1,288,128]{2,1,0:T(8,128)S(1)}, f32[1,288,128]{2,1,0:T(8,128)S(1)}, u32[]{:S(2)}, u32[]{:S(2)}) collective-permute-start(f32[1,288,128]{2,1,0:T(8,128)S(1)} %slice_select_fusion.2), channel_id=1, source_target_pairs={{0,64},{8,72},{16,80},{24,88},{32,96},{40,104},{48,112},{56,120},{... | collective-permute-start | bytes 442376 | tf_op jit(solution)/shard_map/ppermute | solution.py:73
  168.3 4.3 %fusion = bf16[256,1024]{1,0:T(8,128)(2,1)} fusion(f32[256,1024]{1,0:T(8,128)S(1)} %bitcast.45, bf16[256,2048]{1,0:T(8,128)(2,1)S(1)} %copy-done.1, bf16[1024,2048]{1,0:T(8,128)(2,1)} %param.7), kind=kOutput, calls=%fused_computation.3 | convolution fusion | flops 1074266112 | bytes 6815744 | tf_op jit(solution)/shard_map/dot_general | solution.py:162
  172.7 2.5 %collective-permute-done.6 = f32[1,288,128]{2,1,0:T(8,128)S(1)} collective-permute-done((f32[1,288,128]{2,1,0:T(8,128)S(1)}, f32[1,288,128]{2,1,0:T(8,128)S(1)}, u32[]{:S(2)}, u32[]{:S(2)}) %collective-permute-start.6) | collective-permute-done | bytes 147488 | tf_op jit(solution)/shard_map/ppermute | solution.py:73
  176.3 0.8 copy.36
  177.2 26.7 %reduce-scatter.2.cloned.1.call-done = f32[32,2048]{1,0:T(8,128)} async-done(((f32[256,2048]{1,0:T(8,128)}), f32[32,2048]{1,0:T(8,128)}) %reduce-scatter.2.cloned.1.call-update) | async-done | bytes 262160 | tf_op jit(solution)/shard_map/reduce_scatter | solution.py:160
  203.9 1.6 convert_element_type.29
  (52 shorter events, 6.5 us)
Async XLA Ops:
  7.2 72.9 %copy-start = (bf16[256,1024]{1,0:T(8,128)(2,1)S(1)}, bf16[256,1024]{1,0:T(8,128)(2,1)}, u32[]{:S(2)}) copy-start(bf16[256,1024]{1,0:T(8,128)(2,1)} %param.6) | copy-start | bytes 1572868
  7.2 93.5 %all-gather.2.cloned.1.call-start = ((), (), s32[]{:S(2)}) async-start(), calls=%async_computation.2 | async-start | bytes 1179648 | tf_op jit(solution)/shard_map/all_gather | solution.py:122
  7.9 196.0 %reduce-scatter.2.cloned.1.call-start = ((), (), s32[]{:S(2)}) async-start(), calls=%async_computation.1 | async-start | bytes 2359296 | tf_op jit(solution)/shard_map/reduce_scatter | solution.py:160
  119.1 4.1 %copy-start.2 = (s32[2,1]{0,1:T(1,128)S(1)}, s32[2,1]{0,1:T(1,128)}, u32[]{:S(2)}) copy-start(s32[2,1]{0,1:T(1,128)} %param.10) | copy-start | bytes 28
  119.3 8.0 %collective-permute-start.2 = (f32[2,288,128]{2,1,0:T(8,128)S(1)}, f32[2,288,128]{2,1,0:T(8,128)S(1)}, u32[]{:S(2)}, u32[]{:S(2)}) collective-permute-start(f32[2,288,128]{2,1,0:T(8,128)S(1)} %bitcast.42), channel_id=1, source_target_pairs={{0,128},{8,136},{16,144},{24,152},{32,160},{40,168},{48,176},{56,1... | collective-permute-start | bytes 884744 | tf_op jit(solution)/shard_map/ppermute | solution.py:73
  123.2 4.3 %collective-permute-start = (s32[2]{0:T(128)S(1)}, s32[2]{0:T(128)S(1)}, u32[]{:S(2)}, u32[]{:S(2)}) collective-permute-start(s32[2]{0:T(128)S(1)} %bitcast.54), channel_id=1, source_target_pairs={{0,128},{8,136},{16,144},{24,152},{32,160},{40,168},{48,176},{56,1... | collective-permute-start | bytes 32 | tf_op jit(solution)/shard_map/ppermute | solution.py:73
  127.4 2.3 %collective-permute-start.3 = (f32[4,288,128]{2,1,0:T(8,128)S(1)}, f32[4,288,128]{2,1,0:T(8,128)S(1)}, u32[]{:S(2)}, u32[]{:S(2)}) collective-permute-start(f32[4,288,128]{2,1,0:T(8,128)S(1)} %pad_maximum_fusion.1), channel_id=1, source_target_pairs={{0,8},{8,0},{16,24},{24,16},{32,40},{40,32},{48,56},{56,48},{64,72... | collective-permute-start | bytes 1769480 | tf_op jit(solution)/shard_map/ppermute | solution.py:73
  127.6 1.9 collective-permute-start.1
  130.9 15.5 %collective-permute-start.4 = (f32[4,288,128]{2,1,0:T(8,128)S(1)}, f32[4,288,128]{2,1,0:T(8,128)S(1)}, u32[]{:S(2)}, u32[]{:S(2)}) collective-permute-start(f32[4,288,128]{2,1,0:T(8,128)S(1)} %slice_select_fusion), channel_id=1, source_target_pairs={{0,16},{8,24},{16,0},{24,8},{32,48},{40,56},{48,32},{56,40},{64,80... | collective-permute-start | bytes 1769480 | tf_op jit(solution)/shard_map/ppermute | solution.py:73
  146.4 21.9 %copy-start.1 = (bf16[256,2048]{1,0:T(8,128)(2,1)S(1)}, bf16[256,2048]{1,0:T(8,128)(2,1)}, u32[]{:S(2)}) copy-start(bf16[256,2048]{1,0:T(8,128)(2,1)} %all-gather.2.cloned.1.call-done) | copy-start | bytes 3145732
  146.5 15.6 %collective-permute-start.5 = (f32[2,288,128]{2,1,0:T(8,128)S(1)}, f32[2,288,128]{2,1,0:T(8,128)S(1)}, u32[]{:S(2)}, u32[]{:S(2)}) collective-permute-start(f32[2,288,128]{2,1,0:T(8,128)S(1)} %slice_select_fusion.1), channel_id=1, source_target_pairs={{0,32},{8,40},{16,48},{24,56},{32,0},{40,8},{48,16},{56,24},{64,96... | collective-permute-start | bytes 884744 | tf_op jit(solution)/shard_map/ppermute | solution.py:73
  162.2 13.0 %collective-permute-start.6 = (f32[1,288,128]{2,1,0:T(8,128)S(1)}, f32[1,288,128]{2,1,0:T(8,128)S(1)}, u32[]{:S(2)}, u32[]{:S(2)}) collective-permute-start(f32[1,288,128]{2,1,0:T(8,128)S(1)} %slice_select_fusion.2), channel_id=1, source_target_pairs={{0,64},{8,72},{16,80},{24,88},{32,96},{40,104},{48,112},{56,120},{... | collective-permute-start | bytes 442376 | tf_op jit(solution)/shard_map/ppermute | solution.py:73
Sparse Core Ops, SparseCore 0:
  10.7 59.5 all-gather.1
  123.3 80.5 reduce-scatter.1

commit v5 on v4

--- a/solution.py
+++ b/solution.py
@@ -100,6 +100,42 @@
     return dense
 
 
+def fetch_factors(rows, ids, per):
+    count = lax.axis_size("blk")
+    me = lax.axis_index("blk")
+    nbits = count.bit_length() - 1
+    order = [count // 2] + [1 << k for k in range(nbits - 1)]
+    far, near = order[0], order[1]
+    dense = order[2:][::-1]
+    held = rows
+    for bit in dense:
+        got = _swap(held, bit, count)
+        upper = (me & bit) != 0
+        held = jnp.where(upper, jnp.concatenate([got, held]), jnp.concatenate([held, got]))
+    group = far | near
+
+    def lookup(want):
+        owner = want // per
+        k = want % per
+        for i, bit in enumerate(dense):
+            k = k + ((owner & bit) != 0).astype(jnp.int32) * (per << i)
+        mine = (owner & group) == (me & group)
+        found = jnp.take(held, k, axis=0)
+        return mine, found, owner
+
+    pair_ids = jnp.concatenate([ids, _swap(ids, far, count)])
+    their_ids = _swap(pair_ids, near, count)
+    mine, found, _ = lookup(their_ids)
+    sent = jnp.where(mine[:, None, None], found, jnp.zeros_like(found))
+    got = _swap(sent, near, count)
+    mine, found, owner = lookup(pair_ids)
+    side = (owner & far) == (me & far)
+    cand = jnp.where(mine[:, None, None], found, got)
+    half = ids.shape[0]
+    got = _swap(cand[half:], far, count)
+    return jnp.where(side[:half, None, None], cand[:half], got)
+
+
 def on_device(tokens, weight, bank_a, bank_b, tile_map, grad_out):
     f32, bf16 = jnp.float32, jnp.bfloat16
     tile_ids = tile_map[:, 0]
@@ -118,10 +154,9 @@
     local = bank_a.shape[0]
     a_len = feats * rank_two // 128
     packed = jnp.concatenate([bank_a.reshape(local, -1, 128), b_cols.reshape(local, -1, 128)], axis=1)
-    all_ab = gather_axis(packed.reshape(-1, 128), "blk", 0).reshape(-1, packed.shape[1], 128)
+    picked = fetch_factors(packed, tile_ids, local)
     grad_rows = lax.all_gather(grad_out, "tp", axis=0, tiled=True)
 
-    picked = jnp.stack([all_ab[tile_ids[t]] for t in range(tiles)])
     fac_a = picked[:, :a_len].reshape(tiles, feats, rank_two)
     fac_b = picked[:, a_len:].reshape(tiles, rank_two, kv_dev)
 

time: 214 us -> 188 us (0.88)
  Pallas kernels: 86.2 us -> 21.1 us
  waiting for transfers between devices: 64.2 us -> 96.8 us
  starting transfers between devices: 11 us -> 23.6 us
  between operations: 18.2 us -> 14.4 us
    pallas_call x3 -> x2, Pallas kernels: 86.2 us -> 21.1 us  [gather_axis(): pl.pallas_call(functools.partial(_gather_kernel, axis, n), out_shape=jax....]
    ppermute x7 -> x13, waiting for transfers between devices: 36.8 us -> 54 us  [_swap(): return lax.ppermute(x, 'blk', [(i, i ^ bit) for i in range(count)])]
    all_gather x1, waiting for transfers between devices: 0.01 us -> 15.8 us  [on_device(): grad_rows = lax.all_gather(grad_out, 'tp', axis=0, tiled=True)]
    ppermute x7 -> x13, starting transfers between devices: 10.9 us -> 23.6 us  [_swap(): return lax.ppermute(x, 'blk', [(i, i ^ bit) for i in range(count)])]
    dot_general x1, matrix products: 4.31 us -> 2.08 us  [on_device(): backward = jnp.dot(grad_rows, weight.T, preferred_element_type=f32)]
  transfers between devices with their start and end apart: 9 -> 15, of which waited for: 6 -> 13; matrix products, arithmetic and copies ran while one was open for 11% -> 9% of each run, Pallas kernels for 35% -> 6%
where the time goes in v5:
time: 188 us; the launch traced here: 187 us
  waiting for transfers between devices  96.8 us (51%)
  starting transfers between devices  23.6 us (13%)
  Pallas kernels  21.1 us (11%)
  between operations  14.4 us (8%)
  matrix products  12.7 us (7%)
  other arithmetic  9.53 us (5%)
  local copies, waits for them, and re-layouts  8.75 us (5%)
    ppermute x13, waiting for transfers between devices, _swap(): return lax.ppermute(x, 'blk', [(i, i ^ bit) for i in range(count)])  54 us
    reduce_scatter x1, waiting for transfers between devices, on_device(): lax.psum_scatter(base, 'tp', scatter_dimension=0, tiled=True).astype(bf16)  27 us
    ppermute x13, starting transfers between devices, _swap(): return lax.ppermute(x, 'blk', [(i, i ^ bit) for i in range(count)])  23.6 us
    pallas_call x2, Pallas kernels, gather_axis(): pl.pallas_call(functools.partial(_gather_kernel, axis, n), out_shape=jax....  21.1 us
    all_gather x1, waiting for transfers between devices, on_device(): grad_rows = lax.all_gather(grad_out, 'tp', axis=0, tiled=True)  15.8 us
  transfers between devices with their start and end apart: 15, of which 13 were waited for; matrix products, arithmetic and copies ran while one was open for 9% of the time, Pallas kernels for 6%

profile of v5, /device:TPU:2, one launch (start us, length us, event | category | flops | bytes accessed | tf_op | source)
XLA Modules:
  0.0 187.0 jit_solution(9073110989773226810)
XLA Ops:
  7.2 1.1 copy.23
  9.2 7.2 %collective-permute-start.1 = (bf16[1,288,128]{2,1,0:T(8,128)(2,1)S(1)}, bf16[1,288,128]{2,1,0:T(8,128)(2,1)S(1)}, u32[]{:S(2)}, u32[]{:S(2)}) collective-permute-start(bf16[1,288,128]{2,1,0:T(8,128)(2,1)S(1)} %pad_maximum_fusion.2), channel_id=1, source_target_pairs={{0,64},{8,72},{16,80},{24,88},{32,96},{40,104},{48,112},{56,120},{... | collective-permute-start | bytes 221192 | tf_op jit(solution)/shard_map/ppermute | solution.py:73
  16.4 2.8 %collective-permute-done.1 = bf16[1,288,128]{2,1,0:T(8,128)(2,1)S(1)} collective-permute-done((bf16[1,288,128]{2,1,0:T(8,128)(2,1)S(1)}, bf16[1,288,128]{2,1,0:T(8,128)(2,1)S(1)}, u32[]{:S(2)}, u32[]{:S(2)}) %collective-permute-start.1) | collective-permute-done | bytes 73760 | tf_op jit(solution)/shard_map/ppermute | solution.py:73
  19.2 3.0 %collective-permute-start.2 = (bf16[2,288,128]{2,1,0:T(8,128)(2,1)S(1)}, bf16[2,288,128]{2,1,0:T(8,128)(2,1)S(1)}, u32[]{:S(2)}, u32[]{:S(2)}) collective-permute-start(bf16[2,288,128]{2,1,0:T(8,128)(2,1)S(1)} %maximum_select_fusion.2), channel_id=1, source_target_pairs={{0,32},{8,40},{16,48},{24,56},{32,0},{40,8},{48,16},{56,24},{64,96... | collective-permute-start | bytes 442376 | tf_op jit(solution)/shard_map/ppermute | solution.py:73
  22.8 3.1 %collective-permute-done = s32[2]{0:T(128)S(1)} collective-permute-done((s32[2]{0:T(128)}, s32[2]{0:T(128)S(1)}, u32[]{:S(2)}, u32[]{:S(2)}) %collective-permute-start) | collective-permute-done | bytes 40 | tf_op jit(solution)/shard_map/ppermute | solution.py:73
  25.9 1.2 and_select_fusion.1
  28.2 8.5 %collective-permute-done.3 = bf16[4,288,128]{2,1,0:T(8,128)(2,1)S(1)} collective-permute-done((bf16[4,288,128]{2,1,0:T(8,128)(2,1)S(1)}, bf16[4,288,128]{2,1,0:T(8,128)(2,1)S(1)}, u32[]{:S(2)}, u32[]{:S(2)}) %collective-permute-start.3) | collective-permute-done | bytes 294944 | tf_op jit(solution)/shard_map/ppermute | solution.py:73
  39.9 3.4 %fusion.30 = f32[256,2048]{1,0:T(8,128)S(1)} fusion(bf16[256,1024]{1,0:T(8,128)(2,1)S(1)} %copy-done, bf16[1024,2048]{1,0:T(8,128)(2,1)} %param.9), kind=kOutput, calls=%fused_computation.89 | convolution fusion | flops 1073741824 | bytes 6815744 | tf_op jit(solution)/shard_map/dot_general | solution.py:185
  43.3 2.0 %collective-permute-done.6 = bf16[2,288,128]{2,1,0:T(8,128)(2,1)S(1)} collective-permute-done((bf16[2,288,128]{2,1,0:T(8,128)(2,1)S(1)}, bf16[2,288,128]{2,1,0:T(8,128)(2,1)S(1)}, u32[]{:S(2)}, u32[]{:S(2)}) %collective-permute-start.6) | collective-permute-done | bytes 147488 | tf_op jit(solution)/shard_map/ppermute | solution.py:73
  46.8 10.9 %shard_map.93 = f32[8,64,128]{2,1,0:T(8,128)} custom-call(f32[64,128]{1,0:T(8,128)} %reshape.203.x_ref), custom_call_target="tpu_custom_call" | custom-call | tf_op jit(solution)/shard_map/pallas_call | solution.py:58
  57.7 1.0 reduce_sum.27
  59.0 15.8 %all-gather.2.cloned.1.call-done = bf16[256,2048]{1,0:T(8,128)(2,1)} async-done(((bf16[32,2048]{1,0:T(8,128)(2,1)}), bf16[256,2048]{1,0:T(8,128)(2,1)}) %all-gather.2.cloned.1.call-update) | async-done | bytes 1048592 | tf_op jit(solution)/shard_map/all_gather | solution.py:158
  74.7 1.0 fusion.12
  75.7 1.0 fusion.9
  76.7 1.7 fusion.3
  78.4 1.6 fusion.6
  80.9 10.2 %shard_map.94 = f32[8,64,128]{2,1,0:T(8,128)} custom-call(f32[64,128]{1,0:T(8,128)} %reshape.205.x_ref), custom_call_target="tpu_custom_call" | custom-call | tf_op jit(solution)/shard_map/pallas_call | solution.py:58
  91.1 1.0 reduce_sum.28
  94.9 1.5 collective-permute-start.8
  97.4 1.6 constant_dynamic-update-slice_fusion
  99.0 2.8 %collective-permute-done.8 = f32[2,288,128]{2,1,0:T(8,128)S(1)} collective-permute-done((f32[2,288,128]{2,1,0:T(8,128)S(1)}, f32[2,288,128]{2,1,0:T(8,128)S(1)}, u32[]{:S(2)}, u32[]{:S(2)}) %collective-permute-start.8) | collective-permute-done | bytes 294944 | tf_op jit(solution)/shard_map/ppermute | solution.py:73
  102.4 1.5 collective-permute-done.7
  104.1 1.1 select_reduce_fusion
  105.3 1.7 collective-permute-start.10
  107.1 13.9 %collective-permute-done.10 = f32[4,288,128]{2,1,0:T(8,128)S(1)} collective-permute-done((f32[4,288,128]{2,1,0:T(8,128)S(1)}, f32[4,288,128]{2,1,0:T(8,128)S(1)}, u32[]{:S(2)}, u32[]{:S(2)}) %collective-permute-start.10) | collective-permute-done | bytes 589856 | tf_op jit(solution)/shard_map/ppermute | solution.py:73
  121.1 2.5 %collective-permute-start.11 = (f32[2,288,128]{2,1,0:T(8,128)S(1)}, f32[2,288,128]{2,1,0:T(8,128)S(1)}, u32[]{:S(2)}, u32[]{:S(2)}) collective-permute-start(f32[2,288,128]{2,1,0:T(8,128)S(1)} %slice_select_fusion.1), channel_id=1, source_target_pairs={{0,32},{8,40},{16,48},{24,56},{32,0},{40,8},{48,16},{56,24},{64,96... | collective-permute-start | bytes 884744 | tf_op jit(solution)/shard_map/ppermute | solution.py:73
  124.0 12.8 %collective-permute-done.11 = f32[2,288,128]{2,1,0:T(8,128)S(1)} collective-permute-done((f32[2,288,128]{2,1,0:T(8,128)S(1)}, f32[2,288,128]{2,1,0:T(8,128)S(1)}, u32[]{:S(2)}, u32[]{:S(2)}) %collective-permute-start.11) | collective-permute-done | bytes 294944 | tf_op jit(solution)/shard_map/ppermute | solution.py:73
  136.8 5.7 %collective-permute-start.12 = (f32[1,288,128]{2,1,0:T(8,128)S(1)}, f32[1,288,128]{2,1,0:T(8,128)S(1)}, u32[]{:S(2)}, u32[]{:S(2)}) collective-permute-start(f32[1,288,128]{2,1,0:T(8,128)S(1)} %slice_select_fusion.3), channel_id=1, source_target_pairs={{0,64},{8,72},{16,80},{24,88},{32,96},{40,104},{48,112},{56,120},{... | collective-permute-start | bytes 442376 | tf_op jit(solution)/shard_map/ppermute | solution.py:73
  142.6 2.1 %fusion.1 = bf16[256,1024]{1,0:T(8,128)(2,1)} fusion(f32[2,128,1024]{2,1,0:T(8,128)S(1)} %convolution_multiply_fusion, bf16[256,2048]{1,0:T(8,128)(2,1)S(1)} %copy-done.4, bf16[1024,2048]{1,0:T(8,128)(2,1)S(1)} %copy-done.6), kind=kOutput, calls=%fused_computation.11 | convolution fusion | flops 1074266112 | bytes 6815744 | tf_op jit(solution)/shard_map/dot_general | solution.py:197
  144.7 4.8 %collective-permute-done.12 = f32[1,288,128]{2,1,0:T(8,128)S(1)} collective-permute-done((f32[1,288,128]{2,1,0:T(8,128)S(1)}, f32[1,288,128]{2,1,0:T(8,128)S(1)}, u32[]{:S(2)}, u32[]{:S(2)}) %collective-permute-start.12) | collective-permute-done | bytes 147488 | tf_op jit(solution)/shard_map/ppermute | solution.py:73
  151.5 27.0 %reduce-scatter.2.cloned.1.call-done = f32[32,2048]{1,0:T(8,128)} async-done(((f32[256,2048]{1,0:T(8,128)}), f32[32,2048]{1,0:T(8,128)}) %reduce-scatter.2.cloned.1.call-update) | async-done | bytes 262160 | tf_op jit(solution)/shard_map/reduce_scatter | solution.py:195
  178.5 1.6 convert_element_type.41
  (81 shorter events, 15.4 us)
Async XLA Ops:
  7.2 32.7 %copy-start = (bf16[256,1024]{1,0:T(8,128)(2,1)S(1)}, bf16[256,1024]{1,0:T(8,128)(2,1)}, u32[]{:S(2)}) copy-start(bf16[256,1024]{1,0:T(8,128)(2,1)} %param.8) | copy-start | bytes 1572868
  7.2 67.6 %all-gather.2.cloned.1.call-start = ((), (), s32[]{:S(2)}) async-start(), calls=%async_computation.2 | async-start | bytes 1179648 | tf_op jit(solution)/shard_map/all_gather | solution.py:158
  9.2 9.9 %collective-permute-start.1 = (bf16[1,288,128]{2,1,0:T(8,128)(2,1)S(1)}, bf16[1,288,128]{2,1,0:T(8,128)(2,1)S(1)}, u32[]{:S(2)}, u32[]{:S(2)}) collective-permute-start(bf16[1,288,128]{2,1,0:T(8,128)(2,1)S(1)} %pad_maximum_fusion.2), channel_id=1, source_target_pairs={{0,64},{8,72},{16,80},{24,88},{32,96},{40,104},{48,112},{56,120},{... | collective-permute-start | bytes 221192 | tf_op jit(solution)/shard_map/ppermute | solution.py:73
  19.2 8.9 %collective-permute-start.2 = (bf16[2,288,128]{2,1,0:T(8,128)(2,1)S(1)}, bf16[2,288,128]{2,1,0:T(8,128)(2,1)S(1)}, u32[]{:S(2)}, u32[]{:S(2)}) collective-permute-start(bf16[2,288,128]{2,1,0:T(8,128)(2,1)S(1)} %maximum_select_fusion.2), channel_id=1, source_target_pairs={{0,32},{8,40},{16,48},{24,56},{32,0},{40,8},{48,16},{56,24},{64,96... | collective-permute-start | bytes 442376 | tf_op jit(solution)/shard_map/ppermute | solution.py:73
  22.2 3.7 %collective-permute-start = (s32[2]{0:T(128)}, s32[2]{0:T(128)S(1)}, u32[]{:S(2)}, u32[]{:S(2)}) collective-permute-start(s32[2]{0:T(128)} %bitcast.52), channel_id=1, source_target_pairs={{0,128},{8,136},{16,144},{24,152},{32,160},{40,168},{48,176},{56,1... | collective-permute-start | bytes 32 | tf_op jit(solution)/shard_map/ppermute | solution.py:73
  22.7 155.8 %reduce-scatter.2.cloned.1.call-start = ((), (), s32[]{:S(2)}) async-start(), calls=%async_computation.1 | async-start | bytes 2359296 | tf_op jit(solution)/shard_map/reduce_scatter | solution.py:195
  27.1 1.1 collective-permute-start.4
  28.1 8.7 %collective-permute-start.3 = (bf16[4,288,128]{2,1,0:T(8,128)(2,1)S(1)}, bf16[4,288,128]{2,1,0:T(8,128)(2,1)S(1)}, u32[]{:S(2)}, u32[]{:S(2)}) collective-permute-start(bf16[4,288,128]{2,1,0:T(8,128)(2,1)S(1)} %maximum_select_fusion.1), channel_id=1, source_target_pairs={{0,16},{8,24},{16,0},{24,8},{32,48},{40,56},{48,32},{56,40},{64,80... | collective-permute-start | bytes 884744 | tf_op jit(solution)/shard_map/ppermute | solution.py:73
  37.6 1.7 collective-permute-start.5
  39.4 6.0 %collective-permute-start.6 = (bf16[2,288,128]{2,1,0:T(8,128)(2,1)S(1)}, bf16[2,288,128]{2,1,0:T(8,128)(2,1)S(1)}, u32[]{:S(2)}, u32[]{:S(2)}) collective-permute-start(bf16[2,288,128]{2,1,0:T(8,128)(2,1)S(1)} %slice.82), channel_id=1, source_target_pairs={{0,128},{8,136},{16,144},{24,152},{32,160},{40,168},{48,176},{56,1... | collective-permute-start | bytes 442376 | tf_op jit(solution)/shard_map/ppermute | solution.py:73
  45.4 34.7 %copy-start.2 = (bf16[2,288,128]{2,1,0:T(8,128)(2,1)}, bf16[2,288,128]{2,1,0:T(8,128)(2,1)S(1)}, u32[]{:S(2)}) copy-start(bf16[2,288,128]{2,1,0:T(8,128)(2,1)S(1)} %slice_select_fusion.2) | copy-start | bytes 442372
  59.0 34.6 %copy-start.1 = (f32[256,2048]{1,0:T(8,128)}, f32[256,2048]{1,0:T(8,128)S(1)}, u32[]{:S(2)}) copy-start(f32[256,2048]{1,0:T(8,128)S(1)} %constant_dynamic-update-slice_fusion.1) | copy-start | bytes 6291460
  93.8 0.9 copy-start.3
  94.9 7.0 %copy-start.5 = (s32[4]{0:T(128)S(1)}, s32[4]{0:T(128)}, u32[]{:S(2)}) copy-start(s32[4]{0:T(128)} %get-tuple-element.15) | copy-start | bytes 52
  94.9 6.8 %collective-permute-start.8 = (f32[2,288,128]{2,1,0:T(8,128)S(1)}, f32[2,288,128]{2,1,0:T(8,128)S(1)}, u32[]{:S(2)}, u32[]{:S(2)}) collective-permute-start(f32[2,288,128]{2,1,0:T(8,128)S(1)} %bitcast.40), channel_id=1, source_target_pairs={{0,128},{8,136},{16,144},{24,152},{32,160},{40,168},{48,176},{56,1... | collective-permute-start | bytes 884744 | tf_op jit(solution)/shard_map/ppermute | solution.py:73
  101.8 2.3 %collective-permute-start.9 = (f32[4,288,128]{2,1,0:T(8,128)S(1)}, f32[4,288,128]{2,1,0:T(8,128)S(1)}, u32[]{:S(2)}, u32[]{:S(2)}) collective-permute-start(f32[4,288,128]{2,1,0:T(8,128)S(1)} %pad_maximum_fusion.1), channel_id=1, source_target_pairs={{0,8},{8,0},{16,24},{24,16},{32,40},{40,32},{48,56},{56,48},{64,72... | collective-permute-start | bytes 1769480 | tf_op jit(solution)/shard_map/ppermute | solution.py:73
  101.9 2.0 %collective-permute-start.7 = (s32[4]{0:T(128)S(1)}, s32[4]{0:T(128)S(1)}, u32[]{:S(2)}, u32[]{:S(2)}) collective-permute-start(s32[4]{0:T(128)S(1)} %copy-done.5), channel_id=1, source_target_pairs={{0,8},{8,0},{16,24},{24,16},{32,40},{40,32},{48,56},{56,48},{64,72... | collective-permute-start | bytes 56 | tf_op jit(solution)/shard_map/ppermute | solution.py:73
  105.3 15.6 %collective-permute-start.10 = (f32[4,288,128]{2,1,0:T(8,128)S(1)}, f32[4,288,128]{2,1,0:T(8,128)S(1)}, u32[]{:S(2)}, u32[]{:S(2)}) collective-permute-start(f32[4,288,128]{2,1,0:T(8,128)S(1)} %slice_select_fusion), channel_id=1, source_target_pairs={{0,16},{8,24},{16,0},{24,8},{32,48},{40,56},{48,32},{56,40},{64,80... | collective-permute-start | bytes 1769480 | tf_op jit(solution)/shard_map/ppermute | solution.py:73
  121.0 21.6 %copy-start.6 = (bf16[1024,2048]{1,0:T(8,128)(2,1)S(1)}, bf16[1024,2048]{1,0:T(8,128)(2,1)}, u32[]{:S(2)}) copy-start(bf16[1024,2048]{1,0:T(8,128)(2,1)} %param.9) | copy-start | bytes 12582916
  121.1 21.5 %copy-start.4 = (bf16[256,2048]{1,0:T(8,128)(2,1)S(1)}, bf16[256,2048]{1,0:T(8,128)(2,1)}, u32[]{:S(2)}) copy-start(bf16[256,2048]{1,0:T(8,128)(2,1)} %all-gather.2.cloned.1.call-done) | copy-start | bytes 3145732
  121.1 15.6 %collective-permute-start.11 = (f32[2,288,128]{2,1,0:T(8,128)S(1)}, f32[2,288,128]{2,1,0:T(8,128)S(1)}, u32[]{:S(2)}, u32[]{:S(2)}) collective-permute-start(f32[2,288,128]{2,1,0:T(8,128)S(1)} %slice_select_fusion.1), channel_id=1, source_target_pairs={{0,32},{8,40},{16,48},{24,56},{32,0},{40,8},{48,16},{56,24},{64,96... | collective-permute-start | bytes 884744 | tf_op jit(solution)/shard_map/ppermute | solution.py:73
  136.8 12.6 %collective-permute-start.12 = (f32[1,288,128]{2,1,0:T(8,128)S(1)}, f32[1,288,128]{2,1,0:T(8,128)S(1)}, u32[]{:S(2)}, u32[]{:S(2)}) collective-permute-start(f32[1,288,128]{2,1,0:T(8,128)S(1)} %slice_select_fusion.3), channel_id=1, source_target_pairs={{0,64},{8,72},{16,80},{24,88},{32,96},{40,104},{48,112},{56,120},{... | collective-permute-start | bytes 442376 | tf_op jit(solution)/shard_map/ppermute | solution.py:73
Sparse Core Ops, SparseCore 0:
  22.9 51.8 all-gather.1
  99.1 79.3 reduce-scatter.1

commit v6 on v5

--- a/solution.py
+++ b/solution.py
@@ -100,6 +100,20 @@
     return dense
 
 
+def gather_tp(x):
+    count = lax.axis_size("tp")
+    me = lax.axis_index("tp")
+    held = x[None]
+    bit = count // 2
+    while bit:
+        got = lax.ppermute(held, "tp", [(i, i ^ bit) for i in range(count)])
+        upper = (me & bit) != 0
+        held = jnp.where(upper, jnp.stack([got, held], axis=1), jnp.stack([held, got], axis=1))
+        held = held.reshape((-1,) + x.shape)
+        bit //= 2
+    return held.reshape((-1,) + x.shape[1:])
+
+
 def fetch_factors(rows, ids, per):
     count = lax.axis_size("blk")
     me = lax.axis_index("blk")
@@ -155,7 +169,7 @@
     a_len = feats * rank_two // 128
     packed = jnp.concatenate([bank_a.reshape(local, -1, 128), b_cols.reshape(local, -1, 128)], axis=1)
     picked = fetch_factors(packed, tile_ids, local)
-    grad_rows = lax.all_gather(grad_out, "tp", axis=0, tiled=True)
+    grad_rows = gather_tp(grad_out)
 
     fac_a = picked[:, :a_len].reshape(tiles, feats, rank_two)
     fac_b = picked[:, a_len:].reshape(tiles, rank_two, kv_dev)

time: 188 us -> 174 us (0.926)
  waiting for transfers between devices: 96.8 us -> 81.2 us
  other arithmetic: 9.53 us -> 13.5 us
  matrix products: 12.7 us -> 10.2 us
    all_gather x1 -> x0, waiting for transfers between devices: 15.8 us -> none  [on_device(): grad_rows = lax.all_gather(grad_out, 'tp', axis=0, tiled=True)]
    ppermute x13, starting transfers between devices: 23.6 us -> 15.4 us  [_swap(): return lax.ppermute(x, 'blk', [(i, i ^ bit) for i in range(count)])]
    ppermute x0 -> x3, starting transfers between devices: none -> 7.36 us  [gather_tp(): got = lax.ppermute(held, 'tp', [(i, i ^ bit) for i in range(count)])]
    ppermute x0 -> x3, waiting for transfers between devices: none -> 2.15 us  [gather_tp(): got = lax.ppermute(held, 'tp', [(i, i ^ bit) for i in range(count)])]
    concatenate x2, other arithmetic: 0.12 us -> 2.02 us  [reduce_to_owner(): rows = jnp.concatenate([rows, _swap(rows, bit, count)])]
  transfers between devices with their start and end apart: 15 -> 17, of which waited for: 13 -> 14; matrix products, arithmetic and copies ran while one was open for 9% -> 12% of each run, Pallas kernels for 6% -> 0%
where the time goes in v6:
time: 174 us; the launch traced here: 173 us
  waiting for transfers between devices  81.2 us (47%)
  starting transfers between devices  22.8 us (13%)
  Pallas kernels  21.2 us (12%)
  between operations  14.4 us (8%)
  other arithmetic  13.5 us (8%)
  matrix products  10.2 us (6%)
  local copies, waits for them, and re-layouts  9.54 us (5%)
    ppermute x13, waiting for transfers between devices, _swap(): return lax.ppermute(x, 'blk', [(i, i ^ bit) for i in range(count)])  53.2 us
    reduce_scatter x1, waiting for transfers between devices, on_device(): lax.psum_scatter(base, 'tp', scatter_dimension=0, tiled=True).astype(bf16)  25.8 us
    pallas_call x2, Pallas kernels, gather_axis(): pl.pallas_call(functools.partial(_gather_kernel, axis, n), out_shape=jax....  21.2 us
    ppermute x13, starting transfers between devices, _swap(): return lax.ppermute(x, 'blk', [(i, i ^ bit) for i in range(count)])  15.4 us
    ppermute x3, starting transfers between devices, gather_tp(): got = lax.ppermute(held, 'tp', [(i, i ^ bit) for i in range(count)])  7.36 us
    dot_general x1, matrix products, on_device(): base = jnp.dot(tokens, weight, preferred_element_type=f32)  4.82 us
  transfers between devices with their start and end apart: 17, of which 14 were waited for; matrix products, arithmetic and copies ran while one was open for 12% of the time, Pallas kernels for 0%

profile of v6, /device:TPU:2, one launch (start us, length us, event | category | flops | bytes accessed | tf_op | source)
XLA Modules:
  0.0 172.7 jit_solution(11874298217506478845)
XLA Ops:
  7.2 1.1 copy.27
  9.2 7.2 %collective-permute-start.1 = (bf16[1,288,128]{2,1,0:T(8,128)(2,1)S(1)}, bf16[1,288,128]{2,1,0:T(8,128)(2,1)S(1)}, u32[]{:S(2)}, u32[]{:S(2)}) collective-permute-start(bf16[1,288,128]{2,1,0:T(8,128)(2,1)S(1)} %pad_maximum_fusion.2), channel_id=1, source_target_pairs={{0,64},{8,72},{16,80},{24,88},{32,96},{40,104},{48,112},{56,120},{... | collective-permute-start | bytes 221192 | tf_op jit(solution)/shard_map/ppermute | solution.py:73
  16.9 2.4 %collective-permute-start.7 = (bf16[1,32,2048]{2,1,0:T(8,128)(2,1)}, bf16[1,32,2048]{2,1,0:T(8,128)(2,1)S(1)}, u32[]{:S(2)}, u32[]{:S(2)}) collective-permute-start(bf16[1,32,2048]{2,1,0:T(8,128)(2,1)} %bitcast.64), channel_id=1, source_target_pairs={{0,4},{1,5},{2,6},{3,7},{4,0},{5,1},{6,2},{7,3},{8,12},{9,13},{10,... | collective-permute-start | bytes 393224 | tf_op jit(solution)/shard_map/ppermute | solution.py:109
  19.3 4.8 %fusion.30 = f32[256,2048]{1,0:T(8,128)} fusion(bf16[256,1024]{1,0:T(8,128)(2,1)S(1)} %copy-done, bf16[1024,2048]{1,0:T(8,128)(2,1)} %param.9), kind=kOutput, calls=%fused_computation.93 | convolution fusion | flops 1073741824 | bytes 6815744 | tf_op jit(solution)/shard_map/dot_general | solution.py:199
  24.3 1.1 collective-permute-done.4
  25.5 1.6 collective-permute-start.2
  27.1 3.3 %collective-permute-start.8 = (bf16[2,32,2048]{2,1,0:T(8,128)(2,1)S(1)}, bf16[2,32,2048]{2,1,0:T(8,128)(2,1)S(1)}, u32[]{:S(2)}, u32[]{:S(2)}) collective-permute-start(bf16[2,32,2048]{2,1,0:T(8,128)(2,1)S(1)} %maximum_select_fusion.4), channel_id=1, source_target_pairs={{0,2},{1,3},{2,0},{3,1},{4,6},{5,7},{6,4},{7,5},{8,10},{9,11},{10,... | collective-permute-start | bytes 786440 | tf_op jit(solution)/shard_map/ppermute | solution.py:109
  30.3 5.2 %collective-permute-done.2 = bf16[2,288,128]{2,1,0:T(8,128)(2,1)S(1)} collective-permute-done((bf16[2,288,128]{2,1,0:T(8,128)(2,1)S(1)}, bf16[2,288,128]{2,1,0:T(8,128)(2,1)S(1)}, u32[]{:S(2)}, u32[]{:S(2)}) %collective-permute-start.2) | collective-permute-done | bytes 147488 | tf_op jit(solution)/shard_map/ppermute | solution.py:73
  35.7 1.0 collective-permute-done.8
  36.8 1.7 collective-permute-start.9
  38.5 5.7 %collective-permute-done.3 = bf16[4,288,128]{2,1,0:T(8,128)(2,1)S(1)} collective-permute-done((bf16[4,288,128]{2,1,0:T(8,128)(2,1)S(1)}, bf16[4,288,128]{2,1,0:T(8,128)(2,1)S(1)}, u32[]{:S(2)}, u32[]{:S(2)}) %collective-permute-start.3) | collective-permute-done | bytes 294944 | tf_op jit(solution)/shard_map/ppermute | solution.py:73
  45.8 0.9 collective-permute-done.5
  46.8 1.9 %collective-permute-start.6 = (bf16[2,288,128]{2,1,0:T(8,128)(2,1)S(1)}, bf16[2,288,128]{2,1,0:T(8,128)(2,1)S(1)}, u32[]{:S(2)}, u32[]{:S(2)}) collective-permute-start(bf16[2,288,128]{2,1,0:T(8,128)(2,1)S(1)} %slice.82), channel_id=1, source_target_pairs={{0,128},{8,136},{16,144},{24,152},{32,160},{40,168},{48,176},{56,1... | collective-permute-start | bytes 442376 | tf_op jit(solution)/shard_map/ppermute | solution.py:73
  48.7 1.1 collective-permute-done.9
  50.6 1.5 maximum_select_fusion
  54.4 10.5 %shard_map.93 = f32[8,64,128]{2,1,0:T(8,128)} custom-call(f32[64,128]{1,0:T(8,128)} %reshape.313.x_ref), custom_call_target="tpu_custom_call" | custom-call | tf_op jit(solution)/shard_map/pallas_call | solution.py:58
  64.9 1.0 reduce_sum.27
  68.3 10.6 %shard_map.94 = f32[8,64,128]{2,1,0:T(8,128)} custom-call(f32[64,128]{1,0:T(8,128)} %reshape.314.x_ref), custom_call_target="tpu_custom_call" | custom-call | tf_op jit(solution)/shard_map/pallas_call | solution.py:58
  79.0 1.0 reduce_sum.28
  82.8 1.8 %collective-permute-start.11 = (f32[2,288,128]{2,1,0:T(8,128)S(1)}, f32[2,288,128]{2,1,0:T(8,128)S(1)}, u32[]{:S(2)}, u32[]{:S(2)}) collective-permute-start(f32[2,288,128]{2,1,0:T(8,128)S(1)} %bitcast.51), channel_id=1, source_target_pairs={{0,128},{8,136},{16,144},{24,152},{32,160},{40,168},{48,176},{56,1... | collective-permute-start | bytes 884744 | tf_op jit(solution)/shard_map/ppermute | solution.py:73
  84.6 1.7 constant_dynamic-update-slice_fusion.1
  87.2 1.6 constant_dynamic-update-slice_fusion
  91.0 1.1 collective-permute-done.10
  92.8 1.1 pad_maximum_fusion
  94.0 1.1 select_reduce_fusion
  95.7 14.9 %collective-permute-done.13 = f32[4,288,128]{2,1,0:T(8,128)S(1)} collective-permute-done((f32[4,288,128]{2,1,0:T(8,128)S(1)}, f32[4,288,128]{2,1,0:T(8,128)S(1)}, u32[]{:S(2)}, u32[]{:S(2)}) %collective-permute-start.13) | collective-permute-done | bytes 589856 | tf_op jit(solution)/shard_map/ppermute | solution.py:73
  110.8 1.0 collective-permute-start.14
  112.1 14.2 %collective-permute-done.14 = f32[2,288,128]{2,1,0:T(8,128)S(1)} collective-permute-done((f32[2,288,128]{2,1,0:T(8,128)S(1)}, f32[2,288,128]{2,1,0:T(8,128)S(1)}, u32[]{:S(2)}, u32[]{:S(2)}) %collective-permute-start.14) | collective-permute-done | bytes 294944 | tf_op jit(solution)/shard_map/ppermute | solution.py:73
  126.5 2.1 %fusion.1 = bf16[256,1024]{1,0:T(8,128)(2,1)} fusion(f32[2,128,1024]{2,1,0:T(8,128)S(1)} %convolution_multiply_fusion, bf16[256,2048]{1,0:T(8,128)(2,1)S(1)} %bitcast.60, bf16[1024,2048]{1,0:T(8,128)(2,1)S(1)} %copy-done.5), kind=kOutput, calls=%fused_computation.12 | convolution fusion | flops 1074266112 | bytes 6815744 | tf_op jit(solution)/shard_map/dot_general | solution.py:211
  128.6 7.9 %collective-permute-done.15 = f32[1,288,128]{2,1,0:T(8,128)S(1)} collective-permute-done((f32[1,288,128]{2,1,0:T(8,128)S(1)}, f32[1,288,128]{2,1,0:T(8,128)S(1)}, u32[]{:S(2)}, u32[]{:S(2)}) %collective-permute-start.15) | collective-permute-done | bytes 147488 | tf_op jit(solution)/shard_map/ppermute | solution.py:73
  138.5 25.8 %reduce-scatter.2.cloned.1.call-done = f32[32,2048]{1,0:T(8,128)} async-done(((f32[256,2048]{1,0:T(8,128)}), f32[32,2048]{1,0:T(8,128)}) %reduce-scatter.2.cloned.1.call-update) | async-done | bytes 262160 | tf_op jit(solution)/shard_map/reduce_scatter | solution.py:209
  164.2 1.6 convert_element_type.41
  (86 shorter events, 18.8 us)
Async XLA Ops:
  7.2 12.2 %copy-start = (bf16[256,1024]{1,0:T(8,128)(2,1)S(1)}, bf16[256,1024]{1,0:T(8,128)(2,1)}, u32[]{:S(2)}) copy-start(bf16[256,1024]{1,0:T(8,128)(2,1)} %param.8) | copy-start | bytes 1572868
  7.2 157.1 %reduce-scatter.2.cloned.1.call-start = ((), (), s32[]{:S(2)}) async-start(), calls=%async_computation.1 | async-start | bytes 2359296 | tf_op jit(solution)/shard_map/reduce_scatter | solution.py:209
  9.2 16.2 %collective-permute-start.1 = (bf16[1,288,128]{2,1,0:T(8,128)(2,1)S(1)}, bf16[1,288,128]{2,1,0:T(8,128)(2,1)S(1)}, u32[]{:S(2)}, u32[]{:S(2)}) collective-permute-start(bf16[1,288,128]{2,1,0:T(8,128)(2,1)S(1)} %pad_maximum_fusion.2), channel_id=1, source_target_pairs={{0,64},{8,72},{16,80},{24,88},{32,96},{40,104},{48,112},{56,120},{... | collective-permute-start | bytes 221192 | tf_op jit(solution)/shard_map/ppermute | solution.py:73
  16.4 7.8 %collective-permute-start = (s32[2]{0:T(128)}, s32[2]{0:T(128)S(1)}, u32[]{:S(2)}, u32[]{:S(2)}) collective-permute-start(s32[2]{0:T(128)} %bitcast.72), channel_id=1, source_target_pairs={{0,128},{8,136},{16,144},{24,152},{32,160},{40,168},{48,176},{56,1... | collective-permute-start | bytes 32 | tf_op jit(solution)/shard_map/ppermute | solution.py:73
  16.9 10.1 %collective-permute-start.7 = (bf16[1,32,2048]{2,1,0:T(8,128)(2,1)}, bf16[1,32,2048]{2,1,0:T(8,128)(2,1)S(1)}, u32[]{:S(2)}, u32[]{:S(2)}) collective-permute-start(bf16[1,32,2048]{2,1,0:T(8,128)(2,1)} %bitcast.64), channel_id=1, source_target_pairs={{0,4},{1,5},{2,6},{3,7},{4,0},{5,1},{6,2},{7,3},{8,12},{9,13},{10,... | collective-permute-start | bytes 393224 | tf_op jit(solution)/shard_map/ppermute | solution.py:109
  19.3 4.8 %copy-start.4 = (s32[2,1]{0,1:T(1,128)S(1)}, s32[2,1]{0,1:T(1,128)}, u32[]{:S(2)}) copy-start(s32[2,1]{0,1:T(1,128)} %param.12) | copy-start | bytes 28
  19.3 7.7 %copy-start.3 = (bf16[32,2048]{1,0:T(8,128)(2,1)S(1)}, bf16[32,2048]{1,0:T(8,128)(2,1)}, u32[]{:S(2)}) copy-start(bf16[32,2048]{1,0:T(8,128)(2,1)} %param.13) | copy-start | bytes 393220
  24.2 1.1 collective-permute-start.4
  25.5 10.1 %collective-permute-start.2 = (bf16[2,288,128]{2,1,0:T(8,128)(2,1)S(1)}, bf16[2,288,128]{2,1,0:T(8,128)(2,1)S(1)}, u32[]{:S(2)}, u32[]{:S(2)}) collective-permute-start(bf16[2,288,128]{2,1,0:T(8,128)(2,1)S(1)} %maximum_select_fusion.6), channel_id=1, source_target_pairs={{0,32},{8,40},{16,48},{24,56},{32,0},{40,8},{48,16},{56,24},{64,96... | collective-permute-start | bytes 442376 | tf_op jit(solution)/shard_map/ppermute | solution.py:73
  27.1 9.7 %collective-permute-start.8 = (bf16[2,32,2048]{2,1,0:T(8,128)(2,1)S(1)}, bf16[2,32,2048]{2,1,0:T(8,128)(2,1)S(1)}, u32[]{:S(2)}, u32[]{:S(2)}) collective-permute-start(bf16[2,32,2048]{2,1,0:T(8,128)(2,1)S(1)} %maximum_select_fusion.4), channel_id=1, source_target_pairs={{0,2},{1,3},{2,0},{3,1},{4,6},{5,7},{6,4},{7,5},{8,10},{9,11},{10,... | collective-permute-start | bytes 786440 | tf_op jit(solution)/shard_map/ppermute | solution.py:109
  35.6 8.6 %collective-permute-start.3 = (bf16[4,288,128]{2,1,0:T(8,128)(2,1)S(1)}, bf16[4,288,128]{2,1,0:T(8,128)(2,1)S(1)}, u32[]{:S(2)}, u32[]{:S(2)}) collective-permute-start(bf16[4,288,128]{2,1,0:T(8,128)(2,1)S(1)} %maximum_select_fusion.3), channel_id=1, source_target_pairs={{0,16},{8,24},{16,0},{24,8},{32,48},{40,56},{48,32},{56,40},{64,80... | collective-permute-start | bytes 884744 | tf_op jit(solution)/shard_map/ppermute | solution.py:73
  36.8 13.0 %collective-permute-start.9 = (bf16[4,32,2048]{2,1,0:T(8,128)(2,1)S(1)}, bf16[4,32,2048]{2,1,0:T(8,128)(2,1)S(1)}, u32[]{:S(2)}, u32[]{:S(2)}) collective-permute-start(bf16[4,32,2048]{2,1,0:T(8,128)(2,1)S(1)} %bitcast.54), channel_id=1, source_target_pairs={{0,1},{1,0},{2,3},{3,2},{4,5},{5,4},{6,7},{7,6},{8,9},{9,8},{10,11... | collective-permute-start | bytes 1572872 | tf_op jit(solution)/shard_map/ppermute | solution.py:109
  45.0 1.7 collective-permute-start.5
  46.8 6.0 %collective-permute-start.6 = (bf16[2,288,128]{2,1,0:T(8,128)(2,1)S(1)}, bf16[2,288,128]{2,1,0:T(8,128)(2,1)S(1)}, u32[]{:S(2)}, u32[]{:S(2)}) collective-permute-start(bf16[2,288,128]{2,1,0:T(8,128)(2,1)S(1)} %slice.82), channel_id=1, source_target_pairs={{0,128},{8,136},{16,144},{24,152},{32,160},{40,168},{48,176},{56,1... | collective-permute-start | bytes 442376 | tf_op jit(solution)/shard_map/ppermute | solution.py:73
  49.8 0.8 copy-start.2
  53.0 27.8 %copy-start.1 = (bf16[2,288,128]{2,1,0:T(8,128)(2,1)}, bf16[2,288,128]{2,1,0:T(8,128)(2,1)S(1)}, u32[]{:S(2)}) copy-start(bf16[2,288,128]{2,1,0:T(8,128)(2,1)S(1)} %slice_select_fusion.2) | copy-start | bytes 442372
  82.8 6.8 %collective-permute-start.11 = (f32[2,288,128]{2,1,0:T(8,128)S(1)}, f32[2,288,128]{2,1,0:T(8,128)S(1)}, u32[]{:S(2)}, u32[]{:S(2)}) collective-permute-start(f32[2,288,128]{2,1,0:T(8,128)S(1)} %bitcast.51), channel_id=1, source_target_pairs={{0,128},{8,136},{16,144},{24,152},{32,160},{40,168},{48,176},{56,1... | collective-permute-start | bytes 884744 | tf_op jit(solution)/shard_map/ppermute | solution.py:73
  90.5 2.3 %collective-permute-start.12 = (f32[4,288,128]{2,1,0:T(8,128)}, f32[4,288,128]{2,1,0:T(8,128)}, u32[]{:S(2)}, u32[]{:S(2)}) collective-permute-start(f32[4,288,128]{2,1,0:T(8,128)} %pad_maximum_fusion.1), channel_id=1, source_target_pairs={{0,8},{8,0},{16,24},{24,16},{32,40},{40,32},{48,56},{56,48},{64,72... | collective-permute-start | bytes 1769480 | tf_op jit(solution)/shard_map/ppermute | solution.py:73
  90.5 1.6 collective-permute-start.10
  95.2 15.5 %collective-permute-start.13 = (f32[4,288,128]{2,1,0:T(8,128)S(1)}, f32[4,288,128]{2,1,0:T(8,128)S(1)}, u32[]{:S(2)}, u32[]{:S(2)}) collective-permute-start(f32[4,288,128]{2,1,0:T(8,128)S(1)} %slice_select_fusion), channel_id=1, source_target_pairs={{0,16},{8,24},{16,0},{24,8},{32,48},{40,56},{48,32},{56,40},{64,80... | collective-permute-start | bytes 1769480 | tf_op jit(solution)/shard_map/ppermute | solution.py:73
  110.6 15.9 %copy-start.5 = (bf16[1024,2048]{1,0:T(8,128)(2,1)S(1)}, bf16[1024,2048]{1,0:T(8,128)(2,1)}, u32[]{:S(2)}) copy-start(bf16[1024,2048]{1,0:T(8,128)(2,1)} %param.9) | copy-start | bytes 12582916
  110.8 15.5 %collective-permute-start.14 = (f32[2,288,128]{2,1,0:T(8,128)S(1)}, f32[2,288,128]{2,1,0:T(8,128)S(1)}, u32[]{:S(2)}, u32[]{:S(2)}) collective-permute-start(f32[2,288,128]{2,1,0:T(8,128)S(1)} %slice_select_fusion.1), channel_id=1, source_target_pairs={{0,32},{8,40},{16,48},{24,56},{32,0},{40,8},{48,16},{56,24},{64,96... | collective-permute-start | bytes 884744 | tf_op jit(solution)/shard_map/ppermute | solution.py:73
  126.4 10.1 %collective-permute-start.15 = (f32[1,288,128]{2,1,0:T(8,128)S(1)}, f32[1,288,128]{2,1,0:T(8,128)S(1)}, u32[]{:S(2)}, u32[]{:S(2)}) collective-permute-start(f32[1,288,128]{2,1,0:T(8,128)S(1)} %slice_select_fusion.3), channel_id=1, source_target_pairs={{0,64},{8,72},{16,80},{24,88},{32,96},{40,104},{48,112},{56,120},{... | collective-permute-start | bytes 442376 | tf_op jit(solution)/shard_map/ppermute | solution.py:73
Sparse Core Ops, SparseCore 0:
  88.9 75.2 reduce-scatter.1

commit v7 on v6

--- a/solution.py
+++ b/solution.py
@@ -176,7 +176,6 @@
 
     tok_t = tokens.reshape(tiles, tile_rows, feats)
     act_part = jnp.einsum("tre,tek->trk", tok_t, fac_a, preferred_element_type=f32)
-    rank_act = gather_axis(act_part.reshape(-1, 128), "tp", 2).sum(0).reshape(act_part.shape).astype(bf16)
 
     g_t = grad_rows.reshape(tiles, tile_rows, 2 * kv_width)
     g_key = lax.dynamic_slice_in_dim(g_t, col0, kv_dev, 2)
@@ -188,7 +187,10 @@
         ],
         axis=2,
     )
-    rank_grad = gather_axis(grad_part.reshape(-1, 128), "tp", 3).sum(0).reshape(grad_part.shape).astype(bf16)
+    parts = jnp.stack([act_part, grad_part])
+    both = gather_axis(parts.reshape(-1, 128), "tp", 2).sum(0).reshape(parts.shape)
+    rank_act = both[0].astype(bf16)
+    rank_grad = both[1].astype(bf16)
 
     lora_key = jnp.einsum(
         "trk,tkc->trc", rank_act[:, :, :rank_one], fac_b[:, :rank_one], preferred_element_type=f32

time: 174 us -> 165 us (0.948)
  Pallas kernels: 21.2 us -> 12.3 us
  waiting for transfers between devices: 81.2 us -> 84.1 us
    pallas_call x2 -> x1, Pallas kernels: 21.2 us -> 12.3 us  [gather_axis(): pl.pallas_call(functools.partial(_gather_kernel, axis, n), out_shape=jax....]
  transfers between devices with their start and end apart: 17 -> 17, of which waited for: 14 -> 14; matrix products, arithmetic and copies ran while one was open for 12% -> 13% of each run, Pallas kernels for 0% -> 0%
where the time goes in v7:
time: 165 us; the launch traced here: 164 us
  waiting for transfers between devices  84.1 us (51%)
  starting transfers between devices  22.3 us (14%)
  between operations  14.4 us (9%)
  other arithmetic  12.5 us (8%)
  Pallas kernels  12.3 us (7%)
  matrix products  10.2 us (6%)
  local copies, waits for them, and re-layouts  7.94 us (5%)
    ppermute x13, waiting for transfers between devices, _swap(): return lax.ppermute(x, 'blk', [(i, i ^ bit) for i in range(count)])  54.5 us
    reduce_scatter x1, waiting for transfers between devices, on_device(): lax.psum_scatter(base, 'tp', scatter_dimension=0, tiled=True).astype(bf16)  27.3 us
    ppermute x13, starting transfers between devices, _swap(): return lax.ppermute(x, 'blk', [(i, i ^ bit) for i in range(count)])  16.6 us
    pallas_call x1, Pallas kernels, gather_axis(): pl.pallas_call(functools.partial(_gather_kernel, axis, n), out_shape=jax....  12.3 us
    ppermute x3, starting transfers between devices, gather_tp(): got = lax.ppermute(held, 'tp', [(i, i ^ bit) for i in range(count)])  5.63 us
    dot_general x1, matrix products, on_device(): base = jnp.dot(tokens, weight, preferred_element_type=f32)  4.82 us
  transfers between devices with their start and end apart: 17, of which 14 were waited for; matrix products, arithmetic and copies ran while one was open for 13% of the time, Pallas kernels for 0%

profile of v7, /device:TPU:2, one launch (start us, length us, event | category | flops | bytes accessed | tf_op | source)
XLA Modules:
  0.0 163.7 jit_solution(4377394091539296621)
XLA Ops:
  7.2 2.4 %collective-permute-start = (s32[2]{0:T(128)}, s32[2]{0:T(128)S(1)}, u32[]{:S(2)}, u32[]{:S(2)}) collective-permute-start(s32[2]{0:T(128)} %bitcast.77), channel_id=1, source_target_pairs={{0,128},{8,136},{16,144},{24,152},{32,160},{40,168},{48,176},{56,1... | collective-permute-start | bytes 32 | tf_op jit(solution)/shard_map/ppermute | solution.py:73
  10.3 1.0 copy.25
  12.2 7.2 %collective-permute-start.1 = (bf16[1,288,128]{2,1,0:T(8,128)(2,1)S(1)}, bf16[1,288,128]{2,1,0:T(8,128)(2,1)S(1)}, u32[]{:S(2)}, u32[]{:S(2)}) collective-permute-start(bf16[1,288,128]{2,1,0:T(8,128)(2,1)S(1)} %pad_maximum_fusion.2), channel_id=1, source_target_pairs={{0,64},{8,72},{16,80},{24,88},{32,96},{40,104},{48,112},{56,120},{... | collective-permute-start | bytes 221192 | tf_op jit(solution)/shard_map/ppermute | solution.py:73
  19.4 4.8 %fusion.31 = f32[256,2048]{1,0:T(8,128)} fusion(bf16[256,1024]{1,0:T(8,128)(2,1)S(1)} %copy-done, bf16[1024,2048]{1,0:T(8,128)(2,1)} %param.9), kind=kOutput, calls=%fused_computation.95 | convolution fusion | flops 1073741824 | bytes 6815744 | tf_op jit(solution)/shard_map/dot_general | solution.py:201
  24.3 1.1 collective-permute-done.4
  25.5 1.6 collective-permute-start.2
  27.1 3.3 %collective-permute-start.8 = (bf16[2,32,2048]{2,1,0:T(8,128)(2,1)S(1)}, bf16[2,32,2048]{2,1,0:T(8,128)(2,1)S(1)}, u32[]{:S(2)}, u32[]{:S(2)}) collective-permute-start(bf16[2,32,2048]{2,1,0:T(8,128)(2,1)S(1)} %maximum_select_fusion.4), channel_id=1, source_target_pairs={{0,2},{1,3},{2,0},{3,1},{4,6},{5,7},{6,4},{7,5},{8,10},{9,11},{10,... | collective-permute-start | bytes 786440 | tf_op jit(solution)/shard_map/ppermute | solution.py:109
  30.4 5.2 %collective-permute-done.2 = bf16[2,288,128]{2,1,0:T(8,128)(2,1)S(1)} collective-permute-done((bf16[2,288,128]{2,1,0:T(8,128)(2,1)S(1)}, bf16[2,288,128]{2,1,0:T(8,128)(2,1)S(1)}, u32[]{:S(2)}, u32[]{:S(2)}) %collective-permute-start.2) | collective-permute-done | bytes 147488 | tf_op jit(solution)/shard_map/ppermute | solution.py:73
  35.8 1.0 collective-permute-done.8
  36.9 1.7 %collective-permute-start.9 = (bf16[4,32,2048]{2,1,0:T(8,128)(2,1)S(1)}, bf16[4,32,2048]{2,1,0:T(8,128)(2,1)}, u32[]{:S(2)}, u32[]{:S(2)}) collective-permute-start(bf16[4,32,2048]{2,1,0:T(8,128)(2,1)S(1)} %bitcast.60), channel_id=1, source_target_pairs={{0,1},{1,0},{2,3},{3,2},{4,5},{5,4},{6,7},{7,6},{8,9},{9,8},{10,11... | collective-permute-start | bytes 1572872 | tf_op jit(solution)/shard_map/ppermute | solution.py:109
  38.5 5.7 %collective-permute-done.3 = bf16[4,288,128]{2,1,0:T(8,128)(2,1)S(1)} collective-permute-done((bf16[4,288,128]{2,1,0:T(8,128)(2,1)S(1)}, bf16[4,288,128]{2,1,0:T(8,128)(2,1)S(1)}, u32[]{:S(2)}, u32[]{:S(2)}) %collective-permute-start.3) | collective-permute-done | bytes 294944 | tf_op jit(solution)/shard_map/ppermute | solution.py:73
  45.8 0.9 collective-permute-done.5
  46.9 1.9 %collective-permute-start.6 = (bf16[2,288,128]{2,1,0:T(8,128)(2,1)S(1)}, bf16[2,288,128]{2,1,0:T(8,128)(2,1)S(1)}, u32[]{:S(2)}, u32[]{:S(2)}) collective-permute-start(bf16[2,288,128]{2,1,0:T(8,128)(2,1)S(1)} %slice.94), channel_id=1, source_target_pairs={{0,128},{8,136},{16,144},{24,152},{32,160},{40,168},{48,176},{56,1... | collective-permute-start | bytes 442376 | tf_op jit(solution)/shard_map/ppermute | solution.py:73
  48.7 1.2 collective-permute-done.9
  50.0 1.3 maximum_select_fusion
  51.3 1.6 collective-permute-done.6
  54.8 12.3 %shard_map.93 = f32[8,128,128]{2,1,0:T(8,128)} custom-call(f32[128,128]{1,0:T(8,128)} %reshape.313.x_ref), custom_call_target="tpu_custom_call" | custom-call | tf_op jit(solution)/shard_map/pallas_call | solution.py:58
  67.1 1.1 reduce_sum.18
  72.4 1.6 collective-permute-start.11
  74.0 1.7 %constant_dynamic-update-slice_fusion.1 = f32[256,2048]{1,0:T(8,128)} fusion(f32[256,2048]{1,0:T(8,128)} %fusion.31, s32[]{:T(128)S(6)} %select_n.202, f32[2,128,128]{2,1,0:T(8,128)} %convolution_multiply_fusion.3), kind=kLoop, calls=%fused_computation.78 | loop fusion | flops 32768 | bytes 393220 | tf_op jit(solution)/shard_map/dynamic_update_slice | solution.py:202
  75.6 0.9 convolution_multiply_fusion.2
  76.6 1.6 constant_dynamic-update-slice_fusion
  78.2 1.0 collective-permute-done.11
  80.6 1.1 collective-permute-done.10
  82.4 1.1 pad_maximum_fusion
  83.6 1.1 select_reduce_fusion
  85.1 15.1 %collective-permute-done.13 = f32[4,288,128]{2,1,0:T(8,128)S(1)} collective-permute-done((f32[4,288,128]{2,1,0:T(8,128)S(1)}, f32[4,288,128]{2,1,0:T(8,128)S(1)}, u32[]{:S(2)}, u32[]{:S(2)}) %collective-permute-start.13) | collective-permute-done | bytes 589856 | tf_op jit(solution)/shard_map/ppermute | solution.py:73
  101.5 14.2 %collective-permute-done.14 = f32[2,288,128]{2,1,0:T(8,128)S(1)} collective-permute-done((f32[2,288,128]{2,1,0:T(8,128)S(1)}, f32[2,288,128]{2,1,0:T(8,128)S(1)}, u32[]{:S(2)}, u32[]{:S(2)}) %collective-permute-start.14) | collective-permute-done | bytes 294944 | tf_op jit(solution)/shard_map/ppermute | solution.py:73
  115.9 2.1 %fusion.1 = bf16[256,1024]{1,0:T(8,128)(2,1)} fusion(f32[2,128,1024]{2,1,0:T(8,128)S(1)} %convolution_multiply_fusion, bf16[256,2048]{1,0:T(8,128)(2,1)S(1)} %bitcast.66, bf16[1024,2048]{1,0:T(8,128)(2,1)S(1)} %copy-done.4), kind=kOutput, calls=%fused_computation.12 | convolution fusion | flops 1074266112 | bytes 6815744 | tf_op jit(solution)/shard_map/dot_general | solution.py:213
  118.0 7.9 %collective-permute-done.15 = f32[1,288,128]{2,1,0:T(8,128)S(1)} collective-permute-done((f32[1,288,128]{2,1,0:T(8,128)S(1)}, f32[1,288,128]{2,1,0:T(8,128)S(1)}, u32[]{:S(2)}, u32[]{:S(2)}) %collective-permute-start.15) | collective-permute-done | bytes 147488 | tf_op jit(solution)/shard_map/ppermute | solution.py:73
  127.9 27.3 %reduce-scatter.2.cloned.1.call-done = f32[32,2048]{1,0:T(8,128)} async-done(((f32[256,2048]{1,0:T(8,128)}), f32[32,2048]{1,0:T(8,128)}) %reduce-scatter.2.cloned.1.call-update) | async-done | bytes 262160 | tf_op jit(solution)/shard_map/reduce_scatter | solution.py:211
  155.2 1.6 convert_element_type.36
  (82 shorter events, 15.6 us)
Async XLA Ops:
  7.2 12.2 %copy-start = (bf16[256,1024]{1,0:T(8,128)(2,1)S(1)}, bf16[256,1024]{1,0:T(8,128)(2,1)}, u32[]{:S(2)}) copy-start(bf16[256,1024]{1,0:T(8,128)(2,1)} %param.8) | copy-start | bytes 1572868
  7.2 148.0 %reduce-scatter.2.cloned.1.call-start = ((), (), s32[]{:S(2)}) async-start(), calls=%async_computation.1 | async-start | bytes 2359296 | tf_op jit(solution)/shard_map/reduce_scatter | solution.py:211
  7.2 17.0 %collective-permute-start = (s32[2]{0:T(128)}, s32[2]{0:T(128)S(1)}, u32[]{:S(2)}, u32[]{:S(2)}) collective-permute-start(s32[2]{0:T(128)} %bitcast.77), channel_id=1, source_target_pairs={{0,128},{8,136},{16,144},{24,152},{32,160},{40,168},{48,176},{56,1... | collective-permute-start | bytes 32 | tf_op jit(solution)/shard_map/ppermute | solution.py:73
  9.6 17.5 %collective-permute-start.7 = (bf16[1,32,2048]{2,1,0:T(8,128)(2,1)}, bf16[1,32,2048]{2,1,0:T(8,128)(2,1)S(1)}, u32[]{:S(2)}, u32[]{:S(2)}) collective-permute-start(bf16[1,32,2048]{2,1,0:T(8,128)(2,1)} %bitcast.69), channel_id=1, source_target_pairs={{0,4},{1,5},{2,6},{3,7},{4,0},{5,1},{6,2},{7,3},{8,12},{9,13},{10,... | collective-permute-start | bytes 393224 | tf_op jit(solution)/shard_map/ppermute | solution.py:109
  12.2 13.3 %collective-permute-start.1 = (bf16[1,288,128]{2,1,0:T(8,128)(2,1)S(1)}, bf16[1,288,128]{2,1,0:T(8,128)(2,1)S(1)}, u32[]{:S(2)}, u32[]{:S(2)}) collective-permute-start(bf16[1,288,128]{2,1,0:T(8,128)(2,1)S(1)} %pad_maximum_fusion.2), channel_id=1, source_target_pairs={{0,64},{8,72},{16,80},{24,88},{32,96},{40,104},{48,112},{56,120},{... | collective-permute-start | bytes 221192 | tf_op jit(solution)/shard_map/ppermute | solution.py:73
  19.4 4.8 %copy-start.3 = (s32[2,1]{0,1:T(1,128)S(1)}, s32[2,1]{0,1:T(1,128)}, u32[]{:S(2)}) copy-start(s32[2,1]{0,1:T(1,128)} %param.12) | copy-start | bytes 28
  19.4 7.7 %copy-start.2 = (bf16[32,2048]{1,0:T(8,128)(2,1)S(1)}, bf16[32,2048]{1,0:T(8,128)(2,1)}, u32[]{:S(2)}) copy-start(bf16[32,2048]{1,0:T(8,128)(2,1)} %param.13) | copy-start | bytes 393220
  24.3 1.1 collective-permute-start.4
  25.5 10.1 %collective-permute-start.2 = (bf16[2,288,128]{2,1,0:T(8,128)(2,1)S(1)}, bf16[2,288,128]{2,1,0:T(8,128)(2,1)S(1)}, u32[]{:S(2)}, u32[]{:S(2)}) collective-permute-start(bf16[2,288,128]{2,1,0:T(8,128)(2,1)S(1)} %maximum_select_fusion.6), channel_id=1, source_target_pairs={{0,32},{8,40},{16,48},{24,56},{32,0},{40,8},{48,16},{56,24},{64,96... | collective-permute-start | bytes 442376 | tf_op jit(solution)/shard_map/ppermute | solution.py:73
  27.1 9.7 %collective-permute-start.8 = (bf16[2,32,2048]{2,1,0:T(8,128)(2,1)S(1)}, bf16[2,32,2048]{2,1,0:T(8,128)(2,1)S(1)}, u32[]{:S(2)}, u32[]{:S(2)}) collective-permute-start(bf16[2,32,2048]{2,1,0:T(8,128)(2,1)S(1)} %maximum_select_fusion.4), channel_id=1, source_target_pairs={{0,2},{1,3},{2,0},{3,1},{4,6},{5,7},{6,4},{7,5},{8,10},{9,11},{10,... | collective-permute-start | bytes 786440 | tf_op jit(solution)/shard_map/ppermute | solution.py:109
  35.6 8.6 %collective-permute-start.3 = (bf16[4,288,128]{2,1,0:T(8,128)(2,1)S(1)}, bf16[4,288,128]{2,1,0:T(8,128)(2,1)S(1)}, u32[]{:S(2)}, u32[]{:S(2)}) collective-permute-start(bf16[4,288,128]{2,1,0:T(8,128)(2,1)S(1)} %maximum_select_fusion.3), channel_id=1, source_target_pairs={{0,16},{8,24},{16,0},{24,8},{32,48},{40,56},{48,32},{56,40},{64,80... | collective-permute-start | bytes 884744 | tf_op jit(solution)/shard_map/ppermute | solution.py:73
  36.9 13.1 %collective-permute-start.9 = (bf16[4,32,2048]{2,1,0:T(8,128)(2,1)S(1)}, bf16[4,32,2048]{2,1,0:T(8,128)(2,1)}, u32[]{:S(2)}, u32[]{:S(2)}) collective-permute-start(bf16[4,32,2048]{2,1,0:T(8,128)(2,1)S(1)} %bitcast.60), channel_id=1, source_target_pairs={{0,1},{1,0},{2,3},{3,2},{4,5},{5,4},{6,7},{7,6},{8,9},{9,8},{10,11... | collective-permute-start | bytes 1572872 | tf_op jit(solution)/shard_map/ppermute | solution.py:109
  45.1 1.7 %collective-permute-start.5 = (bf16[4,288,128]{2,1,0:T(8,128)(2,1)S(1)}, bf16[4,288,128]{2,1,0:T(8,128)(2,1)S(1)}, u32[]{:S(2)}, u32[]{:S(2)}) collective-permute-start(bf16[4,288,128]{2,1,0:T(8,128)(2,1)S(1)} %select_select_fusion), channel_id=1, source_target_pairs={{0,8},{8,0},{16,24},{24,16},{32,40},{40,32},{48,56},{56,48},{64,72... | collective-permute-start | bytes 884744 | tf_op jit(solution)/shard_map/ppermute | solution.py:73
  46.9 6.0 %collective-permute-start.6 = (bf16[2,288,128]{2,1,0:T(8,128)(2,1)S(1)}, bf16[2,288,128]{2,1,0:T(8,128)(2,1)S(1)}, u32[]{:S(2)}, u32[]{:S(2)}) collective-permute-start(bf16[2,288,128]{2,1,0:T(8,128)(2,1)S(1)} %slice.94), channel_id=1, source_target_pairs={{0,128},{8,136},{16,144},{24,152},{32,160},{40,168},{48,176},{56,1... | collective-permute-start | bytes 442376 | tf_op jit(solution)/shard_map/ppermute | solution.py:73
  53.0 17.3 %copy-start.1 = (bf16[2,288,128]{2,1,0:T(8,128)(2,1)}, bf16[2,288,128]{2,1,0:T(8,128)(2,1)S(1)}, u32[]{:S(2)}) copy-start(bf16[2,288,128]{2,1,0:T(8,128)(2,1)S(1)} %slice_select_fusion.2) | copy-start | bytes 442372
  72.4 6.8 %collective-permute-start.11 = (f32[2,288,128]{2,1,0:T(8,128)S(1)}, f32[2,288,128]{2,1,0:T(8,128)S(1)}, u32[]{:S(2)}, u32[]{:S(2)}) collective-permute-start(f32[2,288,128]{2,1,0:T(8,128)S(1)} %bitcast.57), channel_id=1, source_target_pairs={{0,128},{8,136},{16,144},{24,152},{32,160},{40,168},{48,176},{56,1... | collective-permute-start | bytes 884744 | tf_op jit(solution)/shard_map/ppermute | solution.py:73
  80.1 2.3 %collective-permute-start.12 = (f32[4,288,128]{2,1,0:T(8,128)}, f32[4,288,128]{2,1,0:T(8,128)}, u32[]{:S(2)}, u32[]{:S(2)}) collective-permute-start(f32[4,288,128]{2,1,0:T(8,128)} %pad_maximum_fusion.1), channel_id=1, source_target_pairs={{0,8},{8,0},{16,24},{24,16},{32,40},{40,32},{48,56},{56,48},{64,72... | collective-permute-start | bytes 1769480 | tf_op jit(solution)/shard_map/ppermute | solution.py:73
  80.1 1.6 collective-permute-start.10
  84.7 15.5 %collective-permute-start.13 = (f32[4,288,128]{2,1,0:T(8,128)S(1)}, f32[4,288,128]{2,1,0:T(8,128)S(1)}, u32[]{:S(2)}, u32[]{:S(2)}) collective-permute-start(f32[4,288,128]{2,1,0:T(8,128)S(1)} %slice_select_fusion), channel_id=1, source_target_pairs={{0,16},{8,24},{16,0},{24,8},{32,48},{40,56},{48,32},{56,40},{64,80... | collective-permute-start | bytes 1769480 | tf_op jit(solution)/shard_map/ppermute | solution.py:73
  100.2 15.7 %copy-start.4 = (bf16[1024,2048]{1,0:T(8,128)(2,1)S(1)}, bf16[1024,2048]{1,0:T(8,128)(2,1)}, u32[]{:S(2)}) copy-start(bf16[1024,2048]{1,0:T(8,128)(2,1)} %param.9) | copy-start | bytes 12582916
  100.4 15.4 %collective-permute-start.14 = (f32[2,288,128]{2,1,0:T(8,128)S(1)}, f32[2,288,128]{2,1,0:T(8,128)S(1)}, u32[]{:S(2)}, u32[]{:S(2)}) collective-permute-start(f32[2,288,128]{2,1,0:T(8,128)S(1)} %slice_select_fusion.1), channel_id=1, source_target_pairs={{0,32},{8,40},{16,48},{24,56},{32,0},{40,8},{48,16},{56,24},{64,96... | collective-permute-start | bytes 884744 | tf_op jit(solution)/shard_map/ppermute | solution.py:73
  115.8 10.1 %collective-permute-start.15 = (f32[1,288,128]{2,1,0:T(8,128)S(1)}, f32[1,288,128]{2,1,0:T(8,128)S(1)}, u32[]{:S(2)}, u32[]{:S(2)}) collective-permute-start(f32[1,288,128]{2,1,0:T(8,128)S(1)} %slice_select_fusion.3), channel_id=1, source_target_pairs={{0,64},{8,72},{16,80},{24,88},{32,96},{40,104},{48,112},{56,120},{... | collective-permute-start | bytes 442376 | tf_op jit(solution)/shard_map/ppermute | solution.py:73
Sparse Core Ops, SparseCore 0:
  78.3 76.8 reduce-scatter.1

commit v8 on v7

--- a/solution.py
+++ b/solution.py
@@ -114,6 +114,23 @@
     return held.reshape((-1,) + x.shape[1:])
 
 
+def reduce_scatter_tp(x):
+    count = lax.axis_size("tp")
+    me = lax.axis_index("tp")
+    nbits = count.bit_length() - 1
+    held = x.reshape((2,) * nbits + (x.shape[0] // count,) + x.shape[1:])
+    for k in range(nbits):
+        bit = 1 << k
+        axis = nbits - 1 - k
+        low = lax.index_in_dim(held, 0, axis, keepdims=False)
+        high = lax.index_in_dim(held, 1, axis, keepdims=False)
+        upper = (me & bit) != 0
+        keep = jnp.where(upper, high, low)
+        send = jnp.where(upper, low, high)
+        held = keep + lax.ppermute(send, "tp", [(i, i ^ bit) for i in range(count)])
+    return held
+
+
 def fetch_factors(rows, ids, per):
     count = lax.axis_size("blk")
     me = lax.axis_index("blk")
@@ -187,28 +204,32 @@
         ],
         axis=2,
     )
+    base_out = reduce_scatter_tp(jnp.dot(tokens, weight, preferred_element_type=f32))
+
     parts = jnp.stack([act_part, grad_part])
-    both = gather_axis(parts.reshape(-1, 128), "tp", 2).sum(0).reshape(parts.shape)
+    flat_parts = parts.reshape(-1, 128)
+    payload = jnp.concatenate([flat_parts, fac_b.astype(f32).reshape(-1, 128)])
+    got = gather_axis(payload, "tp", 2)
+    both = got[:, : flat_parts.shape[0]].sum(0).reshape(parts.shape)
     rank_act = both[0].astype(bf16)
     rank_grad = both[1].astype(bf16)
-
-    lora_key = jnp.einsum(
-        "trk,tkc->trc", rank_act[:, :, :rank_one], fac_b[:, :rank_one], preferred_element_type=f32
-    ).reshape(rows, kv_dev)
-    lora_val = jnp.einsum(
-        "trk,tkc->trc", rank_act[:, :, rank_one:], fac_b[:, rank_one:], preferred_element_type=f32
-    ).reshape(rows, kv_dev)
-    base = jnp.dot(tokens, weight, preferred_element_type=f32)
-    base = lax.dynamic_update_slice_in_dim(
-        base, lax.dynamic_slice_in_dim(base, col0, kv_dev, 1) + adapter_scale * lora_key, col0, 1
-    )
-    base = lax.dynamic_update_slice_in_dim(
-        base,
-        lax.dynamic_slice_in_dim(base, kv_width + col0, kv_dev, 1) + adapter_scale * lora_val,
-        kv_width + col0,
-        1,
-    )
-    key_value_output = lax.psum_scatter(base, "tp", scatter_dimension=0, tiled=True).astype(bf16)
+    full_b = got[:, flat_parts.shape[0] :].reshape(tp_count, tiles, rank_two, kv_dev)
+    full_b = full_b.transpose(1, 2, 0, 3).reshape(tiles, rank_two, kv_width).astype(bf16)
+
+    out_rows = rows // tp_count
+    mine = max(1, out_rows // tile_rows)
+    span = min(out_rows, tile_rows)
+    first = tp_id * out_rows
+    my_act = lax.dynamic_slice(rank_act, (first // tile_rows, first % tile_rows, 0), (mine, span, rank_two))
+    my_b = lax.dynamic_slice(full_b, (first // tile_rows, 0, 0), (mine, rank_two, kv_width))
+    lora = jnp.concatenate(
+        [
+            jnp.einsum("trk,tkc->trc", my_act[:, :, :rank_one], my_b[:, :rank_one], preferred_element_type=f32),
+            jnp.einsum("trk,tkc->trc", my_act[:, :, rank_one:], my_b[:, rank_one:], preferred_element_type=f32),
+        ],
+        axis=2,
+    ).reshape(out_rows, 2 * kv_width)
+    key_value_output = (base_out + adapter_scale * lora).astype(bf16)
 
     backward = jnp.dot(grad_rows, weight.T, preferred_element_type=f32)
     adapter_back = jnp.einsum("tru,tyu->try", rank_grad, fac_a, preferred_element_type=f32)

time: 165 us -> 147 us (0.89)
  waiting for transfers between devices: 84.1 us -> 64.9 us
  between operations: 14.4 us -> 1.08 us
  starting transfers between devices: 22.3 us -> 27.3 us
  local copies, waits for them, and re-layouts: 7.94 us -> 11.8 us
  matrix products: 10.2 us -> 12.3 us
    reduce_scatter x1 -> x0, waiting for transfers between devices: 27.3 us -> none  [on_device(): lax.psum_scatter(base, 'tp', scatter_dimension=0, tiled=True).astype(bf16)]
    ppermute x3, waiting for transfers between devices: 2.26 us -> 24.5 us  [gather_tp(): got = lax.ppermute(held, 'tp', [(i, i ^ bit) for i in range(count)])]
    ppermute x13, waiting for transfers between devices: 54.5 us -> 35.7 us  [_swap(): return lax.ppermute(x, 'blk', [(i, i ^ bit) for i in range(count)])]
    ppermute x0 -> x3, starting transfers between devices: none -> 4.93 us  [reduce_scatter_tp(): held = keep + lax.ppermute(send, 'tp', [(i, i ^ bit) for i in range(count)])]
    ppermute x0 -> x3, waiting for transfers between devices: none -> 4.77 us  [reduce_scatter_tp(): held = keep + lax.ppermute(send, 'tp', [(i, i ^ bit) for i in range(count)])]
    dynamic_update_slice x2 -> x0, other arithmetic: 3.26 us -> none  [the longest x1 1.67 us: on_device(): lax.dynamic_update_slice_in_dim(base, lax.dynamic_slice_in_dim(base, col0...]
    add x0 -> x2, other arithmetic: none -> 2.58 us  [reduce_scatter_tp(): held = keep + lax.ppermute(send, 'tp', [(i, i ^ bit) for i in range(count)])]
    convert_element_type x0 -> x2, local copies, waits for them, and re-layouts: none -> 2.36 us  [on_device(): full_b.transpose(1, 2, 0, 3).reshape(tiles, rank_two, kv_width).astype(bf16)]
  transfers between devices with their start and end apart: 17 -> 19, of which waited for: 14 -> 10; matrix products, arithmetic and copies ran while one was open for 13% -> 24% of each run, Pallas kernels for 0% -> 9%
where the time goes in v8:
time: 147 us; the launch traced here: 144 us
  waiting for transfers between devices  64.9 us (44%)
  starting transfers between devices  27.3 us (19%)
  other arithmetic  14 us (10%)
  Pallas kernels  13.1 us (9%)
  matrix products  12.3 us (8%)
  local copies, waits for them, and re-layouts  11.8 us (8%)
    ppermute x13, waiting for transfers between devices, _swap(): return lax.ppermute(x, 'blk', [(i, i ^ bit) for i in range(count)])  35.7 us
    ppermute x3, waiting for transfers between devices, gather_tp(): got = lax.ppermute(held, 'tp', [(i, i ^ bit) for i in range(count)])  24.5 us
    ppermute x13, starting transfers between devices, _swap(): return lax.ppermute(x, 'blk', [(i, i ^ bit) for i in range(count)])  18.5 us
    pallas_call x1, Pallas kernels, gather_axis(): pl.pallas_call(functools.partial(_gather_kernel, axis, n), out_shape=jax....  13.1 us
    ppermute x3, starting transfers between devices, reduce_scatter_tp(): held = keep + lax.ppermute(send, 'tp', [(i, i ^ bit) for i in range(count)])  4.93 us
    ppermute x3, waiting for transfers between devices, reduce_scatter_tp(): held = keep + lax.ppermute(send, 'tp', [(i, i ^ bit) for i in range(count)])  4.77 us
    ppermute x3, starting transfers between devices, gather_tp(): got = lax.ppermute(held, 'tp', [(i, i ^ bit) for i in range(count)])  3.89 us
    unnamed x18, local copies, waits for them, and re-layouts  3.47 us
  transfers between devices with their start and end apart: 19, of which 10 were waited for; matrix products, arithmetic and copies ran while one was open for 24% of the time, Pallas kernels for 9%

profile of v8, /device:TPU:2, one launch (start us, length us, event | category | flops | bytes accessed | tf_op | source)
XLA Modules:
  0.0 144.5 jit_solution(14923034200211127449)
XLA Ops:
  0.6 2.4 %collective-permute-start.3 = (s32[2]{0:T(128)}, s32[2]{0:T(128)S(1)}, u32[]{:S(2)}, u32[]{:S(2)}) collective-permute-start(s32[2]{0:T(128)} %bitcast.123), channel_id=1, source_target_pairs={{0,128},{8,136},{16,144},{24,152},{32,160},{40,168},{48,176},{56,1... | collective-permute-start | bytes 32 | tf_op jit(solution)/shard_map/ppermute | solution.py:73
  5.6 7.2 %collective-permute-start.4 = (bf16[1,288,128]{2,1,0:T(8,128)(2,1)S(1)}, bf16[1,288,128]{2,1,0:T(8,128)(2,1)S(1)}, u32[]{:S(2)}, u32[]{:S(2)}) collective-permute-start(bf16[1,288,128]{2,1,0:T(8,128)(2,1)S(1)} %pad_maximum_fusion.3), channel_id=1, source_target_pairs={{0,64},{8,72},{16,80},{24,88},{32,96},{40,104},{48,112},{56,120},{... | collective-permute-start | bytes 221192 | tf_op jit(solution)/shard_map/ppermute | solution.py:73
  12.8 3.4 %fusion.33 = f32[256,2048]{1,0:T(8,128)S(1)} fusion(bf16[256,1024]{1,0:T(8,128)(2,1)S(1)} %copy-done, bf16[1024,2048]{1,0:T(8,128)(2,1)} %param.9), kind=kOutput, calls=%fused_computation.109 | convolution fusion | flops 1073741824 | bytes 6815744 | tf_op jit(solution)/shard_map/dot_general | solution.py:207
  17.4 1.1 select_bitcast_fusion
  18.5 1.6 %collective-permute-start = (f32[2,2,32,2048]{3,2,0,1:T(8,128)}, f32[2,2,32,2048]{3,2,0,1:T(8,128)}, u32[]{:S(2)}, u32[]{:S(2)}) collective-permute-start(f32[2,2,32,2048]{3,2,0,1:T(8,128)} %select_bitcast_fusion), channel_id=1, source_target_pairs={{0,1},{1,0},{2,3},{3,2},{4,5},{5,4},{6,7},{7,6},{8,9},{9,8},{10,11... | collective-permute-start | bytes 3145736 | tf_op jit(solution)/shard_map/ppermute | solution.py:130
  21.4 1.6 %collective-permute-start.5 = (bf16[2,288,128]{2,1,0:T(8,128)(2,1)S(1)}, bf16[2,288,128]{2,1,0:T(8,128)(2,1)S(1)}, u32[]{:S(2)}, u32[]{:S(2)}) collective-permute-start(bf16[2,288,128]{2,1,0:T(8,128)(2,1)S(1)} %maximum_select_fusion.6), channel_id=1, source_target_pairs={{0,32},{8,40},{16,48},{24,56},{32,0},{40,8},{48,16},{56,24},{64,96... | collective-permute-start | bytes 442376 | tf_op jit(solution)/shard_map/ppermute | solution.py:73
  23.0 3.0 %collective-permute-start.11 = (bf16[2,32,2048]{2,1,0:T(8,128)(2,1)S(1)}, bf16[2,32,2048]{2,1,0:T(8,128)(2,1)S(1)}, u32[]{:S(2)}, u32[]{:S(2)}) collective-permute-start(bf16[2,32,2048]{2,1,0:T(8,128)(2,1)S(1)} %maximum_select_fusion.4), channel_id=1, source_target_pairs={{0,2},{1,3},{2,0},{3,1},{4,6},{5,7},{6,4},{7,5},{8,10},{9,11},{10,... | collective-permute-start | bytes 786440 | tf_op jit(solution)/shard_map/ppermute | solution.py:109
  26.0 5.5 %collective-permute-done.5 = bf16[2,288,128]{2,1,0:T(8,128)(2,1)S(1)} collective-permute-done((bf16[2,288,128]{2,1,0:T(8,128)(2,1)S(1)}, bf16[2,288,128]{2,1,0:T(8,128)(2,1)S(1)}, u32[]{:S(2)}, u32[]{:S(2)}) %collective-permute-start.5) | collective-permute-done | bytes 147488 | tf_op jit(solution)/shard_map/ppermute | solution.py:73
  31.7 19.2 %collective-permute-done.11 = bf16[2,32,2048]{2,1,0:T(8,128)(2,1)S(1)} collective-permute-done((bf16[2,32,2048]{2,1,0:T(8,128)(2,1)S(1)}, bf16[2,32,2048]{2,1,0:T(8,128)(2,1)S(1)}, u32[]{:S(2)}, u32[]{:S(2)}) %collective-permute-start.11) | collective-permute-done | bytes 262176 | tf_op jit(solution)/shard_map/ppermute | solution.py:109
  53.4 1.2 collective-permute-done.8
  54.6 1.1 select_select_fusion.1
  55.7 1.9 %collective-permute-start.9 = (bf16[2,288,128]{2,1,0:T(8,128)(2,1)S(1)}, bf16[2,288,128]{2,1,0:T(8,128)(2,1)S(1)}, u32[]{:S(2)}, u32[]{:S(2)}) collective-permute-start(bf16[2,288,128]{2,1,0:T(8,128)(2,1)S(1)} %slice.148), channel_id=1, source_target_pairs={{0,128},{8,136},{16,144},{24,152},{32,160},{40,168},{48,176},{56,1... | collective-permute-start | bytes 442376 | tf_op jit(solution)/shard_map/ppermute | solution.py:73
  57.6 5.3 %collective-permute-done.12 = bf16[4,32,2048]{2,1,0:T(8,128)(2,1)S(1)} collective-permute-done((bf16[4,32,2048]{2,1,0:T(8,128)(2,1)S(1)}, bf16[4,32,2048]{2,1,0:T(8,128)(2,1)S(1)}, u32[]{:S(2)}, u32[]{:S(2)}) %collective-permute-start.12) | collective-permute-done | bytes 524320 | tf_op jit(solution)/shard_map/ppermute | solution.py:109
  62.9 1.1 maximum_select_fusion
  67.6 13.1 %shard_map.93 = f32[8,192,128]{2,1,0:T(8,128)} custom-call(f32[192,128]{1,0:T(8,128)} %pad_maximum_fusion.2.x_ref), custom_call_target="tpu_custom_call" | custom-call | tf_op jit(solution)/shard_map/pallas_call | solution.py:58
  80.7 1.1 slice_reduce_fusion
  81.9 1.0 fusion.7
  82.9 1.1 fusion.5
  86.9 1.8 %collective-permute-start.14 = (f32[2,288,128]{2,1,0:T(8,128)S(1)}, f32[2,288,128]{2,1,0:T(8,128)S(1)}, u32[]{:S(2)}, u32[]{:S(2)}) collective-permute-start(f32[2,288,128]{2,1,0:T(8,128)S(1)} %bitcast.99), channel_id=1, source_target_pairs={{0,128},{8,136},{16,144},{24,152},{32,160},{40,168},{48,176},{56,1... | collective-permute-start | bytes 884744 | tf_op jit(solution)/shard_map/ppermute | solution.py:73
  89.1 6.5 %collective-permute-done.14 = f32[2,288,128]{2,1,0:T(8,128)S(1)} collective-permute-done((f32[2,288,128]{2,1,0:T(8,128)S(1)}, f32[2,288,128]{2,1,0:T(8,128)S(1)}, u32[]{:S(2)}, u32[]{:S(2)}) %collective-permute-start.14) | collective-permute-done | bytes 294944 | tf_op jit(solution)/shard_map/ppermute | solution.py:73
  95.8 1.5 %bitcast_add_fusion.1 = f32[2,2,32,2048]{3,2,0,1:T(8,128)S(1)} fusion(f32[2,2,32,2048]{3,2,0,1:T(8,128)} %collective-permute-done, f32[2,2,1,32,2048]{4,3,2,1,0:T(8,128)S(1)} %copy-done.2, f32[2,2,1,32,2048]{4,3,2,1,0:T(8,128)S(1)} %get-tuple-element.21, pred[]{:T(512)S(6)} %ne.127), kind=kLoop, calls=%fused_computation.13 | loop fusion | flops 524288 | bytes 4194305 | tf_op jit(solution)/shard_map/add | solution.py:130
  99.1 1.1 select_reduce_fusion
  101.1 1.0 collective-permute-start.16
  102.2 2.1 %fusion.1 = bf16[256,1024]{1,0:T(8,128)(2,1)} fusion(f32[2,128,1024]{2,1,0:T(8,128)S(1)} %convolution_multiply_fusion, bf16[256,2048]{1,0:T(8,128)(2,1)S(1)} %bitcast.109, bf16[1024,2048]{1,0:T(8,128)(2,1)S(1)} %copy-done.6), kind=kOutput, calls=%fused_computation.12 | convolution fusion | flops 1074266112 | bytes 6815744 | tf_op jit(solution)/shard_map/dot_general | solution.py:234
  106.0 1.6 %convert_element_type.49 = bf16[2,32,1024]{2,1,0:T(8,128)(2,1)} reshape(bf16[2,32,8,128]{3,2,1,0:T(8,128)(2,1)} %bitcast.118) | data formatting | bytes 262144 | tf_op jit(solution)/shard_map/convert_element_type | solution.py:217
  109.4 4.8 %collective-permute-done.1 = f32[2,32,2048]{2,1,0:T(8,128)} collective-permute-done((f32[2,32,2048]{2,1,0:T(8,128)}, f32[2,32,2048]{2,1,0:T(8,128)}, u32[]{:S(2)}, u32[]{:S(2)}) %collective-permute-start.1) | collective-permute-done | bytes 524320 | tf_op jit(solution)/shard_map/ppermute | solution.py:130
  114.2 1.1 bitcast_add_fusion.2
  115.3 1.5 %collective-permute-done.16 = f32[4,288,128]{2,1,0:T(8,128)S(1)} collective-permute-done((f32[4,288,128]{2,1,0:T(8,128)}, f32[4,288,128]{2,1,0:T(8,128)S(1)}, u32[]{:S(2)}, u32[]{:S(2)}) %collective-permute-start.16) | collective-permute-done | bytes 589856 | tf_op jit(solution)/shard_map/ppermute | solution.py:73
  116.9 1.6 %collective-permute-start.17 = (f32[2,288,128]{2,1,0:T(8,128)S(1)}, f32[2,288,128]{2,1,0:T(8,128)S(1)}, u32[]{:S(2)}, u32[]{:S(2)}) collective-permute-start(f32[2,288,128]{2,1,0:T(8,128)S(1)} %slice_select_fusion.1), channel_id=1, source_target_pairs={{0,32},{8,40},{16,48},{24,56},{32,0},{40,8},{48,16},{56,24},{64,96... | collective-permute-start | bytes 884744 | tf_op jit(solution)/shard_map/ppermute | solution.py:73
  118.5 2.4 %collective-permute-start.2 = (f32[32,2048]{1,0:T(8,128)S(1)}, f32[32,2048]{1,0:T(8,128)S(1)}, u32[]{:S(2)}, u32[]{:S(2)}) collective-permute-start(f32[32,2048]{1,0:T(8,128)S(1)} %select_bitcast_fusion.2), channel_id=1, source_target_pairs={{0,4},{1,5},{2,6},{3,7},{4,0},{5,1},{6,2},{7,3},{8,12},{9,13},{10,... | collective-permute-start | bytes 786440 | tf_op jit(solution)/shard_map/ppermute | solution.py:130
  120.9 11.6 %collective-permute-done.17 = f32[2,288,128]{2,1,0:T(8,128)S(1)} collective-permute-done((f32[2,288,128]{2,1,0:T(8,128)S(1)}, f32[2,288,128]{2,1,0:T(8,128)S(1)}, u32[]{:S(2)}, u32[]{:S(2)}) %collective-permute-start.17) | collective-permute-done | bytes 294944 | tf_op jit(solution)/shard_map/ppermute | solution.py:73
  133.7 8.8 %collective-permute-done.18 = f32[1,288,128]{2,1,0:T(8,128)S(1)} collective-permute-done((f32[1,288,128]{2,1,0:T(8,128)S(1)}, f32[1,288,128]{2,1,0:T(8,128)S(1)}, u32[]{:S(2)}, u32[]{:S(2)}) %collective-permute-start.18) | collective-permute-done | bytes 147488 | tf_op jit(solution)/shard_map/ppermute | solution.py:73
  (99 shorter events, 24.4 us)
Async XLA Ops:
  0.6 12.2 %copy-start = (bf16[256,1024]{1,0:T(8,128)(2,1)S(1)}, bf16[256,1024]{1,0:T(8,128)(2,1)}, u32[]{:S(2)}) copy-start(bf16[256,1024]{1,0:T(8,128)(2,1)} %param.8) | copy-start | bytes 1572868
  0.6 19.5 %collective-permute-start.3 = (s32[2]{0:T(128)}, s32[2]{0:T(128)S(1)}, u32[]{:S(2)}, u32[]{:S(2)}) collective-permute-start(s32[2]{0:T(128)} %bitcast.123), channel_id=1, source_target_pairs={{0,128},{8,136},{16,144},{24,152},{32,160},{40,168},{48,176},{56,1... | collective-permute-start | bytes 32 | tf_op jit(solution)/shard_map/ppermute | solution.py:73
  3.0 20.0 %collective-permute-start.10 = (bf16[1,32,2048]{2,1,0:T(8,128)(2,1)}, bf16[1,32,2048]{2,1,0:T(8,128)(2,1)S(1)}, u32[]{:S(2)}, u32[]{:S(2)}) collective-permute-start(bf16[1,32,2048]{2,1,0:T(8,128)(2,1)} %bitcast.113), channel_id=1, source_target_pairs={{0,4},{1,5},{2,6},{3,7},{4,0},{5,1},{6,2},{7,3},{8,12},{9,13},{10,... | collective-permute-start | bytes 393224 | tf_op jit(solution)/shard_map/ppermute | solution.py:109
  5.6 15.8 %collective-permute-start.4 = (bf16[1,288,128]{2,1,0:T(8,128)(2,1)S(1)}, bf16[1,288,128]{2,1,0:T(8,128)(2,1)S(1)}, u32[]{:S(2)}, u32[]{:S(2)}) collective-permute-start(bf16[1,288,128]{2,1,0:T(8,128)(2,1)S(1)} %pad_maximum_fusion.3), channel_id=1, source_target_pairs={{0,64},{8,72},{16,80},{24,88},{32,96},{40,104},{48,112},{56,120},{... | collective-permute-start | bytes 221192 | tf_op jit(solution)/shard_map/ppermute | solution.py:73
  16.4 1.0 copy-start.1
  16.5 3.6 %copy-start.5 = (s32[2,1]{0,1:T(1,128)S(1)}, s32[2,1]{0,1:T(1,128)}, u32[]{:S(2)}) copy-start(s32[2,1]{0,1:T(1,128)} %param.12) | copy-start | bytes 28
  16.5 6.5 %copy-start.4 = (bf16[32,2048]{1,0:T(8,128)(2,1)S(1)}, bf16[32,2048]{1,0:T(8,128)(2,1)}, u32[]{:S(2)}) copy-start(bf16[32,2048]{1,0:T(8,128)(2,1)} %param.13) | copy-start | bytes 393220
  18.5 77.2 %collective-permute-start = (f32[2,2,32,2048]{3,2,0,1:T(8,128)}, f32[2,2,32,2048]{3,2,0,1:T(8,128)}, u32[]{:S(2)}, u32[]{:S(2)}) collective-permute-start(f32[2,2,32,2048]{3,2,0,1:T(8,128)} %select_bitcast_fusion), channel_id=1, source_target_pairs={{0,1},{1,0},{2,3},{3,2},{4,5},{5,4},{6,7},{7,6},{8,9},{9,8},{10,11... | collective-permute-start | bytes 3145736 | tf_op jit(solution)/shard_map/ppermute | solution.py:130
  20.2 1.1 collective-permute-start.7
  20.3 32.4 %collective-permute-start.13 = (s32[4]{0:T(128)S(1)}, s32[4]{0:T(128)S(1)}, u32[]{:S(2)}, u32[]{:S(2)}) collective-permute-start(s32[4]{0:T(128)S(1)} %get-tuple-element.15), channel_id=1, source_target_pairs={{0,8},{8,0},{16,24},{24,16},{32,40},{40,32},{48,56},{56,48},{64,72... | collective-permute-start | bytes 56 | tf_op jit(solution)/shard_map/ppermute | solution.py:73
  21.4 10.1 %collective-permute-start.5 = (bf16[2,288,128]{2,1,0:T(8,128)(2,1)S(1)}, bf16[2,288,128]{2,1,0:T(8,128)(2,1)S(1)}, u32[]{:S(2)}, u32[]{:S(2)}) collective-permute-start(bf16[2,288,128]{2,1,0:T(8,128)(2,1)S(1)} %maximum_select_fusion.6), channel_id=1, source_target_pairs={{0,32},{8,40},{16,48},{24,56},{32,0},{40,8},{48,16},{56,24},{64,96... | collective-permute-start | bytes 442376 | tf_op jit(solution)/shard_map/ppermute | solution.py:73
  23.0 27.9 %collective-permute-start.11 = (bf16[2,32,2048]{2,1,0:T(8,128)(2,1)S(1)}, bf16[2,32,2048]{2,1,0:T(8,128)(2,1)S(1)}, u32[]{:S(2)}, u32[]{:S(2)}) collective-permute-start(bf16[2,32,2048]{2,1,0:T(8,128)(2,1)S(1)} %maximum_select_fusion.4), channel_id=1, source_target_pairs={{0,2},{1,3},{2,0},{3,1},{4,6},{5,7},{6,4},{7,5},{8,10},{9,11},{10,... | collective-permute-start | bytes 786440 | tf_op jit(solution)/shard_map/ppermute | solution.py:109
  31.5 19.6 %collective-permute-start.6 = (bf16[4,288,128]{2,1,0:T(8,128)(2,1)S(1)}, bf16[4,288,128]{2,1,0:T(8,128)(2,1)S(1)}, u32[]{:S(2)}, u32[]{:S(2)}) collective-permute-start(bf16[4,288,128]{2,1,0:T(8,128)(2,1)S(1)} %maximum_select_fusion.3), channel_id=1, source_target_pairs={{0,16},{8,24},{16,0},{24,8},{32,48},{40,56},{48,32},{56,40},{64,80... | collective-permute-start | bytes 884744 | tf_op jit(solution)/shard_map/ppermute | solution.py:73
  50.9 12.0 %collective-permute-start.12 = (bf16[4,32,2048]{2,1,0:T(8,128)(2,1)S(1)}, bf16[4,32,2048]{2,1,0:T(8,128)(2,1)S(1)}, u32[]{:S(2)}, u32[]{:S(2)}) collective-permute-start(bf16[4,32,2048]{2,1,0:T(8,128)(2,1)S(1)} %bitcast.102), channel_id=1, source_target_pairs={{0,1},{1,0},{2,3},{3,2},{4,5},{5,4},{6,7},{7,6},{8,9},{9,8},{10,11... | collective-permute-start | bytes 1572872 | tf_op jit(solution)/shard_map/ppermute | solution.py:109
  52.7 1.9 %collective-permute-start.8 = (bf16[4,288,128]{2,1,0:T(8,128)(2,1)}, bf16[4,288,128]{2,1,0:T(8,128)(2,1)}, u32[]{:S(2)}, u32[]{:S(2)}) collective-permute-start(bf16[4,288,128]{2,1,0:T(8,128)(2,1)} %select_select_fusion), channel_id=1, source_target_pairs={{0,8},{8,0},{16,24},{24,16},{32,40},{40,32},{48,56},{56,48},{64,72... | collective-permute-start | bytes 884744 | tf_op jit(solution)/shard_map/ppermute | solution.py:73
  55.7 8.3 %collective-permute-start.9 = (bf16[2,288,128]{2,1,0:T(8,128)(2,1)S(1)}, bf16[2,288,128]{2,1,0:T(8,128)(2,1)S(1)}, u32[]{:S(2)}, u32[]{:S(2)}) collective-permute-start(bf16[2,288,128]{2,1,0:T(8,128)(2,1)S(1)} %slice.148), channel_id=1, source_target_pairs={{0,128},{8,136},{16,144},{24,152},{32,160},{40,168},{48,176},{56,1... | collective-permute-start | bytes 442376 | tf_op jit(solution)/shard_map/ppermute | solution.py:73
  85.9 9.9 %copy-start.2 = (f32[2,2,1,32,2048]{4,3,2,1,0:T(8,128)S(1)}, f32[2,2,1,32,2048]{4,3,2,1,0:T(8,128)}, u32[]{:S(2)}) copy-start(f32[2,2,1,32,2048]{4,3,2,1,0:T(8,128)} %copy-done.1) | copy-start | bytes 3145732
  86.9 8.7 %collective-permute-start.14 = (f32[2,288,128]{2,1,0:T(8,128)S(1)}, f32[2,288,128]{2,1,0:T(8,128)S(1)}, u32[]{:S(2)}, u32[]{:S(2)}) collective-permute-start(f32[2,288,128]{2,1,0:T(8,128)S(1)} %bitcast.99), channel_id=1, source_target_pairs={{0,128},{8,136},{16,144},{24,152},{32,160},{40,168},{48,176},{56,1... | collective-permute-start | bytes 884744 | tf_op jit(solution)/shard_map/ppermute | solution.py:73
  95.6 3.4 %collective-permute-start.15 = (f32[4,288,128]{2,1,0:T(8,128)S(1)}, f32[4,288,128]{2,1,0:T(8,128)S(1)}, u32[]{:S(2)}, u32[]{:S(2)}) collective-permute-start(f32[4,288,128]{2,1,0:T(8,128)S(1)} %pad_maximum_fusion.1), channel_id=1, source_target_pairs={{0,8},{8,0},{16,24},{24,16},{32,40},{40,32},{48,56},{56,48},{64,72... | collective-permute-start | bytes 1769480 | tf_op jit(solution)/shard_map/ppermute | solution.py:73
  98.1 16.1 %collective-permute-start.1 = (f32[2,32,2048]{2,1,0:T(8,128)}, f32[2,32,2048]{2,1,0:T(8,128)}, u32[]{:S(2)}, u32[]{:S(2)}) collective-permute-start(f32[2,32,2048]{2,1,0:T(8,128)} %select_bitcast_fusion.1), channel_id=1, source_target_pairs={{0,2},{1,3},{2,0},{3,1},{4,6},{5,7},{6,4},{7,5},{8,10},{9,11},{10,... | collective-permute-start | bytes 1572872 | tf_op jit(solution)/shard_map/ppermute | solution.py:130
  99.0 3.1 %copy-start.6 = (bf16[1024,2048]{1,0:T(8,128)(2,1)S(1)}, bf16[1024,2048]{1,0:T(8,128)(2,1)}, u32[]{:S(2)}) copy-start(bf16[1024,2048]{1,0:T(8,128)(2,1)} %param.9) | copy-start | bytes 12582916
  99.1 3.0 %copy-start.3 = (bf16[4,2,32,2048]{3,2,1,0:T(8,128)(2,1)S(1)}, bf16[4,2,32,2048]{3,2,1,0:T(8,128)(2,1)}, u32[]{:S(2)}) copy-start(bf16[4,2,32,2048]{3,2,1,0:T(8,128)(2,1)} %maximum_select_fusion) | copy-start | bytes 3145732
  101.1 15.6 %collective-permute-start.16 = (f32[4,288,128]{2,1,0:T(8,128)}, f32[4,288,128]{2,1,0:T(8,128)S(1)}, u32[]{:S(2)}, u32[]{:S(2)}) collective-permute-start(f32[4,288,128]{2,1,0:T(8,128)} %slice_select_fusion), channel_id=1, source_target_pairs={{0,16},{8,24},{16,0},{24,8},{32,48},{40,56},{48,32},{56,40},{64,80... | collective-permute-start | bytes 1769480 | tf_op jit(solution)/shard_map/ppermute | solution.py:73
  116.9 15.6 %collective-permute-start.17 = (f32[2,288,128]{2,1,0:T(8,128)S(1)}, f32[2,288,128]{2,1,0:T(8,128)S(1)}, u32[]{:S(2)}, u32[]{:S(2)}) collective-permute-start(f32[2,288,128]{2,1,0:T(8,128)S(1)} %slice_select_fusion.1), channel_id=1, source_target_pairs={{0,32},{8,40},{16,48},{24,56},{32,0},{40,8},{48,16},{56,24},{64,96... | collective-permute-start | bytes 884744 | tf_op jit(solution)/shard_map/ppermute | solution.py:73
  118.5 14.5 %collective-permute-start.2 = (f32[32,2048]{1,0:T(8,128)S(1)}, f32[32,2048]{1,0:T(8,128)S(1)}, u32[]{:S(2)}, u32[]{:S(2)}) collective-permute-start(f32[32,2048]{1,0:T(8,128)S(1)} %select_bitcast_fusion.2), channel_id=1, source_target_pairs={{0,4},{1,5},{2,6},{3,7},{4,0},{5,1},{6,2},{7,3},{8,12},{9,13},{10,... | collective-permute-start | bytes 786440 | tf_op jit(solution)/shard_map/ppermute | solution.py:130
  132.6 9.9 %collective-permute-start.18 = (f32[1,288,128]{2,1,0:T(8,128)S(1)}, f32[1,288,128]{2,1,0:T(8,128)S(1)}, u32[]{:S(2)}, u32[]{:S(2)}) collective-permute-start(f32[1,288,128]{2,1,0:T(8,128)S(1)} %slice_select_fusion.3), channel_id=1, source_target_pairs={{0,64},{8,72},{16,80},{24,88},{32,96},{40,104},{48,112},{56,120},{... | collective-permute-start | bytes 442376 | tf_op jit(solution)/shard_map/ppermute | solution.py:73

commit v9 on v8

--- a/solution.py
+++ b/solution.py
@@ -204,7 +204,8 @@
         ],
         axis=2,
     )
-    base_out = reduce_scatter_tp(jnp.dot(tokens, weight, preferred_element_type=f32))
+    base, fac_b = lax.optimization_barrier((jnp.dot(tokens, weight, preferred_element_type=f32), fac_b))
+    base_out = reduce_scatter_tp(base)
 
     parts = jnp.stack([act_part, grad_part])
     flat_parts = parts.reshape(-1, 128)

time: 147 us -> 140 us (0.952)
  other arithmetic: 14 us -> 8.17 us
  starting transfers between devices: 27.3 us -> 29.9 us
  Pallas kernels: 13.1 us -> 15.3 us
  matrix products: 12.3 us -> 10.4 us
  local copies, waits for them, and re-layouts: 11.8 us -> 10.3 us
    ppermute x3, waiting for transfers between devices: 4.77 us -> 28.2 us  [reduce_scatter_tp(): held = keep + lax.ppermute(send, 'tp', [(i, i ^ bit) for i in range(count)])]
    ppermute x3, waiting for transfers between devices: 24.5 us -> 2.15 us  [gather_tp(): got = lax.ppermute(held, 'tp', [(i, i ^ bit) for i in range(count)])]
    ppermute x3, starting transfers between devices: 4.93 us -> 7.63 us  [reduce_scatter_tp(): held = keep + lax.ppermute(send, 'tp', [(i, i ^ bit) for i in range(count)])]
    ppermute x13, waiting for transfers between devices: 35.7 us -> 33.4 us  [_swap(): return lax.ppermute(x, 'blk', [(i, i ^ bit) for i in range(count)])]
    pallas_call x1, Pallas kernels: 13.1 us -> 15.3 us  [gather_axis(): pl.pallas_call(functools.partial(_gather_kernel, axis, n), out_shape=jax....]
    ppermute x13, starting transfers between devices: 18.5 us -> 16.7 us  [_swap(): return lax.ppermute(x, 'blk', [(i, i ^ bit) for i in range(count)])]
    ppermute x3, starting transfers between devices: 3.89 us -> 5.63 us  [gather_tp(): got = lax.ppermute(held, 'tp', [(i, i ^ bit) for i in range(count)])]
    unnamed x18 -> x16, local copies, waits for them, and re-layouts: 3.47 us -> 1.91 us
  transfers between devices with their start and end apart: 19 -> 19, of which waited for: 10 -> 14; matrix products, arithmetic and copies ran while one was open for 24% -> 16% of each run, Pallas kernels for 9% -> 0%
where the time goes in v9:
time: 140 us; the launch traced here: 139 us
  waiting for transfers between devices  63.8 us (46%)
  starting transfers between devices  29.9 us (21%)
  Pallas kernels  15.3 us (11%)
  matrix products  10.4 us (7%)
  local copies, waits for them, and re-layouts  10.3 us (7%)
  other arithmetic  8.17 us (6%)
    ppermute x13, waiting for transfers between devices, _swap(): return lax.ppermute(x, 'blk', [(i, i ^ bit) for i in range(count)])  33.4 us
    ppermute x3, waiting for transfers between devices, reduce_scatter_tp(): held = keep + lax.ppermute(send, 'tp', [(i, i ^ bit) for i in range(count)])  28.2 us
    ppermute x13, starting transfers between devices, _swap(): return lax.ppermute(x, 'blk', [(i, i ^ bit) for i in range(count)])  16.7 us
    pallas_call x1, Pallas kernels, gather_axis(): pl.pallas_call(functools.partial(_gather_kernel, axis, n), out_shape=jax....  15.3 us
    ppermute x3, starting transfers between devices, reduce_scatter_tp(): held = keep + lax.ppermute(send, 'tp', [(i, i ^ bit) for i in range(count)])  7.63 us
    ppermute x3, starting transfers between devices, gather_tp(): got = lax.ppermute(held, 'tp', [(i, i ^ bit) for i in range(count)])  5.63 us
    dot_general x1, matrix products, on_device(): jnp.dot(tokens, weight, preferred_element_type=f32)  4.8 us
  transfers between devices with their start and end apart: 19, of which 14 were waited for; matrix products, arithmetic and copies ran while one was open for 16% of the time, Pallas kernels for 0%

profile of v9, /device:TPU:2, one launch (start us, length us, event | category | flops | bytes accessed | tf_op | source)
XLA Modules:
  0.0 138.9 jit_solution(8819597053575075913)
XLA Ops:
  0.6 2.4 %collective-permute-start = (s32[2]{0:T(128)}, s32[2]{0:T(128)S(1)}, u32[]{:S(2)}, u32[]{:S(2)}) collective-permute-start(s32[2]{0:T(128)} %bitcast.123), channel_id=1, source_target_pairs={{0,128},{8,136},{16,144},{24,152},{32,160},{40,168},{48,176},{56,1... | collective-permute-start | bytes 32 | tf_op jit(solution)/shard_map/ppermute | solution.py:73
  3.7 1.0 copy.30
  5.6 7.2 %collective-permute-start.1 = (bf16[1,288,128]{2,1,0:T(8,128)(2,1)S(1)}, bf16[1,288,128]{2,1,0:T(8,128)(2,1)S(1)}, u32[]{:S(2)}, u32[]{:S(2)}) collective-permute-start(bf16[1,288,128]{2,1,0:T(8,128)(2,1)S(1)} %pad_maximum_fusion.3), channel_id=1, source_target_pairs={{0,64},{8,72},{16,80},{24,88},{32,96},{40,104},{48,112},{56,120},{... | collective-permute-start | bytes 221192 | tf_op jit(solution)/shard_map/ppermute | solution.py:73
  12.8 4.8 %fusion.33 = f32[256,2048]{1,0:T(8,128)} fusion(bf16[256,1024]{1,0:T(8,128)(2,1)S(1)} %copy-done, bf16[1024,2048]{1,0:T(8,128)(2,1)} %param.9), kind=kOutput, calls=%fused_computation.109 | convolution fusion | flops 1073741824 | bytes 6815744 | tf_op jit(solution)/shard_map/dot_general | solution.py:207
  18.9 1.6 %collective-permute-start.2 = (bf16[2,288,128]{2,1,0:T(8,128)(2,1)S(1)}, bf16[2,288,128]{2,1,0:T(8,128)(2,1)S(1)}, u32[]{:S(2)}, u32[]{:S(2)}) collective-permute-start(bf16[2,288,128]{2,1,0:T(8,128)(2,1)S(1)} %maximum_select_fusion.6), channel_id=1, source_target_pairs={{0,32},{8,40},{16,48},{24,56},{32,0},{40,8},{48,16},{56,24},{64,96... | collective-permute-start | bytes 442376 | tf_op jit(solution)/shard_map/ppermute | solution.py:73
  20.5 3.3 %collective-permute-start.11 = (bf16[2,32,2048]{2,1,0:T(8,128)(2,1)S(1)}, bf16[2,32,2048]{2,1,0:T(8,128)(2,1)S(1)}, u32[]{:S(2)}, u32[]{:S(2)}) collective-permute-start(bf16[2,32,2048]{2,1,0:T(8,128)(2,1)S(1)} %maximum_select_fusion.4), channel_id=1, source_target_pairs={{0,2},{1,3},{2,0},{3,1},{4,6},{5,7},{6,4},{7,5},{8,10},{9,11},{10,... | collective-permute-start | bytes 786440 | tf_op jit(solution)/shard_map/ppermute | solution.py:109
  23.8 5.2 %collective-permute-done.2 = bf16[2,288,128]{2,1,0:T(8,128)(2,1)S(1)} collective-permute-done((bf16[2,288,128]{2,1,0:T(8,128)(2,1)S(1)}, bf16[2,288,128]{2,1,0:T(8,128)(2,1)S(1)}, u32[]{:S(2)}, u32[]{:S(2)}) %collective-permute-start.2) | collective-permute-done | bytes 147488 | tf_op jit(solution)/shard_map/ppermute | solution.py:73
  29.2 1.0 collective-permute-done.11
  30.3 1.7 %collective-permute-start.12 = (bf16[4,32,2048]{2,1,0:T(8,128)(2,1)S(1)}, bf16[4,32,2048]{2,1,0:T(8,128)(2,1)S(1)}, u32[]{:S(2)}, u32[]{:S(2)}) collective-permute-start(bf16[4,32,2048]{2,1,0:T(8,128)(2,1)S(1)} %bitcast.102), channel_id=1, source_target_pairs={{0,1},{1,0},{2,3},{3,2},{4,5},{5,4},{6,7},{7,6},{8,9},{9,8},{10,11... | collective-permute-start | bytes 1572872 | tf_op jit(solution)/shard_map/ppermute | solution.py:109
  31.9 5.7 %collective-permute-done.3 = bf16[4,288,128]{2,1,0:T(8,128)(2,1)S(1)} collective-permute-done((bf16[4,288,128]{2,1,0:T(8,128)(2,1)S(1)}, bf16[4,288,128]{2,1,0:T(8,128)(2,1)S(1)}, u32[]{:S(2)}, u32[]{:S(2)}) %collective-permute-start.3) | collective-permute-done | bytes 294944 | tf_op jit(solution)/shard_map/ppermute | solution.py:73
  40.3 1.9 %collective-permute-start.6 = (bf16[2,288,128]{2,1,0:T(8,128)(2,1)S(1)}, bf16[2,288,128]{2,1,0:T(8,128)(2,1)S(1)}, u32[]{:S(2)}, u32[]{:S(2)}) collective-permute-start(bf16[2,288,128]{2,1,0:T(8,128)(2,1)S(1)} %slice.142), channel_id=1, source_target_pairs={{0,128},{8,136},{16,144},{24,152},{32,160},{40,168},{48,176},{56,1... | collective-permute-start | bytes 442376 | tf_op jit(solution)/shard_map/ppermute | solution.py:73
  42.2 1.1 collective-permute-done.12
  43.4 2.9 %collective-permute-done.6 = bf16[2,288,128]{2,1,0:T(8,128)(2,1)S(1)} collective-permute-done((bf16[2,288,128]{2,1,0:T(8,128)(2,1)S(1)}, bf16[2,288,128]{2,1,0:T(8,128)(2,1)S(1)}, u32[]{:S(2)}, u32[]{:S(2)}) %collective-permute-start.6) | collective-permute-done | bytes 147488 | tf_op jit(solution)/shard_map/ppermute | solution.py:73
  48.2 15.3 %shard_map.93 = f32[8,192,128]{2,1,0:T(8,128)} custom-call(f32[192,128]{1,0:T(8,128)} %pad_maximum_fusion.2.x_ref), custom_call_target="tpu_custom_call" | custom-call | tf_op jit(solution)/shard_map/pallas_call | solution.py:58
  63.5 1.1 slice_reduce_fusion
  66.6 1.6 %collective-permute-start.14 = (f32[2,288,128]{2,1,0:T(8,128)S(1)}, f32[2,288,128]{2,1,0:T(8,128)S(1)}, u32[]{:S(2)}, u32[]{:S(2)}) collective-permute-start(f32[2,288,128]{2,1,0:T(8,128)S(1)} %bitcast.99), channel_id=1, source_target_pairs={{0,128},{8,136},{16,144},{24,152},{32,160},{40,168},{48,176},{56,1... | collective-permute-start | bytes 884744 | tf_op jit(solution)/shard_map/ppermute | solution.py:73
  68.2 1.8 %fusion.31 = (f32[2,2,1,32,2048]{4,3,2,1,0:T(8,128)S(1)}, f32[2,2,1,32,2048]{4,3,2,1,0:T(8,128)S(1)}) fusion(f32[2,2,2,32,2048]{4,3,2,1,0:T(8,128)} %bitcast.104), kind=kLoop, calls=%fused_computation.107 | loop fusion | bytes 4194304 | tf_op jit(solution)/shard_map/slice | solution.py:126
  70.0 3.5 %collective-permute-done.14 = f32[2,288,128]{2,1,0:T(8,128)S(1)} collective-permute-done((f32[2,288,128]{2,1,0:T(8,128)S(1)}, f32[2,288,128]{2,1,0:T(8,128)S(1)}, u32[]{:S(2)}, u32[]{:S(2)}) %collective-permute-start.14) | collective-permute-done | bytes 294944 | tf_op jit(solution)/shard_map/ppermute | solution.py:73
  74.5 1.0 collective-permute-done.15
  75.7 1.1 select_reduce_fusion
  77.9 21.6 %collective-permute-done.7 = f32[2,2,32,2048]{3,2,0,1:T(8,128)S(1)} collective-permute-done((f32[2,2,32,2048]{3,2,0,1:T(8,128)S(1)}, f32[2,2,32,2048]{3,2,0,1:T(8,128)S(1)}, u32[]{:S(2)}, u32[]{:S(2)}) %collective-permute-start.7) | collective-permute-done | bytes 1048608 | tf_op jit(solution)/shard_map/ppermute | solution.py:130
  100.6 4.7 %collective-permute-start.8 = (f32[2,32,2048]{2,1,0:T(8,128)}, f32[2,32,2048]{2,1,0:T(8,128)}, u32[]{:S(2)}, u32[]{:S(2)}) collective-permute-start(f32[2,32,2048]{2,1,0:T(8,128)} %select_bitcast_fusion.1), channel_id=1, source_target_pairs={{0,2},{1,3},{2,0},{3,1},{4,6},{5,7},{6,4},{7,5},{8,10},{9,11},{10,... | collective-permute-start | bytes 1572872 | tf_op jit(solution)/shard_map/ppermute | solution.py:130
  105.3 2.1 %fusion.1 = bf16[256,1024]{1,0:T(8,128)(2,1)} fusion(f32[2,128,1024]{2,1,0:T(8,128)S(1)} %convolution_multiply_fusion, bf16[256,2048]{1,0:T(8,128)(2,1)S(1)} %bitcast.109, bf16[1024,2048]{1,0:T(8,128)(2,1)S(1)} %copy-done.5), kind=kOutput, calls=%fused_computation.12 | convolution fusion | flops 1074266112 | bytes 6815744 | tf_op jit(solution)/shard_map/dot_general | solution.py:235
  107.4 1.0 slice.198
  109.1 0.9 convolution_bitcast_fusion.1
  110.0 1.0 convolution_bitcast_fusion
  112.0 5.6 %collective-permute-done.8 = f32[2,32,2048]{2,1,0:T(8,128)} collective-permute-done((f32[2,32,2048]{2,1,0:T(8,128)}, f32[2,32,2048]{2,1,0:T(8,128)}, u32[]{:S(2)}, u32[]{:S(2)}) %collective-permute-start.8) | collective-permute-done | bytes 524320 | tf_op jit(solution)/shard_map/ppermute | solution.py:130
  117.6 1.1 bitcast_add_fusion.2
  118.8 2.5 %collective-permute-start.9 = (f32[32,2048]{1,0:T(8,128)S(1)}, f32[32,2048]{1,0:T(8,128)S(1)}, u32[]{:S(2)}, u32[]{:S(2)}) collective-permute-start(f32[32,2048]{1,0:T(8,128)S(1)} %select_bitcast_fusion.2), channel_id=1, source_target_pairs={{0,4},{1,5},{2,6},{3,7},{4,0},{5,1},{6,2},{7,3},{8,12},{9,13},{10,... | collective-permute-start | bytes 786440 | tf_op jit(solution)/shard_map/ppermute | solution.py:130
  121.2 5.5 %collective-permute-done.17 = f32[2,288,128]{2,1,0:T(8,128)S(1)} collective-permute-done((f32[2,288,128]{2,1,0:T(8,128)S(1)}, f32[2,288,128]{2,1,0:T(8,128)S(1)}, u32[]{:S(2)}, u32[]{:S(2)}) %collective-permute-start.17) | collective-permute-done | bytes 294944 | tf_op jit(solution)/shard_map/ppermute | solution.py:73
  126.9 1.0 collective-permute-done.9
  128.7 8.2 %collective-permute-done.18 = f32[1,288,128]{2,1,0:T(8,128)S(1)} collective-permute-done((f32[1,288,128]{2,1,0:T(8,128)S(1)}, f32[1,288,128]{2,1,0:T(8,128)S(1)}, u32[]{:S(2)}, u32[]{:S(2)}) %collective-permute-start.18) | collective-permute-done | bytes 147488 | tf_op jit(solution)/shard_map/ppermute | solution.py:73
  (97 shorter events, 17.6 us)
Async XLA Ops:
  0.6 12.2 %copy-start = (bf16[256,1024]{1,0:T(8,128)(2,1)S(1)}, bf16[256,1024]{1,0:T(8,128)(2,1)}, u32[]{:S(2)}) copy-start(bf16[256,1024]{1,0:T(8,128)(2,1)} %param.8) | copy-start | bytes 1572868
  0.6 17.0 %collective-permute-start = (s32[2]{0:T(128)}, s32[2]{0:T(128)S(1)}, u32[]{:S(2)}, u32[]{:S(2)}) collective-permute-start(s32[2]{0:T(128)} %bitcast.123), channel_id=1, source_target_pairs={{0,128},{8,136},{16,144},{24,152},{32,160},{40,168},{48,176},{56,1... | collective-permute-start | bytes 32 | tf_op jit(solution)/shard_map/ppermute | solution.py:73
  3.0 17.5 %collective-permute-start.10 = (bf16[1,32,2048]{2,1,0:T(8,128)(2,1)}, bf16[1,32,2048]{2,1,0:T(8,128)(2,1)S(1)}, u32[]{:S(2)}, u32[]{:S(2)}) collective-permute-start(bf16[1,32,2048]{2,1,0:T(8,128)(2,1)} %bitcast.113), channel_id=1, source_target_pairs={{0,4},{1,5},{2,6},{3,7},{4,0},{5,1},{6,2},{7,3},{8,12},{9,13},{10,... | collective-permute-start | bytes 393224 | tf_op jit(solution)/shard_map/ppermute | solution.py:109
  5.6 13.3 %collective-permute-start.1 = (bf16[1,288,128]{2,1,0:T(8,128)(2,1)S(1)}, bf16[1,288,128]{2,1,0:T(8,128)(2,1)S(1)}, u32[]{:S(2)}, u32[]{:S(2)}) collective-permute-start(bf16[1,288,128]{2,1,0:T(8,128)(2,1)S(1)} %pad_maximum_fusion.3), channel_id=1, source_target_pairs={{0,64},{8,72},{16,80},{24,88},{32,96},{40,104},{48,112},{56,120},{... | collective-permute-start | bytes 221192 | tf_op jit(solution)/shard_map/ppermute | solution.py:73
  12.8 4.8 %copy-start.4 = (s32[2,1]{0,1:T(1,128)S(1)}, s32[2,1]{0,1:T(1,128)}, u32[]{:S(2)}) copy-start(s32[2,1]{0,1:T(1,128)} %param.12) | copy-start | bytes 28
  12.8 7.7 %copy-start.3 = (bf16[32,2048]{1,0:T(8,128)(2,1)S(1)}, bf16[32,2048]{1,0:T(8,128)(2,1)}, u32[]{:S(2)}) copy-start(bf16[32,2048]{1,0:T(8,128)(2,1)} %param.13) | copy-start | bytes 393220
  17.7 1.1 collective-permute-start.4
  17.8 20.8 %collective-permute-start.13 = (s32[4]{0:T(128)S(1)}, s32[4]{0:T(128)S(1)}, u32[]{:S(2)}, u32[]{:S(2)}) collective-permute-start(s32[4]{0:T(128)S(1)} %get-tuple-element.19), channel_id=1, source_target_pairs={{0,8},{8,0},{16,24},{24,16},{32,40},{40,32},{48,56},{56,48},{64,72... | collective-permute-start | bytes 56 | tf_op jit(solution)/shard_map/ppermute | solution.py:73
  18.9 10.1 %collective-permute-start.2 = (bf16[2,288,128]{2,1,0:T(8,128)(2,1)S(1)}, bf16[2,288,128]{2,1,0:T(8,128)(2,1)S(1)}, u32[]{:S(2)}, u32[]{:S(2)}) collective-permute-start(bf16[2,288,128]{2,1,0:T(8,128)(2,1)S(1)} %maximum_select_fusion.6), channel_id=1, source_target_pairs={{0,32},{8,40},{16,48},{24,56},{32,0},{40,8},{48,16},{56,24},{64,96... | collective-permute-start | bytes 442376 | tf_op jit(solution)/shard_map/ppermute | solution.py:73
  20.5 9.7 %collective-permute-start.11 = (bf16[2,32,2048]{2,1,0:T(8,128)(2,1)S(1)}, bf16[2,32,2048]{2,1,0:T(8,128)(2,1)S(1)}, u32[]{:S(2)}, u32[]{:S(2)}) collective-permute-start(bf16[2,32,2048]{2,1,0:T(8,128)(2,1)S(1)} %maximum_select_fusion.4), channel_id=1, source_target_pairs={{0,2},{1,3},{2,0},{3,1},{4,6},{5,7},{6,4},{7,5},{8,10},{9,11},{10,... | collective-permute-start | bytes 786440 | tf_op jit(solution)/shard_map/ppermute | solution.py:109
  29.0 8.6 %collective-permute-start.3 = (bf16[4,288,128]{2,1,0:T(8,128)(2,1)S(1)}, bf16[4,288,128]{2,1,0:T(8,128)(2,1)S(1)}, u32[]{:S(2)}, u32[]{:S(2)}) collective-permute-start(bf16[4,288,128]{2,1,0:T(8,128)(2,1)S(1)} %maximum_select_fusion.3), channel_id=1, source_target_pairs={{0,16},{8,24},{16,0},{24,8},{32,48},{40,56},{48,32},{56,40},{64,80... | collective-permute-start | bytes 884744 | tf_op jit(solution)/shard_map/ppermute | solution.py:73
  30.3 13.0 %collective-permute-start.12 = (bf16[4,32,2048]{2,1,0:T(8,128)(2,1)S(1)}, bf16[4,32,2048]{2,1,0:T(8,128)(2,1)S(1)}, u32[]{:S(2)}, u32[]{:S(2)}) collective-permute-start(bf16[4,32,2048]{2,1,0:T(8,128)(2,1)S(1)} %bitcast.102), channel_id=1, source_target_pairs={{0,1},{1,0},{2,3},{3,2},{4,5},{5,4},{6,7},{7,6},{8,9},{9,8},{10,11... | collective-permute-start | bytes 1572872 | tf_op jit(solution)/shard_map/ppermute | solution.py:109
  38.5 1.7 %collective-permute-start.5 = (bf16[4,288,128]{2,1,0:T(8,128)(2,1)S(1)}, bf16[4,288,128]{2,1,0:T(8,128)(2,1)S(1)}, u32[]{:S(2)}, u32[]{:S(2)}) collective-permute-start(bf16[4,288,128]{2,1,0:T(8,128)(2,1)S(1)} %select_select_fusion), channel_id=1, source_target_pairs={{0,8},{8,0},{16,24},{24,16},{32,40},{40,32},{48,56},{56,48},{64,72... | collective-permute-start | bytes 884744 | tf_op jit(solution)/shard_map/ppermute | solution.py:73
  40.3 6.0 %collective-permute-start.6 = (bf16[2,288,128]{2,1,0:T(8,128)(2,1)S(1)}, bf16[2,288,128]{2,1,0:T(8,128)(2,1)S(1)}, u32[]{:S(2)}, u32[]{:S(2)}) collective-permute-start(bf16[2,288,128]{2,1,0:T(8,128)(2,1)S(1)} %slice.142), channel_id=1, source_target_pairs={{0,128},{8,136},{16,144},{24,152},{32,160},{40,168},{48,176},{56,1... | collective-permute-start | bytes 442376 | tf_op jit(solution)/shard_map/ppermute | solution.py:73
  43.4 21.5 %copy-start.1 = (bf16[4,2,32,2048]{3,2,1,0:T(8,128)(2,1)}, bf16[4,2,32,2048]{3,2,1,0:T(8,128)(2,1)S(1)}, u32[]{:S(2)}) copy-start(bf16[4,2,32,2048]{3,2,1,0:T(8,128)(2,1)S(1)} %maximum_select_fusion) | copy-start | bytes 3145732
  66.6 6.8 %collective-permute-start.14 = (f32[2,288,128]{2,1,0:T(8,128)S(1)}, f32[2,288,128]{2,1,0:T(8,128)S(1)}, u32[]{:S(2)}, u32[]{:S(2)}) collective-permute-start(f32[2,288,128]{2,1,0:T(8,128)S(1)} %bitcast.99), channel_id=1, source_target_pairs={{0,128},{8,136},{16,144},{24,152},{32,160},{40,168},{48,176},{56,1... | collective-permute-start | bytes 884744 | tf_op jit(solution)/shard_map/ppermute | solution.py:73
  73.5 2.1 %collective-permute-start.15 = (f32[4,288,128]{2,1,0:T(8,128)S(1)}, f32[4,288,128]{2,1,0:T(8,128)S(1)}, u32[]{:S(2)}, u32[]{:S(2)}) collective-permute-start(f32[4,288,128]{2,1,0:T(8,128)S(1)} %pad_maximum_fusion.1), channel_id=1, source_target_pairs={{0,8},{8,0},{16,24},{24,16},{32,40},{40,32},{48,56},{56,48},{64,72... | collective-permute-start | bytes 1769480 | tf_op jit(solution)/shard_map/ppermute | solution.py:73
  73.7 25.8 %collective-permute-start.7 = (f32[2,2,32,2048]{3,2,0,1:T(8,128)S(1)}, f32[2,2,32,2048]{3,2,0,1:T(8,128)S(1)}, u32[]{:S(2)}, u32[]{:S(2)}) collective-permute-start(f32[2,2,32,2048]{3,2,0,1:T(8,128)S(1)} %select_bitcast_fusion), channel_id=1, source_target_pairs={{0,1},{1,0},{2,3},{3,2},{4,5},{5,4},{6,7},{7,6},{8,9},{9,8},{10,11... | collective-permute-start | bytes 3145736 | tf_op jit(solution)/shard_map/ppermute | solution.py:130
  77.7 27.6 %copy-start.2 = (bf16[4,2,32,2048]{3,2,1,0:T(8,128)(2,1)S(1)}, bf16[4,2,32,2048]{3,2,1,0:T(8,128)(2,1)}, u32[]{:S(2)}) copy-start(bf16[4,2,32,2048]{3,2,1,0:T(8,128)(2,1)} %copy-done.1) | copy-start | bytes 3145732
  77.7 27.6 %copy-start.5 = (bf16[1024,2048]{1,0:T(8,128)(2,1)S(1)}, bf16[1024,2048]{1,0:T(8,128)(2,1)}, u32[]{:S(2)}) copy-start(bf16[1024,2048]{1,0:T(8,128)(2,1)} %param.9) | copy-start | bytes 12582916
  77.7 33.4 %collective-permute-start.16 = (f32[4,288,128]{2,1,0:T(8,128)}, f32[4,288,128]{2,1,0:T(8,128)S(1)}, u32[]{:S(2)}, u32[]{:S(2)}) collective-permute-start(f32[4,288,128]{2,1,0:T(8,128)} %slice_select_fusion), channel_id=1, source_target_pairs={{0,16},{8,24},{16,0},{24,8},{32,48},{40,56},{48,32},{56,40},{64,80... | collective-permute-start | bytes 1769480 | tf_op jit(solution)/shard_map/ppermute | solution.py:73
  100.6 17.0 %collective-permute-start.8 = (f32[2,32,2048]{2,1,0:T(8,128)}, f32[2,32,2048]{2,1,0:T(8,128)}, u32[]{:S(2)}, u32[]{:S(2)}) collective-permute-start(f32[2,32,2048]{2,1,0:T(8,128)} %select_bitcast_fusion.1), channel_id=1, source_target_pairs={{0,2},{1,3},{2,0},{3,1},{4,6},{5,7},{6,4},{7,5},{8,10},{9,11},{10,... | collective-permute-start | bytes 1572872 | tf_op jit(solution)/shard_map/ppermute | solution.py:130
  111.2 15.6 %collective-permute-start.17 = (f32[2,288,128]{2,1,0:T(8,128)S(1)}, f32[2,288,128]{2,1,0:T(8,128)S(1)}, u32[]{:S(2)}, u32[]{:S(2)}) collective-permute-start(f32[2,288,128]{2,1,0:T(8,128)S(1)} %slice_select_fusion.1), channel_id=1, source_target_pairs={{0,32},{8,40},{16,48},{24,56},{32,0},{40,8},{48,16},{56,24},{64,96... | collective-permute-start | bytes 884744 | tf_op jit(solution)/shard_map/ppermute | solution.py:73
  118.8 9.2 %collective-permute-start.9 = (f32[32,2048]{1,0:T(8,128)S(1)}, f32[32,2048]{1,0:T(8,128)S(1)}, u32[]{:S(2)}, u32[]{:S(2)}) collective-permute-start(f32[32,2048]{1,0:T(8,128)S(1)} %select_bitcast_fusion.2), channel_id=1, source_target_pairs={{0,4},{1,5},{2,6},{3,7},{4,0},{5,1},{6,2},{7,3},{8,12},{9,13},{10,... | collective-permute-start | bytes 786440 | tf_op jit(solution)/shard_map/ppermute | solution.py:130
  126.8 10.1 %collective-permute-start.18 = (f32[1,288,128]{2,1,0:T(8,128)S(1)}, f32[1,288,128]{2,1,0:T(8,128)S(1)}, u32[]{:S(2)}, u32[]{:S(2)}) collective-permute-start(f32[1,288,128]{2,1,0:T(8,128)S(1)} %slice_select_fusion.3), channel_id=1, source_target_pairs={{0,64},{8,72},{16,80},{24,88},{32,96},{40,104},{48,112},{56,120},{... | collective-permute-start | bytes 442376 | tf_op jit(solution)/shard_map/ppermute | solution.py:73

commit v10 on v9

--- a/solution.py
+++ b/solution.py
@@ -114,14 +114,15 @@
     return held.reshape((-1,) + x.shape[1:])
 
 
-def reduce_scatter_tp(x):
+def reduce_scatter_tp(x, order):
     count = lax.axis_size("tp")
     me = lax.axis_index("tp")
     nbits = count.bit_length() - 1
     held = x.reshape((2,) * nbits + (x.shape[0] // count,) + x.shape[1:])
-    for k in range(nbits):
-        bit = 1 << k
-        axis = nbits - 1 - k
+    left = [1 << (nbits - 1 - k) for k in range(nbits)]
+    for bit in order:
+        axis = left.index(bit)
+        left.remove(bit)
         low = lax.index_in_dim(held, 0, axis, keepdims=False)
         high = lax.index_in_dim(held, 1, axis, keepdims=False)
         upper = (me & bit) != 0
@@ -205,7 +206,11 @@
         axis=2,
     )
     base, fac_b = lax.optimization_barrier((jnp.dot(tokens, weight, preferred_element_type=f32), fac_b))
-    base_out = reduce_scatter_tp(base)
+    bits = [1 << k for k in range(tp_count.bit_length() - 1)]
+    half = base.shape[1] // 2
+    base_out = jnp.concatenate(
+        [reduce_scatter_tp(base[:, :half], bits), reduce_scatter_tp(base[:, half:], bits[::-1])], axis=1
+    )
 
     parts = jnp.stack([act_part, grad_part])
     flat_parts = parts.reshape(-1, 128)

time: 140 us -> 151 us (1.079)
  other arithmetic: 8.17 us -> 13.2 us
  matrix products: 10.4 us -> 14.4 us
  local copies, waits for them, and re-layouts: 10.3 us -> 12.4 us
    ppermute x13, waiting for transfers between devices: 33.4 us -> 52.7 us  [_swap(): return lax.ppermute(x, 'blk', [(i, i ^ bit) for i in range(count)])]
    ppermute x3 -> x6, waiting for transfers between devices: 28.2 us -> 9.62 us  [reduce_scatter_tp(): held = keep + lax.ppermute(send, 'tp', [(i, i ^ bit) for i in range(count)])]
    dot_general x1, matrix products: 2.08 us -> 4.88 us  [on_device(): backward = jnp.dot(grad_rows, weight.T, preferred_element_type=f32)]
    gather x2, local copies, waits for them, and re-layouts: 1.21 us -> 3.33 us  [lookup(): found = jnp.take(held, k, axis=0)]
    ppermute x3, starting transfers between devices: 5.63 us -> 7.37 us  [gather_tp(): got = lax.ppermute(held, 'tp', [(i, i ^ bit) for i in range(count)])]
    slice x1, local copies, waits for them, and re-layouts: 1.76 us -> 0.1 us  [reduce_scatter_tp(): high = lax.index_in_dim(held, 1, axis, keepdims=False)]
    convert_element_type x2, local copies, waits for them, and re-layouts: 0.81 us -> 2.36 us  [on_device(): full_b.transpose(1, 2, 0, 3).reshape(tiles, rank_two, kv_width).astype(bf16)]
    ppermute x3 -> x6, starting transfers between devices: 7.63 us -> 6.49 us  [reduce_scatter_tp(): held = keep + lax.ppermute(send, 'tp', [(i, i ^ bit) for i in range(count)])]
  transfers between devices with their start and end apart: 19 -> 22, of which waited for: 14 -> 13; matrix products, arithmetic and copies ran while one was open for 16% -> 19% of each run, Pallas kernels for 0% -> 0%
where the time goes in v10:
time: 151 us; the launch traced here: 150 us
  waiting for transfers between devices  63.4 us (42%)
  starting transfers between devices  29.4 us (19%)
  Pallas kernels  15.6 us (10%)
  matrix products  14.4 us (10%)
  other arithmetic  13.2 us (9%)
  local copies, waits for them, and re-layouts  12.4 us (8%)
    ppermute x13, waiting for transfers between devices, _swap(): return lax.ppermute(x, 'blk', [(i, i ^ bit) for i in range(count)])  52.7 us
    pallas_call x1, Pallas kernels, gather_axis(): pl.pallas_call(functools.partial(_gather_kernel, axis, n), out_shape=jax....  15.6 us
    ppermute x13, starting transfers between devices, _swap(): return lax.ppermute(x, 'blk', [(i, i ^ bit) for i in range(count)])  15.5 us
    ppermute x6, waiting for transfers between devices, reduce_scatter_tp(): held = keep + lax.ppermute(send, 'tp', [(i, i ^ bit) for i in range(count)])  9.62 us
    ppermute x3, starting transfers between devices, gather_tp(): got = lax.ppermute(held, 'tp', [(i, i ^ bit) for i in range(count)])  7.37 us
    ppermute x6, starting transfers between devices, reduce_scatter_tp(): held = keep + lax.ppermute(send, 'tp', [(i, i ^ bit) for i in range(count)])  6.49 us
    dot_general x1, matrix products, on_device(): backward = jnp.dot(grad_rows, weight.T, preferred_element_type=f32)  4.88 us
    dot_general x1, matrix products, on_device(): jnp.dot(tokens, weight, preferred_element_type=f32)  3.47 us
  transfers between devices with their start and end apart: 22, of which 13 were waited for; matrix products, arithmetic and copies ran while one was open for 19% of the time, Pallas kernels for 0%

profile of v10, /device:TPU:2, one launch (start us, length us, event | category | flops | bytes accessed | tf_op | source)
XLA Modules:
  0.0 149.7 jit_solution(4879072922554514073)
XLA Ops:
  2.6 7.2 %collective-permute-start.1 = (bf16[1,288,128]{2,1,0:T(8,128)(2,1)S(1)}, bf16[1,288,128]{2,1,0:T(8,128)(2,1)S(1)}, u32[]{:S(2)}, u32[]{:S(2)}) collective-permute-start(bf16[1,288,128]{2,1,0:T(8,128)(2,1)S(1)} %pad_maximum_fusion.3), channel_id=1, source_target_pairs={{0,64},{8,72},{16,80},{24,88},{32,96},{40,104},{48,112},{56,120},{... | collective-permute-start | bytes 221192 | tf_op jit(solution)/shard_map/ppermute | solution.py:73
  10.3 2.4 %collective-permute-start.13 = (bf16[1,32,2048]{2,1,0:T(8,128)(2,1)}, bf16[1,32,2048]{2,1,0:T(8,128)(2,1)S(1)}, u32[]{:S(2)}, u32[]{:S(2)}) collective-permute-start(bf16[1,32,2048]{2,1,0:T(8,128)(2,1)} %bitcast.120), channel_id=1, source_target_pairs={{0,4},{1,5},{2,6},{3,7},{4,0},{5,1},{6,2},{7,3},{8,12},{9,13},{10,... | collective-permute-start | bytes 393224 | tf_op jit(solution)/shard_map/ppermute | solution.py:109
  12.8 3.5 %fusion.32 = f32[256,2048]{1,0:T(8,128)S(1)} fusion(bf16[256,1024]{1,0:T(8,128)(2,1)S(1)} %copy-done, bf16[1024,2048]{1,0:T(8,128)(2,1)} %param.9), kind=kOutput, calls=%fused_computation.115 | convolution fusion | flops 1073741824 | bytes 6815744 | tf_op jit(solution)/shard_map/dot_general | solution.py:208
  18.0 1.6 %collective-permute-start.2 = (bf16[2,288,128]{2,1,0:T(8,128)(2,1)S(1)}, bf16[2,288,128]{2,1,0:T(8,128)(2,1)S(1)}, u32[]{:S(2)}, u32[]{:S(2)}) collective-permute-start(bf16[2,288,128]{2,1,0:T(8,128)(2,1)S(1)} %maximum_select_fusion.6), channel_id=1, source_target_pairs={{0,32},{8,40},{16,48},{24,56},{32,0},{40,8},{48,16},{56,24},{64,96... | collective-permute-start | bytes 442376 | tf_op jit(solution)/shard_map/ppermute | solution.py:73
  19.6 3.3 %collective-permute-start.14 = (bf16[2,32,2048]{2,1,0:T(8,128)(2,1)S(1)}, bf16[2,32,2048]{2,1,0:T(8,128)(2,1)S(1)}, u32[]{:S(2)}, u32[]{:S(2)}) collective-permute-start(bf16[2,32,2048]{2,1,0:T(8,128)(2,1)S(1)} %maximum_select_fusion.4), channel_id=1, source_target_pairs={{0,2},{1,3},{2,0},{3,1},{4,6},{5,7},{6,4},{7,5},{8,10},{9,11},{10,... | collective-permute-start | bytes 786440 | tf_op jit(solution)/shard_map/ppermute | solution.py:109
  22.8 5.3 %collective-permute-done.2 = bf16[2,288,128]{2,1,0:T(8,128)(2,1)S(1)} collective-permute-done((bf16[2,288,128]{2,1,0:T(8,128)(2,1)S(1)}, bf16[2,288,128]{2,1,0:T(8,128)(2,1)S(1)}, u32[]{:S(2)}, u32[]{:S(2)}) %collective-permute-start.2) | collective-permute-done | bytes 147488 | tf_op jit(solution)/shard_map/ppermute | solution.py:73
  29.4 1.7 %collective-permute-start.15 = (bf16[4,32,2048]{2,1,0:T(8,128)(2,1)S(1)}, bf16[4,32,2048]{2,1,0:T(8,128)(2,1)}, u32[]{:S(2)}, u32[]{:S(2)}) collective-permute-start(bf16[4,32,2048]{2,1,0:T(8,128)(2,1)S(1)} %bitcast.110), channel_id=1, source_target_pairs={{0,1},{1,0},{2,3},{3,2},{4,5},{5,4},{6,7},{7,6},{8,9},{9,8},{10,11... | collective-permute-start | bytes 1572872 | tf_op jit(solution)/shard_map/ppermute | solution.py:109
  31.1 5.7 %collective-permute-done.3 = bf16[4,288,128]{2,1,0:T(8,128)(2,1)S(1)} collective-permute-done((bf16[4,288,128]{2,1,0:T(8,128)(2,1)S(1)}, bf16[4,288,128]{2,1,0:T(8,128)(2,1)S(1)}, u32[]{:S(2)}, u32[]{:S(2)}) %collective-permute-start.3) | collective-permute-done | bytes 294944 | tf_op jit(solution)/shard_map/ppermute | solution.py:73
  37.7 1.7 %gather_fusion.1 = bf16[4,288,128]{2,1,0:T(8,128)(2,1)S(1)} fusion(bf16[8,288,128]{2,1,0:T(8,128)(2,1)} %maximum_select_fusion.1, s32[1024]{0:T(1024)S(1)} %pad_clamp_fusion), kind=kCustom, calls=%fused_computation.1.clone | custom fusion | bytes 589840 | tf_op jit(solution)/shard_map/jit(_take)/gather | solution.py:155
  40.3 1.7 %gather_fusion = bf16[4,288,128]{2,1,0:T(8,128)(2,1)S(1)} fusion(bf16[8,288,128]{2,1,0:T(8,128)(2,1)} %maximum_select_fusion.1, s32[1024]{0:T(1024)S(1)} %pad_clamp_fusion.1), kind=kCustom, calls=%fused_computation.clone | custom fusion | bytes 589840 | tf_op jit(solution)/shard_map/jit(_take)/gather | solution.py:155
  43.2 1.9 %collective-permute-start.6 = (bf16[2,288,128]{2,1,0:T(8,128)(2,1)S(1)}, bf16[2,288,128]{2,1,0:T(8,128)(2,1)S(1)}, u32[]{:S(2)}, u32[]{:S(2)}) collective-permute-start(bf16[2,288,128]{2,1,0:T(8,128)(2,1)S(1)} %slice.175), channel_id=1, source_target_pairs={{0,128},{8,136},{16,144},{24,152},{32,160},{40,168},{48,176},{56,1... | collective-permute-start | bytes 442376 | tf_op jit(solution)/shard_map/ppermute | solution.py:73
  45.1 1.3 maximum_select_fusion
  46.5 3.0 %collective-permute-done.6 = bf16[2,288,128]{2,1,0:T(8,128)(2,1)S(1)} collective-permute-done((bf16[2,288,128]{2,1,0:T(8,128)(2,1)S(1)}, bf16[2,288,128]{2,1,0:T(8,128)(2,1)S(1)}, u32[]{:S(2)}, u32[]{:S(2)}) %collective-permute-start.6) | collective-permute-done | bytes 147488 | tf_op jit(solution)/shard_map/ppermute | solution.py:73
  49.6 1.1 slice_select_fusion.1
  52.5 15.6 %shard_map.93 = f32[8,192,128]{2,1,0:T(8,128)} custom-call(f32[192,128]{1,0:T(8,128)} %pad_maximum_fusion.2.x_ref), custom_call_target="tpu_custom_call" | custom-call | tf_op jit(solution)/shard_map/pallas_call | solution.py:58
  68.1 1.1 slice_reduce_fusion
  69.3 1.1 fusion.4
  71.6 1.3 convolution_multiply_fusion
  73.1 2.4 %collective-permute-start.10 = (f32[2,2,32,1024]{3,2,1,0:T(8,128)S(1)}, f32[2,2,32,1024]{3,2,1,0:T(8,128)}, u32[]{:S(2)}, u32[]{:S(2)}) collective-permute-start(f32[2,2,32,1024]{3,2,1,0:T(8,128)S(1)} %bitcast.119), channel_id=1, source_target_pairs={{0,4},{1,5},{2,6},{3,7},{4,0},{5,1},{6,2},{7,3},{8,12},{9,13},{10,... | collective-permute-start | bytes 1572872 | tf_op jit(solution)/shard_map/ppermute | solution.py:131
  77.8 1.8 %collective-permute-start.17 = (f32[2,288,128]{2,1,0:T(8,128)S(1)}, f32[2,288,128]{2,1,0:T(8,128)S(1)}, u32[]{:S(2)}, u32[]{:S(2)}) collective-permute-start(f32[2,288,128]{2,1,0:T(8,128)S(1)} %bitcast.106), channel_id=1, source_target_pairs={{0,128},{8,136},{16,144},{24,152},{32,160},{40,168},{48,176},{56,1... | collective-permute-start | bytes 884744 | tf_op jit(solution)/shard_map/ppermute | solution.py:73
  79.5 4.9 %fusion.1 = bf16[256,1024]{1,0:T(8,128)(2,1)} fusion(f32[2,128,1024]{2,1,0:T(8,128)} %convolution_multiply_fusion, bf16[256,2048]{1,0:T(8,128)(2,1)} %bitcast.116, bf16[1024,2048]{1,0:T(8,128)(2,1)} %param.9), kind=kOutput, calls=%fused_computation.12 | convolution fusion | flops 1074266112 | bytes 6815744 | tf_op jit(solution)/shard_map/dot_general | solution.py:240
  86.2 1.6 %convert_element_type.49 = bf16[2,32,1024]{2,1,0:T(8,128)(2,1)} reshape(bf16[2,32,8,128]{3,2,1,0:T(8,128)(2,1)} %bitcast.125) | data formatting | bytes 262144 | tf_op jit(solution)/shard_map/convert_element_type | solution.py:223
  89.7 5.4 %collective-permute-done.17 = f32[2,288,128]{2,1,0:T(8,128)S(1)} collective-permute-done((f32[2,288,128]{2,1,0:T(8,128)S(1)}, f32[2,288,128]{2,1,0:T(8,128)S(1)}, u32[]{:S(2)}, u32[]{:S(2)}) %collective-permute-start.17) | collective-permute-done | bytes 294944 | tf_op jit(solution)/shard_map/ppermute | solution.py:73
  95.2 1.1 add.117
  96.7 1.1 bitcast_add_fusion.1
  97.9 3.4 %collective-permute-start.8 = (f32[2,32,1024]{2,1,0:T(8,128)S(1)}, f32[2,32,1024]{2,1,0:T(8,128)S(1)}, u32[]{:S(2)}, u32[]{:S(2)}) collective-permute-start(f32[2,32,1024]{2,1,0:T(8,128)S(1)} %select_bitcast_fusion.2), channel_id=1, source_target_pairs={{0,2},{1,3},{2,0},{3,1},{4,6},{5,7},{6,4},{7,5},{8,10},{9,11},{10,... | collective-permute-start | bytes 786440 | tf_op jit(solution)/shard_map/ppermute | solution.py:131
  101.3 5.8 %collective-permute-done.11 = f32[2,32,1024]{2,1,0:T(8,128)S(1)} collective-permute-done((f32[2,32,1024]{2,1,0:T(8,128)S(1)}, f32[2,32,1024]{2,1,0:T(8,128)S(1)}, u32[]{:S(2)}, u32[]{:S(2)}) %collective-permute-start.11) | collective-permute-done | bytes 262176 | tf_op jit(solution)/shard_map/ppermute | solution.py:131
  107.2 1.1 select_reduce_fusion
  108.9 3.8 %collective-permute-done.8 = f32[2,32,1024]{2,1,0:T(8,128)S(1)} collective-permute-done((f32[2,32,1024]{2,1,0:T(8,128)S(1)}, f32[2,32,1024]{2,1,0:T(8,128)S(1)}, u32[]{:S(2)}, u32[]{:S(2)}) %collective-permute-start.8) | collective-permute-done | bytes 262176 | tf_op jit(solution)/shard_map/ppermute | solution.py:131
  112.9 10.1 %collective-permute-done.19 = f32[4,288,128]{2,1,0:T(8,128)S(1)} collective-permute-done((f32[4,288,128]{2,1,0:T(8,128)S(1)}, f32[4,288,128]{2,1,0:T(8,128)S(1)}, u32[]{:S(2)}, u32[]{:S(2)}) %collective-permute-start.19) | collective-permute-done | bytes 589856 | tf_op jit(solution)/shard_map/ppermute | solution.py:73
  124.1 13.4 %collective-permute-done.20 = f32[2,288,128]{2,1,0:T(8,128)S(1)} collective-permute-done((f32[2,288,128]{2,1,0:T(8,128)S(1)}, f32[2,288,128]{2,1,0:T(8,128)S(1)}, u32[]{:S(2)}, u32[]{:S(2)}) %collective-permute-start.20) | collective-permute-done | bytes 294944 | tf_op jit(solution)/shard_map/ppermute | solution.py:73
  138.8 8.8 %collective-permute-done.21 = f32[1,288,128]{2,1,0:T(8,128)S(1)} collective-permute-done((f32[1,288,128]{2,1,0:T(8,128)S(1)}, f32[1,288,128]{2,1,0:T(8,128)S(1)}, u32[]{:S(2)}, u32[]{:S(2)}) %collective-permute-start.21) | collective-permute-done | bytes 147488 | tf_op jit(solution)/shard_map/ppermute | solution.py:73
  (114 shorter events, 23.5 us)
Async XLA Ops:
  0.6 12.1 %copy-start = (bf16[256,1024]{1,0:T(8,128)(2,1)S(1)}, bf16[256,1024]{1,0:T(8,128)(2,1)}, u32[]{:S(2)}) copy-start(bf16[256,1024]{1,0:T(8,128)(2,1)} %param.8) | copy-start | bytes 1572868
  2.6 15.3 %collective-permute-start.1 = (bf16[1,288,128]{2,1,0:T(8,128)(2,1)S(1)}, bf16[1,288,128]{2,1,0:T(8,128)(2,1)S(1)}, u32[]{:S(2)}, u32[]{:S(2)}) collective-permute-start(bf16[1,288,128]{2,1,0:T(8,128)(2,1)S(1)} %pad_maximum_fusion.3), channel_id=1, source_target_pairs={{0,64},{8,72},{16,80},{24,88},{32,96},{40,104},{48,112},{56,120},{... | collective-permute-start | bytes 221192 | tf_op jit(solution)/shard_map/ppermute | solution.py:73
  9.8 6.5 %collective-permute-start = (s32[2]{0:T(128)}, s32[2]{0:T(128)S(1)}, u32[]{:S(2)}, u32[]{:S(2)}) collective-permute-start(s32[2]{0:T(128)} %bitcast.130), channel_id=1, source_target_pairs={{0,128},{8,136},{16,144},{24,152},{32,160},{40,168},{48,176},{56,1... | collective-permute-start | bytes 32 | tf_op jit(solution)/shard_map/ppermute | solution.py:73
  10.3 9.2 %collective-permute-start.13 = (bf16[1,32,2048]{2,1,0:T(8,128)(2,1)}, bf16[1,32,2048]{2,1,0:T(8,128)(2,1)S(1)}, u32[]{:S(2)}, u32[]{:S(2)}) collective-permute-start(bf16[1,32,2048]{2,1,0:T(8,128)(2,1)} %bitcast.120), channel_id=1, source_target_pairs={{0,4},{1,5},{2,6},{3,7},{4,0},{5,1},{6,2},{7,3},{8,12},{9,13},{10,... | collective-permute-start | bytes 393224 | tf_op jit(solution)/shard_map/ppermute | solution.py:109
  12.8 3.5 %copy-start.6 = (s32[2,1]{0,1:T(1,128)S(1)}, s32[2,1]{0,1:T(1,128)}, u32[]{:S(2)}) copy-start(s32[2,1]{0,1:T(1,128)} %param.12) | copy-start | bytes 28
  12.8 6.8 %copy-start.5 = (bf16[32,2048]{1,0:T(8,128)(2,1)S(1)}, bf16[32,2048]{1,0:T(8,128)(2,1)}, u32[]{:S(2)}) copy-start(bf16[32,2048]{1,0:T(8,128)(2,1)} %param.13) | copy-start | bytes 393220
  16.2 34.5 %copy-start.1 = (f32[256,2048]{1,0:T(8,128)}, f32[256,2048]{1,0:T(8,128)S(1)}, u32[]{:S(2)}) copy-start(f32[256,2048]{1,0:T(8,128)S(1)} %fusion.32) | copy-start | bytes 6291460
  16.4 1.1 collective-permute-start.4
  16.4 1.4 collective-permute-start.16
  18.0 10.2 %collective-permute-start.2 = (bf16[2,288,128]{2,1,0:T(8,128)(2,1)S(1)}, bf16[2,288,128]{2,1,0:T(8,128)(2,1)S(1)}, u32[]{:S(2)}, u32[]{:S(2)}) collective-permute-start(bf16[2,288,128]{2,1,0:T(8,128)(2,1)S(1)} %maximum_select_fusion.6), channel_id=1, source_target_pairs={{0,32},{8,40},{16,48},{24,56},{32,0},{40,8},{48,16},{56,24},{64,96... | collective-permute-start | bytes 442376 | tf_op jit(solution)/shard_map/ppermute | solution.py:73
  19.6 9.8 %collective-permute-start.14 = (bf16[2,32,2048]{2,1,0:T(8,128)(2,1)S(1)}, bf16[2,32,2048]{2,1,0:T(8,128)(2,1)S(1)}, u32[]{:S(2)}, u32[]{:S(2)}) collective-permute-start(bf16[2,32,2048]{2,1,0:T(8,128)(2,1)S(1)} %maximum_select_fusion.4), channel_id=1, source_target_pairs={{0,2},{1,3},{2,0},{3,1},{4,6},{5,7},{6,4},{7,5},{8,10},{9,11},{10,... | collective-permute-start | bytes 786440 | tf_op jit(solution)/shard_map/ppermute | solution.py:109
  28.2 8.6 %collective-permute-start.3 = (bf16[4,288,128]{2,1,0:T(8,128)(2,1)S(1)}, bf16[4,288,128]{2,1,0:T(8,128)(2,1)S(1)}, u32[]{:S(2)}, u32[]{:S(2)}) collective-permute-start(bf16[4,288,128]{2,1,0:T(8,128)(2,1)S(1)} %maximum_select_fusion.3), channel_id=1, source_target_pairs={{0,16},{8,24},{16,0},{24,8},{32,48},{40,56},{48,32},{56,40},{64,80... | collective-permute-start | bytes 884744 | tf_op jit(solution)/shard_map/ppermute | solution.py:73
  29.4 15.7 %collective-permute-start.15 = (bf16[4,32,2048]{2,1,0:T(8,128)(2,1)S(1)}, bf16[4,32,2048]{2,1,0:T(8,128)(2,1)}, u32[]{:S(2)}, u32[]{:S(2)}) collective-permute-start(bf16[4,32,2048]{2,1,0:T(8,128)(2,1)S(1)} %bitcast.110), channel_id=1, source_target_pairs={{0,1},{1,0},{2,3},{3,2},{4,5},{5,4},{6,7},{7,6},{8,9},{9,8},{10,11... | collective-permute-start | bytes 1572872 | tf_op jit(solution)/shard_map/ppermute | solution.py:109
  40.2 1.9 %collective-permute-start.5 = (bf16[4,288,128]{2,1,0:T(8,128)(2,1)}, bf16[4,288,128]{2,1,0:T(8,128)(2,1)}, u32[]{:S(2)}, u32[]{:S(2)}) collective-permute-start(bf16[4,288,128]{2,1,0:T(8,128)(2,1)} %select_select_fusion), channel_id=1, source_target_pairs={{0,8},{8,0},{16,24},{24,16},{32,40},{40,32},{48,56},{56,48},{64,72... | collective-permute-start | bytes 884744 | tf_op jit(solution)/shard_map/ppermute | solution.py:73
  43.2 6.3 %collective-permute-start.6 = (bf16[2,288,128]{2,1,0:T(8,128)(2,1)S(1)}, bf16[2,288,128]{2,1,0:T(8,128)(2,1)S(1)}, u32[]{:S(2)}, u32[]{:S(2)}) collective-permute-start(bf16[2,288,128]{2,1,0:T(8,128)(2,1)S(1)} %slice.175), channel_id=1, source_target_pairs={{0,128},{8,136},{16,144},{24,152},{32,160},{40,168},{48,176},{56,1... | collective-permute-start | bytes 442376 | tf_op jit(solution)/shard_map/ppermute | solution.py:73
  46.5 4.4 %copy-start.3 = (bf16[4,2,32,2048]{3,2,1,0:T(8,128)(2,1)}, bf16[4,2,32,2048]{3,2,1,0:T(8,128)(2,1)S(1)}, u32[]{:S(2)}) copy-start(bf16[4,2,32,2048]{3,2,1,0:T(8,128)(2,1)S(1)} %maximum_select_fusion) | copy-start | bytes 3145732
  52.5 20.5 %copy-start.4 = (f32[128,1024]{1,0:T(8,128)S(1)}, f32[128,1024]{1,0:T(8,128)}, u32[]{:S(2)}) copy-start(f32[128,1024]{1,0:T(8,128)} %get-tuple-element.25) | copy-start | bytes 1572868
  52.5 23.0 %slice-start = ((f32[256,2048]{1,0:T(8,128)}), f32[256,1024]{1,0:T(8,128)S(1)}, s32[]{:S(2)}) async-start(f32[256,2048]{1,0:T(8,128)} %copy-done.1), calls=%async_computation | async-start | bytes 2097152 | tf_op jit(solution)/shard_map/slice | solution.py:212
  73.1 22.1 %collective-permute-start.10 = (f32[2,2,32,1024]{3,2,1,0:T(8,128)S(1)}, f32[2,2,32,1024]{3,2,1,0:T(8,128)}, u32[]{:S(2)}, u32[]{:S(2)}) collective-permute-start(f32[2,2,32,1024]{3,2,1,0:T(8,128)S(1)} %bitcast.119), channel_id=1, source_target_pairs={{0,4},{1,5},{2,6},{3,7},{4,0},{5,1},{6,2},{7,3},{8,12},{9,13},{10,... | collective-permute-start | bytes 1572872 | tf_op jit(solution)/shard_map/ppermute | solution.py:131
  76.5 20.3 %collective-permute-start.7 = (f32[2,2,32,1024]{3,2,0,1:T(8,128)}, f32[2,2,32,1024]{3,2,0,1:T(8,128)}, u32[]{:S(2)}, u32[]{:S(2)}) collective-permute-start(f32[2,2,32,1024]{3,2,0,1:T(8,128)} %select_bitcast_fusion), channel_id=1, source_target_pairs={{0,1},{1,0},{2,3},{3,2},{4,5},{5,4},{6,7},{7,6},{8,9},{9,8},{10,11... | collective-permute-start | bytes 1572872 | tf_op jit(solution)/shard_map/ppermute | solution.py:131
  77.8 17.3 %collective-permute-start.17 = (f32[2,288,128]{2,1,0:T(8,128)S(1)}, f32[2,288,128]{2,1,0:T(8,128)S(1)}, u32[]{:S(2)}, u32[]{:S(2)}) collective-permute-start(f32[2,288,128]{2,1,0:T(8,128)S(1)} %bitcast.106), channel_id=1, source_target_pairs={{0,128},{8,136},{16,144},{24,152},{32,160},{40,168},{48,176},{56,1... | collective-permute-start | bytes 884744 | tf_op jit(solution)/shard_map/ppermute | solution.py:73
  84.4 10.8 %copy-start.2 = (f32[128,1024]{1,0:T(8,128)S(1)}, f32[128,1024]{1,0:T(8,128)}, u32[]{:S(2)}) copy-start(f32[128,1024]{1,0:T(8,128)} %get-tuple-element.26) | copy-start | bytes 1572868
  95.1 12.0 %collective-permute-start.18 = (f32[4,288,128]{2,1,0:T(8,128)S(1)}, f32[4,288,128]{2,1,0:T(8,128)S(1)}, u32[]{:S(2)}, u32[]{:S(2)}) collective-permute-start(f32[4,288,128]{2,1,0:T(8,128)S(1)} %pad_maximum_fusion.1), channel_id=1, source_target_pairs={{0,8},{8,0},{16,24},{24,16},{32,40},{40,32},{48,56},{56,48},{64,72... | collective-permute-start | bytes 1769480 | tf_op jit(solution)/shard_map/ppermute | solution.py:73
  96.4 10.7 %collective-permute-start.11 = (f32[2,32,1024]{2,1,0:T(8,128)S(1)}, f32[2,32,1024]{2,1,0:T(8,128)S(1)}, u32[]{:S(2)}, u32[]{:S(2)}) collective-permute-start(f32[2,32,1024]{2,1,0:T(8,128)S(1)} %select_bitcast_fusion.1), channel_id=1, source_target_pairs={{0,2},{1,3},{2,0},{3,1},{4,6},{5,7},{6,4},{7,5},{8,10},{9,11},{10,... | collective-permute-start | bytes 786440 | tf_op jit(solution)/shard_map/ppermute | solution.py:131
  97.9 14.8 %collective-permute-start.8 = (f32[2,32,1024]{2,1,0:T(8,128)S(1)}, f32[2,32,1024]{2,1,0:T(8,128)S(1)}, u32[]{:S(2)}, u32[]{:S(2)}) collective-permute-start(f32[2,32,1024]{2,1,0:T(8,128)S(1)} %select_bitcast_fusion.2), channel_id=1, source_target_pairs={{0,2},{1,3},{2,0},{3,1},{4,6},{5,7},{6,4},{7,5},{8,10},{9,11},{10,... | collective-permute-start | bytes 786440 | tf_op jit(solution)/shard_map/ppermute | solution.py:131
  108.4 14.6 %collective-permute-start.19 = (f32[4,288,128]{2,1,0:T(8,128)S(1)}, f32[4,288,128]{2,1,0:T(8,128)S(1)}, u32[]{:S(2)}, u32[]{:S(2)}) collective-permute-start(f32[4,288,128]{2,1,0:T(8,128)S(1)} %slice_select_fusion), channel_id=1, source_target_pairs={{0,16},{8,24},{16,0},{24,8},{32,48},{40,56},{48,32},{56,40},{64,80... | collective-permute-start | bytes 1769480 | tf_op jit(solution)/shard_map/ppermute | solution.py:73
  108.8 15.2 %collective-permute-start.12 = (f32[32,1024]{1,0:T(8,128)S(1)}, f32[32,1024]{1,0:T(8,128)S(1)}, u32[]{:S(2)}, u32[]{:S(2)}) collective-permute-start(f32[32,1024]{1,0:T(8,128)S(1)} %select_bitcast_fusion.3), channel_id=1, source_target_pairs={{0,1},{1,0},{2,3},{3,2},{4,5},{5,4},{6,7},{7,6},{8,9},{9,8},{10,11... | collective-permute-start | bytes 393224 | tf_op jit(solution)/shard_map/ppermute | solution.py:131
  112.8 11.3 %collective-permute-start.9 = (f32[32,1024]{1,0:T(8,128)S(1)}, f32[32,1024]{1,0:T(8,128)S(1)}, u32[]{:S(2)}, u32[]{:S(2)}) collective-permute-start(f32[32,1024]{1,0:T(8,128)S(1)} %select_bitcast_fusion.4), channel_id=1, source_target_pairs={{0,4},{1,5},{2,6},{3,7},{4,0},{5,1},{6,2},{7,3},{8,12},{9,13},{10,... | collective-permute-start | bytes 393224 | tf_op jit(solution)/shard_map/ppermute | solution.py:131
  123.2 14.3 %collective-permute-start.20 = (f32[2,288,128]{2,1,0:T(8,128)S(1)}, f32[2,288,128]{2,1,0:T(8,128)S(1)}, u32[]{:S(2)}, u32[]{:S(2)}) collective-permute-start(f32[2,288,128]{2,1,0:T(8,128)S(1)} %slice_select_fusion.3), channel_id=1, source_target_pairs={{0,32},{8,40},{16,48},{24,56},{32,0},{40,8},{48,16},{56,24},{64,96... | collective-permute-start | bytes 884744 | tf_op jit(solution)/shard_map/ppermute | solution.py:73
  137.6 10.1 %collective-permute-start.21 = (f32[1,288,128]{2,1,0:T(8,128)S(1)}, f32[1,288,128]{2,1,0:T(8,128)S(1)}, u32[]{:S(2)}, u32[]{:S(2)}) collective-permute-start(f32[1,288,128]{2,1,0:T(8,128)S(1)} %slice_select_fusion.5), channel_id=1, source_target_pairs={{0,64},{8,72},{16,80},{24,88},{32,96},{40,104},{48,112},{56,120},{... | collective-permute-start | bytes 442376 | tf_op jit(solution)/shard_map/ppermute | solution.py:73

commit v11 on v10

--- a/solution.py
+++ b/solution.py
@@ -209,7 +209,7 @@
     bits = [1 << k for k in range(tp_count.bit_length() - 1)]
     half = base.shape[1] // 2
     base_out = jnp.concatenate(
-        [reduce_scatter_tp(base[:, :half], bits), reduce_scatter_tp(base[:, half:], bits[::-1])], axis=1
+        [reduce_scatter_tp(base[:, :half], bits), reduce_scatter_tp(base[:, half:], bits[1::-1] + bits[2:])], axis=1
     )
 
     parts = jnp.stack([act_part, grad_part])

time: 151 us -> 147 us (0.974)
  other arithmetic: 13.2 us -> 9.89 us
  starting transfers between devices: 29.4 us -> 32.7 us
  waiting for transfers between devices: 63.4 us -> 61 us
    ppermute x13, waiting for transfers between devices: 52.7 us -> 43.6 us  [_swap(): return lax.ppermute(x, 'blk', [(i, i ^ bit) for i in range(count)])]
    ppermute x6, waiting for transfers between devices: 9.62 us -> 15.2 us  [reduce_scatter_tp(): held = keep + lax.ppermute(send, 'tp', [(i, i ^ bit) for i in range(count)])]
    ppermute x6, starting transfers between devices: 6.49 us -> 9.25 us  [reduce_scatter_tp(): held = keep + lax.ppermute(send, 'tp', [(i, i ^ bit) for i in range(count)])]
    convert_element_type x2, local copies, waits for them, and re-layouts: 2.36 us -> 0.15 us  [on_device(): full_b.transpose(1, 2, 0, 3).reshape(tiles, rank_two, kv_width).astype(bf16)]
    gather x2, local copies, waits for them, and re-layouts: 3.33 us -> 1.21 us  [lookup(): found = jnp.take(held, k, axis=0)]
  transfers between devices with their start and end apart: 22 -> 22, of which waited for: 13 -> 15; matrix products, arithmetic and copies ran while one was open for 19% -> 15% of each run, Pallas kernels for 0% -> 0%
where the time goes in v11:
time: 147 us; the launch traced here: 146 us
  waiting for transfers between devices  61 us (41%)
  starting transfers between devices  32.7 us (22%)
  Pallas kernels  15.3 us (10%)
  matrix products  14.9 us (10%)
  local copies, waits for them, and re-layouts  11.4 us (8%)
  other arithmetic  9.89 us (7%)
    ppermute x13, waiting for transfers between devices, _swap(): return lax.ppermute(x, 'blk', [(i, i ^ bit) for i in range(count)])  43.6 us
    ppermute x13, starting transfers between devices, _swap(): return lax.ppermute(x, 'blk', [(i, i ^ bit) for i in range(count)])  16.1 us
    pallas_call x1, Pallas kernels, gather_axis(): pl.pallas_call(functools.partial(_gather_kernel, axis, n), out_shape=jax....  15.3 us
    ppermute x6, waiting for transfers between devices, reduce_scatter_tp(): held = keep + lax.ppermute(send, 'tp', [(i, i ^ bit) for i in range(count)])  15.2 us
    ppermute x6, starting transfers between devices, reduce_scatter_tp(): held = keep + lax.ppermute(send, 'tp', [(i, i ^ bit) for i in range(count)])  9.25 us
    ppermute x3, starting transfers between devices, gather_tp(): got = lax.ppermute(held, 'tp', [(i, i ^ bit) for i in range(count)])  7.36 us
    dot_general x1, matrix products, on_device(): backward = jnp.dot(grad_rows, weight.T, preferred_element_type=f32)  4.87 us
    dot_general x1, matrix products, on_device(): jnp.dot(tokens, weight, preferred_element_type=f32)  4.82 us
  transfers between devices with their start and end apart: 22, of which 15 were waited for; matrix products, arithmetic and copies ran while one was open for 15% of the time, Pallas kernels for 0%

profile of v11, /device:TPU:2, one launch (start us, length us, event | category | flops | bytes accessed | tf_op | source)
XLA Modules:
  0.0 146.4 jit_solution(440303833261569733)
XLA Ops:
  2.6 7.2 %collective-permute-start.1 = (bf16[1,288,128]{2,1,0:T(8,128)(2,1)S(1)}, bf16[1,288,128]{2,1,0:T(8,128)(2,1)S(1)}, u32[]{:S(2)}, u32[]{:S(2)}) collective-permute-start(bf16[1,288,128]{2,1,0:T(8,128)(2,1)S(1)} %pad_maximum_fusion.3), channel_id=1, source_target_pairs={{0,64},{8,72},{16,80},{24,88},{32,96},{40,104},{48,112},{56,120},{... | collective-permute-start | bytes 221192 | tf_op jit(solution)/shard_map/ppermute | solution.py:73
  10.3 2.4 %collective-permute-start.13 = (bf16[1,32,2048]{2,1,0:T(8,128)(2,1)}, bf16[1,32,2048]{2,1,0:T(8,128)(2,1)S(1)}, u32[]{:S(2)}, u32[]{:S(2)}) collective-permute-start(bf16[1,32,2048]{2,1,0:T(8,128)(2,1)} %bitcast.123), channel_id=1, source_target_pairs={{0,4},{1,5},{2,6},{3,7},{4,0},{5,1},{6,2},{7,3},{8,12},{9,13},{10,... | collective-permute-start | bytes 393224 | tf_op jit(solution)/shard_map/ppermute | solution.py:109
  12.8 4.8 %fusion.34 = f32[256,2048]{1,0:T(8,128)} fusion(bf16[256,1024]{1,0:T(8,128)(2,1)S(1)} %copy-done, bf16[1024,2048]{1,0:T(8,128)(2,1)} %param.9), kind=kOutput, calls=%fused_computation.117 | convolution fusion | flops 1073741824 | bytes 6815744 | tf_op jit(solution)/shard_map/dot_general | solution.py:208
  19.3 1.6 %collective-permute-start.2 = (bf16[2,288,128]{2,1,0:T(8,128)(2,1)S(1)}, bf16[2,288,128]{2,1,0:T(8,128)(2,1)S(1)}, u32[]{:S(2)}, u32[]{:S(2)}) collective-permute-start(bf16[2,288,128]{2,1,0:T(8,128)(2,1)S(1)} %maximum_select_fusion.6), channel_id=1, source_target_pairs={{0,32},{8,40},{16,48},{24,56},{32,0},{40,8},{48,16},{56,24},{64,96... | collective-permute-start | bytes 442376 | tf_op jit(solution)/shard_map/ppermute | solution.py:73
  20.8 3.3 %collective-permute-start.14 = (bf16[2,32,2048]{2,1,0:T(8,128)(2,1)S(1)}, bf16[2,32,2048]{2,1,0:T(8,128)(2,1)S(1)}, u32[]{:S(2)}, u32[]{:S(2)}) collective-permute-start(bf16[2,32,2048]{2,1,0:T(8,128)(2,1)S(1)} %maximum_select_fusion.4), channel_id=1, source_target_pairs={{0,2},{1,3},{2,0},{3,1},{4,6},{5,7},{6,4},{7,5},{8,10},{9,11},{10,... | collective-permute-start | bytes 786440 | tf_op jit(solution)/shard_map/ppermute | solution.py:109
  24.1 5.3 %collective-permute-done.2 = bf16[2,288,128]{2,1,0:T(8,128)(2,1)S(1)} collective-permute-done((bf16[2,288,128]{2,1,0:T(8,128)(2,1)S(1)}, bf16[2,288,128]{2,1,0:T(8,128)(2,1)S(1)}, u32[]{:S(2)}, u32[]{:S(2)}) %collective-permute-start.2) | collective-permute-done | bytes 147488 | tf_op jit(solution)/shard_map/ppermute | solution.py:73
  30.7 1.7 %collective-permute-start.15 = (bf16[4,32,2048]{2,1,0:T(8,128)(2,1)S(1)}, bf16[4,32,2048]{2,1,0:T(8,128)(2,1)S(1)}, u32[]{:S(2)}, u32[]{:S(2)}) collective-permute-start(bf16[4,32,2048]{2,1,0:T(8,128)(2,1)S(1)} %bitcast.113), channel_id=1, source_target_pairs={{0,1},{1,0},{2,3},{3,2},{4,5},{5,4},{6,7},{7,6},{8,9},{9,8},{10,11... | collective-permute-start | bytes 1572872 | tf_op jit(solution)/shard_map/ppermute | solution.py:109
  32.4 5.7 %collective-permute-done.3 = bf16[4,288,128]{2,1,0:T(8,128)(2,1)S(1)} collective-permute-done((bf16[4,288,128]{2,1,0:T(8,128)(2,1)S(1)}, bf16[4,288,128]{2,1,0:T(8,128)(2,1)S(1)}, u32[]{:S(2)}, u32[]{:S(2)}) %collective-permute-start.3) | collective-permute-done | bytes 294944 | tf_op jit(solution)/shard_map/ppermute | solution.py:73
  40.7 1.9 %collective-permute-start.6 = (bf16[2,288,128]{2,1,0:T(8,128)(2,1)S(1)}, bf16[2,288,128]{2,1,0:T(8,128)(2,1)S(1)}, u32[]{:S(2)}, u32[]{:S(2)}) collective-permute-start(bf16[2,288,128]{2,1,0:T(8,128)(2,1)S(1)} %slice.174), channel_id=1, source_target_pairs={{0,128},{8,136},{16,144},{24,152},{32,160},{40,168},{48,176},{56,1... | collective-permute-start | bytes 442376 | tf_op jit(solution)/shard_map/ppermute | solution.py:73
  42.6 1.2 collective-permute-done.15
  43.9 2.9 %collective-permute-done.6 = bf16[2,288,128]{2,1,0:T(8,128)(2,1)S(1)} collective-permute-done((bf16[2,288,128]{2,1,0:T(8,128)(2,1)S(1)}, bf16[2,288,128]{2,1,0:T(8,128)(2,1)S(1)}, u32[]{:S(2)}, u32[]{:S(2)}) %collective-permute-start.6) | collective-permute-done | bytes 147488 | tf_op jit(solution)/shard_map/ppermute | solution.py:73
  48.8 15.3 %shard_map.93 = f32[8,192,128]{2,1,0:T(8,128)} custom-call(f32[192,128]{1,0:T(8,128)} %pad_maximum_fusion.2.x_ref), custom_call_target="tpu_custom_call" | custom-call | tf_op jit(solution)/shard_map/pallas_call | solution.py:58
  64.1 1.8 %slice.244 = bf16[8,64,128]{2,1,0:T(8,128)(2,1)} slice(f32[8,192,128]{2,1,0:T(8,128)} %shard_map.93), slice={[0:8], [128:192], [0:128]} | slice | bytes 262144 | tf_op jit(solution)/shard_map/slice | solution.py:222
  68.1 1.6 %fusion.6 = f32[2,16,128]{2,1,0:T(8,128)} fusion(bf16[2,128,32]{2,1,0:T(8,128)(2,1)S(1)} %convert_element_type.46, bf16[2,128,2048]{2,1,0:T(8,128)(2,1)} %bitcast.118, s32[]{:T(128)S(6)} %select_n.366), kind=kOutput, calls=%fused_computation.55 | convolution fusion | flops 1048576 | bytes 98308 | tf_op jit(solution)/shard_map/trk,trc->tkc/dot_general | solution.py:247
  69.9 1.3 convolution_multiply_fusion
  72.6 3.4 %collective-permute-start.10 = (f32[2,2,32,1024]{3,2,0,1:T(8,128)}, f32[2,2,32,1024]{3,2,0,1:T(8,128)}, u32[]{:S(2)}, u32[]{:S(2)}) collective-permute-start(f32[2,2,32,1024]{3,2,0,1:T(8,128)} %select_bitcast_fusion), channel_id=1, source_target_pairs={{0,2},{1,3},{2,0},{3,1},{4,6},{5,7},{6,4},{7,5},{8,10},{9,11},{10,... | collective-permute-start | bytes 1572872 | tf_op jit(solution)/shard_map/ppermute | solution.py:131
  77.0 2.5 %collective-permute-start.7 = (f32[2,2,32,1024]{3,2,0,1:T(8,128)}, f32[2,2,32,1024]{3,2,0,1:T(8,128)}, u32[]{:S(2)}, u32[]{:S(2)}) collective-permute-start(f32[2,2,32,1024]{3,2,0,1:T(8,128)} %select_bitcast_fusion.1), channel_id=1, source_target_pairs={{0,1},{1,0},{2,3},{3,2},{4,5},{5,4},{6,7},{7,6},{8,9},{9,8},{10,11... | collective-permute-start | bytes 1572872 | tf_op jit(solution)/shard_map/ppermute | solution.py:131
  80.1 1.3 copy.47
  81.4 1.8 %reshape.373 = f32[2,32768]{1,0:T(2,128)S(1)} reshape(f32[2,1024,32]{2,1,0:T(8,128)} %copy.47) | data formatting | bytes 524288 | tf_op jit(solution)/shard_map/reshape | solution.py:253
  83.3 1.8 %collective-permute-start.17 = (f32[2,288,128]{2,1,0:T(8,128)S(1)}, f32[2,288,128]{2,1,0:T(8,128)S(1)}, u32[]{:S(2)}, u32[]{:S(2)}) collective-permute-start(f32[2,288,128]{2,1,0:T(8,128)S(1)} %bitcast.110), channel_id=1, source_target_pairs={{0,128},{8,136},{16,144},{24,152},{32,160},{40,168},{48,176},{56,1... | collective-permute-start | bytes 884744 | tf_op jit(solution)/shard_map/ppermute | solution.py:73
  85.1 4.9 %fusion.1 = bf16[256,1024]{1,0:T(8,128)(2,1)} fusion(f32[2,128,1024]{2,1,0:T(8,128)} %convolution_multiply_fusion, bf16[256,2048]{1,0:T(8,128)(2,1)} %bitcast.119, bf16[1024,2048]{1,0:T(8,128)(2,1)} %param.9), kind=kOutput, calls=%fused_computation.12 | convolution fusion | flops 1074266112 | bytes 6815744 | tf_op jit(solution)/shard_map/dot_general | solution.py:240
  90.3 1.1 bitcast_add_fusion.1
  91.5 1.4 collective-permute-start.11
  92.9 10.0 %collective-permute-done.7 = f32[2,2,32,1024]{3,2,0,1:T(8,128)} collective-permute-done((f32[2,2,32,1024]{3,2,0,1:T(8,128)}, f32[2,2,32,1024]{3,2,0,1:T(8,128)}, u32[]{:S(2)}, u32[]{:S(2)}) %collective-permute-start.7) | collective-permute-done | bytes 524320 | tf_op jit(solution)/shard_map/ppermute | solution.py:131
  102.9 1.1 bitcast_add_fusion.2
  104.8 2.7 %collective-permute-done.11 = f32[2,32,1024]{2,1,0:T(8,128)S(1)} collective-permute-done((f32[2,32,1024]{2,1,0:T(8,128)S(1)}, f32[2,32,1024]{2,1,0:T(8,128)S(1)}, u32[]{:S(2)}, u32[]{:S(2)}) %collective-permute-start.11) | collective-permute-done | bytes 262176 | tf_op jit(solution)/shard_map/ppermute | solution.py:131
  107.7 1.1 select_reduce_fusion
  109.6 2.4 %collective-permute-done.8 = f32[2,32,1024]{2,1,0:T(8,128)S(1)} collective-permute-done((f32[2,32,1024]{2,1,0:T(8,128)S(1)}, f32[2,32,1024]{2,1,0:T(8,128)S(1)}, u32[]{:S(2)}, u32[]{:S(2)}) %collective-permute-start.8) | collective-permute-done | bytes 262176 | tf_op jit(solution)/shard_map/ppermute | solution.py:131
  113.0 9.0 %collective-permute-done.19 = f32[4,288,128]{2,1,0:T(8,128)S(1)} collective-permute-done((f32[4,288,128]{2,1,0:T(8,128)S(1)}, f32[4,288,128]{2,1,0:T(8,128)S(1)}, u32[]{:S(2)}, u32[]{:S(2)}) %collective-permute-start.19) | collective-permute-done | bytes 589856 | tf_op jit(solution)/shard_map/ppermute | solution.py:73
  123.1 12.1 %collective-permute-done.20 = f32[2,288,128]{2,1,0:T(8,128)S(1)} collective-permute-done((f32[2,288,128]{2,1,0:T(8,128)S(1)}, f32[2,288,128]{2,1,0:T(8,128)S(1)}, u32[]{:S(2)}, u32[]{:S(2)}) %collective-permute-start.20) | collective-permute-done | bytes 294944 | tf_op jit(solution)/shard_map/ppermute | solution.py:73
  135.2 1.1 collective-permute-start.21
  137.0 7.3 %collective-permute-done.21 = f32[1,288,128]{2,1,0:T(8,128)S(1)} collective-permute-done((f32[1,288,128]{2,1,0:T(8,128)S(1)}, f32[1,288,128]{2,1,0:T(8,128)S(1)}, u32[]{:S(2)}, u32[]{:S(2)}) %collective-permute-start.21) | collective-permute-done | bytes 147488 | tf_op jit(solution)/shard_map/ppermute | solution.py:73
  (116 shorter events, 22.2 us)
Async XLA Ops:
  0.6 12.1 %copy-start = (bf16[256,1024]{1,0:T(8,128)(2,1)S(1)}, bf16[256,1024]{1,0:T(8,128)(2,1)}, u32[]{:S(2)}) copy-start(bf16[256,1024]{1,0:T(8,128)(2,1)} %param.8) | copy-start | bytes 1572868
  2.6 16.6 %collective-permute-start.1 = (bf16[1,288,128]{2,1,0:T(8,128)(2,1)S(1)}, bf16[1,288,128]{2,1,0:T(8,128)(2,1)S(1)}, u32[]{:S(2)}, u32[]{:S(2)}) collective-permute-start(bf16[1,288,128]{2,1,0:T(8,128)(2,1)S(1)} %pad_maximum_fusion.3), channel_id=1, source_target_pairs={{0,64},{8,72},{16,80},{24,88},{32,96},{40,104},{48,112},{56,120},{... | collective-permute-start | bytes 221192 | tf_op jit(solution)/shard_map/ppermute | solution.py:73
  9.8 7.8 %collective-permute-start = (s32[2]{0:T(128)}, s32[2]{0:T(128)S(1)}, u32[]{:S(2)}, u32[]{:S(2)}) collective-permute-start(s32[2]{0:T(128)} %bitcast.133), channel_id=1, source_target_pairs={{0,128},{8,136},{16,144},{24,152},{32,160},{40,168},{48,176},{56,1... | collective-permute-start | bytes 32 | tf_op jit(solution)/shard_map/ppermute | solution.py:73
  10.3 10.5 %collective-permute-start.13 = (bf16[1,32,2048]{2,1,0:T(8,128)(2,1)}, bf16[1,32,2048]{2,1,0:T(8,128)(2,1)S(1)}, u32[]{:S(2)}, u32[]{:S(2)}) collective-permute-start(bf16[1,32,2048]{2,1,0:T(8,128)(2,1)} %bitcast.123), channel_id=1, source_target_pairs={{0,4},{1,5},{2,6},{3,7},{4,0},{5,1},{6,2},{7,3},{8,12},{9,13},{10,... | collective-permute-start | bytes 393224 | tf_op jit(solution)/shard_map/ppermute | solution.py:109
  12.8 4.8 %copy-start.7 = (s32[2,1]{0,1:T(1,128)S(1)}, s32[2,1]{0,1:T(1,128)}, u32[]{:S(2)}) copy-start(s32[2,1]{0,1:T(1,128)} %param.12) | copy-start | bytes 28
  12.8 8.1 %copy-start.3 = (bf16[32,2048]{1,0:T(8,128)(2,1)S(1)}, bf16[32,2048]{1,0:T(8,128)(2,1)}, u32[]{:S(2)}) copy-start(bf16[32,2048]{1,0:T(8,128)(2,1)} %param.13) | copy-start | bytes 393220
  17.7 1.1 collective-permute-start.4
  17.7 1.4 collective-permute-start.16
  19.3 10.2 %collective-permute-start.2 = (bf16[2,288,128]{2,1,0:T(8,128)(2,1)S(1)}, bf16[2,288,128]{2,1,0:T(8,128)(2,1)S(1)}, u32[]{:S(2)}, u32[]{:S(2)}) collective-permute-start(bf16[2,288,128]{2,1,0:T(8,128)(2,1)S(1)} %maximum_select_fusion.6), channel_id=1, source_target_pairs={{0,32},{8,40},{16,48},{24,56},{32,0},{40,8},{48,16},{56,24},{64,96... | collective-permute-start | bytes 442376 | tf_op jit(solution)/shard_map/ppermute | solution.py:73
  20.8 9.8 %collective-permute-start.14 = (bf16[2,32,2048]{2,1,0:T(8,128)(2,1)S(1)}, bf16[2,32,2048]{2,1,0:T(8,128)(2,1)S(1)}, u32[]{:S(2)}, u32[]{:S(2)}) collective-permute-start(bf16[2,32,2048]{2,1,0:T(8,128)(2,1)S(1)} %maximum_select_fusion.4), channel_id=1, source_target_pairs={{0,2},{1,3},{2,0},{3,1},{4,6},{5,7},{6,4},{7,5},{8,10},{9,11},{10,... | collective-permute-start | bytes 786440 | tf_op jit(solution)/shard_map/ppermute | solution.py:109
  29.5 8.6 %collective-permute-start.3 = (bf16[4,288,128]{2,1,0:T(8,128)(2,1)S(1)}, bf16[4,288,128]{2,1,0:T(8,128)(2,1)S(1)}, u32[]{:S(2)}, u32[]{:S(2)}) collective-permute-start(bf16[4,288,128]{2,1,0:T(8,128)(2,1)S(1)} %maximum_select_fusion.3), channel_id=1, source_target_pairs={{0,16},{8,24},{16,0},{24,8},{32,48},{40,56},{48,32},{56,40},{64,80... | collective-permute-start | bytes 884744 | tf_op jit(solution)/shard_map/ppermute | solution.py:73
  30.7 13.1 %collective-permute-start.15 = (bf16[4,32,2048]{2,1,0:T(8,128)(2,1)S(1)}, bf16[4,32,2048]{2,1,0:T(8,128)(2,1)S(1)}, u32[]{:S(2)}, u32[]{:S(2)}) collective-permute-start(bf16[4,32,2048]{2,1,0:T(8,128)(2,1)S(1)} %bitcast.113), channel_id=1, source_target_pairs={{0,1},{1,0},{2,3},{3,2},{4,5},{5,4},{6,7},{7,6},{8,9},{9,8},{10,11... | collective-permute-start | bytes 1572872 | tf_op jit(solution)/shard_map/ppermute | solution.py:109
  38.9 1.7 %collective-permute-start.5 = (bf16[4,288,128]{2,1,0:T(8,128)(2,1)S(1)}, bf16[4,288,128]{2,1,0:T(8,128)(2,1)S(1)}, u32[]{:S(2)}, u32[]{:S(2)}) collective-permute-start(bf16[4,288,128]{2,1,0:T(8,128)(2,1)S(1)} %select_select_fusion), channel_id=1, source_target_pairs={{0,8},{8,0},{16,24},{24,16},{32,40},{40,32},{48,56},{56,48},{64,72... | collective-permute-start | bytes 884744 | tf_op jit(solution)/shard_map/ppermute | solution.py:73
  40.7 6.1 %collective-permute-start.6 = (bf16[2,288,128]{2,1,0:T(8,128)(2,1)S(1)}, bf16[2,288,128]{2,1,0:T(8,128)(2,1)S(1)}, u32[]{:S(2)}, u32[]{:S(2)}) collective-permute-start(bf16[2,288,128]{2,1,0:T(8,128)(2,1)S(1)} %slice.174), channel_id=1, source_target_pairs={{0,128},{8,136},{16,144},{24,152},{32,160},{40,168},{48,176},{56,1... | collective-permute-start | bytes 442376 | tf_op jit(solution)/shard_map/ppermute | solution.py:73
  43.9 3.2 %copy-start.2 = (bf16[4,2,32,2048]{3,2,1,0:T(8,128)(2,1)}, bf16[4,2,32,2048]{3,2,1,0:T(8,128)(2,1)S(1)}, u32[]{:S(2)}) copy-start(bf16[4,2,32,2048]{3,2,1,0:T(8,128)(2,1)S(1)} %maximum_select_fusion) | copy-start | bytes 3145732
  64.1 7.3 %copy-start.1 = (f32[256,2048]{1,0:T(8,128)S(1)}, f32[256,2048]{1,0:T(8,128)}, u32[]{:S(2)}) copy-start(f32[256,2048]{1,0:T(8,128)} %fusion.34) | copy-start | bytes 6291460
  72.6 6.8 %copy-start.4 = (bf16[8,64,128]{2,1,0:T(8,128)(2,1)S(1)}, bf16[8,64,128]{2,1,0:T(8,128)(2,1)}, u32[]{:S(2)}) copy-start(bf16[8,64,128]{2,1,0:T(8,128)(2,1)} %slice.244) | copy-start | bytes 393220
  72.6 17.7 %collective-permute-start.10 = (f32[2,2,32,1024]{3,2,0,1:T(8,128)}, f32[2,2,32,1024]{3,2,0,1:T(8,128)}, u32[]{:S(2)}, u32[]{:S(2)}) collective-permute-start(f32[2,2,32,1024]{3,2,0,1:T(8,128)} %select_bitcast_fusion), channel_id=1, source_target_pairs={{0,2},{1,3},{2,0},{3,1},{4,6},{5,7},{6,4},{7,5},{8,10},{9,11},{10,... | collective-permute-start | bytes 1572872 | tf_op jit(solution)/shard_map/ppermute | solution.py:131
  76.0 4.0 %copy-start.5 = (f32[2,16,128]{2,1,0:T(8,128)S(1)}, f32[2,16,128]{2,1,0:T(8,128)}, u32[]{:S(2)}) copy-start(f32[2,16,128]{2,1,0:T(8,128)} %fusion.6) | copy-start | bytes 49156
  77.0 25.9 %collective-permute-start.7 = (f32[2,2,32,1024]{3,2,0,1:T(8,128)}, f32[2,2,32,1024]{3,2,0,1:T(8,128)}, u32[]{:S(2)}, u32[]{:S(2)}) collective-permute-start(f32[2,2,32,1024]{3,2,0,1:T(8,128)} %select_bitcast_fusion.1), channel_id=1, source_target_pairs={{0,1},{1,0},{2,3},{3,2},{4,5},{5,4},{6,7},{7,6},{8,9},{9,8},{10,11... | collective-permute-start | bytes 1572872 | tf_op jit(solution)/shard_map/ppermute | solution.py:131
  83.3 6.8 %collective-permute-start.17 = (f32[2,288,128]{2,1,0:T(8,128)S(1)}, f32[2,288,128]{2,1,0:T(8,128)S(1)}, u32[]{:S(2)}, u32[]{:S(2)}) collective-permute-start(f32[2,288,128]{2,1,0:T(8,128)S(1)} %bitcast.110), channel_id=1, source_target_pairs={{0,128},{8,136},{16,144},{24,152},{32,160},{40,168},{48,176},{56,1... | collective-permute-start | bytes 884744 | tf_op jit(solution)/shard_map/ppermute | solution.py:73
  90.2 17.4 %collective-permute-start.18 = (f32[4,288,128]{2,1,0:T(8,128)S(1)}, f32[4,288,128]{2,1,0:T(8,128)S(1)}, u32[]{:S(2)}, u32[]{:S(2)}) collective-permute-start(f32[4,288,128]{2,1,0:T(8,128)S(1)} %pad_maximum_fusion.1), channel_id=1, source_target_pairs={{0,8},{8,0},{16,24},{24,16},{32,40},{40,32},{48,56},{56,48},{64,72... | collective-permute-start | bytes 1769480 | tf_op jit(solution)/shard_map/ppermute | solution.py:73
  91.5 16.0 %collective-permute-start.11 = (f32[2,32,1024]{2,1,0:T(8,128)S(1)}, f32[2,32,1024]{2,1,0:T(8,128)S(1)}, u32[]{:S(2)}, u32[]{:S(2)}) collective-permute-start(f32[2,32,1024]{2,1,0:T(8,128)S(1)} %select_bitcast_fusion.2), channel_id=1, source_target_pairs={{0,1},{1,0},{2,3},{3,2},{4,5},{5,4},{6,7},{7,6},{8,9},{9,8},{10,11... | collective-permute-start | bytes 786440 | tf_op jit(solution)/shard_map/ppermute | solution.py:131
  104.0 3.6 %copy-start.6 = (pred[8,8]{1,0:T(8,128)(4,1)S(1)}, pred[8,8]{1,0:T(8,128)(4,1)}, u32[]{:S(2)}) copy-start(pred[8,8]{1,0:T(8,128)(4,1)} %fusion.17) | copy-start | bytes 196
  104.1 8.0 %collective-permute-start.8 = (f32[2,32,1024]{2,1,0:T(8,128)S(1)}, f32[2,32,1024]{2,1,0:T(8,128)S(1)}, u32[]{:S(2)}, u32[]{:S(2)}) collective-permute-start(f32[2,32,1024]{2,1,0:T(8,128)S(1)} %select_bitcast_fusion.3), channel_id=1, source_target_pairs={{0,2},{1,3},{2,0},{3,1},{4,6},{5,7},{6,4},{7,5},{8,10},{9,11},{10,... | collective-permute-start | bytes 786440 | tf_op jit(solution)/shard_map/ppermute | solution.py:131
  108.9 13.1 %collective-permute-start.19 = (f32[4,288,128]{2,1,0:T(8,128)S(1)}, f32[4,288,128]{2,1,0:T(8,128)S(1)}, u32[]{:S(2)}, u32[]{:S(2)}) collective-permute-start(f32[4,288,128]{2,1,0:T(8,128)S(1)} %slice_select_fusion), channel_id=1, source_target_pairs={{0,16},{8,24},{16,0},{24,8},{32,48},{40,56},{48,32},{56,40},{64,80... | collective-permute-start | bytes 1769480 | tf_op jit(solution)/shard_map/ppermute | solution.py:73
  109.3 13.7 %collective-permute-start.12 = (f32[32,1024]{1,0:T(8,128)S(1)}, f32[32,1024]{1,0:T(8,128)S(1)}, u32[]{:S(2)}, u32[]{:S(2)}) collective-permute-start(f32[32,1024]{1,0:T(8,128)S(1)} %select_bitcast_fusion.4), channel_id=1, source_target_pairs={{0,4},{1,5},{2,6},{3,7},{4,0},{5,1},{6,2},{7,3},{8,12},{9,13},{10,... | collective-permute-start | bytes 393224 | tf_op jit(solution)/shard_map/ppermute | solution.py:131
  112.1 10.9 %collective-permute-start.9 = (f32[32,1024]{1,0:T(8,128)S(1)}, f32[32,1024]{1,0:T(8,128)S(1)}, u32[]{:S(2)}, u32[]{:S(2)}) collective-permute-start(f32[32,1024]{1,0:T(8,128)S(1)} %select_bitcast_fusion.5), channel_id=1, source_target_pairs={{0,4},{1,5},{2,6},{3,7},{4,0},{5,1},{6,2},{7,3},{8,12},{9,13},{10,... | collective-permute-start | bytes 393224 | tf_op jit(solution)/shard_map/ppermute | solution.py:131
  122.2 13.0 %collective-permute-start.20 = (f32[2,288,128]{2,1,0:T(8,128)S(1)}, f32[2,288,128]{2,1,0:T(8,128)S(1)}, u32[]{:S(2)}, u32[]{:S(2)}) collective-permute-start(f32[2,288,128]{2,1,0:T(8,128)S(1)} %slice_select_fusion.1), channel_id=1, source_target_pairs={{0,32},{8,40},{16,48},{24,56},{32,0},{40,8},{48,16},{56,24},{64,96... | collective-permute-start | bytes 884744 | tf_op jit(solution)/shard_map/ppermute | solution.py:73
  135.2 9.1 %collective-permute-start.21 = (f32[1,288,128]{2,1,0:T(8,128)S(1)}, f32[1,288,128]{2,1,0:T(8,128)S(1)}, u32[]{:S(2)}, u32[]{:S(2)}) collective-permute-start(f32[1,288,128]{2,1,0:T(8,128)S(1)} %slice_select_fusion.3), channel_id=1, source_target_pairs={{0,64},{8,72},{16,80},{24,88},{32,96},{40,104},{48,112},{56,120},{... | collective-permute-start | bytes 442376 | tf_op jit(solution)/shard_map/ppermute | solution.py:73

commit v12 on v8

--- a/solution.py
+++ b/solution.py
@@ -114,7 +114,7 @@
     return held.reshape((-1,) + x.shape[1:])
 
 
-def reduce_scatter_tp(x):
+def reduce_scatter_tp(x, tie):
     count = lax.axis_size("tp")
     me = lax.axis_index("tp")
     nbits = count.bit_length() - 1
@@ -128,7 +128,9 @@
         keep = jnp.where(upper, high, low)
         send = jnp.where(upper, low, high)
         held = keep + lax.ppermute(send, "tp", [(i, i ^ bit) for i in range(count)])
-    return held
+        if k == 0:
+            held, tie = lax.optimization_barrier((held, tie))
+    return held, tie
 
 
 def fetch_factors(rows, ids, per):
@@ -204,8 +206,6 @@
         ],
         axis=2,
     )
-    base_out = reduce_scatter_tp(jnp.dot(tokens, weight, preferred_element_type=f32))
-
     parts = jnp.stack([act_part, grad_part])
     flat_parts = parts.reshape(-1, 128)
     payload = jnp.concatenate([flat_parts, fac_b.astype(f32).reshape(-1, 128)])
@@ -229,7 +229,6 @@
         ],
         axis=2,
     ).reshape(out_rows, 2 * kv_width)
-    key_value_output = (base_out + adapter_scale * lora).astype(bf16)
 
     backward = jnp.dot(grad_rows, weight.T, preferred_element_type=f32)
     adapter_back = jnp.einsum("tru,tyu->try", rank_grad, fac_a, preferred_element_type=f32)
@@ -245,6 +244,10 @@
     )
     size_a = feats * rank_two
     flat = jnp.concatenate([down_grad.reshape(tiles, -1), up_grad.reshape(tiles, -1)], axis=1)
+    base, fac_b = lax.optimization_barrier((jnp.dot(tokens, weight, preferred_element_type=f32), fac_b))
+
+    base_out, flat = reduce_scatter_tp(base, flat)
+    key_value_output = (base_out + adapter_scale * lora).astype(bf16)
     summed = reduce_to_owner(flat.reshape(tiles, -1, 128), tile_ids, bank_a.shape[0]).reshape(bank_a.shape[0], -1)
     grad_a = summed[:, :size_a].reshape(bank_a.shape[0], feats, rank_two)
     grad_b = summed[:, size_a:].reshape(bank_a.shape[0], rank_two, kv_dev)

time: 147 us -> 153 us (1.041)
  waiting for transfers between devices: 64.9 us -> 77.1 us
  other arithmetic: 14 us -> 8.29 us
  Pallas kernels: 13.1 us -> 15.3 us
  matrix products: 12.3 us -> 10.3 us
    ppermute x3, waiting for transfers between devices: 24.5 us -> 1.46 us  [gather_tp(): got = lax.ppermute(held, 'tp', [(i, i ^ bit) for i in range(count)])]
    ppermute x3, waiting for transfers between devices: 4.77 us -> 26.2 us  [reduce_scatter_tp(): held = keep + lax.ppermute(send, 'tp', [(i, i ^ bit) for i in range(count)])]
    ppermute x13, waiting for transfers between devices: 35.7 us -> 49.4 us  [_swap(): return lax.ppermute(x, 'blk', [(i, i ^ bit) for i in range(count)])]
    add x2, other arithmetic: 2.58 us -> 0.24 us  [reduce_scatter_tp(): held = keep + lax.ppermute(send, 'tp', [(i, i ^ bit) for i in range(count)])]
    pallas_call x1, Pallas kernels: 13.1 us -> 15.3 us  [gather_axis(): pl.pallas_call(functools.partial(_gather_kernel, axis, n), out_shape=jax....]
    ppermute x13, starting transfers between devices: 18.5 us -> 16.4 us  [_swap(): return lax.ppermute(x, 'blk', [(i, i ^ bit) for i in range(count)])]
    ppermute x3, starting transfers between devices: 3.89 us -> 5.63 us  [gather_tp(): got = lax.ppermute(held, 'tp', [(i, i ^ bit) for i in range(count)])]
    ppermute x3, starting transfers between devices: 4.93 us -> 6.65 us  [reduce_scatter_tp(): held = keep + lax.ppermute(send, 'tp', [(i, i ^ bit) for i in range(count)])]
  transfers between devices with their start and end apart: 19 -> 19, of which waited for: 10 -> 13; matrix products, arithmetic and copies ran while one was open for 24% -> 12% of each run, Pallas kernels for 9% -> 0%
where the time goes in v12:
time: 153 us; the launch traced here: 151 us
  waiting for transfers between devices  77.1 us (50%)
  starting transfers between devices  28.7 us (19%)
  Pallas kernels  15.3 us (10%)
  local copies, waits for them, and re-layouts  10.5 us (7%)
  matrix products  10.3 us (7%)
  other arithmetic  8.29 us (5%)
    ppermute x13, waiting for transfers between devices, _swap(): return lax.ppermute(x, 'blk', [(i, i ^ bit) for i in range(count)])  49.4 us
    ppermute x3, waiting for transfers between devices, reduce_scatter_tp(): held = keep + lax.ppermute(send, 'tp', [(i, i ^ bit) for i in range(count)])  26.2 us
    ppermute x13, starting transfers between devices, _swap(): return lax.ppermute(x, 'blk', [(i, i ^ bit) for i in range(count)])  16.4 us
    pallas_call x1, Pallas kernels, gather_axis(): pl.pallas_call(functools.partial(_gather_kernel, axis, n), out_shape=jax....  15.3 us
    ppermute x3, starting transfers between devices, reduce_scatter_tp(): held = keep + lax.ppermute(send, 'tp', [(i, i ^ bit) for i in range(count)])  6.65 us
    ppermute x3, starting transfers between devices, gather_tp(): got = lax.ppermute(held, 'tp', [(i, i ^ bit) for i in range(count)])  5.63 us
    dot_general x1, matrix products, on_device(): jnp.dot(tokens, weight, preferred_element_type=f32)  4.8 us
  transfers between devices with their start and end apart: 19, of which 13 were waited for; matrix products, arithmetic and copies ran while one was open for 12% of the time, Pallas kernels for 0%

profile of v12, /device:TPU:2, one launch (start us, length us, event | category | flops | bytes accessed | tf_op | source)
XLA Modules:
  0.0 151.3 jit_solution(13261478067621948980)
XLA Ops:
  0.6 2.4 %collective-permute-start = (s32[2]{0:T(128)}, s32[2]{0:T(128)S(1)}, u32[]{:S(2)}, u32[]{:S(2)}) collective-permute-start(s32[2]{0:T(128)} %bitcast.123), channel_id=1, source_target_pairs={{0,128},{8,136},{16,144},{24,152},{32,160},{40,168},{48,176},{56,1... | collective-permute-start | bytes 32 | tf_op jit(solution)/shard_map/ppermute | solution.py:73
  3.7 1.0 copy.30
  5.6 7.2 %collective-permute-start.1 = (bf16[1,288,128]{2,1,0:T(8,128)(2,1)S(1)}, bf16[1,288,128]{2,1,0:T(8,128)(2,1)S(1)}, u32[]{:S(2)}, u32[]{:S(2)}) collective-permute-start(bf16[1,288,128]{2,1,0:T(8,128)(2,1)S(1)} %pad_maximum_fusion.4), channel_id=1, source_target_pairs={{0,64},{8,72},{16,80},{24,88},{32,96},{40,104},{48,112},{56,120},{... | collective-permute-start | bytes 221192 | tf_op jit(solution)/shard_map/ppermute | solution.py:73
  12.8 4.8 %fusion.33 = f32[256,2048]{1,0:T(8,128)} fusion(bf16[256,1024]{1,0:T(8,128)(2,1)S(1)} %copy-done, bf16[1024,2048]{1,0:T(8,128)(2,1)} %param.9), kind=kOutput, calls=%fused_computation.109 | convolution fusion | flops 1073741824 | bytes 6815744 | tf_op jit(solution)/shard_map/dot_general | solution.py:247
  17.7 1.1 collective-permute-done.4
  18.9 1.6 %collective-permute-start.2 = (bf16[2,288,128]{2,1,0:T(8,128)(2,1)S(1)}, bf16[2,288,128]{2,1,0:T(8,128)(2,1)S(1)}, u32[]{:S(2)}, u32[]{:S(2)}) collective-permute-start(bf16[2,288,128]{2,1,0:T(8,128)(2,1)S(1)} %maximum_select_fusion.6), channel_id=1, source_target_pairs={{0,32},{8,40},{16,48},{24,56},{32,0},{40,8},{48,16},{56,24},{64,96... | collective-permute-start | bytes 442376 | tf_op jit(solution)/shard_map/ppermute | solution.py:73
  20.5 3.3 %collective-permute-start.9 = (bf16[2,32,2048]{2,1,0:T(8,128)(2,1)S(1)}, bf16[2,32,2048]{2,1,0:T(8,128)(2,1)S(1)}, u32[]{:S(2)}, u32[]{:S(2)}) collective-permute-start(bf16[2,32,2048]{2,1,0:T(8,128)(2,1)S(1)} %maximum_select_fusion.4), channel_id=1, source_target_pairs={{0,2},{1,3},{2,0},{3,1},{4,6},{5,7},{6,4},{7,5},{8,10},{9,11},{10,... | collective-permute-start | bytes 786440 | tf_op jit(solution)/shard_map/ppermute | solution.py:109
  23.8 5.2 %collective-permute-done.2 = bf16[2,288,128]{2,1,0:T(8,128)(2,1)S(1)} collective-permute-done((bf16[2,288,128]{2,1,0:T(8,128)(2,1)S(1)}, bf16[2,288,128]{2,1,0:T(8,128)(2,1)S(1)}, u32[]{:S(2)}, u32[]{:S(2)}) %collective-permute-start.2) | collective-permute-done | bytes 147488 | tf_op jit(solution)/shard_map/ppermute | solution.py:73
  29.2 1.0 collective-permute-done.9
  30.3 1.7 %collective-permute-start.10 = (bf16[4,32,2048]{2,1,0:T(8,128)(2,1)S(1)}, bf16[4,32,2048]{2,1,0:T(8,128)(2,1)S(1)}, u32[]{:S(2)}, u32[]{:S(2)}) collective-permute-start(bf16[4,32,2048]{2,1,0:T(8,128)(2,1)S(1)} %bitcast.101), channel_id=1, source_target_pairs={{0,1},{1,0},{2,3},{3,2},{4,5},{5,4},{6,7},{7,6},{8,9},{9,8},{10,11... | collective-permute-start | bytes 1572872 | tf_op jit(solution)/shard_map/ppermute | solution.py:109
  32.0 5.7 %collective-permute-done.3 = bf16[4,288,128]{2,1,0:T(8,128)(2,1)S(1)} collective-permute-done((bf16[4,288,128]{2,1,0:T(8,128)(2,1)S(1)}, bf16[4,288,128]{2,1,0:T(8,128)(2,1)S(1)}, u32[]{:S(2)}, u32[]{:S(2)}) %collective-permute-start.3) | collective-permute-done | bytes 294944 | tf_op jit(solution)/shard_map/ppermute | solution.py:73
  39.2 1.0 collective-permute-done.13
  41.0 1.9 %collective-permute-start.6 = (bf16[2,288,128]{2,1,0:T(8,128)(2,1)S(1)}, bf16[2,288,128]{2,1,0:T(8,128)(2,1)S(1)}, u32[]{:S(2)}, u32[]{:S(2)}) collective-permute-start(bf16[2,288,128]{2,1,0:T(8,128)(2,1)S(1)} %slice.142), channel_id=1, source_target_pairs={{0,128},{8,136},{16,144},{24,152},{32,160},{40,168},{48,176},{56,1... | collective-permute-start | bytes 442376 | tf_op jit(solution)/shard_map/ppermute | solution.py:73
  43.4 3.6 %collective-permute-done.6 = bf16[2,288,128]{2,1,0:T(8,128)(2,1)S(1)} collective-permute-done((bf16[2,288,128]{2,1,0:T(8,128)(2,1)S(1)}, bf16[2,288,128]{2,1,0:T(8,128)(2,1)S(1)}, u32[]{:S(2)}, u32[]{:S(2)}) %collective-permute-start.6) | collective-permute-done | bytes 147488 | tf_op jit(solution)/shard_map/ppermute | solution.py:73
  49.0 15.3 %shard_map.93 = f32[8,192,128]{2,1,0:T(8,128)} custom-call(f32[192,128]{1,0:T(8,128)} %pad_maximum_fusion.3.x_ref), custom_call_target="tpu_custom_call" | custom-call | tf_op jit(solution)/shard_map/pallas_call | solution.py:58
  64.2 1.1 slice_reduce_fusion
  67.2 1.7 %fusion.31 = (f32[2,2,1,32,2048]{4,3,2,1,0:T(8,128)S(1)}, f32[2,2,1,32,2048]{4,3,2,1,0:T(8,128)S(1)}) fusion(f32[2,2,2,32,2048]{4,3,2,1,0:T(8,128)} %bitcast.103), kind=kLoop, calls=%fused_computation.107 | loop fusion | bytes 4194304 | tf_op jit(solution)/shard_map/slice | solution.py:126
  69.4 21.8 %collective-permute-done.7 = f32[2,2,32,2048]{3,2,0,1:T(8,128)S(1)} collective-permute-done((f32[2,2,32,2048]{3,2,0,1:T(8,128)S(1)}, f32[2,2,32,2048]{3,2,0,1:T(8,128)S(1)}, u32[]{:S(2)}, u32[]{:S(2)}) %collective-permute-start.7) | collective-permute-done | bytes 1048608 | tf_op jit(solution)/shard_map/ppermute | solution.py:130
  91.4 1.2 collective-permute-start.14
  92.7 5.6 %collective-permute-done.14 = f32[2,288,128]{2,1,0:T(8,128)S(1)} collective-permute-done((f32[2,288,128]{2,1,0:T(8,128)S(1)}, f32[2,288,128]{2,1,0:T(8,128)S(1)}, u32[]{:S(2)}, u32[]{:S(2)}) %collective-permute-start.14) | collective-permute-done | bytes 294944 | tf_op jit(solution)/shard_map/ppermute | solution.py:73
  99.8 4.9 %collective-permute-start.11 = (f32[2,32,2048]{2,1,0:T(8,128)}, f32[2,32,2048]{2,1,0:T(8,128)S(1)}, u32[]{:S(2)}, u32[]{:S(2)}) collective-permute-start(f32[2,32,2048]{2,1,0:T(8,128)} %select_bitcast_fusion.1), channel_id=1, source_target_pairs={{0,2},{1,3},{2,0},{3,1},{4,6},{5,7},{6,4},{7,5},{8,10},{9,11},{10,... | collective-permute-start | bytes 1572872 | tf_op jit(solution)/shard_map/ppermute | solution.py:130
  104.8 1.1 select_reduce_fusion
  107.4 2.1 %fusion.1 = bf16[256,1024]{1,0:T(8,128)(2,1)} fusion(f32[2,128,1024]{2,1,0:T(8,128)S(1)} %convolution_multiply_fusion, bf16[256,2048]{1,0:T(8,128)(2,1)S(1)} %bitcast.108, bf16[1024,2048]{1,0:T(8,128)(2,1)S(1)} %copy-done.5), kind=kOutput, calls=%fused_computation.12 | convolution fusion | flops 1074266112 | bytes 6815744 | tf_op jit(solution)/shard_map/dot_general | solution.py:233
  109.5 1.0 slice.196
  111.3 0.9 convolution_bitcast_fusion.1
  112.2 1.0 convolution_bitcast_fusion
  113.2 4.3 %collective-permute-done.11 = f32[2,32,2048]{2,1,0:T(8,128)S(1)} collective-permute-done((f32[2,32,2048]{2,1,0:T(8,128)}, f32[2,32,2048]{2,1,0:T(8,128)S(1)}, u32[]{:S(2)}, u32[]{:S(2)}) %collective-permute-start.11) | collective-permute-done | bytes 524320 | tf_op jit(solution)/shard_map/ppermute | solution.py:130
  117.6 5.0 %collective-permute-done.16 = f32[4,288,128]{2,1,0:T(8,128)} collective-permute-done((f32[4,288,128]{2,1,0:T(8,128)}, f32[4,288,128]{2,1,0:T(8,128)}, u32[]{:S(2)}, u32[]{:S(2)}) %collective-permute-start.16) | collective-permute-done | bytes 589856 | tf_op jit(solution)/shard_map/ppermute | solution.py:73
  122.6 1.2 select_add_fusion
  124.7 1.5 collective-permute-start.12
  126.1 13.0 %collective-permute-done.17 = f32[2,288,128]{2,1,0:T(8,128)S(1)} collective-permute-done((f32[2,288,128]{2,1,0:T(8,128)S(1)}, f32[2,288,128]{2,1,0:T(8,128)S(1)}, u32[]{:S(2)}, u32[]{:S(2)}) %collective-permute-start.17) | collective-permute-done | bytes 294944 | tf_op jit(solution)/shard_map/ppermute | solution.py:73
  140.1 9.3 %collective-permute-done.18 = f32[1,288,128]{2,1,0:T(8,128)S(1)} collective-permute-done((f32[1,288,128]{2,1,0:T(8,128)S(1)}, f32[1,288,128]{2,1,0:T(8,128)S(1)}, u32[]{:S(2)}, u32[]{:S(2)}) %collective-permute-start.18) | collective-permute-done | bytes 147488 | tf_op jit(solution)/shard_map/ppermute | solution.py:73
  (97 shorter events, 17.0 us)
Async XLA Ops:
  0.6 12.2 %copy-start = (bf16[256,1024]{1,0:T(8,128)(2,1)S(1)}, bf16[256,1024]{1,0:T(8,128)(2,1)}, u32[]{:S(2)}) copy-start(bf16[256,1024]{1,0:T(8,128)(2,1)} %param.8) | copy-start | bytes 1572868
  0.6 17.0 %collective-permute-start = (s32[2]{0:T(128)}, s32[2]{0:T(128)S(1)}, u32[]{:S(2)}, u32[]{:S(2)}) collective-permute-start(s32[2]{0:T(128)} %bitcast.123), channel_id=1, source_target_pairs={{0,128},{8,136},{16,144},{24,152},{32,160},{40,168},{48,176},{56,1... | collective-permute-start | bytes 32 | tf_op jit(solution)/shard_map/ppermute | solution.py:73
  3.0 17.5 %collective-permute-start.8 = (bf16[1,32,2048]{2,1,0:T(8,128)(2,1)}, bf16[1,32,2048]{2,1,0:T(8,128)(2,1)S(1)}, u32[]{:S(2)}, u32[]{:S(2)}) collective-permute-start(bf16[1,32,2048]{2,1,0:T(8,128)(2,1)} %bitcast.113), channel_id=1, source_target_pairs={{0,4},{1,5},{2,6},{3,7},{4,0},{5,1},{6,2},{7,3},{8,12},{9,13},{10,... | collective-permute-start | bytes 393224 | tf_op jit(solution)/shard_map/ppermute | solution.py:109
  5.6 13.3 %collective-permute-start.1 = (bf16[1,288,128]{2,1,0:T(8,128)(2,1)S(1)}, bf16[1,288,128]{2,1,0:T(8,128)(2,1)S(1)}, u32[]{:S(2)}, u32[]{:S(2)}) collective-permute-start(bf16[1,288,128]{2,1,0:T(8,128)(2,1)S(1)} %pad_maximum_fusion.4), channel_id=1, source_target_pairs={{0,64},{8,72},{16,80},{24,88},{32,96},{40,104},{48,112},{56,120},{... | collective-permute-start | bytes 221192 | tf_op jit(solution)/shard_map/ppermute | solution.py:73
  12.8 4.8 %copy-start.4 = (s32[2,1]{0,1:T(1,128)S(1)}, s32[2,1]{0,1:T(1,128)}, u32[]{:S(2)}) copy-start(s32[2,1]{0,1:T(1,128)} %param.12) | copy-start | bytes 28
  12.8 7.7 %copy-start.3 = (bf16[32,2048]{1,0:T(8,128)(2,1)S(1)}, bf16[32,2048]{1,0:T(8,128)(2,1)}, u32[]{:S(2)}) copy-start(bf16[32,2048]{1,0:T(8,128)(2,1)} %param.13) | copy-start | bytes 393220
  17.7 1.1 collective-permute-start.4
  18.9 10.1 %collective-permute-start.2 = (bf16[2,288,128]{2,1,0:T(8,128)(2,1)S(1)}, bf16[2,288,128]{2,1,0:T(8,128)(2,1)S(1)}, u32[]{:S(2)}, u32[]{:S(2)}) collective-permute-start(bf16[2,288,128]{2,1,0:T(8,128)(2,1)S(1)} %maximum_select_fusion.6), channel_id=1, source_target_pairs={{0,32},{8,40},{16,48},{24,56},{32,0},{40,8},{48,16},{56,24},{64,96... | collective-permute-start | bytes 442376 | tf_op jit(solution)/shard_map/ppermute | solution.py:73
  20.5 9.7 %collective-permute-start.9 = (bf16[2,32,2048]{2,1,0:T(8,128)(2,1)S(1)}, bf16[2,32,2048]{2,1,0:T(8,128)(2,1)S(1)}, u32[]{:S(2)}, u32[]{:S(2)}) collective-permute-start(bf16[2,32,2048]{2,1,0:T(8,128)(2,1)S(1)} %maximum_select_fusion.4), channel_id=1, source_target_pairs={{0,2},{1,3},{2,0},{3,1},{4,6},{5,7},{6,4},{7,5},{8,10},{9,11},{10,... | collective-permute-start | bytes 786440 | tf_op jit(solution)/shard_map/ppermute | solution.py:109
  29.0 8.6 %collective-permute-start.3 = (bf16[4,288,128]{2,1,0:T(8,128)(2,1)S(1)}, bf16[4,288,128]{2,1,0:T(8,128)(2,1)S(1)}, u32[]{:S(2)}, u32[]{:S(2)}) collective-permute-start(bf16[4,288,128]{2,1,0:T(8,128)(2,1)S(1)} %maximum_select_fusion.3), channel_id=1, source_target_pairs={{0,16},{8,24},{16,0},{24,8},{32,48},{40,56},{48,32},{56,40},{64,80... | collective-permute-start | bytes 884744 | tf_op jit(solution)/shard_map/ppermute | solution.py:73
  30.3 13.0 %collective-permute-start.10 = (bf16[4,32,2048]{2,1,0:T(8,128)(2,1)S(1)}, bf16[4,32,2048]{2,1,0:T(8,128)(2,1)S(1)}, u32[]{:S(2)}, u32[]{:S(2)}) collective-permute-start(bf16[4,32,2048]{2,1,0:T(8,128)(2,1)S(1)} %bitcast.101), channel_id=1, source_target_pairs={{0,1},{1,0},{2,3},{3,2},{4,5},{5,4},{6,7},{7,6},{8,9},{9,8},{10,11... | collective-permute-start | bytes 1572872 | tf_op jit(solution)/shard_map/ppermute | solution.py:109
  38.5 2.4 %collective-permute-start.5 = (bf16[4,288,128]{2,1,0:T(8,128)(2,1)S(1)}, bf16[4,288,128]{2,1,0:T(8,128)(2,1)S(1)}, u32[]{:S(2)}, u32[]{:S(2)}) collective-permute-start(bf16[4,288,128]{2,1,0:T(8,128)(2,1)S(1)} %select_select_fusion), channel_id=1, source_target_pairs={{0,8},{8,0},{16,24},{24,16},{32,40},{40,32},{48,56},{56,48},{64,72... | collective-permute-start | bytes 884744 | tf_op jit(solution)/shard_map/ppermute | solution.py:73
  38.6 1.5 %collective-permute-start.13 = (s32[4]{0:T(128)S(1)}, s32[4]{0:T(128)S(1)}, u32[]{:S(2)}, u32[]{:S(2)}) collective-permute-start(s32[4]{0:T(128)S(1)} %get-tuple-element.21), channel_id=1, source_target_pairs={{0,8},{8,0},{16,24},{24,16},{32,40},{40,32},{48,56},{56,48},{64,72... | collective-permute-start | bytes 56 | tf_op jit(solution)/shard_map/ppermute | solution.py:73
  41.0 6.1 %collective-permute-start.6 = (bf16[2,288,128]{2,1,0:T(8,128)(2,1)S(1)}, bf16[2,288,128]{2,1,0:T(8,128)(2,1)S(1)}, u32[]{:S(2)}, u32[]{:S(2)}) collective-permute-start(bf16[2,288,128]{2,1,0:T(8,128)(2,1)S(1)} %slice.142), channel_id=1, source_target_pairs={{0,128},{8,136},{16,144},{24,152},{32,160},{40,168},{48,176},{56,1... | collective-permute-start | bytes 442376 | tf_op jit(solution)/shard_map/ppermute | solution.py:73
  43.4 22.2 %copy-start.1 = (bf16[4,2,32,2048]{3,2,1,0:T(8,128)(2,1)}, bf16[4,2,32,2048]{3,2,1,0:T(8,128)(2,1)S(1)}, u32[]{:S(2)}) copy-start(bf16[4,2,32,2048]{3,2,1,0:T(8,128)(2,1)S(1)} %maximum_select_fusion) | copy-start | bytes 3145732
  69.0 22.2 %collective-permute-start.7 = (f32[2,2,32,2048]{3,2,0,1:T(8,128)S(1)}, f32[2,2,32,2048]{3,2,0,1:T(8,128)S(1)}, u32[]{:S(2)}, u32[]{:S(2)}) collective-permute-start(f32[2,2,32,2048]{3,2,0,1:T(8,128)S(1)} %select_bitcast_fusion), channel_id=1, source_target_pairs={{0,1},{1,0},{2,3},{3,2},{4,5},{5,4},{6,7},{7,6},{8,9},{9,8},{10,11... | collective-permute-start | bytes 3145736 | tf_op jit(solution)/shard_map/ppermute | solution.py:130
  91.4 6.8 %collective-permute-start.14 = (f32[2,288,128]{2,1,0:T(8,128)S(1)}, f32[2,288,128]{2,1,0:T(8,128)S(1)}, u32[]{:S(2)}, u32[]{:S(2)}) collective-permute-start(f32[2,288,128]{2,1,0:T(8,128)S(1)} %bitcast.98), channel_id=1, source_target_pairs={{0,128},{8,136},{16,144},{24,152},{32,160},{40,168},{48,176},{56,1... | collective-permute-start | bytes 884744 | tf_op jit(solution)/shard_map/ppermute | solution.py:73
  98.3 6.4 %collective-permute-start.15 = (f32[4,288,128]{2,1,0:T(8,128)S(1)}, f32[4,288,128]{2,1,0:T(8,128)S(1)}, u32[]{:S(2)}, u32[]{:S(2)}) collective-permute-start(f32[4,288,128]{2,1,0:T(8,128)S(1)} %pad_maximum_fusion.1), channel_id=1, source_target_pairs={{0,8},{8,0},{16,24},{24,16},{32,40},{40,32},{48,56},{56,48},{64,72... | collective-permute-start | bytes 1769480 | tf_op jit(solution)/shard_map/ppermute | solution.py:73
  99.8 17.7 %collective-permute-start.11 = (f32[2,32,2048]{2,1,0:T(8,128)}, f32[2,32,2048]{2,1,0:T(8,128)S(1)}, u32[]{:S(2)}, u32[]{:S(2)}) collective-permute-start(f32[2,32,2048]{2,1,0:T(8,128)} %select_bitcast_fusion.1), channel_id=1, source_target_pairs={{0,2},{1,3},{2,0},{3,1},{4,6},{5,7},{6,4},{7,5},{8,10},{9,11},{10,... | collective-permute-start | bytes 1572872 | tf_op jit(solution)/shard_map/ppermute | solution.py:130
  104.7 2.4 %copy-start.5 = (bf16[1024,2048]{1,0:T(8,128)(2,1)S(1)}, bf16[1024,2048]{1,0:T(8,128)(2,1)}, u32[]{:S(2)}) copy-start(bf16[1024,2048]{1,0:T(8,128)(2,1)} %param.9) | copy-start | bytes 12582916
  104.8 2.6 %copy-start.2 = (bf16[4,2,32,2048]{3,2,1,0:T(8,128)(2,1)S(1)}, bf16[4,2,32,2048]{3,2,1,0:T(8,128)(2,1)}, u32[]{:S(2)}) copy-start(bf16[4,2,32,2048]{3,2,1,0:T(8,128)(2,1)} %copy-done.1) | copy-start | bytes 3145732
  106.8 15.8 %collective-permute-start.16 = (f32[4,288,128]{2,1,0:T(8,128)}, f32[4,288,128]{2,1,0:T(8,128)}, u32[]{:S(2)}, u32[]{:S(2)}) collective-permute-start(f32[4,288,128]{2,1,0:T(8,128)} %slice_select_fusion), channel_id=1, source_target_pairs={{0,16},{8,24},{16,0},{24,8},{32,48},{40,56},{48,32},{56,40},{64,80... | collective-permute-start | bytes 1769480 | tf_op jit(solution)/shard_map/ppermute | solution.py:73
  123.8 15.3 %collective-permute-start.17 = (f32[2,288,128]{2,1,0:T(8,128)S(1)}, f32[2,288,128]{2,1,0:T(8,128)S(1)}, u32[]{:S(2)}, u32[]{:S(2)}) collective-permute-start(f32[2,288,128]{2,1,0:T(8,128)S(1)} %slice_select_fusion.1), channel_id=1, source_target_pairs={{0,32},{8,40},{16,48},{24,56},{32,0},{40,8},{48,16},{56,24},{64,96... | collective-permute-start | bytes 884744 | tf_op jit(solution)/shard_map/ppermute | solution.py:73
  124.7 14.7 %collective-permute-start.12 = (f32[32,2048]{1,0:T(8,128)S(1)}, f32[32,2048]{1,0:T(8,128)S(1)}, u32[]{:S(2)}, u32[]{:S(2)}) collective-permute-start(f32[32,2048]{1,0:T(8,128)S(1)} %select_bitcast_fusion.2), channel_id=1, source_target_pairs={{0,4},{1,5},{2,6},{3,7},{4,0},{5,1},{6,2},{7,3},{8,12},{9,13},{10,... | collective-permute-start | bytes 786440 | tf_op jit(solution)/shard_map/ppermute | solution.py:130
  139.2 10.1 %collective-permute-start.18 = (f32[1,288,128]{2,1,0:T(8,128)S(1)}, f32[1,288,128]{2,1,0:T(8,128)S(1)}, u32[]{:S(2)}, u32[]{:S(2)}) collective-permute-start(f32[1,288,128]{2,1,0:T(8,128)S(1)} %slice_select_fusion.3), channel_id=1, source_target_pairs={{0,64},{8,72},{16,80},{24,88},{32,96},{40,104},{48,112},{56,120},{... | collective-permute-start | bytes 442376 | tf_op jit(solution)/shard_map/ppermute | solution.py:73

commit v13 on v9

--- a/solution.py
+++ b/solution.py
@@ -205,7 +205,14 @@
         axis=2,
     )
     base, fac_b = lax.optimization_barrier((jnp.dot(tokens, weight, preferred_element_type=f32), fac_b))
-    base_out = reduce_scatter_tp(base)
+    half = base.shape[1] // 2
+    base_out = jnp.concatenate(
+        [
+            lax.psum_scatter(base[:, :half], "tp", scatter_dimension=0, tiled=True),
+            reduce_scatter_tp(base[:, half:]),
+        ],
+        axis=1,
+    )
 
     parts = jnp.stack([act_part, grad_part])
     flat_parts = parts.reshape(-1, 128)

time: 140 us -> 168 us (1.20)
  between operations: 1.1 us -> 14.5 us
  waiting for transfers between devices: 63.8 us -> 76.5 us
  other arithmetic: 8.17 us -> 11.2 us
    reduce_scatter x0 -> x1, waiting for transfers between devices: none -> 26.9 us  [on_device(): lax.psum_scatter(base[:, :half], 'tp', scatter_dimension=0, tiled=True)]
    ppermute x3, waiting for transfers between devices: 28.2 us -> 12.2 us  [reduce_scatter_tp(): held = keep + lax.ppermute(send, 'tp', [(i, i ^ bit) for i in range(count)])]
    slice x0 -> x1, local copies, waits for them, and re-layouts: none -> 2.72 us  [on_device(): base[:, :half]]
    ppermute x13, starting transfers between devices: 16.7 us -> 14.8 us  [_swap(): return lax.ppermute(x, 'blk', [(i, i ^ bit) for i in range(count)])]
    ppermute x3, starting transfers between devices: 5.63 us -> 7.37 us  [gather_tp(): got = lax.ppermute(held, 'tp', [(i, i ^ bit) for i in range(count)])]
    slice x1, local copies, waits for them, and re-layouts: 1.76 us -> 0.07 us  [reduce_scatter_tp(): high = lax.index_in_dim(held, 1, axis, keepdims=False)]
  transfers between devices with their start and end apart: 19 -> 20, of which waited for: 14 -> 15; matrix products, arithmetic and copies ran while one was open for 16% -> 14% of each run, Pallas kernels for 0% -> 0%
where the time goes in v13:
time: 168 us; the launch traced here: 167 us
  waiting for transfers between devices  76.5 us (46%)
  starting transfers between devices  29.6 us (18%)
  Pallas kernels  15.2 us (9%)
  between operations  14.5 us (9%)
  other arithmetic  11.2 us (7%)
  local copies, waits for them, and re-layouts  10.7 us (6%)
  matrix products  9.52 us (6%)
    ppermute x13, waiting for transfers between devices, _swap(): return lax.ppermute(x, 'blk', [(i, i ^ bit) for i in range(count)])  35.1 us
    reduce_scatter x1, waiting for transfers between devices, on_device(): lax.psum_scatter(base[:, :half], 'tp', scatter_dimension=0, tiled=True)  26.9 us
    pallas_call x1, Pallas kernels, gather_axis(): pl.pallas_call(functools.partial(_gather_kernel, axis, n), out_shape=jax....  15.2 us
    ppermute x13, starting transfers between devices, _swap(): return lax.ppermute(x, 'blk', [(i, i ^ bit) for i in range(count)])  14.8 us
    ppermute x3, waiting for transfers between devices, reduce_scatter_tp(): held = keep + lax.ppermute(send, 'tp', [(i, i ^ bit) for i in range(count)])  12.2 us
    ppermute x3, starting transfers between devices, reduce_scatter_tp(): held = keep + lax.ppermute(send, 'tp', [(i, i ^ bit) for i in range(count)])  7.4 us
    ppermute x3, starting transfers between devices, gather_tp(): got = lax.ppermute(held, 'tp', [(i, i ^ bit) for i in range(count)])  7.37 us
    dot_general x1, matrix products, on_device(): jnp.dot(tokens, weight, preferred_element_type=f32)  4.82 us
  transfers between devices with their start and end apart: 20, of which 15 were waited for; matrix products, arithmetic and copies ran while one was open for 14% of the time, Pallas kernels for 0%

profile of v13, /device:TPU:2, one launch (start us, length us, event | category | flops | bytes accessed | tf_op | source)
XLA Modules:
  0.0 167.3 jit_solution(2735223462406718455)
XLA Ops:
  7.2 1.1 copy.30
  9.2 7.2 %collective-permute-start.1 = (bf16[1,288,128]{2,1,0:T(8,128)(2,1)S(1)}, bf16[1,288,128]{2,1,0:T(8,128)(2,1)S(1)}, u32[]{:S(2)}, u32[]{:S(2)}) collective-permute-start(bf16[1,288,128]{2,1,0:T(8,128)(2,1)S(1)} %pad_maximum_fusion.3), channel_id=1, source_target_pairs={{0,64},{8,72},{16,80},{24,88},{32,96},{40,104},{48,112},{56,120},{... | collective-permute-start | bytes 221192 | tf_op jit(solution)/shard_map/ppermute | solution.py:73
  16.9 2.4 %collective-permute-start.10 = (bf16[1,32,2048]{2,1,0:T(8,128)(2,1)}, bf16[1,32,2048]{2,1,0:T(8,128)(2,1)S(1)}, u32[]{:S(2)}, u32[]{:S(2)}) collective-permute-start(bf16[1,32,2048]{2,1,0:T(8,128)(2,1)} %bitcast.109), channel_id=1, source_target_pairs={{0,4},{1,5},{2,6},{3,7},{4,0},{5,1},{6,2},{7,3},{8,12},{9,13},{10,... | collective-permute-start | bytes 393224 | tf_op jit(solution)/shard_map/ppermute | solution.py:109
  19.3 4.8 %fusion.33 = f32[256,2048]{1,0:T(8,128)} fusion(bf16[256,1024]{1,0:T(8,128)(2,1)S(1)} %copy-done, bf16[1024,2048]{1,0:T(8,128)(2,1)} %param.9), kind=kOutput, calls=%fused_computation.110 | convolution fusion | flops 1073741824 | bytes 6815744 | tf_op jit(solution)/shard_map/dot_general | solution.py:207
  25.8 1.6 collective-permute-start.2
  27.4 3.3 %collective-permute-start.11 = (bf16[2,32,2048]{2,1,0:T(8,128)(2,1)S(1)}, bf16[2,32,2048]{2,1,0:T(8,128)(2,1)S(1)}, u32[]{:S(2)}, u32[]{:S(2)}) collective-permute-start(bf16[2,32,2048]{2,1,0:T(8,128)(2,1)S(1)} %maximum_select_fusion.4), channel_id=1, source_target_pairs={{0,2},{1,3},{2,0},{3,1},{4,6},{5,7},{6,4},{7,5},{8,10},{9,11},{10,... | collective-permute-start | bytes 786440 | tf_op jit(solution)/shard_map/ppermute | solution.py:109
  30.7 5.3 %collective-permute-done.2 = bf16[2,288,128]{2,1,0:T(8,128)(2,1)S(1)} collective-permute-done((bf16[2,288,128]{2,1,0:T(8,128)(2,1)S(1)}, bf16[2,288,128]{2,1,0:T(8,128)(2,1)S(1)}, u32[]{:S(2)}, u32[]{:S(2)}) %collective-permute-start.2) | collective-permute-done | bytes 147488 | tf_op jit(solution)/shard_map/ppermute | solution.py:73
  36.2 1.0 collective-permute-done.11
  37.3 1.7 collective-permute-start.12
  39.0 5.7 %collective-permute-done.3 = bf16[4,288,128]{2,1,0:T(8,128)(2,1)S(1)} collective-permute-done((bf16[4,288,128]{2,1,0:T(8,128)(2,1)S(1)}, bf16[4,288,128]{2,1,0:T(8,128)(2,1)S(1)}, u32[]{:S(2)}, u32[]{:S(2)}) %collective-permute-start.3) | collective-permute-done | bytes 294944 | tf_op jit(solution)/shard_map/ppermute | solution.py:73
  47.3 1.9 %collective-permute-start.6 = (bf16[2,288,128]{2,1,0:T(8,128)(2,1)S(1)}, bf16[2,288,128]{2,1,0:T(8,128)(2,1)S(1)}, u32[]{:S(2)}, u32[]{:S(2)}) collective-permute-start(bf16[2,288,128]{2,1,0:T(8,128)(2,1)S(1)} %slice.150), channel_id=1, source_target_pairs={{0,128},{8,136},{16,144},{24,152},{32,160},{40,168},{48,176},{56,1... | collective-permute-start | bytes 442376 | tf_op jit(solution)/shard_map/ppermute | solution.py:73
  49.2 1.2 collective-permute-done.12
  50.5 2.8 %collective-permute-done.6 = bf16[2,288,128]{2,1,0:T(8,128)(2,1)S(1)} collective-permute-done((bf16[2,288,128]{2,1,0:T(8,128)(2,1)S(1)}, bf16[2,288,128]{2,1,0:T(8,128)(2,1)S(1)}, u32[]{:S(2)}, u32[]{:S(2)}) %collective-permute-start.6) | collective-permute-done | bytes 147488 | tf_op jit(solution)/shard_map/ppermute | solution.py:73
  55.3 15.2 %shard_map.93 = f32[8,192,128]{2,1,0:T(8,128)} custom-call(f32[192,128]{1,0:T(8,128)} %pad_maximum_fusion.2.x_ref), custom_call_target="tpu_custom_call" | custom-call | tf_op jit(solution)/shard_map/pallas_call | solution.py:58
  70.5 1.1 slice_reduce_fusion
  73.7 1.6 collective-permute-start.14
  75.2 2.7 %fusion.30 = (f32[256,1024]{1,0:T(8,128)}, f32[256,1024]{1,0:T(8,128)S(1)}) fusion(f32[256,2048]{1,0:T(8,128)} %fusion.33), kind=kLoop, calls=%fused_computation.107 | loop fusion | bytes 4194304 | tf_op jit(solution)/shard_map/slice | solution.py:211
  78.0 2.5 %collective-permute-done.14 = f32[2,288,128]{2,1,0:T(8,128)S(1)} collective-permute-done((f32[2,288,128]{2,1,0:T(8,128)S(1)}, f32[2,288,128]{2,1,0:T(8,128)S(1)}, u32[]{:S(2)}, u32[]{:S(2)}) %collective-permute-start.14) | collective-permute-done | bytes 294944 | tf_op jit(solution)/shard_map/ppermute | solution.py:73
  82.7 1.3 pad_maximum_fusion
  84.1 1.1 select_reduce_fusion
  86.3 2.1 %fusion.1 = bf16[256,1024]{1,0:T(8,128)(2,1)} fusion(f32[2,128,1024]{2,1,0:T(8,128)S(1)} %convolution_multiply_fusion, bf16[256,2048]{1,0:T(8,128)(2,1)S(1)} %bitcast.105, bf16[1024,2048]{1,0:T(8,128)(2,1)S(1)} %copy-done.6), kind=kOutput, calls=%fused_computation.12 | convolution fusion | flops 1074266112 | bytes 6815744 | tf_op jit(solution)/shard_map/dot_general | solution.py:242
  88.4 1.0 slice.206
  90.6 6.3 %collective-permute-done.7 = f32[2,2,32,1024]{3,2,0,1:T(8,128)} collective-permute-done((f32[2,2,32,1024]{3,2,0,1:T(8,128)}, f32[2,2,32,1024]{3,2,0,1:T(8,128)}, u32[]{:S(2)}, u32[]{:S(2)}) %collective-permute-start.7) | collective-permute-done | bytes 524320 | tf_op jit(solution)/shard_map/ppermute | solution.py:130
  96.9 1.2 bitcast_add_fusion.1
  98.1 4.9 %collective-permute-start.8 = (f32[2,32,1024]{2,1,0:T(8,128)S(1)}, f32[2,32,1024]{2,1,0:T(8,128)S(1)}, u32[]{:S(2)}, u32[]{:S(2)}) collective-permute-start(f32[2,32,1024]{2,1,0:T(8,128)S(1)} %select_bitcast_fusion.1), channel_id=1, source_target_pairs={{0,2},{1,3},{2,0},{3,1},{4,6},{5,7},{6,4},{7,5},{8,10},{9,11},{10,... | collective-permute-start | bytes 786440 | tf_op jit(solution)/shard_map/ppermute | solution.py:130
  103.0 1.2 select_add_fusion
  105.0 5.9 %collective-permute-done.8 = f32[2,32,1024]{2,1,0:T(8,128)S(1)} collective-permute-done((f32[2,32,1024]{2,1,0:T(8,128)S(1)}, f32[2,32,1024]{2,1,0:T(8,128)S(1)}, u32[]{:S(2)}, u32[]{:S(2)}) %collective-permute-start.8) | collective-permute-done | bytes 262176 | tf_op jit(solution)/shard_map/ppermute | solution.py:130
  111.0 2.3 %collective-permute-start.9 = (f32[32,1024]{1,0:T(8,128)S(1)}, f32[32,1024]{1,0:T(8,128)S(1)}, u32[]{:S(2)}, u32[]{:S(2)}) collective-permute-start(f32[32,1024]{1,0:T(8,128)S(1)} %select_bitcast_fusion.2), channel_id=1, source_target_pairs={{0,4},{1,5},{2,6},{3,7},{4,0},{5,1},{6,2},{7,3},{8,12},{9,13},{10,... | collective-permute-start | bytes 393224 | tf_op jit(solution)/shard_map/ppermute | solution.py:130
  113.3 6.4 %collective-permute-done.17 = f32[2,288,128]{2,1,0:T(8,128)S(1)} collective-permute-done((f32[2,288,128]{2,1,0:T(8,128)S(1)}, f32[2,288,128]{2,1,0:T(8,128)S(1)}, u32[]{:S(2)}, u32[]{:S(2)}) %collective-permute-start.17) | collective-permute-done | bytes 294944 | tf_op jit(solution)/shard_map/ppermute | solution.py:73
  119.9 10.0 %collective-permute-done.18 = f32[1,288,128]{2,1,0:T(8,128)S(1)} collective-permute-done((f32[1,288,128]{2,1,0:T(8,128)S(1)}, f32[1,288,128]{2,1,0:T(8,128)S(1)}, u32[]{:S(2)}, u32[]{:S(2)}) %collective-permute-start.18) | collective-permute-done | bytes 147488 | tf_op jit(solution)/shard_map/ppermute | solution.py:73
  131.9 26.9 %reduce-scatter.2.cloned.1.call-done = f32[32,1024]{1,0:T(8,128)} async-done(((f32[256,1024]{1,0:T(8,128)}), f32[32,1024]{1,0:T(8,128)}) %reduce-scatter.2.cloned.1.call-update) | async-done | bytes 131088 | tf_op jit(solution)/shard_map/reduce_scatter | solution.py:211
  158.8 1.6 fusion.2
  (104 shorter events, 17.5 us)
Async XLA Ops:
  7.2 12.2 %copy-start = (bf16[256,1024]{1,0:T(8,128)(2,1)S(1)}, bf16[256,1024]{1,0:T(8,128)(2,1)}, u32[]{:S(2)}) copy-start(bf16[256,1024]{1,0:T(8,128)(2,1)} %param.8) | copy-start | bytes 1572868
  7.2 151.6 %reduce-scatter.2.cloned.1.call-start = ((), (), s32[]{:S(2)}) async-start(), calls=%async_computation.1 | async-start | bytes 1179648 | tf_op jit(solution)/shard_map/reduce_scatter | solution.py:211
  9.2 16.6 %collective-permute-start.1 = (bf16[1,288,128]{2,1,0:T(8,128)(2,1)S(1)}, bf16[1,288,128]{2,1,0:T(8,128)(2,1)S(1)}, u32[]{:S(2)}, u32[]{:S(2)}) collective-permute-start(bf16[1,288,128]{2,1,0:T(8,128)(2,1)S(1)} %pad_maximum_fusion.3), channel_id=1, source_target_pairs={{0,64},{8,72},{16,80},{24,88},{32,96},{40,104},{48,112},{56,120},{... | collective-permute-start | bytes 221192 | tf_op jit(solution)/shard_map/ppermute | solution.py:73
  16.4 7.8 %collective-permute-start = (s32[2]{0:T(128)}, s32[2]{0:T(128)S(1)}, u32[]{:S(2)}, u32[]{:S(2)}) collective-permute-start(s32[2]{0:T(128)} %bitcast.119), channel_id=1, source_target_pairs={{0,128},{8,136},{16,144},{24,152},{32,160},{40,168},{48,176},{56,1... | collective-permute-start | bytes 32 | tf_op jit(solution)/shard_map/ppermute | solution.py:73
  16.9 10.5 %collective-permute-start.10 = (bf16[1,32,2048]{2,1,0:T(8,128)(2,1)}, bf16[1,32,2048]{2,1,0:T(8,128)(2,1)S(1)}, u32[]{:S(2)}, u32[]{:S(2)}) collective-permute-start(bf16[1,32,2048]{2,1,0:T(8,128)(2,1)} %bitcast.109), channel_id=1, source_target_pairs={{0,4},{1,5},{2,6},{3,7},{4,0},{5,1},{6,2},{7,3},{8,12},{9,13},{10,... | collective-permute-start | bytes 393224 | tf_op jit(solution)/shard_map/ppermute | solution.py:109
  19.3 4.8 %copy-start.5 = (s32[2,1]{0,1:T(1,128)S(1)}, s32[2,1]{0,1:T(1,128)}, u32[]{:S(2)}) copy-start(s32[2,1]{0,1:T(1,128)} %param.12) | copy-start | bytes 28
  19.3 8.1 %copy-start.3 = (bf16[32,2048]{1,0:T(8,128)(2,1)S(1)}, bf16[32,2048]{1,0:T(8,128)(2,1)}, u32[]{:S(2)}) copy-start(bf16[32,2048]{1,0:T(8,128)(2,1)} %param.13) | copy-start | bytes 393220
  24.2 1.1 collective-permute-start.4
  24.3 1.4 collective-permute-start.13
  25.8 10.2 %collective-permute-start.2 = (bf16[2,288,128]{2,1,0:T(8,128)(2,1)S(1)}, bf16[2,288,128]{2,1,0:T(8,128)(2,1)S(1)}, u32[]{:S(2)}, u32[]{:S(2)}) collective-permute-start(bf16[2,288,128]{2,1,0:T(8,128)(2,1)S(1)} %maximum_select_fusion.6), channel_id=1, source_target_pairs={{0,32},{8,40},{16,48},{24,56},{32,0},{40,8},{48,16},{56,24},{64,96... | collective-permute-start | bytes 442376 | tf_op jit(solution)/shard_map/ppermute | solution.py:73
  27.4 9.8 %collective-permute-start.11 = (bf16[2,32,2048]{2,1,0:T(8,128)(2,1)S(1)}, bf16[2,32,2048]{2,1,0:T(8,128)(2,1)S(1)}, u32[]{:S(2)}, u32[]{:S(2)}) collective-permute-start(bf16[2,32,2048]{2,1,0:T(8,128)(2,1)S(1)} %maximum_select_fusion.4), channel_id=1, source_target_pairs={{0,2},{1,3},{2,0},{3,1},{4,6},{5,7},{6,4},{7,5},{8,10},{9,11},{10,... | collective-permute-start | bytes 786440 | tf_op jit(solution)/shard_map/ppermute | solution.py:109
  36.1 8.6 %collective-permute-start.3 = (bf16[4,288,128]{2,1,0:T(8,128)(2,1)S(1)}, bf16[4,288,128]{2,1,0:T(8,128)(2,1)S(1)}, u32[]{:S(2)}, u32[]{:S(2)}) collective-permute-start(bf16[4,288,128]{2,1,0:T(8,128)(2,1)S(1)} %maximum_select_fusion.3), channel_id=1, source_target_pairs={{0,16},{8,24},{16,0},{24,8},{32,48},{40,56},{48,32},{56,40},{64,80... | collective-permute-start | bytes 884744 | tf_op jit(solution)/shard_map/ppermute | solution.py:73
  37.3 13.1 %collective-permute-start.12 = (bf16[4,32,2048]{2,1,0:T(8,128)(2,1)S(1)}, bf16[4,32,2048]{2,1,0:T(8,128)(2,1)S(1)}, u32[]{:S(2)}, u32[]{:S(2)}) collective-permute-start(bf16[4,32,2048]{2,1,0:T(8,128)(2,1)S(1)} %bitcast.99), channel_id=1, source_target_pairs={{0,1},{1,0},{2,3},{3,2},{4,5},{5,4},{6,7},{7,6},{8,9},{9,8},{10,11... | collective-permute-start | bytes 1572872 | tf_op jit(solution)/shard_map/ppermute | solution.py:109
  45.5 1.7 collective-permute-start.5
  47.3 6.0 %collective-permute-start.6 = (bf16[2,288,128]{2,1,0:T(8,128)(2,1)S(1)}, bf16[2,288,128]{2,1,0:T(8,128)(2,1)S(1)}, u32[]{:S(2)}, u32[]{:S(2)}) collective-permute-start(bf16[2,288,128]{2,1,0:T(8,128)(2,1)S(1)} %slice.150), channel_id=1, source_target_pairs={{0,128},{8,136},{16,144},{24,152},{32,160},{40,168},{48,176},{56,1... | collective-permute-start | bytes 442376 | tf_op jit(solution)/shard_map/ppermute | solution.py:73
  50.5 21.5 %copy-start.1 = (bf16[4,2,32,2048]{3,2,1,0:T(8,128)(2,1)}, bf16[4,2,32,2048]{3,2,1,0:T(8,128)(2,1)S(1)}, u32[]{:S(2)}) copy-start(bf16[4,2,32,2048]{3,2,1,0:T(8,128)(2,1)S(1)} %maximum_select_fusion) | copy-start | bytes 3145732
  73.7 6.8 %collective-permute-start.14 = (f32[2,288,128]{2,1,0:T(8,128)S(1)}, f32[2,288,128]{2,1,0:T(8,128)S(1)}, u32[]{:S(2)}, u32[]{:S(2)}) collective-permute-start(f32[2,288,128]{2,1,0:T(8,128)S(1)} %bitcast.96), channel_id=1, source_target_pairs={{0,128},{8,136},{16,144},{24,152},{32,160},{40,168},{48,176},{56,1... | collective-permute-start | bytes 884744 | tf_op jit(solution)/shard_map/ppermute | solution.py:73
  80.5 2.2 %collective-permute-start.15 = (f32[4,288,128]{2,1,0:T(8,128)S(1)}, f32[4,288,128]{2,1,0:T(8,128)}, u32[]{:S(2)}, u32[]{:S(2)}) collective-permute-start(f32[4,288,128]{2,1,0:T(8,128)S(1)} %pad_maximum_fusion.1), channel_id=1, source_target_pairs={{0,8},{8,0},{16,24},{24,16},{32,40},{40,32},{48,56},{56,48},{64,72... | collective-permute-start | bytes 1769480 | tf_op jit(solution)/shard_map/ppermute | solution.py:73
  81.6 15.3 %collective-permute-start.7 = (f32[2,2,32,1024]{3,2,0,1:T(8,128)}, f32[2,2,32,1024]{3,2,0,1:T(8,128)}, u32[]{:S(2)}, u32[]{:S(2)}) collective-permute-start(f32[2,2,32,1024]{3,2,0,1:T(8,128)} %select_bitcast_fusion), channel_id=1, source_target_pairs={{0,1},{1,0},{2,3},{3,2},{4,5},{5,4},{6,7},{7,6},{8,9},{9,8},{10,11... | collective-permute-start | bytes 1572872 | tf_op jit(solution)/shard_map/ppermute | solution.py:130
  82.7 3.6 %copy-start.6 = (bf16[1024,2048]{1,0:T(8,128)(2,1)S(1)}, bf16[1024,2048]{1,0:T(8,128)(2,1)}, u32[]{:S(2)}) copy-start(bf16[1024,2048]{1,0:T(8,128)(2,1)} %param.9) | copy-start | bytes 12582916
  84.1 2.3 %copy-start.2 = (bf16[4,2,32,2048]{3,2,1,0:T(8,128)(2,1)S(1)}, bf16[4,2,32,2048]{3,2,1,0:T(8,128)(2,1)}, u32[]{:S(2)}) copy-start(bf16[4,2,32,2048]{3,2,1,0:T(8,128)(2,1)} %copy-done.1) | copy-start | bytes 3145732
  86.1 16.9 %collective-permute-start.16 = (f32[4,288,128]{2,1,0:T(8,128)}, f32[4,288,128]{2,1,0:T(8,128)}, u32[]{:S(2)}, u32[]{:S(2)}) collective-permute-start(f32[4,288,128]{2,1,0:T(8,128)} %slice_select_fusion), channel_id=1, source_target_pairs={{0,16},{8,24},{16,0},{24,8},{32,48},{40,56},{48,32},{56,40},{64,80... | collective-permute-start | bytes 1769480 | tf_op jit(solution)/shard_map/ppermute | solution.py:73
  98.1 12.8 %collective-permute-start.8 = (f32[2,32,1024]{2,1,0:T(8,128)S(1)}, f32[2,32,1024]{2,1,0:T(8,128)S(1)}, u32[]{:S(2)}, u32[]{:S(2)}) collective-permute-start(f32[2,32,1024]{2,1,0:T(8,128)S(1)} %select_bitcast_fusion.1), channel_id=1, source_target_pairs={{0,2},{1,3},{2,0},{3,1},{4,6},{5,7},{6,4},{7,5},{8,10},{9,11},{10,... | collective-permute-start | bytes 786440 | tf_op jit(solution)/shard_map/ppermute | solution.py:130
  104.2 15.5 %collective-permute-start.17 = (f32[2,288,128]{2,1,0:T(8,128)S(1)}, f32[2,288,128]{2,1,0:T(8,128)S(1)}, u32[]{:S(2)}, u32[]{:S(2)}) collective-permute-start(f32[2,288,128]{2,1,0:T(8,128)S(1)} %slice_select_fusion.1), channel_id=1, source_target_pairs={{0,32},{8,40},{16,48},{24,56},{32,0},{40,8},{48,16},{56,24},{64,96... | collective-permute-start | bytes 884744 | tf_op jit(solution)/shard_map/ppermute | solution.py:73
  111.0 47.9 %copy-start.4 = (f32[1,32,1024]{2,1,0:T(8,128)S(1)}, f32[1,32,1024]{2,1,0:T(8,128)}, u32[]{:S(2)}) copy-start(f32[1,32,1024]{2,1,0:T(8,128)} %convolution_bitcast_fusion) | copy-start | bytes 393220
  111.0 8.9 %collective-permute-start.9 = (f32[32,1024]{1,0:T(8,128)S(1)}, f32[32,1024]{1,0:T(8,128)S(1)}, u32[]{:S(2)}, u32[]{:S(2)}) collective-permute-start(f32[32,1024]{1,0:T(8,128)S(1)} %select_bitcast_fusion.2), channel_id=1, source_target_pairs={{0,4},{1,5},{2,6},{3,7},{4,0},{5,1},{6,2},{7,3},{8,12},{9,13},{10,... | collective-permute-start | bytes 393224 | tf_op jit(solution)/shard_map/ppermute | solution.py:130
  119.8 10.1 %collective-permute-start.18 = (f32[1,288,128]{2,1,0:T(8,128)S(1)}, f32[1,288,128]{2,1,0:T(8,128)S(1)}, u32[]{:S(2)}, u32[]{:S(2)}) collective-permute-start(f32[1,288,128]{2,1,0:T(8,128)S(1)} %slice_select_fusion.3), channel_id=1, source_target_pairs={{0,64},{8,72},{16,80},{24,88},{32,96},{40,104},{48,112},{56,120},{... | collective-permute-start | bytes 442376 | tf_op jit(solution)/shard_map/ppermute | solution.py:73
Sparse Core Ops, SparseCore 0:
  81.9 76.8 reduce-scatter.1

commit v14 on v12

--- a/solution.py
+++ b/solution.py
@@ -246,9 +246,9 @@
     flat = jnp.concatenate([down_grad.reshape(tiles, -1), up_grad.reshape(tiles, -1)], axis=1)
     base, fac_b = lax.optimization_barrier((jnp.dot(tokens, weight, preferred_element_type=f32), fac_b))
 
-    base_out, flat = reduce_scatter_tp(base, flat)
+    summed = reduce_to_owner(flat.reshape(tiles, -1, 128), tile_ids, bank_a.shape[0]).reshape(bank_a.shape[0], -1)
+    base_out, summed = reduce_scatter_tp(base, summed)
     key_value_output = (base_out + adapter_scale * lora).astype(bf16)
-    summed = reduce_to_owner(flat.reshape(tiles, -1, 128), tile_ids, bank_a.shape[0]).reshape(bank_a.shape[0], -1)
     grad_a = summed[:, :size_a].reshape(bank_a.shape[0], feats, rank_two)
     grad_b = summed[:, size_a:].reshape(bank_a.shape[0], rank_two, kv_dev)
     return (key_value_output, token_gradient, grad_a, grad_b)

time: 153 us -> 152 us (level)
  starting transfers between devices: 28.7 us -> 34.3 us
  waiting for transfers between devices: 77.1 us -> 71.8 us
  local copies, waits for them, and re-layouts: 10.5 us -> 8.63 us
    ppermute x3, waiting for transfers between devices: 26.2 us -> 11.8 us  [reduce_scatter_tp(): held = keep + lax.ppermute(send, 'tp', [(i, i ^ bit) for i in range(count)])]
    ppermute x13, waiting for transfers between devices: 49.4 us -> 57.1 us  [_swap(): return lax.ppermute(x, 'blk', [(i, i ^ bit) for i in range(count)])]
    ppermute x13, starting transfers between devices: 16.4 us -> 21 us  [_swap(): return lax.ppermute(x, 'blk', [(i, i ^ bit) for i in range(count)])]
    dot_general x1, matrix products: 2.08 us -> 4.27 us  [on_device(): backward = jnp.dot(grad_rows, weight.T, preferred_element_type=f32)]
    concatenate x2, other arithmetic: 0.12 us -> 2.14 us  [reduce_to_owner(): rows = jnp.concatenate([rows, _swap(rows, bit, count)])]
  transfers between devices with their start and end apart: 19 -> 19, of which waited for: 13 -> 14; matrix products, arithmetic and copies ran while one was open for 12% -> 12% of each run, Pallas kernels for 0% -> 0%
where the time goes in v14:
time: 152 us; the launch traced here: 150 us
  waiting for transfers between devices  71.8 us (47%)
  starting transfers between devices  34.3 us (23%)
  Pallas kernels  15.3 us (10%)
  matrix products  9.65 us (6%)
  other arithmetic  9.22 us (6%)
  local copies, waits for them, and re-layouts  8.63 us (6%)
    ppermute x13, waiting for transfers between devices, _swap(): return lax.ppermute(x, 'blk', [(i, i ^ bit) for i in range(count)])  57.1 us
    ppermute x13, starting transfers between devices, _swap(): return lax.ppermute(x, 'blk', [(i, i ^ bit) for i in range(count)])  21 us
    pallas_call x1, Pallas kernels, gather_axis(): pl.pallas_call(functools.partial(_gather_kernel, axis, n), out_shape=jax....  15.3 us
    ppermute x3, waiting for transfers between devices, reduce_scatter_tp(): held = keep + lax.ppermute(send, 'tp', [(i, i ^ bit) for i in range(count)])  11.8 us
    ppermute x3, starting transfers between devices, reduce_scatter_tp(): held = keep + lax.ppermute(send, 'tp', [(i, i ^ bit) for i in range(count)])  7.72 us
    ppermute x3, starting transfers between devices, gather_tp(): got = lax.ppermute(held, 'tp', [(i, i ^ bit) for i in range(count)])  5.63 us
    dot_general x1, matrix products, on_device(): backward = jnp.dot(grad_rows, weight.T, preferred_element_type=f32)  4.27 us
    dot_general x1, matrix products, on_device(): jnp.dot(tokens, weight, preferred_element_type=f32)  3.44 us
  transfers between devices with their start and end apart: 19, of which 14 were waited for; matrix products, arithmetic and copies ran while one was open for 12% of the time, Pallas kernels for 0%

profile of v14, /device:TPU:2, one launch (start us, length us, event | category | flops | bytes accessed | tf_op | source)
XLA Modules:
  0.0 150.0 jit_solution(10718247319758663939)
XLA Ops:
  0.7 2.4 %collective-permute-start = (s32[2]{0:T(128)}, s32[2]{0:T(128)S(1)}, u32[]{:S(2)}, u32[]{:S(2)}) collective-permute-start(s32[2]{0:T(128)} %bitcast.123), channel_id=1, source_target_pairs={{0,128},{8,136},{16,144},{24,152},{32,160},{40,168},{48,176},{56,1... | collective-permute-start | bytes 32 | tf_op jit(solution)/shard_map/ppermute | solution.py:73
  3.7 1.0 copy.30
  5.6 7.2 %collective-permute-start.1 = (bf16[1,288,128]{2,1,0:T(8,128)(2,1)S(1)}, bf16[1,288,128]{2,1,0:T(8,128)(2,1)S(1)}, u32[]{:S(2)}, u32[]{:S(2)}) collective-permute-start(bf16[1,288,128]{2,1,0:T(8,128)(2,1)S(1)} %pad_maximum_fusion.3), channel_id=1, source_target_pairs={{0,64},{8,72},{16,80},{24,88},{32,96},{40,104},{48,112},{56,120},{... | collective-permute-start | bytes 221192 | tf_op jit(solution)/shard_map/ppermute | solution.py:73
  13.6 1.1 collective-permute-done.4
  15.3 2.9 %collective-permute-start.2 = (bf16[2,288,128]{2,1,0:T(8,128)(2,1)S(1)}, bf16[2,288,128]{2,1,0:T(8,128)(2,1)S(1)}, u32[]{:S(2)}, u32[]{:S(2)}) collective-permute-start(bf16[2,288,128]{2,1,0:T(8,128)(2,1)S(1)} %maximum_select_fusion.6), channel_id=1, source_target_pairs={{0,32},{8,40},{16,48},{24,56},{32,0},{40,8},{48,16},{56,24},{64,96... | collective-permute-start | bytes 442376 | tf_op jit(solution)/shard_map/ppermute | solution.py:73
  18.2 1.0 maximum_select_fusion.4
  19.2 3.3 %collective-permute-start.10 = (bf16[2,32,2048]{2,1,0:T(8,128)(2,1)S(1)}, bf16[2,32,2048]{2,1,0:T(8,128)(2,1)S(1)}, u32[]{:S(2)}, u32[]{:S(2)}) collective-permute-start(bf16[2,32,2048]{2,1,0:T(8,128)(2,1)S(1)} %maximum_select_fusion.4), channel_id=1, source_target_pairs={{0,2},{1,3},{2,0},{3,1},{4,6},{5,7},{6,4},{7,5},{8,10},{9,11},{10,... | collective-permute-start | bytes 786440 | tf_op jit(solution)/shard_map/ppermute | solution.py:109
  22.5 2.4 %collective-permute-done.2 = bf16[2,288,128]{2,1,0:T(8,128)(2,1)S(1)} collective-permute-done((bf16[2,288,128]{2,1,0:T(8,128)(2,1)S(1)}, bf16[2,288,128]{2,1,0:T(8,128)(2,1)S(1)}, u32[]{:S(2)}, u32[]{:S(2)}) %collective-permute-start.2) | collective-permute-done | bytes 147488 | tf_op jit(solution)/shard_map/ppermute | solution.py:73
  25.0 2.1 %collective-permute-done.10 = bf16[2,32,2048]{2,1,0:T(8,128)(2,1)S(1)} collective-permute-done((bf16[2,32,2048]{2,1,0:T(8,128)(2,1)S(1)}, bf16[2,32,2048]{2,1,0:T(8,128)(2,1)S(1)}, u32[]{:S(2)}, u32[]{:S(2)}) %collective-permute-start.10) | collective-permute-done | bytes 262176 | tf_op jit(solution)/shard_map/ppermute | solution.py:109
  27.2 1.7 %collective-permute-start.11 = (bf16[4,32,2048]{2,1,0:T(8,128)(2,1)S(1)}, bf16[4,32,2048]{2,1,0:T(8,128)(2,1)S(1)}, u32[]{:S(2)}, u32[]{:S(2)}) collective-permute-start(bf16[4,32,2048]{2,1,0:T(8,128)(2,1)S(1)} %bitcast.102), channel_id=1, source_target_pairs={{0,1},{1,0},{2,3},{3,2},{4,5},{5,4},{6,7},{7,6},{8,9},{9,8},{10,11... | collective-permute-start | bytes 1572872 | tf_op jit(solution)/shard_map/ppermute | solution.py:109
  28.9 4.6 %collective-permute-done.3 = bf16[4,288,128]{2,1,0:T(8,128)(2,1)S(1)} collective-permute-done((bf16[4,288,128]{2,1,0:T(8,128)(2,1)S(1)}, bf16[4,288,128]{2,1,0:T(8,128)(2,1)S(1)}, u32[]{:S(2)}, u32[]{:S(2)}) %collective-permute-start.3) | collective-permute-done | bytes 294944 | tf_op jit(solution)/shard_map/ppermute | solution.py:73
  35.0 0.9 collective-permute-done.5
  36.0 1.9 %collective-permute-start.6 = (bf16[2,288,128]{2,1,0:T(8,128)(2,1)S(1)}, bf16[2,288,128]{2,1,0:T(8,128)(2,1)S(1)}, u32[]{:S(2)}, u32[]{:S(2)}) collective-permute-start(bf16[2,288,128]{2,1,0:T(8,128)(2,1)S(1)} %slice.142), channel_id=1, source_target_pairs={{0,128},{8,136},{16,144},{24,152},{32,160},{40,168},{48,176},{56,1... | collective-permute-start | bytes 442376 | tf_op jit(solution)/shard_map/ppermute | solution.py:73
  38.8 3.3 %collective-permute-done.6 = bf16[2,288,128]{2,1,0:T(8,128)(2,1)S(1)} collective-permute-done((bf16[2,288,128]{2,1,0:T(8,128)(2,1)S(1)}, bf16[2,288,128]{2,1,0:T(8,128)(2,1)S(1)}, u32[]{:S(2)}, u32[]{:S(2)}) %collective-permute-start.6) | collective-permute-done | bytes 147488 | tf_op jit(solution)/shard_map/ppermute | solution.py:73
  44.0 15.3 %shard_map.93 = f32[8,192,128]{2,1,0:T(8,128)} custom-call(f32[192,128]{1,0:T(8,128)} %pad_maximum_fusion.2.x_ref), custom_call_target="tpu_custom_call" | custom-call | tf_op jit(solution)/shard_map/pallas_call | solution.py:58
  59.3 1.1 slice_reduce_fusion
  63.0 1.6 %collective-permute-start.12 = (f32[2,288,128]{2,1,0:T(8,128)S(1)}, f32[2,288,128]{2,1,0:T(8,128)S(1)}, u32[]{:S(2)}, u32[]{:S(2)}) collective-permute-start(f32[2,288,128]{2,1,0:T(8,128)S(1)} %bitcast.99), channel_id=1, source_target_pairs={{0,128},{8,136},{16,144},{24,152},{32,160},{40,168},{48,176},{56,1... | collective-permute-start | bytes 884744 | tf_op jit(solution)/shard_map/ppermute | solution.py:73
  64.6 5.2 %collective-permute-done.12 = f32[2,288,128]{2,1,0:T(8,128)S(1)} collective-permute-done((f32[2,288,128]{2,1,0:T(8,128)S(1)}, f32[2,288,128]{2,1,0:T(8,128)S(1)}, u32[]{:S(2)}, u32[]{:S(2)}) %collective-permute-start.12) | collective-permute-done | bytes 294944 | tf_op jit(solution)/shard_map/ppermute | solution.py:73
  69.8 0.9 pad_maximum_fusion.1
  70.7 3.4 %fusion.33 = f32[256,2048]{1,0:T(8,128)S(1)} fusion(bf16[256,1024]{1,0:T(8,128)(2,1)S(1)} %copy-done, bf16[1024,2048]{1,0:T(8,128)(2,1)} %param.9), kind=kOutput, calls=%fused_computation.109 | convolution fusion | flops 1073741824 | bytes 6815744 | tf_op jit(solution)/shard_map/dot_general | solution.py:247
  75.9 1.2 pad_maximum_fusion
  77.2 1.1 select_reduce_fusion
  79.3 14.6 %collective-permute-done.14 = f32[4,288,128]{2,1,0:T(8,128)S(1)} collective-permute-done((f32[4,288,128]{2,1,0:T(8,128)S(1)}, f32[4,288,128]{2,1,0:T(8,128)S(1)}, u32[]{:S(2)}, u32[]{:S(2)}) %collective-permute-start.14) | collective-permute-done | bytes 589856 | tf_op jit(solution)/shard_map/ppermute | solution.py:73
  94.5 15.1 %collective-permute-done.15 = f32[2,288,128]{2,1,0:T(8,128)S(1)} collective-permute-done((f32[2,288,128]{2,1,0:T(8,128)S(1)}, f32[2,288,128]{2,1,0:T(8,128)S(1)}, u32[]{:S(2)}, u32[]{:S(2)}) %collective-permute-start.15) | collective-permute-done | bytes 294944 | tf_op jit(solution)/shard_map/ppermute | solution.py:73
  109.7 3.4 %collective-permute-start.16 = (f32[1,288,128]{2,1,0:T(8,128)S(1)}, f32[1,288,128]{2,1,0:T(8,128)S(1)}, u32[]{:S(2)}, u32[]{:S(2)}) collective-permute-start(f32[1,288,128]{2,1,0:T(8,128)S(1)} %slice_select_fusion.3), channel_id=1, source_target_pairs={{0,64},{8,72},{16,80},{24,88},{32,96},{40,104},{48,112},{56,120},{... | collective-permute-start | bytes 442376 | tf_op jit(solution)/shard_map/ppermute | solution.py:73
  113.2 8.5 %collective-permute-done.16 = f32[1,288,128]{2,1,0:T(8,128)S(1)} collective-permute-done((f32[1,288,128]{2,1,0:T(8,128)S(1)}, f32[1,288,128]{2,1,0:T(8,128)S(1)}, u32[]{:S(2)}, u32[]{:S(2)}) %collective-permute-start.16) | collective-permute-done | bytes 147488 | tf_op jit(solution)/shard_map/ppermute | solution.py:73
  121.8 3.5 %collective-permute-start.17 = (f32[2,32,2048]{2,1,0:T(8,128)S(1)}, f32[2,32,2048]{2,1,0:T(8,128)S(1)}, u32[]{:S(2)}, u32[]{:S(2)}) collective-permute-start(f32[2,32,2048]{2,1,0:T(8,128)S(1)} %select_bitcast_fusion.1), channel_id=1, source_target_pairs={{0,2},{1,3},{2,0},{3,1},{4,6},{5,7},{6,4},{7,5},{8,10},{9,11},{10,... | collective-permute-start | bytes 1572872 | tf_op jit(solution)/shard_map/ppermute | solution.py:130
  125.7 11.8 %collective-permute-done.17 = f32[2,32,2048]{2,1,0:T(8,128)S(1)} collective-permute-done((f32[2,32,2048]{2,1,0:T(8,128)S(1)}, f32[2,32,2048]{2,1,0:T(8,128)S(1)}, u32[]{:S(2)}, u32[]{:S(2)}) %collective-permute-start.17) | collective-permute-done | bytes 524320 | tf_op jit(solution)/shard_map/ppermute | solution.py:130
  137.6 4.0 %collective-permute-start.18 = (f32[32,2048]{1,0:T(8,128)S(1)}, f32[32,2048]{1,0:T(8,128)S(1)}, u32[]{:S(2)}, u32[]{:S(2)}) collective-permute-start(f32[32,2048]{1,0:T(8,128)S(1)} %select_bitcast_fusion.2), channel_id=1, source_target_pairs={{0,4},{1,5},{2,6},{3,7},{4,0},{5,1},{6,2},{7,3},{8,12},{9,13},{10,... | collective-permute-start | bytes 786440 | tf_op jit(solution)/shard_map/ppermute | solution.py:130
  141.5 4.3 %fusion.1 = bf16[256,1024]{1,0:T(8,128)(2,1)} fusion(f32[2,128,1024]{2,1,0:T(8,128)S(1)} %convolution_multiply_fusion, bf16[256,2048]{1,0:T(8,128)(2,1)S(1)} %bitcast.109, bf16[1024,2048]{1,0:T(8,128)(2,1)} %param.9), kind=kOutput, calls=%fused_computation.12 | convolution fusion | flops 1074266112 | bytes 6815744 | tf_op jit(solution)/shard_map/dot_general | solution.py:233
  145.8 1.0 slice.194
  148.4 0.8 copy.44
  (99 shorter events, 16.4 us)
Async XLA Ops:
  0.6 42.1 %copy-start = (bf16[256,1024]{1,0:T(8,128)(2,1)S(1)}, bf16[256,1024]{1,0:T(8,128)(2,1)}, u32[]{:S(2)}) copy-start(bf16[256,1024]{1,0:T(8,128)(2,1)} %param.8) | copy-start | bytes 1572868
  0.6 24.3 %copy-start.6 = (bf16[32,2048]{1,0:T(8,128)(2,1)S(1)}, bf16[32,2048]{1,0:T(8,128)(2,1)}, u32[]{:S(2)}) copy-start(bf16[32,2048]{1,0:T(8,128)(2,1)} %param.13) | copy-start | bytes 393220
  0.7 12.1 %collective-permute-start = (s32[2]{0:T(128)}, s32[2]{0:T(128)S(1)}, u32[]{:S(2)}, u32[]{:S(2)}) collective-permute-start(s32[2]{0:T(128)} %bitcast.123), channel_id=1, source_target_pairs={{0,128},{8,136},{16,144},{24,152},{32,160},{40,168},{48,176},{56,1... | collective-permute-start | bytes 32 | tf_op jit(solution)/shard_map/ppermute | solution.py:73
  3.0 15.1 %collective-permute-start.9 = (bf16[1,32,2048]{2,1,0:T(8,128)(2,1)}, bf16[1,32,2048]{2,1,0:T(8,128)(2,1)S(1)}, u32[]{:S(2)}, u32[]{:S(2)}) collective-permute-start(bf16[1,32,2048]{2,1,0:T(8,128)(2,1)} %bitcast.113), channel_id=1, source_target_pairs={{0,4},{1,5},{2,6},{3,7},{4,0},{5,1},{6,2},{7,3},{8,12},{9,13},{10,... | collective-permute-start | bytes 393224 | tf_op jit(solution)/shard_map/ppermute | solution.py:109
  5.6 9.6 %collective-permute-start.1 = (bf16[1,288,128]{2,1,0:T(8,128)(2,1)S(1)}, bf16[1,288,128]{2,1,0:T(8,128)(2,1)S(1)}, u32[]{:S(2)}, u32[]{:S(2)}) collective-permute-start(bf16[1,288,128]{2,1,0:T(8,128)(2,1)S(1)} %pad_maximum_fusion.3), channel_id=1, source_target_pairs={{0,64},{8,72},{16,80},{24,88},{32,96},{40,104},{48,112},{56,120},{... | collective-permute-start | bytes 221192 | tf_op jit(solution)/shard_map/ppermute | solution.py:73
  13.5 1.1 collective-permute-start.4
  15.3 9.6 %collective-permute-start.2 = (bf16[2,288,128]{2,1,0:T(8,128)(2,1)S(1)}, bf16[2,288,128]{2,1,0:T(8,128)(2,1)S(1)}, u32[]{:S(2)}, u32[]{:S(2)}) collective-permute-start(bf16[2,288,128]{2,1,0:T(8,128)(2,1)S(1)} %maximum_select_fusion.6), channel_id=1, source_target_pairs={{0,32},{8,40},{16,48},{24,56},{32,0},{40,8},{48,16},{56,24},{64,96... | collective-permute-start | bytes 442376 | tf_op jit(solution)/shard_map/ppermute | solution.py:73
  19.2 8.0 %collective-permute-start.10 = (bf16[2,32,2048]{2,1,0:T(8,128)(2,1)S(1)}, bf16[2,32,2048]{2,1,0:T(8,128)(2,1)S(1)}, u32[]{:S(2)}, u32[]{:S(2)}) collective-permute-start(bf16[2,32,2048]{2,1,0:T(8,128)(2,1)S(1)} %maximum_select_fusion.4), channel_id=1, source_target_pairs={{0,2},{1,3},{2,0},{3,1},{4,6},{5,7},{6,4},{7,5},{8,10},{9,11},{10,... | collective-permute-start | bytes 786440 | tf_op jit(solution)/shard_map/ppermute | solution.py:109
  24.9 8.5 %collective-permute-start.3 = (bf16[4,288,128]{2,1,0:T(8,128)(2,1)S(1)}, bf16[4,288,128]{2,1,0:T(8,128)(2,1)S(1)}, u32[]{:S(2)}, u32[]{:S(2)}) collective-permute-start(bf16[4,288,128]{2,1,0:T(8,128)(2,1)S(1)} %maximum_select_fusion.3), channel_id=1, source_target_pairs={{0,16},{8,24},{16,0},{24,8},{32,48},{40,56},{48,32},{56,40},{64,80... | collective-permute-start | bytes 884744 | tf_op jit(solution)/shard_map/ppermute | solution.py:73
  27.2 11.5 %collective-permute-start.11 = (bf16[4,32,2048]{2,1,0:T(8,128)(2,1)S(1)}, bf16[4,32,2048]{2,1,0:T(8,128)(2,1)S(1)}, u32[]{:S(2)}, u32[]{:S(2)}) collective-permute-start(bf16[4,32,2048]{2,1,0:T(8,128)(2,1)S(1)} %bitcast.102), channel_id=1, source_target_pairs={{0,1},{1,0},{2,3},{3,2},{4,5},{5,4},{6,7},{7,6},{8,9},{9,8},{10,11... | collective-permute-start | bytes 1572872 | tf_op jit(solution)/shard_map/ppermute | solution.py:109
  34.2 1.7 %collective-permute-start.5 = (bf16[4,288,128]{2,1,0:T(8,128)(2,1)S(1)}, bf16[4,288,128]{2,1,0:T(8,128)(2,1)S(1)}, u32[]{:S(2)}, u32[]{:S(2)}) collective-permute-start(bf16[4,288,128]{2,1,0:T(8,128)(2,1)S(1)} %select_select_fusion), channel_id=1, source_target_pairs={{0,8},{8,0},{16,24},{24,16},{32,40},{40,32},{48,56},{56,48},{64,72... | collective-permute-start | bytes 884744 | tf_op jit(solution)/shard_map/ppermute | solution.py:73
  36.0 6.0 %collective-permute-start.6 = (bf16[2,288,128]{2,1,0:T(8,128)(2,1)S(1)}, bf16[2,288,128]{2,1,0:T(8,128)(2,1)S(1)}, u32[]{:S(2)}, u32[]{:S(2)}) collective-permute-start(bf16[2,288,128]{2,1,0:T(8,128)(2,1)S(1)} %slice.142), channel_id=1, source_target_pairs={{0,128},{8,136},{16,144},{24,152},{32,160},{40,168},{48,176},{56,1... | collective-permute-start | bytes 442376 | tf_op jit(solution)/shard_map/ppermute | solution.py:73
  38.8 21.9 %copy-start.1 = (bf16[4,2,32,2048]{3,2,1,0:T(8,128)(2,1)}, bf16[4,2,32,2048]{3,2,1,0:T(8,128)(2,1)S(1)}, u32[]{:S(2)}) copy-start(bf16[4,2,32,2048]{3,2,1,0:T(8,128)(2,1)S(1)} %maximum_select_fusion) | copy-start | bytes 3145732
  61.0 0.6 copy-start.4
  63.0 6.8 %collective-permute-start.12 = (f32[2,288,128]{2,1,0:T(8,128)S(1)}, f32[2,288,128]{2,1,0:T(8,128)S(1)}, u32[]{:S(2)}, u32[]{:S(2)}) collective-permute-start(f32[2,288,128]{2,1,0:T(8,128)S(1)} %bitcast.99), channel_id=1, source_target_pairs={{0,128},{8,136},{16,144},{24,152},{32,160},{40,168},{48,176},{56,1... | collective-permute-start | bytes 884744 | tf_op jit(solution)/shard_map/ppermute | solution.py:73
  69.8 0.9 copy-start.3
  70.7 5.2 %collective-permute-start.13 = (f32[4,288,128]{2,1,0:T(8,128)}, f32[4,288,128]{2,1,0:T(8,128)}, u32[]{:S(2)}, u32[]{:S(2)}) collective-permute-start(f32[4,288,128]{2,1,0:T(8,128)} %pad_maximum_fusion.1), channel_id=1, source_target_pairs={{0,8},{8,0},{16,24},{24,16},{32,40},{40,32},{48,56},{56,48},{64,72... | collective-permute-start | bytes 1769480 | tf_op jit(solution)/shard_map/ppermute | solution.py:73
  74.2 1.6 %collective-permute-start.8 = (s32[4]{0:T(128)S(1)}, s32[4]{0:T(128)S(1)}, u32[]{:S(2)}, u32[]{:S(2)}) collective-permute-start(s32[4]{0:T(128)S(1)} %get-tuple-element.21), channel_id=1, source_target_pairs={{0,8},{8,0},{16,24},{24,16},{32,40},{40,32},{48,56},{56,48},{64,72... | collective-permute-start | bytes 56 | tf_op jit(solution)/shard_map/ppermute | solution.py:73
  78.3 15.6 %collective-permute-start.14 = (f32[4,288,128]{2,1,0:T(8,128)S(1)}, f32[4,288,128]{2,1,0:T(8,128)S(1)}, u32[]{:S(2)}, u32[]{:S(2)}) collective-permute-start(f32[4,288,128]{2,1,0:T(8,128)S(1)} %slice_select_fusion), channel_id=1, source_target_pairs={{0,16},{8,24},{16,0},{24,8},{32,48},{40,56},{48,32},{56,40},{64,80... | collective-permute-start | bytes 1769480 | tf_op jit(solution)/shard_map/ppermute | solution.py:73
  79.1 33.9 %collective-permute-start.7 = (f32[2,2,32,2048]{3,2,0,1:T(8,128)S(1)}, f32[2,2,32,2048]{3,2,0,1:T(8,128)S(1)}, u32[]{:S(2)}, u32[]{:S(2)}) collective-permute-start(f32[2,2,32,2048]{3,2,0,1:T(8,128)S(1)} %select_bitcast_fusion), channel_id=1, source_target_pairs={{0,1},{1,0},{2,3},{3,2},{4,5},{5,4},{6,7},{7,6},{8,9},{9,8},{10,11... | collective-permute-start | bytes 3145736 | tf_op jit(solution)/shard_map/ppermute | solution.py:130
  94.1 15.4 %collective-permute-start.15 = (f32[2,288,128]{2,1,0:T(8,128)S(1)}, f32[2,288,128]{2,1,0:T(8,128)S(1)}, u32[]{:S(2)}, u32[]{:S(2)}) collective-permute-start(f32[2,288,128]{2,1,0:T(8,128)S(1)} %slice_select_fusion.1), channel_id=1, source_target_pairs={{0,32},{8,40},{16,48},{24,56},{32,0},{40,8},{48,16},{56,24},{64,96... | collective-permute-start | bytes 884744 | tf_op jit(solution)/shard_map/ppermute | solution.py:73
  109.7 12.1 %collective-permute-start.16 = (f32[1,288,128]{2,1,0:T(8,128)S(1)}, f32[1,288,128]{2,1,0:T(8,128)S(1)}, u32[]{:S(2)}, u32[]{:S(2)}) collective-permute-start(f32[1,288,128]{2,1,0:T(8,128)S(1)} %slice_select_fusion.3), channel_id=1, source_target_pairs={{0,64},{8,72},{16,80},{24,88},{32,96},{40,104},{48,112},{56,120},{... | collective-permute-start | bytes 442376 | tf_op jit(solution)/shard_map/ppermute | solution.py:73
  113.2 12.1 %copy-start.5 = (bf16[2,128,32]{2,1,0:T(8,128)(2,1)S(1)}, bf16[2,128,32]{2,1,0:T(8,128)(2,1)}, u32[]{:S(2)}) copy-start(bf16[2,128,32]{2,1,0:T(8,128)(2,1)} %copy-done.4) | copy-start | bytes 49156
  121.8 15.6 %collective-permute-start.17 = (f32[2,32,2048]{2,1,0:T(8,128)S(1)}, f32[2,32,2048]{2,1,0:T(8,128)S(1)}, u32[]{:S(2)}, u32[]{:S(2)}) collective-permute-start(f32[2,32,2048]{2,1,0:T(8,128)S(1)} %select_bitcast_fusion.1), channel_id=1, source_target_pairs={{0,2},{1,3},{2,0},{3,1},{4,6},{5,7},{6,4},{7,5},{8,10},{9,11},{10,... | collective-permute-start | bytes 1572872 | tf_op jit(solution)/shard_map/ppermute | solution.py:130
  125.4 16.2 %copy-start.2 = (bf16[4,2,32,2048]{3,2,1,0:T(8,128)(2,1)S(1)}, bf16[4,2,32,2048]{3,2,1,0:T(8,128)(2,1)}, u32[]{:S(2)}) copy-start(bf16[4,2,32,2048]{3,2,1,0:T(8,128)(2,1)} %copy-done.1) | copy-start | bytes 3145732
  137.6 11.7 %collective-permute-start.18 = (f32[32,2048]{1,0:T(8,128)S(1)}, f32[32,2048]{1,0:T(8,128)S(1)}, u32[]{:S(2)}, u32[]{:S(2)}) collective-permute-start(f32[32,2048]{1,0:T(8,128)S(1)} %select_bitcast_fusion.2), channel_id=1, source_target_pairs={{0,4},{1,5},{2,6},{3,7},{4,0},{5,1},{6,2},{7,3},{8,12},{9,13},{10,... | collective-permute-start | bytes 786440 | tf_op jit(solution)/shard_map/ppermute | solution.py:130

commit v15 on v9

--- a/solution.py
+++ b/solution.py
@@ -205,7 +205,8 @@
         axis=2,
     )
     base, fac_b = lax.optimization_barrier((jnp.dot(tokens, weight, preferred_element_type=f32), fac_b))
-    base_out = reduce_scatter_tp(base)
+    half = base.shape[1] // 2
+    base_out = jnp.concatenate([reduce_scatter_tp(base[:, :half]), reduce_scatter_tp(base[:, half:])], axis=1)
 
     parts = jnp.stack([act_part, grad_part])
     flat_parts = parts.reshape(-1, 128)

time: 140 us -> 147 us (1.050)
  starting transfers between devices: 29.9 us -> 41.4 us
  waiting for transfers between devices: 63.8 us -> 52.3 us
  matrix products: 10.4 us -> 14.9 us
  other arithmetic: 8.17 us -> 9.89 us
    ppermute x3 -> x6, waiting for transfers between devices: 28.2 us -> 7.62 us  [reduce_scatter_tp(): held = keep + lax.ppermute(send, 'tp', [(i, i ^ bit) for i in range(count)])]
    ppermute x3 -> x6, starting transfers between devices: 7.63 us -> 17.4 us  [reduce_scatter_tp(): held = keep + lax.ppermute(send, 'tp', [(i, i ^ bit) for i in range(count)])]
    ppermute x13, waiting for transfers between devices: 33.4 us -> 42.4 us  [_swap(): return lax.ppermute(x, 'blk', [(i, i ^ bit) for i in range(count)])]
    dot_general x1, matrix products: 2.08 us -> 4.87 us  [on_device(): backward = jnp.dot(grad_rows, weight.T, preferred_element_type=f32)]
    ppermute x3, starting transfers between devices: 5.63 us -> 7.36 us  [gather_tp(): got = lax.ppermute(held, 'tp', [(i, i ^ bit) for i in range(count)])]
    slice x1 -> x2, local copies, waits for them, and re-layouts: 1.76 us -> 0.21 us  [reduce_scatter_tp(): high = lax.index_in_dim(held, 1, axis, keepdims=False)]
  transfers between devices with their start and end apart: 19 -> 22, of which waited for: 14 -> 16; matrix products, arithmetic and copies ran while one was open for 16% -> 15% of each run, Pallas kernels for 0% -> 0%
where the time goes in v15:
time: 147 us; the launch traced here: 146 us
  waiting for transfers between devices  52.3 us (36%)
  starting transfers between devices  41.4 us (28%)
  Pallas kernels  15.3 us (10%)
  matrix products  14.9 us (10%)
  local copies, waits for them, and re-layouts  11.4 us (8%)
  other arithmetic  9.89 us (7%)
    ppermute x13, waiting for transfers between devices, _swap(): return lax.ppermute(x, 'blk', [(i, i ^ bit) for i in range(count)])  42.4 us
    ppermute x6, starting transfers between devices, reduce_scatter_tp(): held = keep + lax.ppermute(send, 'tp', [(i, i ^ bit) for i in range(count)])  17.4 us
    ppermute x13, starting transfers between devices, _swap(): return lax.ppermute(x, 'blk', [(i, i ^ bit) for i in range(count)])  16.7 us
    pallas_call x1, Pallas kernels, gather_axis(): pl.pallas_call(functools.partial(_gather_kernel, axis, n), out_shape=jax....  15.3 us
    ppermute x6, waiting for transfers between devices, reduce_scatter_tp(): held = keep + lax.ppermute(send, 'tp', [(i, i ^ bit) for i in range(count)])  7.62 us
    ppermute x3, starting transfers between devices, gather_tp(): got = lax.ppermute(held, 'tp', [(i, i ^ bit) for i in range(count)])  7.36 us
    dot_general x1, matrix products, on_device(): backward = jnp.dot(grad_rows, weight.T, preferred_element_type=f32)  4.87 us
    dot_general x1, matrix products, on_device(): jnp.dot(tokens, weight, preferred_element_type=f32)  4.82 us
  transfers between devices with their start and end apart: 22, of which 16 were waited for; matrix products, arithmetic and copies ran while one was open for 15% of the time, Pallas kernels for 0%

profile of v15, /device:TPU:2, one launch (start us, length us, event | category | flops | bytes accessed | tf_op | source)
XLA Modules:
  0.0 146.3 jit_solution(12532538264201033720)
XLA Ops:
  2.6 7.2 %collective-permute-start.1 = (bf16[1,288,128]{2,1,0:T(8,128)(2,1)S(1)}, bf16[1,288,128]{2,1,0:T(8,128)(2,1)S(1)}, u32[]{:S(2)}, u32[]{:S(2)}) collective-permute-start(bf16[1,288,128]{2,1,0:T(8,128)(2,1)S(1)} %pad_maximum_fusion.3), channel_id=1, source_target_pairs={{0,64},{8,72},{16,80},{24,88},{32,96},{40,104},{48,112},{56,120},{... | collective-permute-start | bytes 221192 | tf_op jit(solution)/shard_map/ppermute | solution.py:73
  10.3 2.4 %collective-permute-start.13 = (bf16[1,32,2048]{2,1,0:T(8,128)(2,1)}, bf16[1,32,2048]{2,1,0:T(8,128)(2,1)S(1)}, u32[]{:S(2)}, u32[]{:S(2)}) collective-permute-start(bf16[1,32,2048]{2,1,0:T(8,128)(2,1)} %bitcast.123), channel_id=1, source_target_pairs={{0,4},{1,5},{2,6},{3,7},{4,0},{5,1},{6,2},{7,3},{8,12},{9,13},{10,... | collective-permute-start | bytes 393224 | tf_op jit(solution)/shard_map/ppermute | solution.py:109
  12.8 4.8 %fusion.34 = f32[256,2048]{1,0:T(8,128)} fusion(bf16[256,1024]{1,0:T(8,128)(2,1)S(1)} %copy-done, bf16[1024,2048]{1,0:T(8,128)(2,1)} %param.9), kind=kOutput, calls=%fused_computation.117 | convolution fusion | flops 1073741824 | bytes 6815744 | tf_op jit(solution)/shard_map/dot_general | solution.py:207
  19.3 1.6 %collective-permute-start.2 = (bf16[2,288,128]{2,1,0:T(8,128)(2,1)S(1)}, bf16[2,288,128]{2,1,0:T(8,128)(2,1)S(1)}, u32[]{:S(2)}, u32[]{:S(2)}) collective-permute-start(bf16[2,288,128]{2,1,0:T(8,128)(2,1)S(1)} %maximum_select_fusion.6), channel_id=1, source_target_pairs={{0,32},{8,40},{16,48},{24,56},{32,0},{40,8},{48,16},{56,24},{64,96... | collective-permute-start | bytes 442376 | tf_op jit(solution)/shard_map/ppermute | solution.py:73
  20.8 3.3 %collective-permute-start.14 = (bf16[2,32,2048]{2,1,0:T(8,128)(2,1)S(1)}, bf16[2,32,2048]{2,1,0:T(8,128)(2,1)S(1)}, u32[]{:S(2)}, u32[]{:S(2)}) collective-permute-start(bf16[2,32,2048]{2,1,0:T(8,128)(2,1)S(1)} %maximum_select_fusion.4), channel_id=1, source_target_pairs={{0,2},{1,3},{2,0},{3,1},{4,6},{5,7},{6,4},{7,5},{8,10},{9,11},{10,... | collective-permute-start | bytes 786440 | tf_op jit(solution)/shard_map/ppermute | solution.py:109
  24.1 5.3 %collective-permute-done.2 = bf16[2,288,128]{2,1,0:T(8,128)(2,1)S(1)} collective-permute-done((bf16[2,288,128]{2,1,0:T(8,128)(2,1)S(1)}, bf16[2,288,128]{2,1,0:T(8,128)(2,1)S(1)}, u32[]{:S(2)}, u32[]{:S(2)}) %collective-permute-start.2) | collective-permute-done | bytes 147488 | tf_op jit(solution)/shard_map/ppermute | solution.py:73
  30.7 1.7 %collective-permute-start.15 = (bf16[4,32,2048]{2,1,0:T(8,128)(2,1)S(1)}, bf16[4,32,2048]{2,1,0:T(8,128)(2,1)S(1)}, u32[]{:S(2)}, u32[]{:S(2)}) collective-permute-start(bf16[4,32,2048]{2,1,0:T(8,128)(2,1)S(1)} %bitcast.113), channel_id=1, source_target_pairs={{0,1},{1,0},{2,3},{3,2},{4,5},{5,4},{6,7},{7,6},{8,9},{9,8},{10,11... | collective-permute-start | bytes 1572872 | tf_op jit(solution)/shard_map/ppermute | solution.py:109
  32.4 5.7 %collective-permute-done.3 = bf16[4,288,128]{2,1,0:T(8,128)(2,1)S(1)} collective-permute-done((bf16[4,288,128]{2,1,0:T(8,128)(2,1)S(1)}, bf16[4,288,128]{2,1,0:T(8,128)(2,1)S(1)}, u32[]{:S(2)}, u32[]{:S(2)}) %collective-permute-start.3) | collective-permute-done | bytes 294944 | tf_op jit(solution)/shard_map/ppermute | solution.py:73
  40.7 1.9 %collective-permute-start.6 = (bf16[2,288,128]{2,1,0:T(8,128)(2,1)S(1)}, bf16[2,288,128]{2,1,0:T(8,128)(2,1)S(1)}, u32[]{:S(2)}, u32[]{:S(2)}) collective-permute-start(bf16[2,288,128]{2,1,0:T(8,128)(2,1)S(1)} %slice.174), channel_id=1, source_target_pairs={{0,128},{8,136},{16,144},{24,152},{32,160},{40,168},{48,176},{56,1... | collective-permute-start | bytes 442376 | tf_op jit(solution)/shard_map/ppermute | solution.py:73
  42.6 1.2 collective-permute-done.15
  43.9 2.9 %collective-permute-done.6 = bf16[2,288,128]{2,1,0:T(8,128)(2,1)S(1)} collective-permute-done((bf16[2,288,128]{2,1,0:T(8,128)(2,1)S(1)}, bf16[2,288,128]{2,1,0:T(8,128)(2,1)S(1)}, u32[]{:S(2)}, u32[]{:S(2)}) %collective-permute-start.6) | collective-permute-done | bytes 147488 | tf_op jit(solution)/shard_map/ppermute | solution.py:73
  48.8 15.3 %shard_map.93 = f32[8,192,128]{2,1,0:T(8,128)} custom-call(f32[192,128]{1,0:T(8,128)} %pad_maximum_fusion.2.x_ref), custom_call_target="tpu_custom_call" | custom-call | tf_op jit(solution)/shard_map/pallas_call | solution.py:58
  64.1 1.8 %slice.244 = bf16[8,64,128]{2,1,0:T(8,128)(2,1)} slice(f32[8,192,128]{2,1,0:T(8,128)} %shard_map.93), slice={[0:8], [128:192], [0:128]} | slice | bytes 262144 | tf_op jit(solution)/shard_map/slice | solution.py:218
  68.1 1.6 %fusion.6 = f32[2,16,128]{2,1,0:T(8,128)} fusion(bf16[2,128,32]{2,1,0:T(8,128)(2,1)S(1)} %convert_element_type.46, bf16[2,128,2048]{2,1,0:T(8,128)(2,1)} %bitcast.118, s32[]{:T(128)S(6)} %select_n.360), kind=kOutput, calls=%fused_computation.55 | convolution fusion | flops 1048576 | bytes 98308 | tf_op jit(solution)/shard_map/trk,trc->tkc/dot_general | solution.py:243
  69.9 1.3 convolution_multiply_fusion
  73.7 1.9 %collective-permute-start.7 = (f32[2,2,32,1024]{3,2,0,1:T(8,128)}, f32[2,2,32,1024]{3,2,0,1:T(8,128)}, u32[]{:S(2)}, u32[]{:S(2)}) collective-permute-start(f32[2,2,32,1024]{3,2,0,1:T(8,128)} %select_bitcast_fusion.1), channel_id=1, source_target_pairs={{0,1},{1,0},{2,3},{3,2},{4,5},{5,4},{6,7},{7,6},{8,9},{9,8},{10,11... | collective-permute-start | bytes 1572872 | tf_op jit(solution)/shard_map/ppermute | solution.py:130
  76.2 1.3 copy.47
  77.6 1.8 %reshape.373 = f32[2,32768]{1,0:T(2,128)S(1)} reshape(f32[2,1024,32]{2,1,0:T(8,128)} %copy.47) | data formatting | bytes 524288 | tf_op jit(solution)/shard_map/reshape | solution.py:249
  79.5 1.6 %collective-permute-start.17 = (f32[2,288,128]{2,1,0:T(8,128)S(1)}, f32[2,288,128]{2,1,0:T(8,128)S(1)}, u32[]{:S(2)}, u32[]{:S(2)}) collective-permute-start(f32[2,288,128]{2,1,0:T(8,128)S(1)} %bitcast.110), channel_id=1, source_target_pairs={{0,128},{8,136},{16,144},{24,152},{32,160},{40,168},{48,176},{56,1... | collective-permute-start | bytes 884744 | tf_op jit(solution)/shard_map/ppermute | solution.py:73
  81.1 4.9 %fusion.1 = bf16[256,1024]{1,0:T(8,128)(2,1)} fusion(f32[2,128,1024]{2,1,0:T(8,128)} %convolution_multiply_fusion, bf16[256,2048]{1,0:T(8,128)(2,1)} %bitcast.119, bf16[1024,2048]{1,0:T(8,128)(2,1)} %param.9), kind=kOutput, calls=%fused_computation.12 | convolution fusion | flops 1074266112 | bytes 6815744 | tf_op jit(solution)/shard_map/dot_general | solution.py:236
  86.5 1.4 collective-permute-done.10
  87.8 1.1 bitcast_add_fusion.1
  89.0 4.5 %collective-permute-start.11 = (f32[2,32,1024]{2,1,0:T(8,128)S(1)}, f32[2,32,1024]{2,1,0:T(8,128)S(1)}, u32[]{:S(2)}, u32[]{:S(2)}) collective-permute-start(f32[2,32,1024]{2,1,0:T(8,128)S(1)} %select_bitcast_fusion.2), channel_id=1, source_target_pairs={{0,2},{1,3},{2,0},{3,1},{4,6},{5,7},{6,4},{7,5},{8,10},{9,11},{10,... | collective-permute-start | bytes 786440 | tf_op jit(solution)/shard_map/ppermute | solution.py:130
  93.5 2.2 %collective-permute-done.7 = f32[2,2,32,1024]{3,2,0,1:T(8,128)} collective-permute-done((f32[2,2,32,1024]{3,2,0,1:T(8,128)}, f32[2,2,32,1024]{3,2,0,1:T(8,128)}, u32[]{:S(2)}, u32[]{:S(2)}) %collective-permute-start.7) | collective-permute-done | bytes 524320 | tf_op jit(solution)/shard_map/ppermute | solution.py:130
  95.7 1.1 bitcast_add_fusion.2
  96.9 7.9 %collective-permute-start.8 = (f32[2,32,1024]{2,1,0:T(8,128)S(1)}, f32[2,32,1024]{2,1,0:T(8,128)S(1)}, u32[]{:S(2)}, u32[]{:S(2)}) collective-permute-start(f32[2,32,1024]{2,1,0:T(8,128)S(1)} %select_bitcast_fusion.3), channel_id=1, source_target_pairs={{0,2},{1,3},{2,0},{3,1},{4,6},{5,7},{6,4},{7,5},{8,10},{9,11},{10,... | collective-permute-start | bytes 786440 | tf_op jit(solution)/shard_map/ppermute | solution.py:130
  104.8 3.3 %collective-permute-done.11 = f32[2,32,1024]{2,1,0:T(8,128)S(1)} collective-permute-done((f32[2,32,1024]{2,1,0:T(8,128)S(1)}, f32[2,32,1024]{2,1,0:T(8,128)S(1)}, u32[]{:S(2)}, u32[]{:S(2)}) %collective-permute-start.11) | collective-permute-done | bytes 262176 | tf_op jit(solution)/shard_map/ppermute | solution.py:130
  111.0 2.6 %collective-permute-start.9 = (f32[32,1024]{1,0:T(8,128)S(1)}, f32[32,1024]{1,0:T(8,128)S(1)}, u32[]{:S(2)}, u32[]{:S(2)}) collective-permute-start(f32[32,1024]{1,0:T(8,128)S(1)} %select_bitcast_fusion.5), channel_id=1, source_target_pairs={{0,4},{1,5},{2,6},{3,7},{4,0},{5,1},{6,2},{7,3},{8,12},{9,13},{10,... | collective-permute-start | bytes 393224 | tf_op jit(solution)/shard_map/ppermute | solution.py:130
  113.6 9.0 %collective-permute-done.19 = f32[4,288,128]{2,1,0:T(8,128)S(1)} collective-permute-done((f32[4,288,128]{2,1,0:T(8,128)S(1)}, f32[4,288,128]{2,1,0:T(8,128)S(1)}, u32[]{:S(2)}, u32[]{:S(2)}) %collective-permute-start.19) | collective-permute-done | bytes 589856 | tf_op jit(solution)/shard_map/ppermute | solution.py:73
  123.7 11.4 %collective-permute-done.20 = f32[2,288,128]{2,1,0:T(8,128)S(1)} collective-permute-done((f32[2,288,128]{2,1,0:T(8,128)S(1)}, f32[2,288,128]{2,1,0:T(8,128)S(1)}, u32[]{:S(2)}, u32[]{:S(2)}) %collective-permute-start.20) | collective-permute-done | bytes 294944 | tf_op jit(solution)/shard_map/ppermute | solution.py:73
  135.2 1.8 %collective-permute-start.21 = (f32[1,288,128]{2,1,0:T(8,128)S(1)}, f32[1,288,128]{2,1,0:T(8,128)S(1)}, u32[]{:S(2)}, u32[]{:S(2)}) collective-permute-start(f32[1,288,128]{2,1,0:T(8,128)S(1)} %slice_select_fusion.3), channel_id=1, source_target_pairs={{0,64},{8,72},{16,80},{24,88},{32,96},{40,104},{48,112},{56,120},{... | collective-permute-start | bytes 442376 | tf_op jit(solution)/shard_map/ppermute | solution.py:73
  137.7 6.6 %collective-permute-done.21 = f32[1,288,128]{2,1,0:T(8,128)S(1)} collective-permute-done((f32[1,288,128]{2,1,0:T(8,128)S(1)}, f32[1,288,128]{2,1,0:T(8,128)S(1)}, u32[]{:S(2)}, u32[]{:S(2)}) %collective-permute-start.21) | collective-permute-done | bytes 147488 | tf_op jit(solution)/shard_map/ppermute | solution.py:73
  (116 shorter events, 22.7 us)
Async XLA Ops:
  0.6 12.1 %copy-start = (bf16[256,1024]{1,0:T(8,128)(2,1)S(1)}, bf16[256,1024]{1,0:T(8,128)(2,1)}, u32[]{:S(2)}) copy-start(bf16[256,1024]{1,0:T(8,128)(2,1)} %param.8) | copy-start | bytes 1572868
  2.6 16.6 %collective-permute-start.1 = (bf16[1,288,128]{2,1,0:T(8,128)(2,1)S(1)}, bf16[1,288,128]{2,1,0:T(8,128)(2,1)S(1)}, u32[]{:S(2)}, u32[]{:S(2)}) collective-permute-start(bf16[1,288,128]{2,1,0:T(8,128)(2,1)S(1)} %pad_maximum_fusion.3), channel_id=1, source_target_pairs={{0,64},{8,72},{16,80},{24,88},{32,96},{40,104},{48,112},{56,120},{... | collective-permute-start | bytes 221192 | tf_op jit(solution)/shard_map/ppermute | solution.py:73
  9.8 7.8 %collective-permute-start = (s32[2]{0:T(128)}, s32[2]{0:T(128)S(1)}, u32[]{:S(2)}, u32[]{:S(2)}) collective-permute-start(s32[2]{0:T(128)} %bitcast.133), channel_id=1, source_target_pairs={{0,128},{8,136},{16,144},{24,152},{32,160},{40,168},{48,176},{56,1... | collective-permute-start | bytes 32 | tf_op jit(solution)/shard_map/ppermute | solution.py:73
  10.3 10.5 %collective-permute-start.13 = (bf16[1,32,2048]{2,1,0:T(8,128)(2,1)}, bf16[1,32,2048]{2,1,0:T(8,128)(2,1)S(1)}, u32[]{:S(2)}, u32[]{:S(2)}) collective-permute-start(bf16[1,32,2048]{2,1,0:T(8,128)(2,1)} %bitcast.123), channel_id=1, source_target_pairs={{0,4},{1,5},{2,6},{3,7},{4,0},{5,1},{6,2},{7,3},{8,12},{9,13},{10,... | collective-permute-start | bytes 393224 | tf_op jit(solution)/shard_map/ppermute | solution.py:109
  12.8 4.8 %copy-start.7 = (s32[2,1]{0,1:T(1,128)S(1)}, s32[2,1]{0,1:T(1,128)}, u32[]{:S(2)}) copy-start(s32[2,1]{0,1:T(1,128)} %param.12) | copy-start | bytes 28
  12.8 8.1 %copy-start.3 = (bf16[32,2048]{1,0:T(8,128)(2,1)S(1)}, bf16[32,2048]{1,0:T(8,128)(2,1)}, u32[]{:S(2)}) copy-start(bf16[32,2048]{1,0:T(8,128)(2,1)} %param.13) | copy-start | bytes 393220
  17.7 1.1 collective-permute-start.4
  17.7 1.4 collective-permute-start.16
  19.3 10.2 %collective-permute-start.2 = (bf16[2,288,128]{2,1,0:T(8,128)(2,1)S(1)}, bf16[2,288,128]{2,1,0:T(8,128)(2,1)S(1)}, u32[]{:S(2)}, u32[]{:S(2)}) collective-permute-start(bf16[2,288,128]{2,1,0:T(8,128)(2,1)S(1)} %maximum_select_fusion.6), channel_id=1, source_target_pairs={{0,32},{8,40},{16,48},{24,56},{32,0},{40,8},{48,16},{56,24},{64,96... | collective-permute-start | bytes 442376 | tf_op jit(solution)/shard_map/ppermute | solution.py:73
  20.8 9.8 %collective-permute-start.14 = (bf16[2,32,2048]{2,1,0:T(8,128)(2,1)S(1)}, bf16[2,32,2048]{2,1,0:T(8,128)(2,1)S(1)}, u32[]{:S(2)}, u32[]{:S(2)}) collective-permute-start(bf16[2,32,2048]{2,1,0:T(8,128)(2,1)S(1)} %maximum_select_fusion.4), channel_id=1, source_target_pairs={{0,2},{1,3},{2,0},{3,1},{4,6},{5,7},{6,4},{7,5},{8,10},{9,11},{10,... | collective-permute-start | bytes 786440 | tf_op jit(solution)/shard_map/ppermute | solution.py:109
  29.5 8.6 %collective-permute-start.3 = (bf16[4,288,128]{2,1,0:T(8,128)(2,1)S(1)}, bf16[4,288,128]{2,1,0:T(8,128)(2,1)S(1)}, u32[]{:S(2)}, u32[]{:S(2)}) collective-permute-start(bf16[4,288,128]{2,1,0:T(8,128)(2,1)S(1)} %maximum_select_fusion.3), channel_id=1, source_target_pairs={{0,16},{8,24},{16,0},{24,8},{32,48},{40,56},{48,32},{56,40},{64,80... | collective-permute-start | bytes 884744 | tf_op jit(solution)/shard_map/ppermute | solution.py:73
  30.7 13.1 %collective-permute-start.15 = (bf16[4,32,2048]{2,1,0:T(8,128)(2,1)S(1)}, bf16[4,32,2048]{2,1,0:T(8,128)(2,1)S(1)}, u32[]{:S(2)}, u32[]{:S(2)}) collective-permute-start(bf16[4,32,2048]{2,1,0:T(8,128)(2,1)S(1)} %bitcast.113), channel_id=1, source_target_pairs={{0,1},{1,0},{2,3},{3,2},{4,5},{5,4},{6,7},{7,6},{8,9},{9,8},{10,11... | collective-permute-start | bytes 1572872 | tf_op jit(solution)/shard_map/ppermute | solution.py:109
  38.9 1.7 %collective-permute-start.5 = (bf16[4,288,128]{2,1,0:T(8,128)(2,1)S(1)}, bf16[4,288,128]{2,1,0:T(8,128)(2,1)S(1)}, u32[]{:S(2)}, u32[]{:S(2)}) collective-permute-start(bf16[4,288,128]{2,1,0:T(8,128)(2,1)S(1)} %select_select_fusion), channel_id=1, source_target_pairs={{0,8},{8,0},{16,24},{24,16},{32,40},{40,32},{48,56},{56,48},{64,72... | collective-permute-start | bytes 884744 | tf_op jit(solution)/shard_map/ppermute | solution.py:73
  40.7 6.1 %collective-permute-start.6 = (bf16[2,288,128]{2,1,0:T(8,128)(2,1)S(1)}, bf16[2,288,128]{2,1,0:T(8,128)(2,1)S(1)}, u32[]{:S(2)}, u32[]{:S(2)}) collective-permute-start(bf16[2,288,128]{2,1,0:T(8,128)(2,1)S(1)} %slice.174), channel_id=1, source_target_pairs={{0,128},{8,136},{16,144},{24,152},{32,160},{40,168},{48,176},{56,1... | collective-permute-start | bytes 442376 | tf_op jit(solution)/shard_map/ppermute | solution.py:73
  43.9 3.2 %copy-start.2 = (bf16[4,2,32,2048]{3,2,1,0:T(8,128)(2,1)}, bf16[4,2,32,2048]{3,2,1,0:T(8,128)(2,1)S(1)}, u32[]{:S(2)}) copy-start(bf16[4,2,32,2048]{3,2,1,0:T(8,128)(2,1)S(1)} %maximum_select_fusion) | copy-start | bytes 3145732
  64.1 7.3 %copy-start.1 = (f32[256,2048]{1,0:T(8,128)S(1)}, f32[256,2048]{1,0:T(8,128)}, u32[]{:S(2)}) copy-start(f32[256,2048]{1,0:T(8,128)} %fusion.34) | copy-start | bytes 6291460
  72.6 3.0 %copy-start.4 = (bf16[8,64,128]{2,1,0:T(8,128)(2,1)S(1)}, bf16[8,64,128]{2,1,0:T(8,128)(2,1)}, u32[]{:S(2)}) copy-start(bf16[8,64,128]{2,1,0:T(8,128)(2,1)} %slice.244) | copy-start | bytes 393220
  72.6 15.2 %collective-permute-start.10 = (f32[2,2,32,1024]{3,2,0,1:T(8,128)}, f32[2,2,32,1024]{3,2,0,1:T(8,128)}, u32[]{:S(2)}, u32[]{:S(2)}) collective-permute-start(f32[2,2,32,1024]{3,2,0,1:T(8,128)} %select_bitcast_fusion), channel_id=1, source_target_pairs={{0,1},{1,0},{2,3},{3,2},{4,5},{5,4},{6,7},{7,6},{8,9},{9,8},{10,11... | collective-permute-start | bytes 1572872 | tf_op jit(solution)/shard_map/ppermute | solution.py:130
  72.8 3.4 %copy-start.5 = (f32[2,16,128]{2,1,0:T(8,128)S(1)}, f32[2,16,128]{2,1,0:T(8,128)}, u32[]{:S(2)}) copy-start(f32[2,16,128]{2,1,0:T(8,128)} %fusion.6) | copy-start | bytes 49156
  73.7 22.0 %collective-permute-start.7 = (f32[2,2,32,1024]{3,2,0,1:T(8,128)}, f32[2,2,32,1024]{3,2,0,1:T(8,128)}, u32[]{:S(2)}, u32[]{:S(2)}) collective-permute-start(f32[2,2,32,1024]{3,2,0,1:T(8,128)} %select_bitcast_fusion.1), channel_id=1, source_target_pairs={{0,1},{1,0},{2,3},{3,2},{4,5},{5,4},{6,7},{7,6},{8,9},{9,8},{10,11... | collective-permute-start | bytes 1572872 | tf_op jit(solution)/shard_map/ppermute | solution.py:130
  79.5 6.8 %collective-permute-start.17 = (f32[2,288,128]{2,1,0:T(8,128)S(1)}, f32[2,288,128]{2,1,0:T(8,128)S(1)}, u32[]{:S(2)}, u32[]{:S(2)}) collective-permute-start(f32[2,288,128]{2,1,0:T(8,128)S(1)} %bitcast.110), channel_id=1, source_target_pairs={{0,128},{8,136},{16,144},{24,152},{32,160},{40,168},{48,176},{56,1... | collective-permute-start | bytes 884744 | tf_op jit(solution)/shard_map/ppermute | solution.py:73
  86.4 21.8 %collective-permute-start.18 = (f32[4,288,128]{2,1,0:T(8,128)S(1)}, f32[4,288,128]{2,1,0:T(8,128)S(1)}, u32[]{:S(2)}, u32[]{:S(2)}) collective-permute-start(f32[4,288,128]{2,1,0:T(8,128)S(1)} %pad_maximum_fusion.1), channel_id=1, source_target_pairs={{0,8},{8,0},{16,24},{24,16},{32,40},{40,32},{48,56},{56,48},{64,72... | collective-permute-start | bytes 1769480 | tf_op jit(solution)/shard_map/ppermute | solution.py:73
  89.0 19.1 %collective-permute-start.11 = (f32[2,32,1024]{2,1,0:T(8,128)S(1)}, f32[2,32,1024]{2,1,0:T(8,128)S(1)}, u32[]{:S(2)}, u32[]{:S(2)}) collective-permute-start(f32[2,32,1024]{2,1,0:T(8,128)S(1)} %select_bitcast_fusion.2), channel_id=1, source_target_pairs={{0,2},{1,3},{2,0},{3,1},{4,6},{5,7},{6,4},{7,5},{8,10},{9,11},{10,... | collective-permute-start | bytes 786440 | tf_op jit(solution)/shard_map/ppermute | solution.py:130
  96.8 11.4 %copy-start.6 = (pred[8,8]{1,0:T(8,128)(4,1)S(1)}, pred[8,8]{1,0:T(8,128)(4,1)}, u32[]{:S(2)}) copy-start(pred[8,8]{1,0:T(8,128)(4,1)} %fusion.17) | copy-start | bytes 196
  96.9 14.0 %collective-permute-start.8 = (f32[2,32,1024]{2,1,0:T(8,128)S(1)}, f32[2,32,1024]{2,1,0:T(8,128)S(1)}, u32[]{:S(2)}, u32[]{:S(2)}) collective-permute-start(f32[2,32,1024]{2,1,0:T(8,128)S(1)} %select_bitcast_fusion.3), channel_id=1, source_target_pairs={{0,2},{1,3},{2,0},{3,1},{4,6},{5,7},{6,4},{7,5},{8,10},{9,11},{10,... | collective-permute-start | bytes 786440 | tf_op jit(solution)/shard_map/ppermute | solution.py:130
  109.5 13.1 %collective-permute-start.19 = (f32[4,288,128]{2,1,0:T(8,128)S(1)}, f32[4,288,128]{2,1,0:T(8,128)S(1)}, u32[]{:S(2)}, u32[]{:S(2)}) collective-permute-start(f32[4,288,128]{2,1,0:T(8,128)S(1)} %slice_select_fusion), channel_id=1, source_target_pairs={{0,16},{8,24},{16,0},{24,8},{32,48},{40,56},{48,32},{56,40},{64,80... | collective-permute-start | bytes 1769480 | tf_op jit(solution)/shard_map/ppermute | solution.py:73
  109.9 13.7 %collective-permute-start.12 = (f32[32,1024]{1,0:T(8,128)S(1)}, f32[32,1024]{1,0:T(8,128)S(1)}, u32[]{:S(2)}, u32[]{:S(2)}) collective-permute-start(f32[32,1024]{1,0:T(8,128)S(1)} %select_bitcast_fusion.4), channel_id=1, source_target_pairs={{0,4},{1,5},{2,6},{3,7},{4,0},{5,1},{6,2},{7,3},{8,12},{9,13},{10,... | collective-permute-start | bytes 393224 | tf_op jit(solution)/shard_map/ppermute | solution.py:130
  111.0 12.6 %collective-permute-start.9 = (f32[32,1024]{1,0:T(8,128)S(1)}, f32[32,1024]{1,0:T(8,128)S(1)}, u32[]{:S(2)}, u32[]{:S(2)}) collective-permute-start(f32[32,1024]{1,0:T(8,128)S(1)} %select_bitcast_fusion.5), channel_id=1, source_target_pairs={{0,4},{1,5},{2,6},{3,7},{4,0},{5,1},{6,2},{7,3},{8,12},{9,13},{10,... | collective-permute-start | bytes 393224 | tf_op jit(solution)/shard_map/ppermute | solution.py:130
  122.8 12.3 %collective-permute-start.20 = (f32[2,288,128]{2,1,0:T(8,128)S(1)}, f32[2,288,128]{2,1,0:T(8,128)S(1)}, u32[]{:S(2)}, u32[]{:S(2)}) collective-permute-start(f32[2,288,128]{2,1,0:T(8,128)S(1)} %slice_select_fusion.1), channel_id=1, source_target_pairs={{0,32},{8,40},{16,48},{24,56},{32,0},{40,8},{48,16},{56,24},{64,96... | collective-permute-start | bytes 884744 | tf_op jit(solution)/shard_map/ppermute | solution.py:73
  135.2 9.1 %collective-permute-start.21 = (f32[1,288,128]{2,1,0:T(8,128)S(1)}, f32[1,288,128]{2,1,0:T(8,128)S(1)}, u32[]{:S(2)}, u32[]{:S(2)}) collective-permute-start(f32[1,288,128]{2,1,0:T(8,128)S(1)} %slice_select_fusion.3), channel_id=1, source_target_pairs={{0,64},{8,72},{16,80},{24,88},{32,96},{40,104},{48,112},{56,120},{... | collective-permute-start | bytes 442376 | tf_op jit(solution)/shard_map/ppermute | solution.py:73

commit v16 on v9

--- a/solution.py
+++ b/solution.py
@@ -119,9 +119,12 @@
     me = lax.axis_index("tp")
     nbits = count.bit_length() - 1
     held = x.reshape((2,) * nbits + (x.shape[0] // count,) + x.shape[1:])
-    for k in range(nbits):
-        bit = 1 << k
-        axis = nbits - 1 - k
+    left = [1 << (nbits - 1 - k) for k in range(nbits)]
+    order = [1 << k for k in range(nbits)]
+    order[:2] = order[1::-1]
+    for bit in order:
+        axis = left.index(bit)
+        left.remove(bit)
         low = lax.index_in_dim(held, 0, axis, keepdims=False)
         high = lax.index_in_dim(held, 1, axis, keepdims=False)
         upper = (me & bit) != 0

time: 140 us -> 140 us (level)
  waiting for transfers between devices: 63.8 us -> 61.6 us
  starting transfers between devices: 29.9 us -> 31.5 us
    ppermute x13, waiting for transfers between devices: 33.4 us -> 31.8 us  [_swap(): return lax.ppermute(x, 'blk', [(i, i ^ bit) for i in range(count)])]
    ppermute x3, starting transfers between devices: 7.63 us -> 9.19 us  [reduce_scatter_tp(): held = keep + lax.ppermute(send, 'tp', [(i, i ^ bit) for i in range(count)])]
  transfers between devices with their start and end apart: 19 -> 19, of which waited for: 14 -> 13; matrix products, arithmetic and copies ran while one was open for 16% -> 16% of each run, Pallas kernels for 0% -> 0%
where the time goes in v16:
time: 140 us; the launch traced here: 138 us
  waiting for transfers between devices  61.6 us (44%)
  starting transfers between devices  31.5 us (22%)
  Pallas kernels  15.3 us (11%)
  matrix products  10.4 us (7%)
  local copies, waits for them, and re-layouts  10.3 us (7%)
  other arithmetic  8.17 us (6%)
    ppermute x13, waiting for transfers between devices, _swap(): return lax.ppermute(x, 'blk', [(i, i ^ bit) for i in range(count)])  31.8 us
    ppermute x3, waiting for transfers between devices, reduce_scatter_tp(): held = keep + lax.ppermute(send, 'tp', [(i, i ^ bit) for i in range(count)])  27.7 us
    ppermute x13, starting transfers between devices, _swap(): return lax.ppermute(x, 'blk', [(i, i ^ bit) for i in range(count)])  16.7 us
    pallas_call x1, Pallas kernels, gather_axis(): pl.pallas_call(functools.partial(_gather_kernel, axis, n), out_shape=jax....  15.3 us
    ppermute x3, starting transfers between devices, reduce_scatter_tp(): held = keep + lax.ppermute(send, 'tp', [(i, i ^ bit) for i in range(count)])  9.19 us
    ppermute x3, starting transfers between devices, gather_tp(): got = lax.ppermute(held, 'tp', [(i, i ^ bit) for i in range(count)])  5.63 us
    dot_general x1, matrix products, on_device(): jnp.dot(tokens, weight, preferred_element_type=f32)  4.8 us
  transfers between devices with their start and end apart: 19, of which 13 were waited for; matrix products, arithmetic and copies ran while one was open for 16% of the time, Pallas kernels for 0%

profile of v16, /device:TPU:2, one launch (start us, length us, event | category | flops | bytes accessed | tf_op | source)
XLA Modules:
  0.0 138.3 jit_solution(13661489377772976754)
XLA Ops:
  0.6 2.4 %collective-permute-start = (s32[2]{0:T(128)}, s32[2]{0:T(128)S(1)}, u32[]{:S(2)}, u32[]{:S(2)}) collective-permute-start(s32[2]{0:T(128)} %bitcast.123), channel_id=1, source_target_pairs={{0,128},{8,136},{16,144},{24,152},{32,160},{40,168},{48,176},{56,1... | collective-permute-start | bytes 32 | tf_op jit(solution)/shard_map/ppermute | solution.py:73
  3.7 1.0 copy.30
  5.6 7.2 %collective-permute-start.1 = (bf16[1,288,128]{2,1,0:T(8,128)(2,1)S(1)}, bf16[1,288,128]{2,1,0:T(8,128)(2,1)S(1)}, u32[]{:S(2)}, u32[]{:S(2)}) collective-permute-start(bf16[1,288,128]{2,1,0:T(8,128)(2,1)S(1)} %pad_maximum_fusion.3), channel_id=1, source_target_pairs={{0,64},{8,72},{16,80},{24,88},{32,96},{40,104},{48,112},{56,120},{... | collective-permute-start | bytes 221192 | tf_op jit(solution)/shard_map/ppermute | solution.py:73
  12.8 4.8 %fusion.33 = f32[256,2048]{1,0:T(8,128)} fusion(bf16[256,1024]{1,0:T(8,128)(2,1)S(1)} %copy-done, bf16[1024,2048]{1,0:T(8,128)(2,1)} %param.9), kind=kOutput, calls=%fused_computation.109 | convolution fusion | flops 1073741824 | bytes 6815744 | tf_op jit(solution)/shard_map/dot_general | solution.py:210
  18.9 1.6 %collective-permute-start.2 = (bf16[2,288,128]{2,1,0:T(8,128)(2,1)S(1)}, bf16[2,288,128]{2,1,0:T(8,128)(2,1)S(1)}, u32[]{:S(2)}, u32[]{:S(2)}) collective-permute-start(bf16[2,288,128]{2,1,0:T(8,128)(2,1)S(1)} %maximum_select_fusion.6), channel_id=1, source_target_pairs={{0,32},{8,40},{16,48},{24,56},{32,0},{40,8},{48,16},{56,24},{64,96... | collective-permute-start | bytes 442376 | tf_op jit(solution)/shard_map/ppermute | solution.py:73
  20.5 3.3 %collective-permute-start.11 = (bf16[2,32,2048]{2,1,0:T(8,128)(2,1)S(1)}, bf16[2,32,2048]{2,1,0:T(8,128)(2,1)S(1)}, u32[]{:S(2)}, u32[]{:S(2)}) collective-permute-start(bf16[2,32,2048]{2,1,0:T(8,128)(2,1)S(1)} %maximum_select_fusion.4), channel_id=1, source_target_pairs={{0,2},{1,3},{2,0},{3,1},{4,6},{5,7},{6,4},{7,5},{8,10},{9,11},{10,... | collective-permute-start | bytes 786440 | tf_op jit(solution)/shard_map/ppermute | solution.py:109
  23.8 5.2 %collective-permute-done.2 = bf16[2,288,128]{2,1,0:T(8,128)(2,1)S(1)} collective-permute-done((bf16[2,288,128]{2,1,0:T(8,128)(2,1)S(1)}, bf16[2,288,128]{2,1,0:T(8,128)(2,1)S(1)}, u32[]{:S(2)}, u32[]{:S(2)}) %collective-permute-start.2) | collective-permute-done | bytes 147488 | tf_op jit(solution)/shard_map/ppermute | solution.py:73
  29.2 1.0 collective-permute-done.11
  30.3 1.7 %collective-permute-start.12 = (bf16[4,32,2048]{2,1,0:T(8,128)(2,1)S(1)}, bf16[4,32,2048]{2,1,0:T(8,128)(2,1)S(1)}, u32[]{:S(2)}, u32[]{:S(2)}) collective-permute-start(bf16[4,32,2048]{2,1,0:T(8,128)(2,1)S(1)} %bitcast.102), channel_id=1, source_target_pairs={{0,1},{1,0},{2,3},{3,2},{4,5},{5,4},{6,7},{7,6},{8,9},{9,8},{10,11... | collective-permute-start | bytes 1572872 | tf_op jit(solution)/shard_map/ppermute | solution.py:109
  31.9 5.7 %collective-permute-done.3 = bf16[4,288,128]{2,1,0:T(8,128)(2,1)S(1)} collective-permute-done((bf16[4,288,128]{2,1,0:T(8,128)(2,1)S(1)}, bf16[4,288,128]{2,1,0:T(8,128)(2,1)S(1)}, u32[]{:S(2)}, u32[]{:S(2)}) %collective-permute-start.3) | collective-permute-done | bytes 294944 | tf_op jit(solution)/shard_map/ppermute | solution.py:73
  40.3 1.9 %collective-permute-start.6 = (bf16[2,288,128]{2,1,0:T(8,128)(2,1)S(1)}, bf16[2,288,128]{2,1,0:T(8,128)(2,1)S(1)}, u32[]{:S(2)}, u32[]{:S(2)}) collective-permute-start(bf16[2,288,128]{2,1,0:T(8,128)(2,1)S(1)} %slice.142), channel_id=1, source_target_pairs={{0,128},{8,136},{16,144},{24,152},{32,160},{40,168},{48,176},{56,1... | collective-permute-start | bytes 442376 | tf_op jit(solution)/shard_map/ppermute | solution.py:73
  42.2 1.1 collective-permute-done.12
  43.4 2.9 %collective-permute-done.6 = bf16[2,288,128]{2,1,0:T(8,128)(2,1)S(1)} collective-permute-done((bf16[2,288,128]{2,1,0:T(8,128)(2,1)S(1)}, bf16[2,288,128]{2,1,0:T(8,128)(2,1)S(1)}, u32[]{:S(2)}, u32[]{:S(2)}) %collective-permute-start.6) | collective-permute-done | bytes 147488 | tf_op jit(solution)/shard_map/ppermute | solution.py:73
  48.2 15.3 %shard_map.93 = f32[8,192,128]{2,1,0:T(8,128)} custom-call(f32[192,128]{1,0:T(8,128)} %pad_maximum_fusion.2.x_ref), custom_call_target="tpu_custom_call" | custom-call | tf_op jit(solution)/shard_map/pallas_call | solution.py:58
  63.5 1.1 slice_reduce_fusion
  66.6 1.6 %collective-permute-start.14 = (f32[2,288,128]{2,1,0:T(8,128)S(1)}, f32[2,288,128]{2,1,0:T(8,128)S(1)}, u32[]{:S(2)}, u32[]{:S(2)}) collective-permute-start(f32[2,288,128]{2,1,0:T(8,128)S(1)} %bitcast.99), channel_id=1, source_target_pairs={{0,128},{8,136},{16,144},{24,152},{32,160},{40,168},{48,176},{56,1... | collective-permute-start | bytes 884744 | tf_op jit(solution)/shard_map/ppermute | solution.py:73
  68.2 1.8 %fusion.31 = (f32[2,1,2,32,2048]{4,3,2,1,0:T(8,128)S(1)}, f32[2,1,2,32,2048]{4,3,2,1,0:T(8,128)S(1)}) fusion(f32[2,2,2,32,2048]{4,3,2,1,0:T(8,128)} %bitcast.104), kind=kLoop, calls=%fused_computation.107 | loop fusion | bytes 4194304 | tf_op jit(solution)/shard_map/slice | solution.py:129
  70.0 3.5 %collective-permute-done.14 = f32[2,288,128]{2,1,0:T(8,128)S(1)} collective-permute-done((f32[2,288,128]{2,1,0:T(8,128)S(1)}, f32[2,288,128]{2,1,0:T(8,128)S(1)}, u32[]{:S(2)}, u32[]{:S(2)}) %collective-permute-start.14) | collective-permute-done | bytes 294944 | tf_op jit(solution)/shard_map/ppermute | solution.py:73
  73.7 3.7 %collective-permute-start.7 = (f32[2,2,32,2048]{3,2,0,1:T(8,128)S(1)}, f32[2,2,32,2048]{3,2,0,1:T(8,128)S(1)}, u32[]{:S(2)}, u32[]{:S(2)}) collective-permute-start(f32[2,2,32,2048]{3,2,0,1:T(8,128)S(1)} %select_bitcast_fusion), channel_id=1, source_target_pairs={{0,2},{1,3},{2,0},{3,1},{4,6},{5,7},{6,4},{7,5},{8,10},{9,11},{10,... | collective-permute-start | bytes 3145736 | tf_op jit(solution)/shard_map/ppermute | solution.py:133
  77.9 1.1 select_reduce_fusion
  80.2 21.0 %collective-permute-done.7 = f32[2,2,32,2048]{3,2,0,1:T(8,128)S(1)} collective-permute-done((f32[2,2,32,2048]{3,2,0,1:T(8,128)S(1)}, f32[2,2,32,2048]{3,2,0,1:T(8,128)S(1)}, u32[]{:S(2)}, u32[]{:S(2)}) %collective-permute-start.7) | collective-permute-done | bytes 1048608 | tf_op jit(solution)/shard_map/ppermute | solution.py:133
  102.2 2.4 %collective-permute-start.8 = (f32[2,32,2048]{2,1,0:T(8,128)}, f32[2,32,2048]{2,1,0:T(8,128)}, u32[]{:S(2)}, u32[]{:S(2)}) collective-permute-start(f32[2,32,2048]{2,1,0:T(8,128)} %select_bitcast_fusion.1), channel_id=1, source_target_pairs={{0,1},{1,0},{2,3},{3,2},{4,5},{5,4},{6,7},{7,6},{8,9},{9,8},{10,11... | collective-permute-start | bytes 1572872 | tf_op jit(solution)/shard_map/ppermute | solution.py:133
  104.7 2.1 %fusion.1 = bf16[256,1024]{1,0:T(8,128)(2,1)} fusion(f32[2,128,1024]{2,1,0:T(8,128)S(1)} %convolution_multiply_fusion, bf16[256,2048]{1,0:T(8,128)(2,1)S(1)} %bitcast.109, bf16[1024,2048]{1,0:T(8,128)(2,1)S(1)} %copy-done.5), kind=kOutput, calls=%fused_computation.12 | convolution fusion | flops 1074266112 | bytes 6815744 | tf_op jit(solution)/shard_map/dot_general | solution.py:238
  106.8 1.0 slice.198
  108.5 0.9 convolution_bitcast_fusion.1
  109.4 1.0 convolution_bitcast_fusion
  111.4 5.6 %collective-permute-done.8 = f32[2,32,2048]{2,1,0:T(8,128)} collective-permute-done((f32[2,32,2048]{2,1,0:T(8,128)}, f32[2,32,2048]{2,1,0:T(8,128)}, u32[]{:S(2)}, u32[]{:S(2)}) %collective-permute-start.8) | collective-permute-done | bytes 524320 | tf_op jit(solution)/shard_map/ppermute | solution.py:133
  117.0 1.1 bitcast_add_fusion.2
  118.2 3.1 %collective-permute-start.9 = (f32[32,2048]{1,0:T(8,128)S(1)}, f32[32,2048]{1,0:T(8,128)S(1)}, u32[]{:S(2)}, u32[]{:S(2)}) collective-permute-start(f32[32,2048]{1,0:T(8,128)S(1)} %select_bitcast_fusion.2), channel_id=1, source_target_pairs={{0,4},{1,5},{2,6},{3,7},{4,0},{5,1},{6,2},{7,3},{8,12},{9,13},{10,... | collective-permute-start | bytes 786440 | tf_op jit(solution)/shard_map/ppermute | solution.py:133
  121.2 4.9 %collective-permute-done.17 = f32[2,288,128]{2,1,0:T(8,128)S(1)} collective-permute-done((f32[2,288,128]{2,1,0:T(8,128)S(1)}, f32[2,288,128]{2,1,0:T(8,128)S(1)}, u32[]{:S(2)}, u32[]{:S(2)}) %collective-permute-start.17) | collective-permute-done | bytes 294944 | tf_op jit(solution)/shard_map/ppermute | solution.py:73
  126.3 1.0 collective-permute-done.9
  128.1 8.2 %collective-permute-done.18 = f32[1,288,128]{2,1,0:T(8,128)S(1)} collective-permute-done((f32[1,288,128]{2,1,0:T(8,128)S(1)}, f32[1,288,128]{2,1,0:T(8,128)S(1)}, u32[]{:S(2)}, u32[]{:S(2)}) %collective-permute-start.18) | collective-permute-done | bytes 147488 | tf_op jit(solution)/shard_map/ppermute | solution.py:73
  (97 shorter events, 17.1 us)
Async XLA Ops:
  0.6 12.2 %copy-start = (bf16[256,1024]{1,0:T(8,128)(2,1)S(1)}, bf16[256,1024]{1,0:T(8,128)(2,1)}, u32[]{:S(2)}) copy-start(bf16[256,1024]{1,0:T(8,128)(2,1)} %param.8) | copy-start | bytes 1572868
  0.6 17.0 %collective-permute-start = (s32[2]{0:T(128)}, s32[2]{0:T(128)S(1)}, u32[]{:S(2)}, u32[]{:S(2)}) collective-permute-start(s32[2]{0:T(128)} %bitcast.123), channel_id=1, source_target_pairs={{0,128},{8,136},{16,144},{24,152},{32,160},{40,168},{48,176},{56,1... | collective-permute-start | bytes 32 | tf_op jit(solution)/shard_map/ppermute | solution.py:73
  3.0 17.5 %collective-permute-start.10 = (bf16[1,32,2048]{2,1,0:T(8,128)(2,1)}, bf16[1,32,2048]{2,1,0:T(8,128)(2,1)S(1)}, u32[]{:S(2)}, u32[]{:S(2)}) collective-permute-start(bf16[1,32,2048]{2,1,0:T(8,128)(2,1)} %bitcast.113), channel_id=1, source_target_pairs={{0,4},{1,5},{2,6},{3,7},{4,0},{5,1},{6,2},{7,3},{8,12},{9,13},{10,... | collective-permute-start | bytes 393224 | tf_op jit(solution)/shard_map/ppermute | solution.py:109
  5.6 13.3 %collective-permute-start.1 = (bf16[1,288,128]{2,1,0:T(8,128)(2,1)S(1)}, bf16[1,288,128]{2,1,0:T(8,128)(2,1)S(1)}, u32[]{:S(2)}, u32[]{:S(2)}) collective-permute-start(bf16[1,288,128]{2,1,0:T(8,128)(2,1)S(1)} %pad_maximum_fusion.3), channel_id=1, source_target_pairs={{0,64},{8,72},{16,80},{24,88},{32,96},{40,104},{48,112},{56,120},{... | collective-permute-start | bytes 221192 | tf_op jit(solution)/shard_map/ppermute | solution.py:73
  12.8 4.8 %copy-start.4 = (s32[2,1]{0,1:T(1,128)S(1)}, s32[2,1]{0,1:T(1,128)}, u32[]{:S(2)}) copy-start(s32[2,1]{0,1:T(1,128)} %param.12) | copy-start | bytes 28
  12.8 7.7 %copy-start.3 = (bf16[32,2048]{1,0:T(8,128)(2,1)S(1)}, bf16[32,2048]{1,0:T(8,128)(2,1)}, u32[]{:S(2)}) copy-start(bf16[32,2048]{1,0:T(8,128)(2,1)} %param.13) | copy-start | bytes 393220
  17.7 1.1 collective-permute-start.4
  17.8 20.8 %collective-permute-start.13 = (s32[4]{0:T(128)S(1)}, s32[4]{0:T(128)S(1)}, u32[]{:S(2)}, u32[]{:S(2)}) collective-permute-start(s32[4]{0:T(128)S(1)} %get-tuple-element.19), channel_id=1, source_target_pairs={{0,8},{8,0},{16,24},{24,16},{32,40},{40,32},{48,56},{56,48},{64,72... | collective-permute-start | bytes 56 | tf_op jit(solution)/shard_map/ppermute | solution.py:73
  18.9 10.1 %collective-permute-start.2 = (bf16[2,288,128]{2,1,0:T(8,128)(2,1)S(1)}, bf16[2,288,128]{2,1,0:T(8,128)(2,1)S(1)}, u32[]{:S(2)}, u32[]{:S(2)}) collective-permute-start(bf16[2,288,128]{2,1,0:T(8,128)(2,1)S(1)} %maximum_select_fusion.6), channel_id=1, source_target_pairs={{0,32},{8,40},{16,48},{24,56},{32,0},{40,8},{48,16},{56,24},{64,96... | collective-permute-start | bytes 442376 | tf_op jit(solution)/shard_map/ppermute | solution.py:73
  20.5 9.7 %collective-permute-start.11 = (bf16[2,32,2048]{2,1,0:T(8,128)(2,1)S(1)}, bf16[2,32,2048]{2,1,0:T(8,128)(2,1)S(1)}, u32[]{:S(2)}, u32[]{:S(2)}) collective-permute-start(bf16[2,32,2048]{2,1,0:T(8,128)(2,1)S(1)} %maximum_select_fusion.4), channel_id=1, source_target_pairs={{0,2},{1,3},{2,0},{3,1},{4,6},{5,7},{6,4},{7,5},{8,10},{9,11},{10,... | collective-permute-start | bytes 786440 | tf_op jit(solution)/shard_map/ppermute | solution.py:109
  29.0 8.6 %collective-permute-start.3 = (bf16[4,288,128]{2,1,0:T(8,128)(2,1)S(1)}, bf16[4,288,128]{2,1,0:T(8,128)(2,1)S(1)}, u32[]{:S(2)}, u32[]{:S(2)}) collective-permute-start(bf16[4,288,128]{2,1,0:T(8,128)(2,1)S(1)} %maximum_select_fusion.3), channel_id=1, source_target_pairs={{0,16},{8,24},{16,0},{24,8},{32,48},{40,56},{48,32},{56,40},{64,80... | collective-permute-start | bytes 884744 | tf_op jit(solution)/shard_map/ppermute | solution.py:73
  30.3 13.0 %collective-permute-start.12 = (bf16[4,32,2048]{2,1,0:T(8,128)(2,1)S(1)}, bf16[4,32,2048]{2,1,0:T(8,128)(2,1)S(1)}, u32[]{:S(2)}, u32[]{:S(2)}) collective-permute-start(bf16[4,32,2048]{2,1,0:T(8,128)(2,1)S(1)} %bitcast.102), channel_id=1, source_target_pairs={{0,1},{1,0},{2,3},{3,2},{4,5},{5,4},{6,7},{7,6},{8,9},{9,8},{10,11... | collective-permute-start | bytes 1572872 | tf_op jit(solution)/shard_map/ppermute | solution.py:109
  38.5 1.7 %collective-permute-start.5 = (bf16[4,288,128]{2,1,0:T(8,128)(2,1)S(1)}, bf16[4,288,128]{2,1,0:T(8,128)(2,1)S(1)}, u32[]{:S(2)}, u32[]{:S(2)}) collective-permute-start(bf16[4,288,128]{2,1,0:T(8,128)(2,1)S(1)} %select_select_fusion), channel_id=1, source_target_pairs={{0,8},{8,0},{16,24},{24,16},{32,40},{40,32},{48,56},{56,48},{64,72... | collective-permute-start | bytes 884744 | tf_op jit(solution)/shard_map/ppermute | solution.py:73
  40.3 6.0 %collective-permute-start.6 = (bf16[2,288,128]{2,1,0:T(8,128)(2,1)S(1)}, bf16[2,288,128]{2,1,0:T(8,128)(2,1)S(1)}, u32[]{:S(2)}, u32[]{:S(2)}) collective-permute-start(bf16[2,288,128]{2,1,0:T(8,128)(2,1)S(1)} %slice.142), channel_id=1, source_target_pairs={{0,128},{8,136},{16,144},{24,152},{32,160},{40,168},{48,176},{56,1... | collective-permute-start | bytes 442376 | tf_op jit(solution)/shard_map/ppermute | solution.py:73
  43.4 21.5 %copy-start.1 = (bf16[4,2,32,2048]{3,2,1,0:T(8,128)(2,1)}, bf16[4,2,32,2048]{3,2,1,0:T(8,128)(2,1)S(1)}, u32[]{:S(2)}) copy-start(bf16[4,2,32,2048]{3,2,1,0:T(8,128)(2,1)S(1)} %maximum_select_fusion) | copy-start | bytes 3145732
  66.6 6.8 %collective-permute-start.14 = (f32[2,288,128]{2,1,0:T(8,128)S(1)}, f32[2,288,128]{2,1,0:T(8,128)S(1)}, u32[]{:S(2)}, u32[]{:S(2)}) collective-permute-start(f32[2,288,128]{2,1,0:T(8,128)S(1)} %bitcast.99), channel_id=1, source_target_pairs={{0,128},{8,136},{16,144},{24,152},{32,160},{40,168},{48,176},{56,1... | collective-permute-start | bytes 884744 | tf_op jit(solution)/shard_map/ppermute | solution.py:73
  73.5 4.3 %collective-permute-start.15 = (f32[4,288,128]{2,1,0:T(8,128)S(1)}, f32[4,288,128]{2,1,0:T(8,128)S(1)}, u32[]{:S(2)}, u32[]{:S(2)}) collective-permute-start(f32[4,288,128]{2,1,0:T(8,128)S(1)} %pad_maximum_fusion.1), channel_id=1, source_target_pairs={{0,8},{8,0},{16,24},{24,16},{32,40},{40,32},{48,56},{56,48},{64,72... | collective-permute-start | bytes 1769480 | tf_op jit(solution)/shard_map/ppermute | solution.py:73
  73.7 27.5 %collective-permute-start.7 = (f32[2,2,32,2048]{3,2,0,1:T(8,128)S(1)}, f32[2,2,32,2048]{3,2,0,1:T(8,128)S(1)}, u32[]{:S(2)}, u32[]{:S(2)}) collective-permute-start(f32[2,2,32,2048]{3,2,0,1:T(8,128)S(1)} %select_bitcast_fusion), channel_id=1, source_target_pairs={{0,2},{1,3},{2,0},{3,1},{4,6},{5,7},{6,4},{7,5},{8,10},{9,11},{10,... | collective-permute-start | bytes 3145736 | tf_op jit(solution)/shard_map/ppermute | solution.py:133
  79.9 24.8 %copy-start.2 = (bf16[4,2,32,2048]{3,2,1,0:T(8,128)(2,1)S(1)}, bf16[4,2,32,2048]{3,2,1,0:T(8,128)(2,1)}, u32[]{:S(2)}) copy-start(bf16[4,2,32,2048]{3,2,1,0:T(8,128)(2,1)} %copy-done.1) | copy-start | bytes 3145732
  79.9 24.8 %copy-start.5 = (bf16[1024,2048]{1,0:T(8,128)(2,1)S(1)}, bf16[1024,2048]{1,0:T(8,128)(2,1)}, u32[]{:S(2)}) copy-start(bf16[1024,2048]{1,0:T(8,128)(2,1)} %param.9) | copy-start | bytes 12582916
  79.9 30.5 %collective-permute-start.16 = (f32[4,288,128]{2,1,0:T(8,128)}, f32[4,288,128]{2,1,0:T(8,128)S(1)}, u32[]{:S(2)}, u32[]{:S(2)}) collective-permute-start(f32[4,288,128]{2,1,0:T(8,128)} %slice_select_fusion), channel_id=1, source_target_pairs={{0,16},{8,24},{16,0},{24,8},{32,48},{40,56},{48,32},{56,40},{64,80... | collective-permute-start | bytes 1769480 | tf_op jit(solution)/shard_map/ppermute | solution.py:73
  102.2 14.7 %collective-permute-start.8 = (f32[2,32,2048]{2,1,0:T(8,128)}, f32[2,32,2048]{2,1,0:T(8,128)}, u32[]{:S(2)}, u32[]{:S(2)}) collective-permute-start(f32[2,32,2048]{2,1,0:T(8,128)} %select_bitcast_fusion.1), channel_id=1, source_target_pairs={{0,1},{1,0},{2,3},{3,2},{4,5},{5,4},{6,7},{7,6},{8,9},{9,8},{10,11... | collective-permute-start | bytes 1572872 | tf_op jit(solution)/shard_map/ppermute | solution.py:133
  110.5 15.6 %collective-permute-start.17 = (f32[2,288,128]{2,1,0:T(8,128)S(1)}, f32[2,288,128]{2,1,0:T(8,128)S(1)}, u32[]{:S(2)}, u32[]{:S(2)}) collective-permute-start(f32[2,288,128]{2,1,0:T(8,128)S(1)} %slice_select_fusion.1), channel_id=1, source_target_pairs={{0,32},{8,40},{16,48},{24,56},{32,0},{40,8},{48,16},{56,24},{64,96... | collective-permute-start | bytes 884744 | tf_op jit(solution)/shard_map/ppermute | solution.py:73
  118.2 9.2 %collective-permute-start.9 = (f32[32,2048]{1,0:T(8,128)S(1)}, f32[32,2048]{1,0:T(8,128)S(1)}, u32[]{:S(2)}, u32[]{:S(2)}) collective-permute-start(f32[32,2048]{1,0:T(8,128)S(1)} %select_bitcast_fusion.2), channel_id=1, source_target_pairs={{0,4},{1,5},{2,6},{3,7},{4,0},{5,1},{6,2},{7,3},{8,12},{9,13},{10,... | collective-permute-start | bytes 786440 | tf_op jit(solution)/shard_map/ppermute | solution.py:133
  126.2 10.1 %collective-permute-start.18 = (f32[1,288,128]{2,1,0:T(8,128)S(1)}, f32[1,288,128]{2,1,0:T(8,128)S(1)}, u32[]{:S(2)}, u32[]{:S(2)}) collective-permute-start(f32[1,288,128]{2,1,0:T(8,128)S(1)} %slice_select_fusion.3), channel_id=1, source_target_pairs={{0,64},{8,72},{16,80},{24,88},{32,96},{40,104},{48,112},{56,120},{... | collective-permute-start | bytes 442376 | tf_op jit(solution)/shard_map/ppermute | solution.py:73

commit v17 on v16

--- a/solution.py
+++ b/solution.py
@@ -104,13 +104,12 @@
     count = lax.axis_size("tp")
     me = lax.axis_index("tp")
     held = x[None]
-    bit = count // 2
-    while bit:
+    bit = 1
+    while bit < count:
         got = lax.ppermute(held, "tp", [(i, i ^ bit) for i in range(count)])
         upper = (me & bit) != 0
-        held = jnp.where(upper, jnp.stack([got, held], axis=1), jnp.stack([held, got], axis=1))
-        held = held.reshape((-1,) + x.shape)
-        bit //= 2
+        held = jnp.where(upper, jnp.concatenate([got, held]), jnp.concatenate([held, got]))
+        bit *= 2
     return held.reshape((-1,) + x.shape[1:])
 
 

time: 140 us -> 139 us (level)
  Pallas kernels: 15.3 us -> 13.5 us
    ppermute x3, waiting for transfers between devices: 27.7 us -> 24.9 us  [reduce_scatter_tp(): held = keep + lax.ppermute(send, 'tp', [(i, i ^ bit) for i in range(count)])]
    ppermute x13, starting transfers between devices: 16.7 us -> 19.3 us  [_swap(): return lax.ppermute(x, 'blk', [(i, i ^ bit) for i in range(count)])]
    ppermute x3, starting transfers between devices: 9.19 us -> 6.87 us  [reduce_scatter_tp(): held = keep + lax.ppermute(send, 'tp', [(i, i ^ bit) for i in range(count)])]
    pallas_call x1, Pallas kernels: 15.3 us -> 13.5 us  [gather_axis(): pl.pallas_call(functools.partial(_gather_kernel, axis, n), out_shape=jax....]
    ppermute x3, waiting for transfers between devices: 2.15 us -> 3.84 us  [gather_tp(): got = lax.ppermute(held, 'tp', [(i, i ^ bit) for i in range(count)])]
  transfers between devices with their start and end apart: 19 -> 19, of which waited for: 13 -> 12; matrix products, arithmetic and copies ran while one was open for 16% -> 16% of each run, Pallas kernels for 0% -> 0%
where the time goes in v17:
time: 139 us; the launch traced here: 137 us
  waiting for transfers between devices  61.7 us (44%)
  starting transfers between devices  31.7 us (23%)
  Pallas kernels  13.5 us (10%)
  matrix products  10.4 us (7%)
  local copies, waits for them, and re-layouts  10.3 us (7%)
  other arithmetic  8.24 us (6%)
    ppermute x13, waiting for transfers between devices, _swap(): return lax.ppermute(x, 'blk', [(i, i ^ bit) for i in range(count)])  33 us
    ppermute x3, waiting for transfers between devices, reduce_scatter_tp(): held = keep + lax.ppermute(send, 'tp', [(i, i ^ bit) for i in range(count)])  24.9 us
    ppermute x13, starting transfers between devices, _swap(): return lax.ppermute(x, 'blk', [(i, i ^ bit) for i in range(count)])  19.3 us
    pallas_call x1, Pallas kernels, gather_axis(): pl.pallas_call(functools.partial(_gather_kernel, axis, n), out_shape=jax....  13.5 us
    ppermute x3, starting transfers between devices, reduce_scatter_tp(): held = keep + lax.ppermute(send, 'tp', [(i, i ^ bit) for i in range(count)])  6.87 us
    ppermute x3, starting transfers between devices, gather_tp(): got = lax.ppermute(held, 'tp', [(i, i ^ bit) for i in range(count)])  5.5 us
    dot_general x1, matrix products, on_device(): jnp.dot(tokens, weight, preferred_element_type=f32)  4.8 us
    ppermute x3, waiting for transfers between devices, gather_tp(): got = lax.ppermute(held, 'tp', [(i, i ^ bit) for i in range(count)])  3.84 us
  transfers between devices with their start and end apart: 19, of which 12 were waited for; matrix products, arithmetic and copies ran while one was open for 16% of the time, Pallas kernels for 0%

profile of v17, /device:TPU:2, one launch (start us, length us, event | category | flops | bytes accessed | tf_op | source)
XLA Modules:
  0.0 136.8 jit_solution(8258114731045014532)
XLA Ops:
  0.6 2.4 %collective-permute-start = (s32[2]{0:T(128)}, s32[2]{0:T(128)S(1)}, u32[]{:S(2)}, u32[]{:S(2)}) collective-permute-start(s32[2]{0:T(128)} %bitcast.106), channel_id=1, source_target_pairs={{0,128},{8,136},{16,144},{24,152},{32,160},{40,168},{48,176},{56,1... | collective-permute-start | bytes 32 | tf_op jit(solution)/shard_map/ppermute | solution.py:73
  3.0 1.0 copy.26
  4.9 7.0 %collective-permute-start.1 = (bf16[1,288,128]{2,1,0:T(8,128)(2,1)S(1)}, bf16[1,288,128]{2,1,0:T(8,128)(2,1)S(1)}, u32[]{:S(2)}, u32[]{:S(2)}) collective-permute-start(bf16[1,288,128]{2,1,0:T(8,128)(2,1)S(1)} %pad_maximum_fusion.3), channel_id=1, source_target_pairs={{0,64},{8,72},{16,80},{24,88},{32,96},{40,104},{48,112},{56,120},{... | collective-permute-start | bytes 221192 | tf_op jit(solution)/shard_map/ppermute | solution.py:73
  12.0 4.8 %fusion.33 = f32[256,2048]{1,0:T(8,128)} fusion(bf16[256,1024]{1,0:T(8,128)(2,1)S(1)} %copy-done, bf16[1024,2048]{1,0:T(8,128)(2,1)} %param.9), kind=kOutput, calls=%fused_computation.108 | convolution fusion | flops 1073741824 | bytes 6815744 | tf_op jit(solution)/shard_map/dot_general | solution.py:209
  17.5 1.6 %collective-permute-start.2 = (bf16[2,288,128]{2,1,0:T(8,128)(2,1)S(1)}, bf16[2,288,128]{2,1,0:T(8,128)(2,1)S(1)}, u32[]{:S(2)}, u32[]{:S(2)}) collective-permute-start(bf16[2,288,128]{2,1,0:T(8,128)(2,1)S(1)} %maximum_select_fusion.5), channel_id=1, source_target_pairs={{0,32},{8,40},{16,48},{24,56},{32,0},{40,8},{48,16},{56,24},{64,96... | collective-permute-start | bytes 442376 | tf_op jit(solution)/shard_map/ppermute | solution.py:73
  19.1 3.0 %collective-permute-start.11 = (bf16[2,32,2048]{2,1,0:T(8,128)(2,1)S(1)}, bf16[2,32,2048]{2,1,0:T(8,128)(2,1)S(1)}, u32[]{:S(2)}, u32[]{:S(2)}) collective-permute-start(bf16[2,32,2048]{2,1,0:T(8,128)(2,1)S(1)} %maximum_select_fusion.4), channel_id=1, source_target_pairs={{0,2},{1,3},{2,0},{3,1},{4,6},{5,7},{6,4},{7,5},{8,10},{9,11},{10,... | collective-permute-start | bytes 786440 | tf_op jit(solution)/shard_map/ppermute | solution.py:109
  22.1 5.3 %collective-permute-done.2 = bf16[2,288,128]{2,1,0:T(8,128)(2,1)S(1)} collective-permute-done((bf16[2,288,128]{2,1,0:T(8,128)(2,1)S(1)}, bf16[2,288,128]{2,1,0:T(8,128)(2,1)S(1)}, u32[]{:S(2)}, u32[]{:S(2)}) %collective-permute-start.2) | collective-permute-done | bytes 147488 | tf_op jit(solution)/shard_map/ppermute | solution.py:73
  27.6 1.1 collective-permute-done.11
  28.8 2.5 %collective-permute-start.12 = (bf16[4,32,2048]{2,1,0:T(8,128)(2,1)S(1)}, bf16[4,32,2048]{2,1,0:T(8,128)(2,1)S(1)}, u32[]{:S(2)}, u32[]{:S(2)}) collective-permute-start(bf16[4,32,2048]{2,1,0:T(8,128)(2,1)S(1)} %maximum_select_fusion.2), channel_id=1, source_target_pairs={{0,4},{1,5},{2,6},{3,7},{4,0},{5,1},{6,2},{7,3},{8,12},{9,13},{10,... | collective-permute-start | bytes 1572872 | tf_op jit(solution)/shard_map/ppermute | solution.py:109
  31.3 4.8 %collective-permute-done.3 = bf16[4,288,128]{2,1,0:T(8,128)(2,1)S(1)} collective-permute-done((bf16[4,288,128]{2,1,0:T(8,128)(2,1)S(1)}, bf16[4,288,128]{2,1,0:T(8,128)(2,1)S(1)}, u32[]{:S(2)}, u32[]{:S(2)}) %collective-permute-start.3) | collective-permute-done | bytes 294944 | tf_op jit(solution)/shard_map/ppermute | solution.py:73
  38.7 1.6 %collective-permute-start.6 = (bf16[2,288,128]{2,1,0:T(8,128)(2,1)S(1)}, bf16[2,288,128]{2,1,0:T(8,128)(2,1)S(1)}, u32[]{:S(2)}, u32[]{:S(2)}) collective-permute-start(bf16[2,288,128]{2,1,0:T(8,128)(2,1)S(1)} %slice.142), channel_id=1, source_target_pairs={{0,128},{8,136},{16,144},{24,152},{32,160},{40,168},{48,176},{56,1... | collective-permute-start | bytes 442376 | tf_op jit(solution)/shard_map/ppermute | solution.py:73
  40.3 2.8 %collective-permute-done.12 = bf16[4,32,2048]{2,1,0:T(8,128)(2,1)S(1)} collective-permute-done((bf16[4,32,2048]{2,1,0:T(8,128)(2,1)S(1)}, bf16[4,32,2048]{2,1,0:T(8,128)(2,1)S(1)}, u32[]{:S(2)}, u32[]{:S(2)}) %collective-permute-start.12) | collective-permute-done | bytes 524320 | tf_op jit(solution)/shard_map/ppermute | solution.py:109
  43.2 3.7 %collective-permute-done.6 = bf16[2,288,128]{2,1,0:T(8,128)(2,1)S(1)} collective-permute-done((bf16[2,288,128]{2,1,0:T(8,128)(2,1)S(1)}, bf16[2,288,128]{2,1,0:T(8,128)(2,1)S(1)}, u32[]{:S(2)}, u32[]{:S(2)}) %collective-permute-start.6) | collective-permute-done | bytes 147488 | tf_op jit(solution)/shard_map/ppermute | solution.py:73
  48.8 13.5 %shard_map.93 = f32[8,192,128]{2,1,0:T(8,128)} custom-call(f32[192,128]{1,0:T(8,128)} %pad_maximum_fusion.2.x_ref), custom_call_target="tpu_custom_call" | custom-call | tf_op jit(solution)/shard_map/pallas_call | solution.py:58
  62.3 1.1 slice_reduce_fusion
  65.4 1.9 %collective-permute-start.14 = (f32[2,288,128]{2,1,0:T(8,128)S(1)}, f32[2,288,128]{2,1,0:T(8,128)S(1)}, u32[]{:S(2)}, u32[]{:S(2)}) collective-permute-start(f32[2,288,128]{2,1,0:T(8,128)S(1)} %bitcast.87), channel_id=1, source_target_pairs={{0,128},{8,136},{16,144},{24,152},{32,160},{40,168},{48,176},{56,1... | collective-permute-start | bytes 884744 | tf_op jit(solution)/shard_map/ppermute | solution.py:73
  67.4 1.8 %fusion.31 = (f32[2,1,2,32,2048]{4,3,2,1,0:T(8,128)S(1)}, f32[2,1,2,32,2048]{4,3,2,1,0:T(8,128)S(1)}) fusion(f32[2,2,2,32,2048]{4,3,2,1,0:T(8,128)} %bitcast.90), kind=kLoop, calls=%fused_computation.106 | loop fusion | bytes 4194304 | tf_op jit(solution)/shard_map/slice | solution.py:128
  69.1 3.3 %collective-permute-done.14 = f32[2,288,128]{2,1,0:T(8,128)S(1)} collective-permute-done((f32[2,288,128]{2,1,0:T(8,128)S(1)}, f32[2,288,128]{2,1,0:T(8,128)S(1)}, u32[]{:S(2)}, u32[]{:S(2)}) %collective-permute-start.14) | collective-permute-done | bytes 294944 | tf_op jit(solution)/shard_map/ppermute | solution.py:73
  72.7 3.2 %collective-permute-start.7 = (f32[2,2,32,2048]{3,2,0,1:T(8,128)S(1)}, f32[2,2,32,2048]{3,2,0,1:T(8,128)S(1)}, u32[]{:S(2)}, u32[]{:S(2)}) collective-permute-start(f32[2,2,32,2048]{3,2,0,1:T(8,128)S(1)} %select_bitcast_fusion), channel_id=1, source_target_pairs={{0,2},{1,3},{2,0},{3,1},{4,6},{5,7},{6,4},{7,5},{8,10},{9,11},{10,... | collective-permute-start | bytes 3145736 | tf_op jit(solution)/shard_map/ppermute | solution.py:132
  76.3 1.1 select_reduce_fusion
  78.3 1.7 %collective-permute-start.16 = (f32[4,288,128]{2,1,0:T(8,128)}, f32[4,288,128]{2,1,0:T(8,128)S(1)}, u32[]{:S(2)}, u32[]{:S(2)}) collective-permute-start(f32[4,288,128]{2,1,0:T(8,128)} %slice_select_fusion), channel_id=1, source_target_pairs={{0,16},{8,24},{16,0},{24,8},{32,48},{40,56},{48,32},{56,40},{64,80... | collective-permute-start | bytes 1769480 | tf_op jit(solution)/shard_map/ppermute | solution.py:73
  80.0 20.0 %collective-permute-done.7 = f32[2,2,32,2048]{3,2,0,1:T(8,128)S(1)} collective-permute-done((f32[2,2,32,2048]{3,2,0,1:T(8,128)S(1)}, f32[2,2,32,2048]{3,2,0,1:T(8,128)S(1)}, u32[]{:S(2)}, u32[]{:S(2)}) %collective-permute-start.7) | collective-permute-done | bytes 1048608 | tf_op jit(solution)/shard_map/ppermute | solution.py:132
  101.0 2.0 %collective-permute-start.8 = (f32[2,32,2048]{2,1,0:T(8,128)}, f32[2,32,2048]{2,1,0:T(8,128)}, u32[]{:S(2)}, u32[]{:S(2)}) collective-permute-start(f32[2,32,2048]{2,1,0:T(8,128)} %select_bitcast_fusion.1), channel_id=1, source_target_pairs={{0,1},{1,0},{2,3},{3,2},{4,5},{5,4},{6,7},{7,6},{8,9},{9,8},{10,11... | collective-permute-start | bytes 1572872 | tf_op jit(solution)/shard_map/ppermute | solution.py:132
  103.0 2.1 %fusion = bf16[256,1024]{1,0:T(8,128)(2,1)} fusion(f32[256,1024]{1,0:T(8,128)S(1)} %bitcast.96, bf16[256,2048]{1,0:T(8,128)(2,1)S(1)} %bitcast.95, bf16[1024,2048]{1,0:T(8,128)(2,1)S(1)} %copy-done.5), kind=kOutput, calls=%fused_computation.5 | convolution fusion | flops 1074266112 | bytes 6815744 | tf_op jit(solution)/shard_map/dot_general | solution.py:237
  105.1 1.0 slice.198
  107.8 1.0 convolution_bitcast_fusion
  108.9 2.2 %collective-permute-start.17 = (f32[2,288,128]{2,1,0:T(8,128)S(1)}, f32[2,288,128]{2,1,0:T(8,128)S(1)}, u32[]{:S(2)}, u32[]{:S(2)}) collective-permute-start(f32[2,288,128]{2,1,0:T(8,128)S(1)} %slice_select_fusion.1), channel_id=1, source_target_pairs={{0,32},{8,40},{16,48},{24,56},{32,0},{40,8},{48,16},{56,24},{64,96... | collective-permute-start | bytes 884744 | tf_op jit(solution)/shard_map/ppermute | solution.py:73
  111.1 4.2 %collective-permute-done.8 = f32[2,32,2048]{2,1,0:T(8,128)} collective-permute-done((f32[2,32,2048]{2,1,0:T(8,128)}, f32[2,32,2048]{2,1,0:T(8,128)}, u32[]{:S(2)}, u32[]{:S(2)}) %collective-permute-start.8) | collective-permute-done | bytes 524320 | tf_op jit(solution)/shard_map/ppermute | solution.py:132
  115.3 1.1 bitcast_add_fusion.1
  116.5 1.7 %collective-permute-start.9 = (f32[32,2048]{1,0:T(8,128)S(1)}, f32[32,2048]{1,0:T(8,128)S(1)}, u32[]{:S(2)}, u32[]{:S(2)}) collective-permute-start(f32[32,2048]{1,0:T(8,128)S(1)} %select_bitcast_fusion.2), channel_id=1, source_target_pairs={{0,4},{1,5},{2,6},{3,7},{4,0},{5,1},{6,2},{7,3},{8,12},{9,13},{10,... | collective-permute-start | bytes 786440 | tf_op jit(solution)/shard_map/ppermute | solution.py:132
  118.2 6.5 %collective-permute-done.17 = f32[2,288,128]{2,1,0:T(8,128)S(1)} collective-permute-done((f32[2,288,128]{2,1,0:T(8,128)S(1)}, f32[2,288,128]{2,1,0:T(8,128)S(1)}, u32[]{:S(2)}, u32[]{:S(2)}) %collective-permute-start.17) | collective-permute-done | bytes 294944 | tf_op jit(solution)/shard_map/ppermute | solution.py:73
  126.3 8.5 %collective-permute-done.18 = f32[1,288,128]{2,1,0:T(8,128)S(1)} collective-permute-done((f32[1,288,128]{2,1,0:T(8,128)S(1)}, f32[1,288,128]{2,1,0:T(8,128)S(1)}, u32[]{:S(2)}, u32[]{:S(2)}) %collective-permute-start.18) | collective-permute-done | bytes 147488 | tf_op jit(solution)/shard_map/ppermute | solution.py:73
  (96 shorter events, 16.5 us)
Async XLA Ops:
  0.6 11.3 %copy-start = (bf16[256,1024]{1,0:T(8,128)(2,1)S(1)}, bf16[256,1024]{1,0:T(8,128)(2,1)}, u32[]{:S(2)}) copy-start(bf16[256,1024]{1,0:T(8,128)(2,1)} %param.8) | copy-start | bytes 1572868
  0.6 16.1 %collective-permute-start = (s32[2]{0:T(128)}, s32[2]{0:T(128)S(1)}, u32[]{:S(2)}, u32[]{:S(2)}) collective-permute-start(s32[2]{0:T(128)} %bitcast.106), channel_id=1, source_target_pairs={{0,128},{8,136},{16,144},{24,152},{32,160},{40,168},{48,176},{56,1... | collective-permute-start | bytes 32 | tf_op jit(solution)/shard_map/ppermute | solution.py:73
  3.0 16.1 %collective-permute-start.10 = (bf16[1,32,2048]{2,1,0:T(8,128)(2,1)}, bf16[1,32,2048]{2,1,0:T(8,128)(2,1)S(1)}, u32[]{:S(2)}, u32[]{:S(2)}) collective-permute-start(bf16[1,32,2048]{2,1,0:T(8,128)(2,1)} %bitcast.101), channel_id=1, source_target_pairs={{0,1},{1,0},{2,3},{3,2},{4,5},{5,4},{6,7},{7,6},{8,9},{9,8},{10,11... | collective-permute-start | bytes 393224 | tf_op jit(solution)/shard_map/ppermute | solution.py:109
  4.9 12.6 %collective-permute-start.1 = (bf16[1,288,128]{2,1,0:T(8,128)(2,1)S(1)}, bf16[1,288,128]{2,1,0:T(8,128)(2,1)S(1)}, u32[]{:S(2)}, u32[]{:S(2)}) collective-permute-start(bf16[1,288,128]{2,1,0:T(8,128)(2,1)S(1)} %pad_maximum_fusion.3), channel_id=1, source_target_pairs={{0,64},{8,72},{16,80},{24,88},{32,96},{40,104},{48,112},{56,120},{... | collective-permute-start | bytes 221192 | tf_op jit(solution)/shard_map/ppermute | solution.py:73
  12.0 4.8 %copy-start.4 = (s32[2,1]{0,1:T(1,128)S(1)}, s32[2,1]{0,1:T(1,128)}, u32[]{:S(2)}) copy-start(s32[2,1]{0,1:T(1,128)} %param.12) | copy-start | bytes 28
  12.0 7.1 %copy-start.3 = (bf16[32,2048]{1,0:T(8,128)(2,1)S(1)}, bf16[32,2048]{1,0:T(8,128)(2,1)}, u32[]{:S(2)}) copy-start(bf16[32,2048]{1,0:T(8,128)(2,1)} %param.13) | copy-start | bytes 393220
  16.8 5.3 %collective-permute-start.4 = (s32[4]{0:T(128)S(1)}, s32[4]{0:T(128)S(1)}, u32[]{:S(2)}, u32[]{:S(2)}) collective-permute-start(s32[4]{0:T(128)S(1)} %get-tuple-element.20), channel_id=1, source_target_pairs={{0,8},{8,0},{16,24},{24,16},{32,40},{40,32},{48,56},{56,48},{64,72... | collective-permute-start | bytes 56 | tf_op jit(solution)/shard_map/ppermute | solution.py:73
  16.9 20.1 %collective-permute-start.13 = (s32[4]{0:T(128)S(1)}, s32[4]{0:T(128)S(1)}, u32[]{:S(2)}, u32[]{:S(2)}) collective-permute-start(s32[4]{0:T(128)S(1)} %get-tuple-element.19), channel_id=1, source_target_pairs={{0,8},{8,0},{16,24},{24,16},{32,40},{40,32},{48,56},{56,48},{64,72... | collective-permute-start | bytes 56 | tf_op jit(solution)/shard_map/ppermute | solution.py:73
  17.5 9.9 %collective-permute-start.2 = (bf16[2,288,128]{2,1,0:T(8,128)(2,1)S(1)}, bf16[2,288,128]{2,1,0:T(8,128)(2,1)S(1)}, u32[]{:S(2)}, u32[]{:S(2)}) collective-permute-start(bf16[2,288,128]{2,1,0:T(8,128)(2,1)S(1)} %maximum_select_fusion.5), channel_id=1, source_target_pairs={{0,32},{8,40},{16,48},{24,56},{32,0},{40,8},{48,16},{56,24},{64,96... | collective-permute-start | bytes 442376 | tf_op jit(solution)/shard_map/ppermute | solution.py:73
  19.1 9.5 %collective-permute-start.11 = (bf16[2,32,2048]{2,1,0:T(8,128)(2,1)S(1)}, bf16[2,32,2048]{2,1,0:T(8,128)(2,1)S(1)}, u32[]{:S(2)}, u32[]{:S(2)}) collective-permute-start(bf16[2,32,2048]{2,1,0:T(8,128)(2,1)S(1)} %maximum_select_fusion.4), channel_id=1, source_target_pairs={{0,2},{1,3},{2,0},{3,1},{4,6},{5,7},{6,4},{7,5},{8,10},{9,11},{10,... | collective-permute-start | bytes 786440 | tf_op jit(solution)/shard_map/ppermute | solution.py:109
  27.5 8.6 %collective-permute-start.3 = (bf16[4,288,128]{2,1,0:T(8,128)(2,1)S(1)}, bf16[4,288,128]{2,1,0:T(8,128)(2,1)S(1)}, u32[]{:S(2)}, u32[]{:S(2)}) collective-permute-start(bf16[4,288,128]{2,1,0:T(8,128)(2,1)S(1)} %maximum_select_fusion.3), channel_id=1, source_target_pairs={{0,16},{8,24},{16,0},{24,8},{32,48},{40,56},{48,32},{56,40},{64,80... | collective-permute-start | bytes 884744 | tf_op jit(solution)/shard_map/ppermute | solution.py:73
  28.8 14.3 %collective-permute-start.12 = (bf16[4,32,2048]{2,1,0:T(8,128)(2,1)S(1)}, bf16[4,32,2048]{2,1,0:T(8,128)(2,1)S(1)}, u32[]{:S(2)}, u32[]{:S(2)}) collective-permute-start(bf16[4,32,2048]{2,1,0:T(8,128)(2,1)S(1)} %maximum_select_fusion.2), channel_id=1, source_target_pairs={{0,4},{1,5},{2,6},{3,7},{4,0},{5,1},{6,2},{7,3},{8,12},{9,13},{10,... | collective-permute-start | bytes 1572872 | tf_op jit(solution)/shard_map/ppermute | solution.py:109
  36.9 1.7 %collective-permute-start.5 = (bf16[4,288,128]{2,1,0:T(8,128)(2,1)S(1)}, bf16[4,288,128]{2,1,0:T(8,128)(2,1)S(1)}, u32[]{:S(2)}, u32[]{:S(2)}) collective-permute-start(bf16[4,288,128]{2,1,0:T(8,128)(2,1)S(1)} %select_select_fusion), channel_id=1, source_target_pairs={{0,8},{8,0},{16,24},{24,16},{32,40},{40,32},{48,56},{56,48},{64,72... | collective-permute-start | bytes 884744 | tf_op jit(solution)/shard_map/ppermute | solution.py:73
  38.7 8.2 %collective-permute-start.6 = (bf16[2,288,128]{2,1,0:T(8,128)(2,1)S(1)}, bf16[2,288,128]{2,1,0:T(8,128)(2,1)S(1)}, u32[]{:S(2)}, u32[]{:S(2)}) collective-permute-start(bf16[2,288,128]{2,1,0:T(8,128)(2,1)S(1)} %slice.142), channel_id=1, source_target_pairs={{0,128},{8,136},{16,144},{24,152},{32,160},{40,168},{48,176},{56,1... | collective-permute-start | bytes 442376 | tf_op jit(solution)/shard_map/ppermute | solution.py:73
  43.2 20.5 %copy-start.1 = (bf16[8,32,2048]{2,1,0:T(8,128)(2,1)}, bf16[8,32,2048]{2,1,0:T(8,128)(2,1)S(1)}, u32[]{:S(2)}) copy-start(bf16[8,32,2048]{2,1,0:T(8,128)(2,1)S(1)} %maximum_select_fusion) | copy-start | bytes 3145732
  65.4 7.0 %collective-permute-start.14 = (f32[2,288,128]{2,1,0:T(8,128)S(1)}, f32[2,288,128]{2,1,0:T(8,128)S(1)}, u32[]{:S(2)}, u32[]{:S(2)}) collective-permute-start(f32[2,288,128]{2,1,0:T(8,128)S(1)} %bitcast.87), channel_id=1, source_target_pairs={{0,128},{8,136},{16,144},{24,152},{32,160},{40,168},{48,176},{56,1... | collective-permute-start | bytes 884744 | tf_op jit(solution)/shard_map/ppermute | solution.py:73
  72.5 3.8 %collective-permute-start.15 = (f32[4,288,128]{2,1,0:T(8,128)S(1)}, f32[4,288,128]{2,1,0:T(8,128)S(1)}, u32[]{:S(2)}, u32[]{:S(2)}) collective-permute-start(f32[4,288,128]{2,1,0:T(8,128)S(1)} %pad_maximum_fusion.1), channel_id=1, source_target_pairs={{0,8},{8,0},{16,24},{24,16},{32,40},{40,32},{48,56},{56,48},{64,72... | collective-permute-start | bytes 1769480 | tf_op jit(solution)/shard_map/ppermute | solution.py:73
  72.7 27.3 %collective-permute-start.7 = (f32[2,2,32,2048]{3,2,0,1:T(8,128)S(1)}, f32[2,2,32,2048]{3,2,0,1:T(8,128)S(1)}, u32[]{:S(2)}, u32[]{:S(2)}) collective-permute-start(f32[2,2,32,2048]{3,2,0,1:T(8,128)S(1)} %select_bitcast_fusion), channel_id=1, source_target_pairs={{0,2},{1,3},{2,0},{3,1},{4,6},{5,7},{6,4},{7,5},{8,10},{9,11},{10,... | collective-permute-start | bytes 3145736 | tf_op jit(solution)/shard_map/ppermute | solution.py:132
  78.3 24.7 %copy-start.2 = (bf16[8,32,2048]{2,1,0:T(8,128)(2,1)S(1)}, bf16[8,32,2048]{2,1,0:T(8,128)(2,1)}, u32[]{:S(2)}) copy-start(bf16[8,32,2048]{2,1,0:T(8,128)(2,1)} %copy-done.1) | copy-start | bytes 3145732
  78.3 24.7 %copy-start.5 = (bf16[1024,2048]{1,0:T(8,128)(2,1)S(1)}, bf16[1024,2048]{1,0:T(8,128)(2,1)}, u32[]{:S(2)}) copy-start(bf16[1024,2048]{1,0:T(8,128)(2,1)} %param.9) | copy-start | bytes 12582916
  78.3 30.4 %collective-permute-start.16 = (f32[4,288,128]{2,1,0:T(8,128)}, f32[4,288,128]{2,1,0:T(8,128)S(1)}, u32[]{:S(2)}, u32[]{:S(2)}) collective-permute-start(f32[4,288,128]{2,1,0:T(8,128)} %slice_select_fusion), channel_id=1, source_target_pairs={{0,16},{8,24},{16,0},{24,8},{32,48},{40,56},{48,32},{56,40},{64,80... | collective-permute-start | bytes 1769480 | tf_op jit(solution)/shard_map/ppermute | solution.py:73
  101.0 14.3 %collective-permute-start.8 = (f32[2,32,2048]{2,1,0:T(8,128)}, f32[2,32,2048]{2,1,0:T(8,128)}, u32[]{:S(2)}, u32[]{:S(2)}) collective-permute-start(f32[2,32,2048]{2,1,0:T(8,128)} %select_bitcast_fusion.1), channel_id=1, source_target_pairs={{0,1},{1,0},{2,3},{3,2},{4,5},{5,4},{6,7},{7,6},{8,9},{9,8},{10,11... | collective-permute-start | bytes 1572872 | tf_op jit(solution)/shard_map/ppermute | solution.py:132
  108.9 15.9 %collective-permute-start.17 = (f32[2,288,128]{2,1,0:T(8,128)S(1)}, f32[2,288,128]{2,1,0:T(8,128)S(1)}, u32[]{:S(2)}, u32[]{:S(2)}) collective-permute-start(f32[2,288,128]{2,1,0:T(8,128)S(1)} %slice_select_fusion.1), channel_id=1, source_target_pairs={{0,32},{8,40},{16,48},{24,56},{32,0},{40,8},{48,16},{56,24},{64,96... | collective-permute-start | bytes 884744 | tf_op jit(solution)/shard_map/ppermute | solution.py:73
  116.5 9.1 %collective-permute-start.9 = (f32[32,2048]{1,0:T(8,128)S(1)}, f32[32,2048]{1,0:T(8,128)S(1)}, u32[]{:S(2)}, u32[]{:S(2)}) collective-permute-start(f32[32,2048]{1,0:T(8,128)S(1)} %select_bitcast_fusion.2), channel_id=1, source_target_pairs={{0,4},{1,5},{2,6},{3,7},{4,0},{5,1},{6,2},{7,3},{8,12},{9,13},{10,... | collective-permute-start | bytes 786440 | tf_op jit(solution)/shard_map/ppermute | solution.py:132
  124.8 10.0 %collective-permute-start.18 = (f32[1,288,128]{2,1,0:T(8,128)S(1)}, f32[1,288,128]{2,1,0:T(8,128)S(1)}, u32[]{:S(2)}, u32[]{:S(2)}) collective-permute-start(f32[1,288,128]{2,1,0:T(8,128)S(1)} %slice_select_fusion.3), channel_id=1, source_target_pairs={{0,64},{8,72},{16,80},{24,88},{32,96},{40,104},{48,112},{56,120},{... | collective-permute-start | bytes 442376 | tf_op jit(solution)/shard_map/ppermute | solution.py:73
